TPU v7x, 32 devices: a whole 2x2x4 slice. The times are simulated.
32 devices in a mesh: dp: 4 (over y, x), ctx: 8 (over z, core).
Axes of the slice: x: 2, y: 2, z: 4, core: 2. Of those that a mesh axis runs over, the one named last changes fastest.
Arguments:
- queries: bfloat16 [4096, 4096], P(('dp', 'ctx')), may hold values from -30 to 30
- key_input: bfloat16 [4096, 1024], P(('dp', 'ctx')), may hold values from -30 to 30
- value_input: bfloat16 [4096, 1024], P(('dp', 'ctx')), may hold values from -6 to 6
- out_grad: bfloat16 [4096, 4096], P(('dp', 'ctx')), may hold values from -6 to 6
- sink_logits: float32 [32], replicated, may hold values from 0 to 5
- doc_lengths: int32 [4, 4], replicated, may hold values from 1 to 4, 8 in all within a row
- assignment: int32 [4], replicated, may hold values from 0 to 3, each once
- stretch_map: int32 [16], replicated, may hold values from 0 to 15, each once
Outputs:
- attn_out: bfloat16 [4096, 4096], P(('dp', 'ctx'))
- query_grad: bfloat16 [4096, 4096], P(('dp', 'ctx'))
- key_grad: bfloat16 [4096, 1024], P(('dp', 'ctx'))
- value_grad: bfloat16 [4096, 1024], P(('dp', 'ctx'))
- sink_grad: float32 [32], replicated
Inputs may be any that keep to these rules, and one draw needn't show every extreme that they name: `doc_lengths`: lengths count blocks of 128 tokens; every row sums to 8 and its longest document has exactly 4 blocks. `assignment`: A permutation of the sequences. `stretch_map`: A permutation of the stretches, the same for every sequence.
All inputs are finite; a program needn't handle non-finite values.
Results may differ from a plain program's by a relative error of at most 0.019.
Values may be sent and summed in bfloat16 or wider, within the bound.
No kernel may reach another device: no remote copies, remote signals or barrier semaphores. Data moves between devices by JAX's collectives and lax.ppermute only.
A program may use at most 128 MiB of HBM per device.

v0:
```python
import jax
import jax.numpy as jnp
from jax import lax
from jax.sharding import PartitionSpec as P

HD = 128
BLOCK = 128


def true_positions(row_count, stretch_len, stretch_map):
    grid_shape = (row_count, stretch_map.shape[0])
    owners = lax.broadcasted_iota(jnp.int32, grid_shape, 0) // stretch_len
    picked = owners == lax.broadcasted_iota(jnp.int32, grid_shape, 1)
    leading = jnp.sum(jnp.where(picked, stretch_map[None, :], 0), axis=1)
    return leading * stretch_len + jnp.arange(row_count, dtype=jnp.int32) % stretch_len


def doc_numbers(positions, lengths):
    doc_ends = jnp.cumsum(lengths) * BLOCK
    return jnp.sum((positions[:, None] >= doc_ends[None, :]).astype(jnp.int32), axis=1)


def key_span():
    return 512


def visible(layout, first_row, block_rows):
    query_pos, query_doc, key_pos, key_doc = layout
    block_pos = lax.dynamic_slice_in_dim(key_pos, first_row, block_rows, 0)
    block_doc = lax.dynamic_slice_in_dim(key_doc, first_row, block_rows, 0)
    return (query_doc[:, None] == block_doc[None, :]) & (block_pos[None, :] <= query_pos[:, None])


def block_loop(row_count, advance, initial):
    block_rows = key_span()

    def one_turn(block_index, running):
        first_row = block_index * block_rows
        return advance(first_row, block_rows, running)

    return lax.fori_loop(0, row_count // block_rows, one_turn, initial)


def key_block(table, first_row, block_rows, query_heads):
    return lax.dynamic_slice_in_dim(table, first_row, block_rows, 0).reshape(
        block_rows, query_heads.shape[1], query_heads.shape[3]
    )


def block_scores(query_heads, key_table, first_row, block_rows, layout):
    key_rows = key_block(key_table, first_row, block_rows, query_heads)
    scores = jnp.einsum(
        "tgrd,ngd->tgrn", query_heads, key_rows, preferred_element_type=jnp.float32
    ) * HD ** (-0.5)
    allowed = visible(layout, first_row, block_rows)[:, None, None, :]
    return (scores, allowed, key_rows)


def block_weights(query_heads, key_table, first_row, block_rows, row_max, row_total, layout):
    scores, allowed, key_rows = block_scores(query_heads, key_table, first_row, block_rows, layout)
    weights = jnp.where(allowed, jnp.exp(scores - row_max[..., None]) / row_total[..., None], 0.0)
    return (weights, key_rows)


def softmax_stats(query_heads, key_table, sink_heads, layout):

    def advance(first_row, block_rows, running):
        row_max, row_total = running
        scores, allowed, key_rows = block_scores(
            query_heads, key_table, first_row, block_rows, layout
        )
        block_max = jnp.max(jnp.where(allowed, scores, -jnp.inf), axis=3)
        fresh_max = jnp.maximum(row_max, block_max)
        exp_terms = jnp.where(allowed, jnp.exp(scores - fresh_max[..., None]), 0.0)
        return (fresh_max, row_total * jnp.exp(row_max - fresh_max) + jnp.sum(exp_terms, axis=3))

    start_max = jnp.broadcast_to(sink_heads[None], query_heads.shape[:3])
    start_total = jnp.ones(query_heads.shape[:3], jnp.float32)
    return block_loop(key_table.shape[0], advance, (start_max, start_total))


def attend_values(query_heads, key_table, value_table, row_max, row_total, layout):

    def advance(first_row, block_rows, partial_value):
        weights, key_rows = block_weights(
            query_heads, key_table, first_row, block_rows, row_max, row_total, layout
        )
        value_rows = key_block(value_table, first_row, block_rows, query_heads)
        return partial_value + jnp.einsum(
            "tgrn,ngd->tgrd",
            weights.astype(jnp.bfloat16),
            value_rows,
            preferred_element_type=jnp.float32,
        )

    return block_loop(key_table.shape[0], advance, jnp.zeros(query_heads.shape, jnp.float32))


def backward_block(
    query_heads, grad_heads, key_table, value_table, row_stats, layout, first_row, block_rows
):
    row_max, row_total, row_dot = row_stats
    weights, key_rows = block_weights(
        query_heads, key_table, first_row, block_rows, row_max, row_total, layout
    )
    value_rows = key_block(value_table, first_row, block_rows, query_heads)
    grad_weights = jnp.einsum(
        "tgrd,ngd->tgrn", grad_heads, value_rows, preferred_element_type=jnp.float32
    )
    grad_scores = (weights * (grad_weights - row_dot[..., None]) * HD ** (-0.5)).astype(
        jnp.bfloat16
    )
    return (weights.astype(jnp.bfloat16), grad_scores, key_rows)


def query_grads(query_heads, grad_heads, key_table, value_table, row_stats, layout):

    def advance(first_row, block_rows, partial_value):
        weights_b, grad_scores, key_rows = backward_block(
            query_heads,
            grad_heads,
            key_table,
            value_table,
            row_stats,
            layout,
            first_row,
            block_rows,
        )
        return partial_value + jnp.einsum(
            "tgrn,ngd->tgrd", grad_scores, key_rows, preferred_element_type=jnp.float32
        )

    return block_loop(key_table.shape[0], advance, jnp.zeros(query_heads.shape, jnp.float32))


def key_grads(query_heads, grad_heads, key_table, value_table, row_stats, layout):
    grad_shape = (key_table.shape[0], query_heads.shape[1], query_heads.shape[3])

    def advance(first_row, block_rows, running):
        key_sum, value_sum = running
        weights_b, grad_scores, key_rows = backward_block(
            query_heads,
            grad_heads,
            key_table,
            value_table,
            row_stats,
            layout,
            first_row,
            block_rows,
        )
        key_part = jnp.einsum(
            "tgrn,tgrd->ngd", grad_scores, query_heads, preferred_element_type=jnp.float32
        )
        value_part = jnp.einsum(
            "tgrn,tgrd->ngd", weights_b, grad_heads, preferred_element_type=jnp.float32
        )
        return (
            lax.dynamic_update_slice_in_dim(key_sum, key_part, first_row, 0),
            lax.dynamic_update_slice_in_dim(value_sum, value_part, first_row, 0),
        )

    initial = (jnp.zeros(grad_shape, jnp.float32), jnp.zeros(grad_shape, jnp.float32))
    return block_loop(key_table.shape[0], advance, initial)


def per_device(
    queries, key_input, value_input, out_grad, sink_logits, doc_lengths, assignment, stretch_map
):
    local_rows = queries.shape[0]
    ctx_size = lax.axis_size("ctx")
    seq_rows = local_rows * ctx_size
    head_count = sink_logits.shape[0]
    kv_heads = key_input.shape[1] // HD
    group_size = head_count // kv_heads
    group_index = lax.axis_index("dp")
    place_index = lax.axis_index("ctx")
    sequence_ids = jnp.arange(doc_lengths.shape[0], dtype=jnp.int32)
    chosen = jnp.sum(jnp.where(sequence_ids == group_index, assignment, 0))
    lengths = jnp.sum(jnp.where((sequence_ids == chosen)[:, None], doc_lengths, 0), axis=0)
    positions = true_positions(seq_rows, local_rows // 2, stretch_map)
    documents = doc_numbers(positions, lengths)
    whole_keys, whole_values = (
        lax.all_gather(key_input, "ctx", axis=0, tiled=True),
        lax.all_gather(value_input, "ctx", axis=0, tiled=True),
    )
    query_heads = queries.reshape(local_rows, kv_heads, group_size, HD)
    grad_heads = out_grad.reshape(local_rows, kv_heads, group_size, HD)
    sink_heads = sink_logits.reshape(kv_heads, group_size)
    query_pos = lax.dynamic_slice_in_dim(positions, place_index * local_rows, local_rows, 0)
    query_doc = lax.dynamic_slice_in_dim(documents, place_index * local_rows, local_rows, 0)
    layout = (query_pos, query_doc, positions, documents)
    row_max, row_total = softmax_stats(query_heads, whole_keys, sink_heads, layout)
    attn_heads = attend_values(
        query_heads, whole_keys, whole_values, row_max, row_total, layout
    ).astype(jnp.bfloat16)
    row_dot = jnp.sum(grad_heads.astype(jnp.float32) * attn_heads.astype(jnp.float32), axis=3)
    partial_sink = (
        -jnp.sum(jnp.exp(sink_heads[None] - row_max) / row_total * row_dot, axis=0)
    ).reshape(head_count)
    row_stats = (row_max, row_total, row_dot)
    query_sum = query_grads(query_heads, grad_heads, whole_keys, whole_values, row_stats, layout)
    local_layout = (query_pos, query_doc, positions, documents)
    key_sum, value_sum = key_grads(
        query_heads, grad_heads, whole_keys, whole_values, row_stats, local_layout
    )
    summed = lax.psum_scatter(
        jnp.stack(
            (
                key_sum.reshape(lax.axis_size("ctx") * local_rows, -1),
                value_sum.reshape(lax.axis_size("ctx") * local_rows, -1),
            ),
            axis=1,
        ),
        "ctx",
        scatter_dimension=0,
        tiled=True,
    )
    attn_out = attn_heads.reshape(local_rows, head_count * HD)
    query_grad = query_sum.astype(jnp.bfloat16).reshape(local_rows, head_count * HD)
    key_grad = summed[:, 0, :].astype(jnp.bfloat16)
    value_grad = summed[:, 1, :].astype(jnp.bfloat16)
    sink_grad = lax.psum(partial_sink, ("dp", "ctx"))
    return (attn_out, query_grad, key_grad, value_grad, sink_grad)


def solution(mesh):
    placed = (
        P(("dp", "ctx"), None),
        P(("dp", "ctx"), None),
        P(("dp", "ctx"), None),
        P(("dp", "ctx"), None),
        P(),
        P(),
        P(),
        P(),
    )
    return jax.shard_map(
        per_device,
        mesh=mesh,
        in_specs=placed,
        out_specs=(
            P(("dp", "ctx"), None),
            P(("dp", "ctx"), None),
            P(("dp", "ctx"), None),
            P(("dp", "ctx"), None),
            P(),
        ),
        check_vma=False,
    )
```

profile of v0, /device:TPU:0, one launch (start us, length us, event | category | flops | bytes accessed | tf_op | source)
XLA Modules:
  0.0 268.9 jit_solution(8948219369799919933)
XLA Ops:
  7.2 1.9 copy.93
  9.2 1.8 copy.92
  15.0 1.6 copy.94
  18.1 1.3 copy.101
  19.4 24.4 %all-gather.5.cloned.1.call-done = bf16[1024,1024]{0,1:T(8,128)(2,1)} async-done(((bf16[128,1024]{0,1:T(8,128)(2,1)}), bf16[1024,1024]{0,1:T(8,128)(2,1)}) %all-gather.5.cloned.1.call-update) | async-done | bytes 2097168 | tf_op jit(solution)/shard_map/all_gather | solution.py:183
  43.8 10.1 %while.60 = (s32[]{:T(128)}, f32[128,8,4]{0,2,1:T(4,128)S(1)}, f32[128,8,4]{0,2,1:T(4,128)S(1)}, s32[128]{0:T(128)S(1)}, s32[1024]{0:T(1024)S(1)}, /*index=5*/s3...) while((s32[]{:T(128)}, f32[128,8,4]{0,2,1:T(4,128)S(1)}, ...), condition=%wide.region_8.9_spmd.clone, body=%wide.region_5.8_spmd.clone.sunk | while | flops 551759872 | bytes 21394624 | solution.py:41
  45.5 1.5 fusion.118
  47.0 1.8 fusion.119
  50.6 1.5 fusion.118
  52.0 1.8 fusion.119
  53.9 21.9 %all-gather.3.cloned.1.call-done = bf16[1024,1024]{0,1:T(8,128)(2,1)} async-done(((bf16[128,1024]{0,1:T(8,128)(2,1)}), bf16[1024,1024]{0,1:T(8,128)(2,1)}) %all-gather.3.cloned.1.call-update) | async-done | bytes 2097168 | tf_op jit(solution)/shard_map/all_gather | solution.py:184
  75.9 13.1 %while.61 = (s32[]{:T(128)}, f32[128,8,4,128]{0,3,2,1:T(8,128)}, bf16[1024,1024]{0,1:T(8,128)(2,1)}, s32[128]{0:T(128)S(1)}, s32[1024]{0:T(1024)S(1)}, /*index=5...) while((s32[]{:T(128)}, f32[128,8,4,128]{0,3,2,1:T(8,128)}, ...), condition=%wide.region_10.11_spmd.clone, body=%wide.region_9.10_spmd.clone.sunk | while | flops 1085472768 | bytes 11711697 | solution.py:41
  76.2 1.7 constant_dynamic-slice_fusion.15
  77.9 3.9 %bitcast_add_fusion.4 = f32[128,8,4,128]{0,3,2,1:T(8,128)} fusion(f32[128,8,4,128]{0,3,2,1:T(8,128)} %get-tuple-element.1586, bf16[512,8,128,1]{0,2,3,1:T(8,128)(2,1)S(1)} %bitcast.221, f32[128,8,4]{0,2,1:T(4,128)S(1)} %get-tuple-element.1610, f32[128,8,4]{0,2,1:T(4,128)S(1)} %get-tuple-element.1609, pred[128,512]{0,1:T(8,128)(4,1)S(1)} %compare_and_fusion.10, ...), kind=kOutput, calls=%fused_computation.39.clone.1 | convolution fusion | flops 1085276160 | bytes 7438337 | tf_op jit(solution)/shard_map/while/body/eval_jaxpr/tgrn,ngd->tgrd/dot_general | solution.py:89
  82.2 1.7 constant_dynamic-slice_fusion.15
  83.9 5.1 %bitcast_add_fusion.4 = f32[128,8,4,128]{0,3,2,1:T(8,128)} fusion(f32[128,8,4,128]{0,3,2,1:T(8,128)} %get-tuple-element.1586, bf16[512,8,128,1]{0,2,3,1:T(8,128)(2,1)S(1)} %bitcast.221, f32[128,8,4]{0,2,1:T(4,128)S(1)} %get-tuple-element.1610, f32[128,8,4]{0,2,1:T(4,128)S(1)} %get-tuple-element.1609, pred[128,512]{0,1:T(8,128)(4,1)S(1)} %compare_and_fusion.10, ...), kind=kOutput, calls=%fused_computation.39.clone.1 | convolution fusion | flops 1085276160 | bytes 7438337 | tf_op jit(solution)/shard_map/while/body/eval_jaxpr/tgrn,ngd->tgrd/dot_general | solution.py:89
  89.0 3.3 %multiply_reduce_fusion = (f32[128,8,4]{0,2,1:T(4,128)S(1)}, bf16[128,8,4,128]{0,3,2,1:T(8,128)(2,1)}) fusion(bf16[128,4096]{0,1:T(8,128)(2,1)} %copy-done.8, f32[128,8,4,128]{0,3,2,1:T(8,128)} %get-tuple-element.790), kind=kLoop, calls=%fused_computation.62 | loop fusion | flops 2617344 | bytes 4210688 | tf_op jit(solution)/shard_map/reduce_sum | solution.py:196
  92.3 2.4 broadcast.265.clone
  94.6 2.3 broadcast.265.clone2
  96.9 55.1 %while.59 = (s32[]{:T(128)}, f32[1024,8,128]{2,1,0:T(8,128)}, f32[1024,8,128]{2,1,0:T(8,128)}, s32[128]{0:T(128)S(1)}, s32[1024]{0:T(1024)S(1)}, /*index=5*/s32[...) while((s32[]{:T(128)}, f32[1024,8,128]{2,1,0:T(8,128)}, ...), condition=%wide.region_15.16_spmd, body=%wide.region_14.15_spmd.sunk | while | flops 2166554624 | bytes 132314512 | solution.py:41
  97.4 4.5 %fusion.113 = f32[128,8,4,512]{0,3,2,1:T(8,128)} fusion(f32[128,8,4]{0,2,1:T(4,128)S(1)} %get-tuple-element.1712, f32[128,8,4]{0,2,1:T(4,128)S(1)} %get-tuple-element.1711, pred[128,512]{0,1:T(8,128)(4,1)S(1)} %compare_and_fusion.8, bf16[512,8,128,1]{0,2,3,1:T(8,128)(2,1)S(1)} %bitcast.222, bf16[128,8,4,128]{3,0,2,1:T(8,128)(2,1)S(1)} %get-tuple-element.1710), kind=kOutput, calls=%fused_computation.7.clone.1 | convolution fusion | flops 545259520 | bytes 10584064 | tf_op jit(solution)/shard_map/while/body/eval_jaxpr/tgrd,ngd->tgrn/dot_general | solution.py:52
  103.0 7.8 %fusion.115 = f32[512,8,128]{2,0,1:T(8,128)} fusion(bf16[128,8,4,128]{3,0,2,1:T(8,128)(2,1)S(1)} %get-tuple-element.1710, f32[128,8,4,512]{0,3,2,1:T(8,128)} %fusion.113, f32[128,8,4]{0,2,1:T(4,128)S(1)} %get-tuple-element.1715, bf16[512,8,128,1]{0,2,3,1:T(8,128)(2,1)} %bitcast.218, bf16[128,8,4,128]{3,0,2,1:T(8,128)(2,1)} %get-tuple-element.1714), kind=kOutput, calls=%fused_computation.17.clone.1 | convolution fusion | flops 1082130432 | bytes 13647872 | tf_op jit(solution)/shard_map/while/body/eval_jaxpr/tgrn,tgrd->ngd/dot_general | solution.py:151
  110.8 5.0 %fusion.114 = f32[512,8,128]{2,0,1:T(8,128)S(1)} fusion(bf16[128,8,4,128]{3,0,2,1:T(8,128)(2,1)} %get-tuple-element.1714, f32[128,8,4,512]{0,3,2,1:T(8,128)} %fusion.113), kind=kOutput, calls=%fused_computation.16.clone.1 | convolution fusion | flops 538968064 | bytes 11534336 | tf_op jit(solution)/shard_map/while/body/eval_jaxpr/tgrn,tgrd->ngd/dot_general | solution.py:154
  117.5 2.9 %copy_dynamic-update-slice_fusion.3 = (f32[1024,8,128]{2,1,0:T(8,128)S(1)}, f32[1024,8,128]{2,1,0:T(8,128)S(1)}) fusion(f32[1024,8,128]{2,1,0:T(8,128)S(1)} %copy-done.6, s32[]{:T(128)S(6)} %select_n.162, f32[512,8,128]{2,0,1:T(8,128)S(1)} %fusion.114, f32[1024,8,128]{2,1,0:T(8,128)S(1)} %copy-done.4, f32[512,8,128]{2,0,1:T(8,128)S(1)} %copy-done.1), kind=kLoop, calls=%fused_computation.14.clone.1 | loop fusion | bytes 8388612 | tf_op jit(solution)/shard_map/while/body/eval_jaxpr/dynamic_update_slice | solution.py:159
  120.4 2.1 copy-done.5
  122.5 2.0 copy-done.7
  124.9 4.5 %fusion.113 = f32[128,8,4,512]{0,3,2,1:T(8,128)} fusion(f32[128,8,4]{0,2,1:T(4,128)S(1)} %get-tuple-element.1712, f32[128,8,4]{0,2,1:T(4,128)S(1)} %get-tuple-element.1711, pred[128,512]{0,1:T(8,128)(4,1)S(1)} %compare_and_fusion.8, bf16[512,8,128,1]{0,2,3,1:T(8,128)(2,1)S(1)} %bitcast.222, bf16[128,8,4,128]{3,0,2,1:T(8,128)(2,1)S(1)} %get-tuple-element.1710), kind=kOutput, calls=%fused_computation.7.clone.1 | convolution fusion | flops 545259520 | bytes 10584064 | tf_op jit(solution)/shard_map/while/body/eval_jaxpr/tgrd,ngd->tgrn/dot_general | solution.py:52
  130.5 7.8 %fusion.115 = f32[512,8,128]{2,0,1:T(8,128)} fusion(bf16[128,8,4,128]{3,0,2,1:T(8,128)(2,1)S(1)} %get-tuple-element.1710, f32[128,8,4,512]{0,3,2,1:T(8,128)} %fusion.113, f32[128,8,4]{0,2,1:T(4,128)S(1)} %get-tuple-element.1715, bf16[512,8,128,1]{0,2,3,1:T(8,128)(2,1)} %bitcast.218, bf16[128,8,4,128]{3,0,2,1:T(8,128)(2,1)} %get-tuple-element.1714), kind=kOutput, calls=%fused_computation.17.clone.1 | convolution fusion | flops 1082130432 | bytes 13647872 | tf_op jit(solution)/shard_map/while/body/eval_jaxpr/tgrn,tgrd->ngd/dot_general | solution.py:151
  138.3 5.0 %fusion.114 = f32[512,8,128]{2,0,1:T(8,128)S(1)} fusion(bf16[128,8,4,128]{3,0,2,1:T(8,128)(2,1)} %get-tuple-element.1714, f32[128,8,4,512]{0,3,2,1:T(8,128)} %fusion.113), kind=kOutput, calls=%fused_computation.16.clone.1 | convolution fusion | flops 538968064 | bytes 11534336 | tf_op jit(solution)/shard_map/while/body/eval_jaxpr/tgrn,tgrd->ngd/dot_general | solution.py:154
  145.1 2.9 %copy_dynamic-update-slice_fusion.3 = (f32[1024,8,128]{2,1,0:T(8,128)S(1)}, f32[1024,8,128]{2,1,0:T(8,128)S(1)}) fusion(f32[1024,8,128]{2,1,0:T(8,128)S(1)} %copy-done.6, s32[]{:T(128)S(6)} %select_n.162, f32[512,8,128]{2,0,1:T(8,128)S(1)} %fusion.114, f32[1024,8,128]{2,1,0:T(8,128)S(1)} %copy-done.4, f32[512,8,128]{2,0,1:T(8,128)S(1)} %copy-done.1), kind=kLoop, calls=%fused_computation.14.clone.1 | loop fusion | bytes 8388612 | tf_op jit(solution)/shard_map/while/body/eval_jaxpr/dynamic_update_slice | solution.py:159
  147.9 2.1 copy-done.5
  150.0 2.0 copy-done.7
  152.0 4.9 %stack_reshape.6 = f32[1024,1,1024]{2,0,1:T(8,128)} reshape(f32[1024,8,128]{2,1,0:T(8,128)} %get-tuple-element.792) | data formatting | bytes 8388608 | tf_op jit(solution)/shard_map/stack;reshape | solution.py:207
  156.9 4.9 %stack_reshape.7 = f32[1024,1,1024]{2,0,1:T(8,128)} reshape(f32[1024,8,128]{2,1,0:T(8,128)} %get-tuple-element.793) | data formatting | bytes 8388608 | tf_op jit(solution)/shard_map/stack;reshape | solution.py:207
  161.8 8.5 %pad_maximum_fusion = f32[1024,2,1024]{2,0,1:T(8,128)} fusion(f32[1024,1,1024]{2,0,1:T(8,128)} %stack_reshape.7, f32[1024,1,1024]{2,0,1:T(8,128)} %stack_reshape.6), kind=kLoop, calls=%fused_computation.61 | loop fusion | flops 2097152 | bytes 16777216 | tf_op jit(solution)/shard_map/stack | solution.py:207
  172.5 1.3 multiply_reduce_fusion.1
  173.9 42.8 %psum.7 = f32[32]{0:T(128)} all-reduce(f32[32]{0:T(128)S(1)} %neg.8), channel_id=1, replica_groups=mesh['dp'=4,'ctx'=8] {'dp','ctx'}, use_global_device_ids=true, to_apply=%region_18.19 | all-reduce | flops 32 | bytes 256 | tf_op jit(solution)/shard_map/psum | solution.py:222
  216.8 34.3 %while.62 = (s32[]{:T(128)}, f32[128,8,4,128]{0,3,2,1:T(8,128)}, bf16[1024,1024]{0,1:T(8,128)(2,1)S(1)}, s32[128]{0:T(128)S(1)}, s32[1024]{0:T(1024)S(1)}, /*ind...) while((s32[]{:T(128)}, f32[128,8,4,128]{0,3,2,1:T(8,128)}, ...), condition=%wide.region_13.14_spmd.clone, body=%wide.region_12.13_spmd.clone.sunk | while | flops 1628635136 | bytes 34796796 | solution.py:41
  217.1 2.4 constant_dynamic-slice_fusion.16
  219.5 4.6 %fusion.131 = f32[8,512,128,4]{2,1,3,0:T(8,128)} fusion(bf16[512,8,128,1]{0,2,3,1:T(8,128)(2,1)S(1)} %bitcast.215, bf16[128,8,4,128]{3,0,2,1:T(8,128)(2,1)S(1)} %get-tuple-element.1656), kind=kOutput, calls=%fused_computation.87.clone.1 | convolution fusion | flops 536870912 | bytes 10485760 | tf_op jit(solution)/shard_map/while/body/eval_jaxpr/tgrd,ngd->tgrn/dot_general | solution.py:52
  224.1 9.5 %bitcast_add_fusion.5 = f32[128,8,4,128]{0,3,2,1:T(8,128)} fusion(f32[128,8,4,128]{0,3,2,1:T(8,128)} %get-tuple-element.1633, bf16[512,8,128,1]{0,2,3,1:T(8,128)(2,1)} %bitcast.216, f32[8,512,128,4]{2,1,3,0:T(8,128)} %fusion.131, f32[128,8,4]{0,2,1:T(4,128)S(1)} %get-tuple-element.1661, f32[128,8,4]{0,2,1:T(4,128)S(1)} %get-tuple-element.1658, ...), kind=kOutput, calls=%fused_computation.55.clone.1 | convolution fusion | flops 1091567616 | bytes 15843329 | tf_op jit(solution)/shard_map/while/body/eval_jaxpr/tgrn,ngd->tgrd/dot_general | solution.py:129
  234.0 2.4 constant_dynamic-slice_fusion.16
  236.4 4.6 %fusion.131 = f32[8,512,128,4]{2,1,3,0:T(8,128)} fusion(bf16[512,8,128,1]{0,2,3,1:T(8,128)(2,1)S(1)} %bitcast.215, bf16[128,8,4,128]{3,0,2,1:T(8,128)(2,1)S(1)} %get-tuple-element.1656), kind=kOutput, calls=%fused_computation.87.clone.1 | convolution fusion | flops 536870912 | bytes 10485760 | tf_op jit(solution)/shard_map/while/body/eval_jaxpr/tgrd,ngd->tgrn/dot_general | solution.py:52
  241.0 10.1 %bitcast_add_fusion.5 = f32[128,8,4,128]{0,3,2,1:T(8,128)} fusion(f32[128,8,4,128]{0,3,2,1:T(8,128)} %get-tuple-element.1633, bf16[512,8,128,1]{0,2,3,1:T(8,128)(2,1)} %bitcast.216, f32[8,512,128,4]{2,1,3,0:T(8,128)} %fusion.131, f32[128,8,4]{0,2,1:T(4,128)S(1)} %get-tuple-element.1661, f32[128,8,4]{0,2,1:T(4,128)S(1)} %get-tuple-element.1658, ...), kind=kOutput, calls=%fused_computation.55.clone.1 | convolution fusion | flops 1091567616 | bytes 15843329 | tf_op jit(solution)/shard_map/while/body/eval_jaxpr/tgrn,ngd->tgrd/dot_general | solution.py:129
  251.1 1.9 convert_element_type.55
  253.0 1.3 copy.128
  254.3 1.3 copy.111
  255.6 4.6 %reduce-scatter.2.cloned.1.call-done = f32[128,2,1024]{2,0,1:T(8,128)} async-done(((f32[1024,2,1024]{2,0,1:T(8,128)}), f32[128,2,1024]{2,0,1:T(8,128)}) %reduce-scatter.2.cloned.1.call-update) | async-done | bytes 1048592 | tf_op jit(solution)/shard_map/reduce_scatter | solution.py:206
  (106 shorter events, 21.2 us)
Async XLA Ops:
  7.2 10.1 %copy-start.13 = (f32[32]{0:T(128)S(1)}, f32[32]{0:T(128)}, u32[]{:S(2)}) copy-start(f32[32]{0:T(128)} %param.20) | copy-start | bytes 388
  7.2 10.2 %copy-start.10 = (bf16[128,4096]{1,0:T(8,128)(2,1)S(1)}, bf16[128,4096]{1,0:T(8,128)(2,1)}, u32[]{:S(2)}) copy-start(bf16[128,4096]{1,0:T(8,128)(2,1)} %param.19) | copy-start | bytes 3145732
  7.2 36.6 %all-gather.5.cloned.1.call-start = ((), (), s32[]{:S(2)}) async-start(), calls=%async_computation.2 | async-start | bytes 2359296 | tf_op jit(solution)/shard_map/all_gather | solution.py:183
  9.1 66.7 %all-gather.3.cloned.1.call-start = ((), (), s32[]{:S(2)}) async-start(), calls=%async_computation.1 | async-start | bytes 2359296 | tf_op jit(solution)/shard_map/all_gather | solution.py:184
  11.0 249.2 %reduce-scatter.2.cloned.1.call-start = ((), (), s32[]{:S(2)}) async-start(), calls=%async_computation.3 | async-start | bytes 9437184 | tf_op jit(solution)/shard_map/reduce_scatter | solution.py:206
  17.4 26.4 %copy-start.11 = (f32[8,4]{1,0:T(8,128)}, f32[8,4]{1,0:T(8,128)S(1)}, u32[]{:S(2)}) copy-start(f32[8,4]{1,0:T(8,128)S(1)} %broadcast_in_dim.233) | copy-start | bytes 388
  18.0 25.8 %copy-start.8 = (bf16[128,4096]{0,1:T(8,128)(2,1)}, bf16[128,4096]{0,1:T(8,128)(2,1)S(1)}, u32[]{:S(2)}) copy-start(bf16[128,4096]{0,1:T(8,128)(2,1)S(1)} %copy.98) | copy-start | bytes 3145732
  92.3 4.6 %copy-start = (bf16[1024,1024]{0,1:T(8,128)(2,1)S(1)}, bf16[1024,1024]{0,1:T(8,128)(2,1)}, u32[]{:S(2)}) copy-start(bf16[1024,1024]{0,1:T(8,128)(2,1)} %get-tuple-element.1728) | copy-start | bytes 6291460
  97.4 4.5 %copy-start.2 = (bf16[1024,1024]{0,1:T(8,128)(2,1)S(1)}, bf16[1024,1024]{0,1:T(8,128)(2,1)}, u32[]{:S(2)}) copy-start(bf16[1024,1024]{0,1:T(8,128)(2,1)} %get-tuple-element.1713) | copy-start | bytes 6291460 | tf_op jit(solution)/shard_map/while
  110.8 5.0 %copy-start.1 = (f32[512,8,128]{2,0,1:T(8,128)S(1)}, f32[512,8,128]{2,0,1:T(8,128)}, u32[]{:S(2)}) copy-start(f32[512,8,128]{2,0,1:T(8,128)} %fusion.115) | copy-start | bytes 6291460 | tf_op jit(solution)/shard_map/while
  110.8 5.5 %copy-start.4 = (f32[1024,8,128]{2,1,0:T(8,128)S(1)}, f32[1024,8,128]{2,1,0:T(8,128)}, u32[]{:S(2)}) copy-start(f32[1024,8,128]{2,1,0:T(8,128)} %get-tuple-element.1685) | copy-start | bytes 12582916 | tf_op jit(solution)/shard_map/while
  110.8 6.7 %copy-start.6 = (f32[1024,8,128]{2,1,0:T(8,128)S(1)}, f32[1024,8,128]{2,1,0:T(8,128)}, u32[]{:S(2)}) copy-start(f32[1024,8,128]{2,1,0:T(8,128)} %get-tuple-element.1686) | copy-start | bytes 12582916 | tf_op jit(solution)/shard_map/while
  120.4 2.1 copy-start.5
  122.5 2.0 copy-start.7
  124.9 4.5 %copy-start.2 = (bf16[1024,1024]{0,1:T(8,128)(2,1)S(1)}, bf16[1024,1024]{0,1:T(8,128)(2,1)}, u32[]{:S(2)}) copy-start(bf16[1024,1024]{0,1:T(8,128)(2,1)} %get-tuple-element.1713) | copy-start | bytes 6291460 | tf_op jit(solution)/shard_map/while
  138.3 5.0 %copy-start.1 = (f32[512,8,128]{2,0,1:T(8,128)S(1)}, f32[512,8,128]{2,0,1:T(8,128)}, u32[]{:S(2)}) copy-start(f32[512,8,128]{2,0,1:T(8,128)} %fusion.115) | copy-start | bytes 6291460 | tf_op jit(solution)/shard_map/while
  138.3 5.5 %copy-start.4 = (f32[1024,8,128]{2,1,0:T(8,128)S(1)}, f32[1024,8,128]{2,1,0:T(8,128)}, u32[]{:S(2)}) copy-start(f32[1024,8,128]{2,1,0:T(8,128)} %get-tuple-element.1685) | copy-start | bytes 12582916 | tf_op jit(solution)/shard_map/while
  138.3 6.7 %copy-start.6 = (f32[1024,8,128]{2,1,0:T(8,128)S(1)}, f32[1024,8,128]{2,1,0:T(8,128)}, u32[]{:S(2)}) copy-start(f32[1024,8,128]{2,1,0:T(8,128)} %get-tuple-element.1686) | copy-start | bytes 12582916 | tf_op jit(solution)/shard_map/while
  147.9 2.1 copy-start.5
  150.0 2.0 copy-start.7
  170.3 1.1 copy-start.12
  219.5 4.6 %copy-start.3 = (bf16[512,1024]{0,1:T(8,128)(2,1)}, bf16[512,1024]{0,1:T(8,128)(2,1)S(1)}, u32[]{:S(2)}) copy-start(bf16[512,1024]{0,1:T(8,128)(2,1)S(1)} %get-tuple-element.1529) | copy-start | bytes 3145732 | tf_op jit(solution)/shard_map/while
  236.4 4.6 %copy-start.3 = (bf16[512,1024]{0,1:T(8,128)(2,1)}, bf16[512,1024]{0,1:T(8,128)(2,1)S(1)}, u32[]{:S(2)}) copy-start(bf16[512,1024]{0,1:T(8,128)(2,1)S(1)} %get-tuple-element.1529) | copy-start | bytes 3145732 | tf_op jit(solution)/shard_map/while
  251.1 3.2 %copy-start.9 = (bf16[128,8,4,128]{0,3,2,1:T(8,128)(2,1)S(1)}, bf16[128,8,4,128]{0,3,2,1:T(8,128)(2,1)}, u32[]{:S(2)}) copy-start(bf16[128,8,4,128]{0,3,2,1:T(8,128)(2,1)} %get-tuple-element.1216) | copy-start | bytes 3145732
Sparse Core Ops, SparseCore 0:
  10.2 33.5 all-gather.4
  45.9 29.8 all-gather.2
  170.5 89.7 reduce-scatter.1
where the time goes:
time: 270 us; the launch traced here: 269 us
  matrix products  75.3 us (28%)
  local copies, waits for them, and re-layouts  59.9 us (22%)
  waiting for transfers between devices  51 us (19%)
  blocking collectives  42.8 us (16%)
  other arithmetic  25.6 us (9%)
  between operations  13.9 us (5%)
    psum x1, blocking collectives, per_device(): sink_grad = lax.psum(partial_sink, ('dp', 'ctx'))  42.8 us
    all_gather x1, waiting for transfers between devices, per_device(): lax.all_gather(key_input, 'ctx', axis=0, tiled=True)  24.4 us
    all_gather x1, waiting for transfers between devices, per_device(): lax.all_gather(value_input, 'ctx', axis=0, tiled=True)  21.9 us
    dot_general x6, matrix products, block_scores(): jnp.einsum('tgrd,ngd->tgrn', query_heads, key_rows, preferred_element_typ...  21.1 us
    dot_general x2, matrix products, advance(): jnp.einsum('tgrn,ngd->tgrd', grad_scores, key_rows, preferred_element_typ...  19.6 us
    dot_general x2, matrix products, advance(): jnp.einsum('tgrn,tgrd->ngd', grad_scores, query_heads, preferred_element_...  15.6 us
    dynamic_slice x10, local copies, waits for them, and re-layouts, key_block(): lax.dynamic_slice_in_dim(table, first_row, block_rows, 0)  13.2 us
    while x30, local copies, waits for them, and re-layouts  11.6 us
  transfers between devices with their start and end apart: 3, of which 3 were waited for; matrix products, arithmetic and copies ran while one was open for 23% of the time, Pallas kernels for 0%

commit v1 on v0

v1 whole, which is shorter than its diff:
```python
import functools
import math

import jax
import jax.numpy as jnp
from jax import lax
from jax.experimental import pallas as pl
from jax.experimental.pallas import tpu as pltpu
from jax.sharding import PartitionSpec as P

HD = 128
BLOCK = 128
STREAMS = 2
SCALE = HD**-0.5
LOG2E = math.log2(math.e)
MASKED = -1e30


def plan_kernel(stretch_len, place_ref, map_ref, lengths_ref, assign_ref, table_ref):
    chip, core, group = place_ref[0], place_ref[1], place_ref[2]
    stretches = map_ref.shape[0]
    sequences, documents = lengths_ref.shape
    chips = place_ref.shape[0] - 3
    per_chip = stretches // chips
    per_core = per_chip // 2
    limit = (table_ref.shape[1] - 1) // 2
    sequence = jnp.int32(0)
    for at in range(sequences):
        sequence = jnp.where(group == at, assign_ref[at], sequence)
    ends = []
    total = jnp.int32(0)
    for at in range(documents):
        total = total + lengths_ref[sequence, at] * (BLOCK // stretch_len)
        ends.append(total)

    def first_of_document(stretch):
        first = jnp.int32(0)
        for end in ends:
            first = jnp.where(stretch >= end, end, first)
        return first

    for row in range(per_chip):
        core_of_row = core if row < per_core else 1 - core
        slot = chip * per_chip + core_of_row * per_core + row % per_core
        mine = map_ref[slot]
        first = first_of_document(mine)

        def rows_of(key_slot):
            key_chip = key_slot // per_chip
            inner = key_slot - key_chip * per_chip
            key_core = inner // per_core
            inner = inner - key_core * per_core
            inner = inner + jnp.where(key_core == core, 0, per_core)
            ahead = key_chip - chip
            table = jnp.where(ahead > 0, chips - 1 + ahead, -ahead)
            partial = jnp.where(ahead < 0, ahead + chips, ahead)
            return (
                (table * per_chip + inner) * stretch_len,
                (partial * per_chip + inner) * stretch_len,
            )

        key_row, sum_row = rows_of(slot)
        for at in range(limit):
            table_ref[row, 1 + 2 * at] = key_row
            table_ref[row, 2 + 2 * at] = sum_row

        def visit(key_slot, count):
            other = map_ref[key_slot]
            seen = (other >= first) & (other < mine)

            @pl.when(seen)
            def _():
                key_row, sum_row = rows_of(key_slot)
                table_ref[row, 1 + 2 * count] = key_row
                table_ref[row, 2 + 2 * count] = sum_row

            return count + seen.astype(jnp.int32)

        table_ref[row, 0] = lax.fori_loop(0, stretches, visit, jnp.int32(1))


def attention_kernel(
    shape,
    place_ref,
    table_ref,
    sink_ref,
    q_ref,
    g_ref,
    pq_ref,
    pg_ref,
    *refs,
):
    heads, ratio, stretch_len, per_chip, chips, limit, stream = shape
    sources = refs[: 2 * chips - 1]
    o_ref, dq_ref, po_ref, pdq_ref = refs[2 * chips - 1 : 2 * chips + 3]
    partials = refs[2 * chips + 3 : 3 * chips + 3]
    sink_out = refs[3 * chips + 3]
    kv, dk_sum, dv_sum, sems = refs[3 * chips + 4 :]
    head = pl.program_id(0)
    rows = per_chip * stretch_len

    def copies(at):
        for index, source in enumerate(sources):
            for part in range(2):
                yield pltpu.make_async_copy(
                    source.at[:, pl.ds((part * heads + at) * HD, HD)],
                    kv.at[at, part, pl.ds(index * rows, rows)],
                    sems.at[at],
                )

    @pl.when(head == 0)
    def _():
        for at in range(heads):
            for copy in copies(at):
                copy.start()

    for at in range(heads):

        @pl.when(head == at)
        def _():
            for copy in copies(at):
                copy.wait()

    dk_sum[...] = jnp.zeros_like(dk_sum)
    dv_sum[...] = jnp.zeros_like(dv_sum)
    first_head = (place_ref[1] * STREAMS + stream) * heads * ratio + head * ratio
    sink = jnp.concatenate(
        [jnp.full((stretch_len, 1), sink_ref[first_head + at], jnp.float32) for at in range(ratio)],
        axis=0,
    ) * LOG2E
    block = ratio * stretch_len
    token = lax.broadcasted_iota(jnp.int32, (block, stretch_len), 0) % stretch_len
    causal = lax.broadcasted_iota(jnp.int32, (block, stretch_len), 1) <= token

    def take(ref, first):
        return jnp.concatenate(
            [ref[pl.ds(first, stretch_len), at * HD : (at + 1) * HD] for at in range(ratio)],
            axis=0,
        )

    def put(ref, first, value):
        for at in range(ratio):
            ref[pl.ds(first, stretch_len), at * HD : (at + 1) * HD] = value[
                at * stretch_len : (at + 1) * stretch_len
            ].astype(ref.dtype)

    def one_block(row, first, q_in, g_in, o_out, dq_out, slots):
        count = table_ref[row, 0]
        query, grad = take(q_in, first), take(g_in, first)
        key_rows = [pl.multiple_of(table_ref[row, 1 + 2 * at], stretch_len) for at in range(slots)]
        sum_rows = [pl.multiple_of(table_ref[row, 2 + 2 * at], stretch_len) for at in range(slots)]
        keys = jnp.concatenate([kv[head, 0, pl.ds(at, stretch_len)] for at in key_rows], axis=0)
        values = jnp.concatenate([kv[head, 1, pl.ds(at, stretch_len)] for at in key_rows], axis=0)
        dims = (((1,), (1,)), ((), ()))
        scores = lax.dot_general(query, keys, dims, preferred_element_type=jnp.float32)
        scores = scores * (SCALE * LOG2E)
        column = lax.broadcasted_iota(jnp.int32, scores.shape, 1)
        seen = column < count * stretch_len
        if slots * stretch_len == causal.shape[1]:
            seen = causal
        else:
            rest = slots * stretch_len - stretch_len
            token_all = lax.broadcasted_iota(jnp.int32, scores.shape, 0) % stretch_len
            seen = seen & ((column <= token_all) | (column >= stretch_len))
        scores = jnp.where(seen, scores, MASKED)
        row_max = jnp.maximum(sink, jnp.max(scores, axis=1, keepdims=True))
        terms = jnp.exp2(scores - row_max)
        sink_term = jnp.exp2(sink - row_max)
        total = sink_term + jnp.sum(terms, axis=1, keepdims=True)
        inverse = 1.0 / total
        weights = terms * inverse
        weights_b = weights.astype(jnp.bfloat16)
        attended = jnp.dot(weights_b, values, preferred_element_type=jnp.float32)
        attended = attended.astype(jnp.bfloat16)
        put(o_out, first, attended)
        row_dot = jnp.sum(
            grad.astype(jnp.float32) * attended.astype(jnp.float32), axis=1, keepdims=True
        )
        grad_weights = lax.dot_general(grad, values, dims, preferred_element_type=jnp.float32)
        grad_scores = (weights * ((grad_weights - row_dot) * SCALE)).astype(jnp.bfloat16)
        put(dq_out, first, jnp.dot(grad_scores, keys, preferred_element_type=jnp.float32))
        over_rows = (((0,), (0,)), ((), ()))
        dk = lax.dot_general(grad_scores, query, over_rows, preferred_element_type=jnp.float32)
        dv = lax.dot_general(weights_b, grad, over_rows, preferred_element_type=jnp.float32)
        for at, target in enumerate(sum_rows):
            part = slice(at * stretch_len, (at + 1) * stretch_len)
            dk_sum[pl.ds(target, stretch_len)] += dk[part]
            dv_sum[pl.ds(target, stretch_len)] += dv[part]
        terms_of_sink = (sink_term * inverse * row_dot).reshape(ratio, stretch_len, 1)
        return jnp.sum(terms_of_sink, axis=1)

    sink_out[0] = jnp.zeros_like(sink_out[0])
    half = per_chip // 2
    widths = []
    width = 2
    while width < limit:
        widths.append(width)
        width *= 2
    widths.append(limit)
    for ins, base in (((q_ref, g_ref, o_ref, dq_ref), 0), ((pq_ref, pg_ref, po_ref, pdq_ref), half)):

        def one_row(at, carry):
            row = base + at
            first = pl.multiple_of(at * stretch_len, stretch_len)
            count = table_ref[row, 0]
            below = 0
            for width in widths:

                @pl.when((count > below) & (count <= width))
                def _():
                    sink_out[0] -= jnp.broadcast_to(
                        one_block(row, first, *ins, width), sink_out.shape[1:]
                    )

                below = width
            return carry

        lax.fori_loop(0, half, one_row, 0)

    for at, partial in enumerate(partials):
        part = pl.ds(at * rows, rows)
        partial[:, :HD] = dk_sum[part].astype(partial.dtype)
        partial[:, HD:] = dv_sum[part].astype(partial.dtype)


def attend(stream, place, table, sinks, queries, out_grad, partner, sources, chips, limit, ratio):
    local_rows = queries.shape[0]
    heads = sources[0].shape[1] // (2 * HD)
    rows = sources[0].shape[0]
    per_chip = table.shape[0]
    stretch_len = rows // per_chip
    wide = ratio * HD
    shape = (heads, ratio, stretch_len, per_chip, chips, limit, stream)
    whole = STREAMS * heads
    here = pl.BlockSpec(
        (local_rows, wide), lambda g, place, table, sinks: (0, place[1] * whole + stream * heads + g)
    )
    there = pl.BlockSpec((local_rows, wide), lambda g, *_: (0, stream * heads + g))
    there_grad = pl.BlockSpec((local_rows, wide), lambda g, *_: (0, whole + stream * heads + g))
    out = pl.BlockSpec((local_rows, wide), lambda g, *_: (0, g))
    wide_out = jax.ShapeDtypeStruct((local_rows, heads * wide), jnp.bfloat16)
    partial = jax.ShapeDtypeStruct((rows, heads * 2 * HD), jnp.bfloat16)
    partial_spec = pl.BlockSpec((rows, 2 * HD), lambda g, *_: (0, g))
    return pl.pallas_call(
        functools.partial(attention_kernel, shape),
        grid_spec=pltpu.PrefetchScalarGridSpec(
            num_scalar_prefetch=3,
            grid=(heads,),
            in_specs=[here, here, there, there_grad]
            + [pl.BlockSpec(memory_space=pl.ANY)] * len(sources),
            out_specs=[out] * 4
            + [partial_spec] * chips
            + [pl.BlockSpec((1, ratio, HD), lambda g, *_: (g, 0, 0))],
            scratch_shapes=[
                pltpu.VMEM((heads, 2, len(sources) * rows, HD), jnp.bfloat16),
                pltpu.VMEM((chips * rows, HD), jnp.float32),
                pltpu.VMEM((chips * rows, HD), jnp.float32),
                pltpu.SemaphoreType.DMA((heads,)),
            ],
        ),
        out_shape=[wide_out] * 4
        + [partial] * chips
        + [jax.ShapeDtypeStruct((heads, ratio, HD), jnp.float32)],
        compiler_params=pltpu.CompilerParams(vmem_limit_bytes=40 << 20),
        cost_estimate=pl.CostEstimate(
            flops=6 * 2 * heads * rows * ratio * limit * stretch_len * HD,
            transcendentals=heads * rows * ratio * limit * stretch_len,
            bytes_accessed=4 << 20,
        ),
    )(place, table, sinks, queries, out_grad, partner, partner, *sources)


def send(value, pairs):
    return lax.ppermute(value, "ctx", pairs)


def along(chips, step, senders):
    return [
        (2 * chip + core, 2 * (chip + step) + core)
        for chip in senders
        if 0 <= chip + step < chips
        for core in range(2)
    ]


def gather_chain(value, chips):
    rightward, leftward = [value], [value]
    for hop in range(1, chips):
        rightward.append(send(rightward[-1], along(chips, 1, range(hop - 1, chips))))
        leftward.append(send(leftward[-1], along(chips, -1, range(0, chips - hop + 1))))
    return [value] + rightward[1:] + leftward[1:]


def add(left, right):
    return (left.astype(jnp.float32) + right.astype(jnp.float32)).astype(jnp.bfloat16)


def scatter_chain(partials, chips):
    rightward, leftward = partials[chips - 1], partials[1]
    for hop in range(1, chips):
        rightward = send(rightward, along(chips, 1, range(0, hop)))
        leftward = send(leftward, along(chips, -1, range(chips - hop, chips)))
        if hop < chips - 1:
            rightward = add(partials[chips - 1 - hop], rightward)
            leftward = add(partials[1 + hop], leftward)
    return (
        partials[0].astype(jnp.float32)
        + rightward.astype(jnp.float32)
        + leftward.astype(jnp.float32)
    ).astype(jnp.bfloat16)


def columns(table, first, count):
    return lax.dynamic_slice_in_dim(table, first, count, 1)


def per_device(
    queries, key_input, value_input, out_grad, sink_logits, doc_lengths, assignment, stretch_map
):
    local_rows = queries.shape[0]
    chips = lax.axis_size("ctx") // 2
    stretches = stretch_map.shape[0]
    stretch_len = local_rows * 2 * chips // stretches
    per_chip = stretches // chips
    head_count = sink_logits.shape[0]
    kv_heads = key_input.shape[1] // HD
    ratio = head_count // kv_heads
    limit = stretches // 2
    group = lax.axis_index("dp")
    index = lax.axis_index("ctx")
    chip, core = index // 2, index % 2
    swap = [(2 * at + side, 2 * at + 1 - side) for at in range(chips) for side in range(2)]
    half = kv_heads // 2 * HD
    width = half // STREAMS

    def key_values(side, stream):
        first = side * half + stream * width
        return jnp.concatenate(
            [columns(key_input, first, width), columns(value_input, first, width)], axis=1
        )

    sources = []
    for stream in range(STREAMS):
        received = send(key_values(1 - core, stream), swap)
        own = jnp.concatenate([key_values(core, stream), received], axis=0)
        sources.append(gather_chain(own, chips))
    partner = send(
        jnp.concatenate(
            [
                columns(queries, (1 - core) * half * ratio, half * ratio),
                columns(out_grad, (1 - core) * half * ratio, half * ratio),
            ],
            axis=1,
        ),
        swap,
    )
    place = jnp.concatenate(
        [jnp.stack([chip, core, group]).astype(jnp.int32), jnp.zeros((chips,), jnp.int32)]
    )
    smem = pl.BlockSpec(memory_space=pltpu.SMEM)
    table = pl.pallas_call(
        functools.partial(plan_kernel, stretch_len),
        in_specs=[smem] * 4,
        out_specs=smem,
        out_shape=jax.ShapeDtypeStruct((per_chip, 1 + 2 * limit), jnp.int32),
    )(place, stretch_map, doc_lengths, assignment)

    attended, query_grads, others, key_sums, sink_parts = [], [], [], [], []
    for stream in range(STREAMS):
        results = attend(
            stream, place, table, sink_logits, queries, out_grad, partner, sources[stream],
            chips, limit, ratio,
        )
        attended.append(results[0])
        query_grads.append(results[1])
        others += [results[2], results[3]]
        key_sums.append(scatter_chain(results[4 : 4 + chips], chips))
        sink_parts.append(results[4 + chips][:, :, 0].reshape(-1))

    sink_half = jnp.concatenate(sink_parts)
    blank = jnp.zeros_like(sink_half)
    sink_own = jnp.where(
        core == 0, jnp.concatenate([sink_half, blank]), jnp.concatenate([blank, sink_half])
    )
    sink_grad = lax.psum(sink_own, ("dp", "ctx"))

    def whole(mine, other):
        return jnp.where(
            core == 0, jnp.concatenate([mine, other], axis=1), jnp.concatenate([other, mine], axis=1)
        )

    back = send(jnp.concatenate(others, axis=1), swap)
    back = jnp.split(back, 2 * STREAMS, axis=1)
    attn_out = whole(jnp.concatenate(attended, axis=1), jnp.concatenate(back[0::2], axis=1))
    query_grad = whole(jnp.concatenate(query_grads, axis=1), jnp.concatenate(back[1::2], axis=1))

    sums = jnp.concatenate(
        [
            part[:, at : at + HD]
            for first in (0, HD)
            for part in key_sums
            for at in range(first, 2 * width, 2 * HD)
        ],
        axis=1,
    )
    mine, theirs = sums[:local_rows], send(sums[local_rows:], swap)
    key_grad = whole(mine[:, :half], theirs[:, :half])
    value_grad = whole(mine[:, half:], theirs[:, half:])
    return (attn_out, query_grad, key_grad, value_grad, sink_grad)


def solution(mesh):
    rows = P(("dp", "ctx"), None)
    return jax.shard_map(
        per_device,
        mesh=mesh,
        in_specs=(rows, rows, rows, rows, P(), P(), P(), P()),
        out_specs=(rows, rows, rows, rows, P()),
        check_vma=False,
    )
```

time: 270 us -> 166 us (0.61)
  matrix products: 75.3 us -> 0 us
  starting transfers between devices: 0.12 us -> 52.2 us
  local copies, waits for them, and re-layouts: 59.9 us -> 11.6 us
  waiting for transfers between devices: 51 us -> 22.5 us
  Pallas kernels: 0 us -> 25.5 us
  other arithmetic: 25.6 us -> 10.1 us
  between operations: 13.9 us -> 1.34 us
    dot_general x14 -> x0, matrix products: 75.3 us -> none  [the longest x6 21.1 us: block_scores(): jnp.einsum('tgrd,ngd->tgrn', query_heads, key_rows, preferred_element_typ...]
    ppermute x0 -> x29, starting transfers between devices: none -> 52.2 us  [send(): return lax.ppermute(value, 'ctx', pairs)]
    all_gather x2 -> x0, waiting for transfers between devices: 46.3 us -> none  [the longest x1 24.4 us: per_device(): lax.all_gather(key_input, 'ctx', axis=0, tiled=True)]
    pallas_call x0 -> x3, Pallas kernels: none -> 25.5 us  [the longest x2 22.5 us: attend(): pl.pallas_call(functools.partial(attention_kernel, shape), grid_spec=pltp...]
    ppermute x0 -> x29, waiting for transfers between devices: none -> 22.5 us  [send(): return lax.ppermute(value, 'ctx', pairs)]
    another operation x4, local copies, waits for them, and re-layouts: 14.4 us -> 0.17 us  [the longest x2 0.16 us: per_device(): sink_parts.append(results[4 + chips][:, :, 0].reshape(-1))]
    dynamic_slice x28 -> x2, local copies, waits for them, and re-layouts: 14.6 us -> 1.37 us  [columns(): return lax.dynamic_slice_in_dim(table, first, count, 1)]
    while x30 -> x0, local copies, waits for them, and re-layouts: 11.6 us -> none
  transfers between devices with their start and end apart: 3 -> 29, of which waited for: 3 -> 8; matrix products, arithmetic and copies ran while one was open for 23% -> 4% of each run, Pallas kernels for 0% -> 15%
where the time goes in v1:
time: 166 us; the launch traced here: 165 us
  starting transfers between devices  52.2 us (31%)
  blocking collectives  41.5 us (25%)
  Pallas kernels  25.5 us (15%)
  waiting for transfers between devices  22.5 us (14%)
  local copies, waits for them, and re-layouts  11.6 us (7%)
  other arithmetic  10.1 us (6%)
    ppermute x29, starting transfers between devices, send(): return lax.ppermute(value, 'ctx', pairs)  52.2 us
    psum x1, blocking collectives, per_device(): sink_grad = lax.psum(sink_own, ('dp', 'ctx'))  41.5 us
    ppermute x29, waiting for transfers between devices, send(): return lax.ppermute(value, 'ctx', pairs)  22.5 us
    pallas_call x2, Pallas kernels, attend(): pl.pallas_call(functools.partial(attention_kernel, shape), grid_spec=pltp...  22.5 us
    unnamed x67, local copies, waits for them, and re-layouts  9.62 us
    convert_element_type x6, other arithmetic, add(): (left.astype(jnp.float32) + right.astype(jnp.float32)).astype(jnp.bfloat16)  4.04 us
    select_n x4, other arithmetic, whole(): jnp.where(core == 0, jnp.concatenate([mine, other], axis=1), jnp.concaten...  4 us
  transfers between devices with their start and end apart: 29, of which 8 were waited for; matrix products, arithmetic and copies ran while one was open for 4% of the time, Pallas kernels for 15%

profile of v1, /device:TPU:0, one launch (start us, length us, event | category | flops | bytes accessed | tf_op | source)
XLA Modules:
  0.0 164.7 jit_solution(4494754794315853164)
XLA Ops:
  0.6 1.3 constant_dynamic-slice_fusion.8
  2.0 1.1 pad_maximum_fusion
  4.3 1.7 %collective-permute-done.1 = bf16[128,512]{1,0:T(8,128)(2,1)S(1)} collective-permute-done((bf16[128,512]{1,0:T(8,128)(2,1)S(1)}, bf16[128,512]{1,0:T(8,128)(2,1)S(1)}, u32[]{:S(2)}, u32[]{:S(2)}) %collective-permute-start.1) | collective-permute-done | bytes 131104 | tf_op jit(solution)/shard_map/ppermute | solution.py:274
  6.0 4.9 %collective-permute-start.2 = (bf16[256,512]{1,0:T(8,128)(2,1)S(1)}, bf16[256,512]{1,0:T(8,128)(2,1)S(1)}, u32[]{:S(2)}, u32[]{:S(2)}) collective-permute-start(bf16[256,512]{1,0:T(8,128)(2,1)S(1)} %pad_maximum_fusion.2.refs_0_), channel_id=1, source_target_pairs={{0,2},{1,3},{2,4},{3,5},{4,6},{5,7},{8,10},{9,11},{10,12},{11,13},... | collective-permute-start | bytes 786440 | tf_op jit(solution)/shard_map/ppermute | solution.py:274
  10.9 1.3 collective-permute-start.5
  12.2 5.3 %collective-permute-start.9 = (bf16[256,512]{1,0:T(8,128)(2,1)S(1)}, bf16[256,512]{1,0:T(8,128)(2,1)}, u32[]{:S(2)}, u32[]{:S(2)}) collective-permute-start(bf16[256,512]{1,0:T(8,128)(2,1)S(1)} %pad_maximum_fusion.3.refs_0_), channel_id=1, source_target_pairs={{0,2},{1,3},{2,4},{3,5},{4,6},{5,7},{8,10},{9,11},{10,12},{11,13},... | collective-permute-start | bytes 786440 | tf_op jit(solution)/shard_map/ppermute | solution.py:274
  17.5 1.3 collective-permute-start.12
  18.8 1.4 collective-permute-start.3
  20.9 1.3 collective-permute-start.6
  22.9 1.4 collective-permute-start.10
  24.2 2.7 %collective-permute-done.12.refs_4_ = bf16[256,512]{1,0:T(8,128)(2,1)} collective-permute-done((bf16[256,512]{1,0:T(8,128)(2,1)S(1)}, bf16[256,512]{1,0:T(8,128)(2,1)}, u32[]{:S(2)}, u32[]{:S(2)}) %collective-permute-start.12) | collective-permute-done | bytes 262176 | tf_op jit(solution)/shard_map/ppermute | solution.py:274
  27.0 1.3 collective-permute-start.13
  28.3 1.4 collective-permute-start.4
  29.7 3.2 %collective-permute-done.6.refs_5_ = bf16[256,512]{1,0:T(8,128)(2,1)} collective-permute-done((bf16[256,512]{1,0:T(8,128)(2,1)S(1)}, bf16[256,512]{1,0:T(8,128)(2,1)}, u32[]{:S(2)}, u32[]{:S(2)}) %collective-permute-start.6) | collective-permute-done | bytes 262176 | tf_op jit(solution)/shard_map/ppermute | solution.py:274
  32.8 1.3 collective-permute-start.7
  34.2 1.4 collective-permute-start.11
  35.5 7.5 %collective-permute-done.13.refs_5_ = bf16[256,512]{1,0:T(8,128)(2,1)} collective-permute-done((bf16[256,512]{1,0:T(8,128)(2,1)}, bf16[256,512]{1,0:T(8,128)(2,1)}, u32[]{:S(2)}, u32[]{:S(2)}) %collective-permute-start.13) | collective-permute-done | bytes 262176 | tf_op jit(solution)/shard_map/ppermute | solution.py:274
  43.0 1.3 collective-permute-start.14
  44.9 3.0 %shard_map.119.table_ref = s32[4,17]{1,0:T(4,128)} custom-call(s32[7]{0:T(128)} %pad_add_fusion.place_ref, s32[16]{0:T(128)} %map_ref.1, s32[4,4]{1,0:T(4,128)} %lengths_ref.1, s32[4]{0:T(128)} %assign_ref.1), custom_call_target="tpu_custom_call" | custom-call | tf_op jit(solution)/shard_map/pallas_call | solution.py:361
  48.7 0.9 copy-done.3
  49.6 0.9 copy-done.13
  50.6 0.9 copy-done.15
  52.8 10.9 %shard_map.120 = (bf16[128,1024]{1,0:T(8,128)(2,1)S(1)}, bf16[128,1024]{1,0:T(8,128)(2,1)S(1)}, bf16[128,1024]{1,0:T(8,128)(2,1)S(1)}, bf16[128,1024]{1,0:T(8,12...) custom-call(s32[7]{0:T(128)S(1)} %copy-done.27, ...), custom_call_target="tpu_custom_call" | custom-call | flops 1610612736 | bytes 4194304 | tf_op jit(solution)/shard_map/pallas_call | solution.py:244
  63.7 0.7 copy-done.4
  65.1 0.7 copy-done.22
  65.8 3.8 %collective-permute-start.16 = (bf16[256,512]{1,0:T(8,128)(2,1)S(1)}, bf16[256,512]{1,0:T(8,128)(2,1)S(1)}, u32[]{:S(2)}, u32[]{:S(2)}) collective-permute-start(bf16[256,512]{1,0:T(8,128)(2,1)S(1)} %get-tuple-element.34), channel_id=1, source_target_pairs={{0,2},{1,3},{8,10},{9,11},{16,18},{17,19},{24,26},{25,27}} | collective-permute-start | bytes 786440 | tf_op jit(solution)/shard_map/ppermute | solution.py:274
  70.4 11.6 %shard_map.121 = (bf16[128,1024]{1,0:T(8,128)(2,1)S(1)}, bf16[128,1024]{1,0:T(8,128)(2,1)S(1)}, bf16[128,1024]{1,0:T(8,128)(2,1)S(1)}, bf16[128,1024]{1,0:T(8,12...) custom-call(s32[7]{0:T(128)S(1)} %copy-done.27, ...), custom_call_target="tpu_custom_call" | custom-call | flops 1610612736 | bytes 4194304 | tf_op jit(solution)/shard_map/pallas_call | solution.py:244
  83.0 1.6 collective-permute-start.22
  85.4 0.8 fusion
  86.2 1.4 collective-permute-start.20
  87.8 1.3 collective-permute-start.17
  89.1 2.5 %collective-permute-done.22 = bf16[256,512]{1,0:T(8,128)(2,1)S(1)} collective-permute-done((bf16[256,512]{1,0:T(8,128)(2,1)}, bf16[256,512]{1,0:T(8,128)(2,1)S(1)}, u32[]{:S(2)}, u32[]{:S(2)}) %collective-permute-start.22) | collective-permute-done | bytes 262176 | tf_op jit(solution)/shard_map/ppermute | solution.py:274
  92.4 4.9 %collective-permute-start.23 = (bf16[256,512]{1,0:T(8,128)(2,1)S(1)}, bf16[256,512]{1,0:T(8,128)(2,1)S(1)}, u32[]{:S(2)}, u32[]{:S(2)}) collective-permute-start(bf16[256,512]{1,0:T(8,128)(2,1)S(1)} %get-tuple-element.57), channel_id=1, source_target_pairs={{0,2},{1,3},{2,4},{3,5},{8,10},{9,11},{10,12},{11,13},{16,18},{17,... | collective-permute-start | bytes 786440 | tf_op jit(solution)/shard_map/ppermute | solution.py:274
  97.3 1.0 add_convert_fusion.4
  98.4 1.4 collective-permute-start.21
  99.9 5.2 %collective-permute-start.18 = (bf16[256,512]{1,0:T(8,128)(2,1)S(1)}, bf16[256,512]{1,0:T(8,128)(2,1)S(1)}, u32[]{:S(2)}, u32[]{:S(2)}) collective-permute-start(bf16[256,512]{1,0:T(8,128)(2,1)S(1)} %add_convert_fusion.5), channel_id=1, source_target_pairs={{0,2},{1,3},{2,4},{3,5},{4,6},{5,7},{8,10},{9,11},{10,12},{11,13},... | collective-permute-start | bytes 786440 | tf_op jit(solution)/shard_map/ppermute | solution.py:274
  105.1 1.0 add_convert_fusion.1
  106.1 1.3 collective-permute-start.27
  107.4 1.0 add_convert_fusion.2
  108.5 4.7 %collective-permute-start.24 = (bf16[256,512]{1,0:T(8,128)(2,1)S(1)}, bf16[256,512]{1,0:T(8,128)(2,1)S(1)}, u32[]{:S(2)}, u32[]{:S(2)}) collective-permute-start(bf16[256,512]{1,0:T(8,128)(2,1)S(1)} %add_convert_fusion.2), channel_id=1, source_target_pairs={{0,2},{1,3},{2,4},{3,5},{4,6},{5,7},{8,10},{9,11},{10,12},{11,13},... | collective-permute-start | bytes 786440 | tf_op jit(solution)/shard_map/ppermute | solution.py:274
  113.4 1.8 %collective-permute-done.27 = bf16[256,512]{1,0:T(8,128)(2,1)S(1)} collective-permute-done((bf16[256,512]{1,0:T(8,128)(2,1)S(1)}, bf16[256,512]{1,0:T(8,128)(2,1)S(1)}, u32[]{:S(2)}, u32[]{:S(2)}) %collective-permute-start.27) | collective-permute-done | bytes 262176 | tf_op jit(solution)/shard_map/ppermute | solution.py:274
  115.2 2.4 %collective-permute-done.24 = bf16[256,512]{1,0:T(8,128)(2,1)S(1)} collective-permute-done((bf16[256,512]{1,0:T(8,128)(2,1)S(1)}, bf16[256,512]{1,0:T(8,128)(2,1)S(1)}, u32[]{:S(2)}, u32[]{:S(2)}) %collective-permute-start.24) | collective-permute-done | bytes 262176 | tf_op jit(solution)/shard_map/ppermute | solution.py:274
  118.1 41.5 %psum.7 = f32[32]{0:T(128)} all-reduce(f32[32]{0:T(128)S(1)} %broadcast_select_fusion), channel_id=1, replica_groups=mesh['dp'=4,'ctx'=8] {'dp','ctx'}, use_global_device_ids=true, to_apply=%region_0.1 | all-reduce | flops 32 | bytes 256 | tf_op jit(solution)/shard_map/psum | solution.py:385
  159.7 0.8 maximum_select_fusion.2
  160.5 0.8 maximum_select_fusion.3
  161.3 0.9 copy-done.7
  162.3 1.2 maximum_select_fusion
  163.5 1.2 maximum_select_fusion.1
  (117 shorter events, 10.3 us)
Async XLA Ops:
  2.0 1.5 copy-start.29
  2.0 1.5 copy-start.30
  3.0 45.6 %collective-permute-start = (bf16[128,4096]{1,0:T(8,128)(2,1)}, bf16[128,4096]{1,0:T(8,128)(2,1)S(1)}, u32[]{:S(2)}, u32[]{:S(2)}) collective-permute-start(bf16[128,4096]{1,0:T(8,128)(2,1)} %pad_maximum_fusion), channel_id=1, source_target_pairs={{0,1},{1,0},{2,3},{3,2},{4,5},{5,4},{6,7},{7,6},{8,9},{9,8},{10,11... | collective-permute-start | bytes 3145736 | tf_op jit(solution)/shard_map/ppermute | solution.py:274
  3.5 45.1 %copy-start.1 = (bf16[128,4096]{1,0:T(8,128)(2,1)S(1)}, bf16[128,4096]{1,0:T(8,128)(2,1)}, u32[]{:S(2)}) copy-start(bf16[128,4096]{1,0:T(8,128)(2,1)} %g_ref.3) | copy-start | bytes 3145732
  3.6 45.1 %copy-start = (bf16[128,4096]{1,0:T(8,128)(2,1)S(1)}, bf16[128,4096]{1,0:T(8,128)(2,1)}, u32[]{:S(2)}) copy-start(bf16[128,4096]{1,0:T(8,128)(2,1)} %q_ref.3) | copy-start | bytes 3145732
  3.6 45.1 %copy-start.28 = (f32[32]{0:T(128)S(1)}, f32[32]{0:T(128)}, u32[]{:S(2)}) copy-start(f32[32]{0:T(128)} %sink_ref.3) | copy-start | bytes 388
  3.6 2.4 %collective-permute-start.1 = (bf16[128,512]{1,0:T(8,128)(2,1)S(1)}, bf16[128,512]{1,0:T(8,128)(2,1)S(1)}, u32[]{:S(2)}, u32[]{:S(2)}) collective-permute-start(bf16[128,512]{1,0:T(8,128)(2,1)S(1)} %pad_maximum_fusion.10), channel_id=1, source_target_pairs={{0,1},{1,0},{2,3},{3,2},{4,5},{5,4},{6,7},{7,6},{8,9},{9,8},{10,11... | collective-permute-start | bytes 393224 | tf_op jit(solution)/shard_map/ppermute | solution.py:274
  3.8 8.4 %collective-permute-start.8 = (bf16[128,512]{1,0:T(8,128)(2,1)S(1)}, bf16[128,512]{1,0:T(8,128)(2,1)S(1)}, u32[]{:S(2)}, u32[]{:S(2)}) collective-permute-start(bf16[128,512]{1,0:T(8,128)(2,1)S(1)} %pad_maximum_fusion.11), channel_id=1, source_target_pairs={{0,1},{1,0},{2,3},{3,2},{4,5},{5,4},{6,7},{7,6},{8,9},{9,8},{10,11... | collective-permute-start | bytes 393224 | tf_op jit(solution)/shard_map/ppermute | solution.py:274
  6.0 21.0 %copy-start.2 = (bf16[256,512]{1,0:T(8,128)(2,1)}, bf16[256,512]{1,0:T(8,128)(2,1)S(1)}, u32[]{:S(2)}) copy-start(bf16[256,512]{1,0:T(8,128)(2,1)S(1)} %pad_maximum_fusion.2.refs_0_) | copy-start | bytes 786436
  6.0 12.8 %collective-permute-start.2 = (bf16[256,512]{1,0:T(8,128)(2,1)S(1)}, bf16[256,512]{1,0:T(8,128)(2,1)S(1)}, u32[]{:S(2)}, u32[]{:S(2)}) collective-permute-start(bf16[256,512]{1,0:T(8,128)(2,1)S(1)} %pad_maximum_fusion.2.refs_0_), channel_id=1, source_target_pairs={{0,2},{1,3},{2,4},{3,5},{4,6},{5,7},{8,10},{9,11},{10,12},{11,13},... | collective-permute-start | bytes 786440 | tf_op jit(solution)/shard_map/ppermute | solution.py:274
  10.9 10.0 %collective-permute-start.5 = (bf16[256,512]{1,0:T(8,128)(2,1)S(1)}, bf16[256,512]{1,0:T(8,128)(2,1)S(1)}, u32[]{:S(2)}, u32[]{:S(2)}) collective-permute-start(bf16[256,512]{1,0:T(8,128)(2,1)S(1)} %pad_maximum_fusion.2.refs_0_), channel_id=1, source_target_pairs={{2,0},{3,1},{4,2},{5,3},{6,4},{7,5},{10,8},{11,9},{12,10},{13,11},... | collective-permute-start | bytes 786440 | tf_op jit(solution)/shard_map/ppermute | solution.py:274
  12.2 10.7 %collective-permute-start.9 = (bf16[256,512]{1,0:T(8,128)(2,1)S(1)}, bf16[256,512]{1,0:T(8,128)(2,1)}, u32[]{:S(2)}, u32[]{:S(2)}) collective-permute-start(bf16[256,512]{1,0:T(8,128)(2,1)S(1)} %pad_maximum_fusion.3.refs_0_), channel_id=1, source_target_pairs={{0,2},{1,3},{2,4},{3,5},{4,6},{5,7},{8,10},{9,11},{10,12},{11,13},... | collective-permute-start | bytes 786440 | tf_op jit(solution)/shard_map/ppermute | solution.py:274
  17.5 9.5 %collective-permute-start.12 = (bf16[256,512]{1,0:T(8,128)(2,1)S(1)}, bf16[256,512]{1,0:T(8,128)(2,1)}, u32[]{:S(2)}, u32[]{:S(2)}) collective-permute-start(bf16[256,512]{1,0:T(8,128)(2,1)S(1)} %pad_maximum_fusion.3.refs_0_), channel_id=1, source_target_pairs={{2,0},{3,1},{4,2},{5,3},{6,4},{7,5},{10,8},{11,9},{12,10},{13,11},... | collective-permute-start | bytes 786440 | tf_op jit(solution)/shard_map/ppermute | solution.py:274
  18.8 9.5 %collective-permute-start.3 = (bf16[256,512]{1,0:T(8,128)(2,1)S(1)}, bf16[256,512]{1,0:T(8,128)(2,1)}, u32[]{:S(2)}, u32[]{:S(2)}) collective-permute-start(bf16[256,512]{1,0:T(8,128)(2,1)S(1)} %collective-permute-done.2.refs_1_), channel_id=1, source_target_pairs={{2,4},{3,5},{4,6},{5,7},{10,12},{11,13},{12,14},{13,15},{18,20},{1... | collective-permute-start | bytes 786440 | tf_op jit(solution)/shard_map/ppermute | solution.py:274
  20.9 12.0 %collective-permute-start.6 = (bf16[256,512]{1,0:T(8,128)(2,1)S(1)}, bf16[256,512]{1,0:T(8,128)(2,1)}, u32[]{:S(2)}, u32[]{:S(2)}) collective-permute-start(bf16[256,512]{1,0:T(8,128)(2,1)S(1)} %collective-permute-done.5.refs_4_), channel_id=1, source_target_pairs={{2,0},{3,1},{4,2},{5,3},{10,8},{11,9},{12,10},{13,11},{18,16},{19,... | collective-permute-start | bytes 786440 | tf_op jit(solution)/shard_map/ppermute | solution.py:274
  22.9 11.3 %collective-permute-start.10 = (bf16[256,512]{1,0:T(8,128)(2,1)}, bf16[256,512]{1,0:T(8,128)(2,1)}, u32[]{:S(2)}, u32[]{:S(2)}) collective-permute-start(bf16[256,512]{1,0:T(8,128)(2,1)} %collective-permute-done.9.refs_1_), channel_id=1, source_target_pairs={{2,4},{3,5},{4,6},{5,7},{10,12},{11,13},{12,14},{13,15},{18,20},{1... | collective-permute-start | bytes 786440 | tf_op jit(solution)/shard_map/ppermute | solution.py:274
  27.0 16.0 %collective-permute-start.13 = (bf16[256,512]{1,0:T(8,128)(2,1)}, bf16[256,512]{1,0:T(8,128)(2,1)}, u32[]{:S(2)}, u32[]{:S(2)}) collective-permute-start(bf16[256,512]{1,0:T(8,128)(2,1)} %collective-permute-done.12.refs_4_), channel_id=1, source_target_pairs={{2,0},{3,1},{4,2},{5,3},{10,8},{11,9},{12,10},{13,11},{18,16},{19,... | collective-permute-start | bytes 786440 | tf_op jit(solution)/shard_map/ppermute | solution.py:274
  28.3 19.6 %collective-permute-start.4 = (bf16[256,512]{1,0:T(8,128)(2,1)}, bf16[256,512]{1,0:T(8,128)(2,1)}, u32[]{:S(2)}, u32[]{:S(2)}) collective-permute-start(bf16[256,512]{1,0:T(8,128)(2,1)} %collective-permute-done.3.refs_2_), channel_id=1, source_target_pairs={{4,6},{5,7},{12,14},{13,15},{20,22},{21,23},{28,30},{29,31}} | collective-permute-start | bytes 786440 | tf_op jit(solution)/shard_map/ppermute | solution.py:274
  32.8 15.8 %collective-permute-start.7 = (bf16[256,512]{1,0:T(8,128)(2,1)}, bf16[256,512]{1,0:T(8,128)(2,1)}, u32[]{:S(2)}, u32[]{:S(2)}) collective-permute-start(bf16[256,512]{1,0:T(8,128)(2,1)} %collective-permute-done.6.refs_5_), channel_id=1, source_target_pairs={{2,0},{3,1},{10,8},{11,9},{18,16},{19,17},{26,24},{27,25}} | collective-permute-start | bytes 786440 | tf_op jit(solution)/shard_map/ppermute | solution.py:274
  34.2 36.2 %collective-permute-start.11 = (bf16[256,512]{1,0:T(8,128)(2,1)}, bf16[256,512]{1,0:T(8,128)(2,1)}, u32[]{:S(2)}, u32[]{:S(2)}) collective-permute-start(bf16[256,512]{1,0:T(8,128)(2,1)} %collective-permute-done.10.refs_2_), channel_id=1, source_target_pairs={{4,6},{5,7},{12,14},{13,15},{20,22},{21,23},{28,30},{29,31}} | collective-permute-start | bytes 786440 | tf_op jit(solution)/shard_map/ppermute | solution.py:274
  43.0 27.4 %collective-permute-start.14 = (bf16[256,512]{1,0:T(8,128)(2,1)}, bf16[256,512]{1,0:T(8,128)(2,1)}, u32[]{:S(2)}, u32[]{:S(2)}) collective-permute-start(bf16[256,512]{1,0:T(8,128)(2,1)} %collective-permute-done.13.refs_5_), channel_id=1, source_target_pairs={{2,0},{3,1},{10,8},{11,9},{18,16},{19,17},{26,24},{27,25}} | collective-permute-start | bytes 786440 | tf_op jit(solution)/shard_map/ppermute | solution.py:274
  48.7 1.0 copy-start.3
  49.6 0.9 copy-start.13
  50.6 0.9 copy-start.15
  65.8 16.2 %copy-start.16 = (bf16[256,512]{1,0:T(8,128)(2,1)}, bf16[256,512]{1,0:T(8,128)(2,1)S(1)}, u32[]{:S(2)}) copy-start(bf16[256,512]{1,0:T(8,128)(2,1)S(1)} %get-tuple-element.32) | copy-start | bytes 786436
  65.8 16.2 %copy-start.18 = (bf16[256,512]{1,0:T(8,128)(2,1)}, bf16[256,512]{1,0:T(8,128)(2,1)S(1)}, u32[]{:S(2)}) copy-start(bf16[256,512]{1,0:T(8,128)(2,1)S(1)} %get-tuple-element.34) | copy-start | bytes 786436
  65.8 19.6 %collective-permute-start.16 = (bf16[256,512]{1,0:T(8,128)(2,1)S(1)}, bf16[256,512]{1,0:T(8,128)(2,1)S(1)}, u32[]{:S(2)}, u32[]{:S(2)}) collective-permute-start(bf16[256,512]{1,0:T(8,128)(2,1)S(1)} %get-tuple-element.34), channel_id=1, source_target_pairs={{0,2},{1,3},{8,10},{9,11},{16,18},{17,19},{24,26},{25,27}} | collective-permute-start | bytes 786440 | tf_op jit(solution)/shard_map/ppermute | solution.py:274
  69.7 15.7 %collective-permute-start.19 = (bf16[256,512]{1,0:T(8,128)(2,1)S(1)}, bf16[256,512]{1,0:T(8,128)(2,1)S(1)}, u32[]{:S(2)}, u32[]{:S(2)}) collective-permute-start(bf16[256,512]{1,0:T(8,128)(2,1)S(1)} %get-tuple-element.32), channel_id=1, source_target_pairs={{6,4},{7,5},{14,12},{15,13},{22,20},{23,21},{30,28},{31,29}} | collective-permute-start | bytes 786440 | tf_op jit(solution)/shard_map/ppermute | solution.py:274
  83.0 78.3 %collective-permute-start.15 = (bf16[128,4096]{1,0:T(8,128)(2,1)S(1)}, bf16[128,4096]{1,0:T(8,128)(2,1)S(1)}, u32[]{:S(2)}, u32[]{:S(2)}) collective-permute-start(bf16[128,4096]{1,0:T(8,128)(2,1)S(1)} %pad_maximum_fusion.1), channel_id=1, source_target_pairs={{0,1},{1,0},{2,3},{3,2},{4,5},{5,4},{6,7},{7,6},{8,9},{9,8},{10,11... | collective-permute-start | bytes 3145736 | tf_op jit(solution)/shard_map/ppermute | solution.py:274
  83.0 8.6 %copy-start.21 = (bf16[256,512]{1,0:T(8,128)(2,1)S(1)}, bf16[256,512]{1,0:T(8,128)(2,1)}, u32[]{:S(2)}) copy-start(bf16[256,512]{1,0:T(8,128)(2,1)} %copy-done.20) | copy-start | bytes 786436
  83.0 8.6 %collective-permute-start.22 = (bf16[256,512]{1,0:T(8,128)(2,1)}, bf16[256,512]{1,0:T(8,128)(2,1)S(1)}, u32[]{:S(2)}, u32[]{:S(2)}) collective-permute-start(bf16[256,512]{1,0:T(8,128)(2,1)} %get-tuple-element.38), channel_id=1, source_target_pairs={{0,2},{1,3},{8,10},{9,11},{16,18},{17,19},{24,26},{25,27}} | collective-permute-start | bytes 786440 | tf_op jit(solution)/shard_map/ppermute | solution.py:274
  84.6 7.0 %collective-permute-start.25 = (bf16[256,512]{1,0:T(8,128)(2,1)}, bf16[256,512]{1,0:T(8,128)(2,1)S(1)}, u32[]{:S(2)}, u32[]{:S(2)}) collective-permute-start(bf16[256,512]{1,0:T(8,128)(2,1)} %get-tuple-element.36), channel_id=1, source_target_pairs={{6,4},{7,5},{14,12},{15,13},{22,20},{23,21},{30,28},{31,29}} | collective-permute-start | bytes 786440 | tf_op jit(solution)/shard_map/ppermute | solution.py:274
  85.4 11.9 %copy-start.19 = (bf16[256,512]{1,0:T(8,128)(2,1)S(1)}, bf16[256,512]{1,0:T(8,128)(2,1)}, u32[]{:S(2)}) copy-start(bf16[256,512]{1,0:T(8,128)(2,1)} %copy-done.18) | copy-start | bytes 786436
  86.2 11.1 %collective-permute-start.20 = (bf16[256,512]{1,0:T(8,128)(2,1)}, bf16[256,512]{1,0:T(8,128)(2,1)}, u32[]{:S(2)}, u32[]{:S(2)}) collective-permute-start(bf16[256,512]{1,0:T(8,128)(2,1)} %get-tuple-element.60), channel_id=1, source_target_pairs={{4,2},{5,3},{6,4},{7,5},{12,10},{13,11},{14,12},{15,13},{20,18},{2... | collective-permute-start | bytes 786440 | tf_op jit(solution)/shard_map/ppermute | solution.py:274
  87.8 12.0 %collective-permute-start.17 = (bf16[256,512]{1,0:T(8,128)(2,1)S(1)}, bf16[256,512]{1,0:T(8,128)(2,1)S(1)}, u32[]{:S(2)}, u32[]{:S(2)}) collective-permute-start(bf16[256,512]{1,0:T(8,128)(2,1)S(1)} %get-tuple-element.59), channel_id=1, source_target_pairs={{0,2},{1,3},{2,4},{3,5},{8,10},{9,11},{10,12},{11,13},{16,18},{17,... | collective-permute-start | bytes 786440 | tf_op jit(solution)/shard_map/ppermute | solution.py:274
  91.6 8.2 %copy-start.17 = (bf16[256,512]{1,0:T(8,128)(2,1)S(1)}, bf16[256,512]{1,0:T(8,128)(2,1)}, u32[]{:S(2)}) copy-start(bf16[256,512]{1,0:T(8,128)(2,1)} %copy-done.16) | copy-start | bytes 786436
  91.7 13.4 %collective-permute-start.26 = (bf16[256,512]{1,0:T(8,128)(2,1)S(1)}, bf16[256,512]{1,0:T(8,128)(2,1)S(1)}, u32[]{:S(2)}, u32[]{:S(2)}) collective-permute-start(bf16[256,512]{1,0:T(8,128)(2,1)S(1)} %get-tuple-element.58), channel_id=1, source_target_pairs={{4,2},{5,3},{6,4},{7,5},{12,10},{13,11},{14,12},{15,13},{20,18},{2... | collective-permute-start | bytes 786440 | tf_op jit(solution)/shard_map/ppermute | solution.py:274
  92.4 15.0 %collective-permute-start.23 = (bf16[256,512]{1,0:T(8,128)(2,1)S(1)}, bf16[256,512]{1,0:T(8,128)(2,1)S(1)}, u32[]{:S(2)}, u32[]{:S(2)}) collective-permute-start(bf16[256,512]{1,0:T(8,128)(2,1)S(1)} %get-tuple-element.57), channel_id=1, source_target_pairs={{0,2},{1,3},{2,4},{3,5},{8,10},{9,11},{10,12},{11,13},{16,18},{17,... | collective-permute-start | bytes 786440 | tf_op jit(solution)/shard_map/ppermute | solution.py:274
  98.4 14.8 %copy-start.23 = (bf16[256,512]{1,0:T(8,128)(2,1)S(1)}, bf16[256,512]{1,0:T(8,128)(2,1)}, u32[]{:S(2)}) copy-start(bf16[256,512]{1,0:T(8,128)(2,1)} %copy-done.22) | copy-start | bytes 786436
  98.4 14.8 %collective-permute-start.21 = (bf16[256,512]{1,0:T(8,128)(2,1)S(1)}, bf16[256,512]{1,0:T(8,128)(2,1)S(1)}, u32[]{:S(2)}, u32[]{:S(2)}) collective-permute-start(bf16[256,512]{1,0:T(8,128)(2,1)S(1)} %add_convert_fusion.4), channel_id=1, source_target_pairs={{2,0},{3,1},{4,2},{5,3},{6,4},{7,5},{10,8},{11,9},{12,10},{13,11},... | collective-permute-start | bytes 786440 | tf_op jit(solution)/shard_map/ppermute | solution.py:274
  99.9 13.3 %collective-permute-start.18 = (bf16[256,512]{1,0:T(8,128)(2,1)S(1)}, bf16[256,512]{1,0:T(8,128)(2,1)S(1)}, u32[]{:S(2)}, u32[]{:S(2)}) collective-permute-start(bf16[256,512]{1,0:T(8,128)(2,1)S(1)} %add_convert_fusion.5), channel_id=1, source_target_pairs={{0,2},{1,3},{2,4},{3,5},{4,6},{5,7},{8,10},{9,11},{10,12},{11,13},... | collective-permute-start | bytes 786440 | tf_op jit(solution)/shard_map/ppermute | solution.py:274
  106.1 9.1 %collective-permute-start.27 = (bf16[256,512]{1,0:T(8,128)(2,1)S(1)}, bf16[256,512]{1,0:T(8,128)(2,1)S(1)}, u32[]{:S(2)}, u32[]{:S(2)}) collective-permute-start(bf16[256,512]{1,0:T(8,128)(2,1)S(1)} %add_convert_fusion.1), channel_id=1, source_target_pairs={{2,0},{3,1},{4,2},{5,3},{6,4},{7,5},{10,8},{11,9},{12,10},{13,11},... | collective-permute-start | bytes 786440 | tf_op jit(solution)/shard_map/ppermute | solution.py:274
  108.4 9.1 %copy-start.25 = (bf16[256,512]{1,0:T(8,128)(2,1)S(1)}, bf16[256,512]{1,0:T(8,128)(2,1)}, u32[]{:S(2)}) copy-start(bf16[256,512]{1,0:T(8,128)(2,1)} %copy-done.24) | copy-start | bytes 786436
  108.5 9.1 %collective-permute-start.24 = (bf16[256,512]{1,0:T(8,128)(2,1)S(1)}, bf16[256,512]{1,0:T(8,128)(2,1)S(1)}, u32[]{:S(2)}, u32[]{:S(2)}) collective-permute-start(bf16[256,512]{1,0:T(8,128)(2,1)S(1)} %add_convert_fusion.2), channel_id=1, source_target_pairs={{0,2},{1,3},{2,4},{3,5},{4,6},{5,7},{8,10},{9,11},{10,12},{11,13},... | collective-permute-start | bytes 786440 | tf_op jit(solution)/shard_map/ppermute | solution.py:274
  117.9 41.7 %collective-permute-start.28 = (bf16[128,1024]{1,0:T(8,128)(2,1)S(1)}, bf16[128,1024]{1,0:T(8,128)(2,1)S(1)}, u32[]{:S(2)}, u32[]{:S(2)}) collective-permute-start(bf16[128,1024]{1,0:T(8,128)(2,1)S(1)} %slice.73), channel_id=1, source_target_pairs={{0,1},{1,0},{2,3},{3,2},{4,5},{5,4},{6,7},{7,6},{8,9},{9,8},{10,11... | collective-permute-start | bytes 786440 | tf_op jit(solution)/shard_map/ppermute | solution.py:274
  161.2 1.0 copy-start.11
  162.3 1.2 copy-start.5
  162.3 1.2 copy-start.9
  (12 other events, 9.0 us)

commit v2 on v1

v2 whole, which is shorter than its diff:
```python
import functools
import math

import jax
import jax.numpy as jnp
from jax import lax
from jax.experimental import pallas as pl
from jax.experimental.pallas import tpu as pltpu
from jax.sharding import PartitionSpec as P

HD = 128
BLOCK = 128
STREAMS = 2
SCALE = HD**-0.5
LOG2E = math.log2(math.e)
MASKED = -1e30


def plan_kernel(stretch_len, place_ref, map_ref, lengths_ref, assign_ref, table_ref):
    chip, core, group = place_ref[0], place_ref[1], place_ref[2]
    stretches = map_ref.shape[0]
    sequences, documents = lengths_ref.shape
    chips = place_ref.shape[0] - 3
    per_chip = stretches // chips
    per_core = per_chip // 2
    limit = (table_ref.shape[1] - 1) // 2
    sequence = jnp.int32(0)
    for at in range(sequences):
        sequence = jnp.where(group == at, assign_ref[at], sequence)
    ends = []
    total = jnp.int32(0)
    for at in range(documents):
        total = total + lengths_ref[sequence, at] * (BLOCK // stretch_len)
        ends.append(total)

    def first_of_document(stretch):
        first = jnp.int32(0)
        for end in ends:
            first = jnp.where(stretch >= end, end, first)
        return first

    for row in range(per_chip):
        core_of_row = core if row < per_core else 1 - core
        slot = chip * per_chip + core_of_row * per_core + row % per_core
        mine = map_ref[slot]
        first = first_of_document(mine)

        def rows_of(key_slot):
            key_chip = key_slot // per_chip
            inner = key_slot - key_chip * per_chip
            key_core = inner // per_core
            inner = inner - key_core * per_core
            inner = inner + jnp.where(key_core == core, 0, per_core)
            ahead = key_chip - chip
            table = jnp.where(ahead > 0, chips - 1 + ahead, -ahead)
            partial = jnp.where(ahead < 0, ahead + chips, ahead)
            return (
                (table * per_chip + inner) * stretch_len,
                (partial * per_chip + inner) * stretch_len,
            )

        key_row, sum_row = rows_of(slot)
        for at in range(limit):
            table_ref[row, 1 + 2 * at] = key_row
            table_ref[row, 2 + 2 * at] = sum_row

        def visit(key_slot, count):
            other = map_ref[key_slot]
            seen = (other >= first) & (other < mine)

            @pl.when(seen)
            def _():
                key_row, sum_row = rows_of(key_slot)
                table_ref[row, 1 + 2 * count] = key_row
                table_ref[row, 2 + 2 * count] = sum_row

            return count + seen.astype(jnp.int32)

        table_ref[row, 0] = lax.fori_loop(0, stretches, visit, jnp.int32(1))


def attention_kernel(shape, place_ref, table_ref, sink_ref, q_hbm, g_hbm, partner_hbm, *refs):
    heads, ratio, stretch_len, per_chip, chips, limit, stream = shape
    count_in = 2 * chips - 1
    sources, outs = refs[:count_in], refs[count_in : count_in + 2]
    partials = refs[count_in + 2 : count_in + 2 + chips]
    sink_out = refs[count_in + 2 + chips]
    kv, q_buf, g_buf, sums, sems = refs[count_in + 3 + chips :]
    chip, core = place_ref[0], place_ref[1]
    rows = per_chip * stretch_len
    local_rows = rows // 2
    wide = heads * ratio * HD
    here = pl.ds(pl.multiple_of((core * STREAMS + stream) * wide, HD), wide)
    loads = [
        (q_hbm.at[:, here], q_buf.at[pl.ds(0, local_rows)]),
        (g_hbm.at[:, here], g_buf.at[pl.ds(0, local_rows)]),
        (
            partner_hbm.at[:, pl.ds(stream * wide, wide)],
            q_buf.at[pl.ds(local_rows, local_rows)],
        ),
        (
            partner_hbm.at[:, pl.ds((STREAMS + stream) * wide, wide)],
            g_buf.at[pl.ds(local_rows, local_rows)],
        ),
    ]
    loads += [(source, kv.at[pl.ds(at * rows, rows)]) for at, source in enumerate(sources)]
    loads = [pltpu.make_async_copy(*pair, sems.at[at]) for at, pair in enumerate(loads)]
    for load in loads:
        load.start()
    sums[...] = jnp.zeros_like(sums)
    sink_out[...] = jnp.zeros_like(sink_out)
    block = ratio * stretch_len
    token = lax.broadcasted_iota(jnp.int32, (2 * stretch_len, block), 1) % stretch_len
    place = lax.broadcasted_iota(jnp.int32, (2 * stretch_len, block), 0)
    owner = lax.broadcasted_iota(jnp.int32, (1, block), 1) // stretch_len
    sinks = []
    for head in range(heads):
        first_head = ((core * STREAMS + stream) * heads + head) * ratio
        sink = jnp.zeros((1, block), jnp.float32)
        for at in range(ratio):
            sink = jnp.where(owner == at, sink_ref[first_head + at] * LOG2E, sink)
        sinks.append(sink)
    for load in loads:
        load.wait()

    def take(ref, first, head):
        first_lane = head * ratio * HD
        return jnp.concatenate(
            [
                ref[pl.ds(first, stretch_len), first_lane + at * HD : first_lane + (at + 1) * HD]
                for at in range(ratio)
            ],
            axis=0,
        )

    def put(ref, first, head, value):
        first_lane = head * ratio * HD
        for at in range(ratio):
            ref[pl.ds(first, stretch_len), first_lane + at * HD : first_lane + (at + 1) * HD] = (
                value[at * stretch_len : (at + 1) * stretch_len].astype(ref.dtype)
            )

    def one_block(row, slots):
        count = table_ref[row, 0]
        first = pl.multiple_of(row * stretch_len, stretch_len)
        key_rows = [pl.multiple_of(table_ref[row, 1 + 2 * at], stretch_len) for at in range(slots)]
        sum_rows = [pl.multiple_of(table_ref[row, 2 + 2 * at], stretch_len) for at in range(slots)]
        order = list(range(1, slots - 1)) + [slots - 1, 0]
        empty = jnp.where(count == slots, 0, 4 * stretch_len)
        seen = jnp.where(place < stretch_len, empty, place - stretch_len) <= token
        across = (((1,), (1,)), ((), ()))
        down = (((0,), (0,)), ((), ()))
        for head in range(heads):
            query, grad = take(q_buf, first, head), take(g_buf, first, head)
            keys = jnp.concatenate(
                [kv[pl.ds(key_rows[at], stretch_len), head * HD : (head + 1) * HD] for at in order],
                axis=0,
            )
            values = jnp.concatenate(
                [
                    kv[
                        pl.ds(key_rows[at], stretch_len),
                        (heads + head) * HD : (heads + head + 1) * HD,
                    ]
                    for at in order
                ],
                axis=0,
            )
            scores = lax.dot_general(keys, query, across, preferred_element_type=jnp.float32)
            grad_weights = lax.dot_general(values, grad, across, preferred_element_type=jnp.float32)
            edge = jnp.where(seen, scores[(slots - 2) * stretch_len :], MASKED)
            if slots > 2:
                scores = jnp.concatenate([scores[: (slots - 2) * stretch_len], edge], axis=0)
            else:
                scores = edge
            scores = scores * (SCALE * LOG2E)
            row_max = jnp.maximum(sinks[head], jnp.max(scores, axis=0, keepdims=True))
            terms = jnp.exp2(scores - row_max)
            sink_term = jnp.exp2(sinks[head] - row_max)
            inverse = 1.0 / (sink_term + jnp.sum(terms, axis=0, keepdims=True))
            weights = terms * inverse
            weights_b = weights.astype(jnp.bfloat16)
            row_dot = jnp.sum(weights * grad_weights, axis=0, keepdims=True)
            grad_scores = (weights * (grad_weights - row_dot)).astype(jnp.bfloat16)
            dv = jnp.dot(weights_b, grad, preferred_element_type=jnp.float32)
            dk = jnp.dot(grad_scores, query, preferred_element_type=jnp.float32)
            attended = lax.dot_general(weights_b, values, down, preferred_element_type=jnp.float32)
            dq = lax.dot_general(grad_scores, keys, down, preferred_element_type=jnp.float32) * SCALE
            put(outs[0], first, head, attended)
            put(outs[1], first, head, dq)
            for spot, at in enumerate(order):
                part = slice(spot * stretch_len, (spot + 1) * stretch_len)
                target = pl.ds(sum_rows[at], stretch_len)
                sums[target, 2 * head * HD : (2 * head + 1) * HD] += dk[part]
                sums[target, (2 * head + 1) * HD : (2 * head + 2) * HD] += dv[part]
            sink_out[head] -= sink_term * inverse * row_dot

    widths = []
    width = 2
    while width < limit:
        widths.append(width)
        width += 2
    widths.append(limit)

    def one_row(row, carry):
        count = table_ref[row, 0]
        below = 0
        for width in widths:

            @pl.when((count > below) & (count <= width))
            def _():
                one_block(row, width)

            below = width
        return carry

    lax.fori_loop(0, per_chip, one_row, 0)
    for at, partial in enumerate(partials):
        for head in range(heads):
            left = slice(2 * head * HD, (2 * head + 1) * HD)
            partial[:, left] = (sums[at * rows : (at + 1) * rows, left] * SCALE).astype(partial.dtype)
            right = slice((2 * head + 1) * HD, (2 * head + 2) * HD)
            partial[:, right] = sums[at * rows : (at + 1) * rows, right].astype(partial.dtype)


def attend(stream, place, table, sinks, queries, out_grad, partner, sources, chips, limit, ratio):
    heads = sources[0].shape[1] // (2 * HD)
    rows = sources[0].shape[0]
    per_chip = table.shape[0]
    stretch_len = rows // per_chip
    wide = heads * ratio * HD
    shape = (heads, ratio, stretch_len, per_chip, chips, limit, stream)
    smem, hbm = pl.BlockSpec(memory_space=pltpu.SMEM), pl.BlockSpec(memory_space=pl.ANY)
    vmem = pl.BlockSpec(memory_space=pltpu.VMEM)
    return pl.pallas_call(
        functools.partial(attention_kernel, shape),
        in_specs=[smem] * 3 + [hbm] * (3 + len(sources)),
        out_specs=[vmem] * (3 + chips),
        scratch_shapes=[
            pltpu.VMEM((len(sources) * rows, heads * 2 * HD), jnp.bfloat16),
            pltpu.VMEM((rows, wide), jnp.bfloat16),
            pltpu.VMEM((rows, wide), jnp.bfloat16),
            pltpu.VMEM((chips * rows, heads * 2 * HD), jnp.float32),
            pltpu.SemaphoreType.DMA((4 + len(sources),)),
        ],
        out_shape=[jax.ShapeDtypeStruct((rows, wide), jnp.bfloat16)] * 2
        + [jax.ShapeDtypeStruct((rows, heads * 2 * HD), jnp.bfloat16)] * chips
        + [jax.ShapeDtypeStruct((heads, 1, ratio * stretch_len), jnp.float32)],
        compiler_params=pltpu.CompilerParams(vmem_limit_bytes=16 << 20),
        cost_estimate=pl.CostEstimate(
            flops=6 * 2 * heads * rows * ratio * limit * stretch_len * HD,
            transcendentals=heads * rows * ratio * limit * stretch_len,
            bytes_accessed=4 << 20,
        ),
    )(place, table, sinks, queries, out_grad, partner, *sources)


def send(value, pairs):
    return lax.ppermute(value, "ctx", pairs)


def along(chips, step, senders):
    return [
        (2 * chip + core, 2 * (chip + step) + core)
        for chip in senders
        if 0 <= chip + step < chips
        for core in range(2)
    ]


def gather_hop(rightward, leftward, hop, chips):
    return (
        send(rightward, along(chips, 1, range(hop - 1, chips))),
        send(leftward, along(chips, -1, range(0, chips - hop + 1))),
    )


def scatter_hop(rightward, leftward, hop, chips):
    return (
        send(rightward, along(chips, 1, range(0, hop))),
        send(leftward, along(chips, -1, range(chips - hop, chips))),
    )


def after(values, *earlier):
    return lax.optimization_barrier((tuple(values), earlier))[0]


def add(left, right):
    return (left.astype(jnp.float32) + right.astype(jnp.float32)).astype(jnp.bfloat16)


def add3(first, second, third):
    total = first.astype(jnp.float32) + second.astype(jnp.float32) + third.astype(jnp.float32)
    return total.astype(jnp.bfloat16)


def columns(table, first, count):
    return lax.dynamic_slice_in_dim(table, first, count, 1)


def per_device(
    queries, key_input, value_input, out_grad, sink_logits, doc_lengths, assignment, stretch_map
):
    local_rows = queries.shape[0]
    chips = lax.axis_size("ctx") // 2
    stretches = stretch_map.shape[0]
    stretch_len = local_rows * 2 * chips // stretches
    per_chip = stretches // chips
    head_count = sink_logits.shape[0]
    kv_heads = key_input.shape[1] // HD
    ratio = head_count // kv_heads
    limit = stretches // 2
    group = lax.axis_index("dp")
    index = lax.axis_index("ctx")
    chip, core = index // 2, index % 2
    swap = [(2 * at + side, 2 * at + 1 - side) for at in range(chips) for side in range(2)]
    half = kv_heads // 2 * HD
    width = half // STREAMS

    def key_values(side, stream):
        first = side * half + stream * width
        return jnp.concatenate(
            [columns(key_input, first, width), columns(value_input, first, width)], axis=1
        )

    received = send(
        jnp.concatenate([key_values(1 - core, stream) for stream in range(STREAMS)], axis=1), swap
    )
    own = [
        jnp.concatenate(
            [key_values(core, at), received[:, 2 * width * at : 2 * width * (at + 1)]], axis=0
        )
        for at in range(STREAMS)
    ]
    partner = send(
        jnp.concatenate(
            [
                columns(queries, (1 - core) * half * ratio, half * ratio),
                columns(out_grad, (1 - core) * half * ratio, half * ratio),
            ],
            axis=1,
        ),
        swap,
    )
    place = jnp.concatenate(
        [jnp.stack([chip, core, group]).astype(jnp.int32), jnp.zeros((chips,), jnp.int32)]
    )
    smem = pl.BlockSpec(memory_space=pltpu.SMEM)
    table = pl.pallas_call(
        functools.partial(plan_kernel, stretch_len),
        in_specs=[smem] * 4,
        out_specs=smem,
        out_shape=jax.ShapeDtypeStruct((per_chip, 1 + 2 * limit), jnp.int32),
    )(place, stretch_map, doc_lengths, assignment)

    def compute(stream, right, left):
        results = attend(
            stream, place, table, sink_logits, queries, out_grad, partner,
            [own[stream]] + right + left, chips, limit, ratio,
        )
        heads = results[-1].shape[0]
        sinks = jnp.sum(results[-1].reshape(heads, ratio, -1), axis=2).reshape(-1)
        others = jnp.concatenate([part[local_rows:] for part in results[:2]], axis=1)
        return results[:2], results[2:-1], sinks, others

    def gathered(stream, right, left, hop):
        rightward, leftward = (right[-1], left[-1]) if right else (own[stream], own[stream])
        rightward, leftward = gather_hop(rightward, leftward, hop, chips)
        right.append(rightward)
        left.append(leftward)

    def scattered(partials, running, hop):
        if running is None:
            return scatter_hop(partials[chips - 1], partials[1], hop, chips)
        return scatter_hop(
            add(partials[chips - hop], running[0]), add(partials[hop], running[1]), hop, chips
        )

    def finished(partials, running):
        total = add3(partials[0], *running)
        return total[:local_rows], send(total[local_rows:], swap)

    first_right, first_left, second_right, second_left = [], [], [], []
    for hop in range(1, chips):
        if hop == chips - 1:
            if first_right:
                (own[1],) = after([own[1]], first_right[-1], first_left[-1])
            gathered(1, second_right, second_left, 1)
        gathered(0, first_right, first_left, hop)
    first_out, first_sums, first_sink, first_others = compute(0, first_right, first_left)
    second_right[0], second_left[0] = after([second_right[0], second_left[0]], first_sink)
    running = None
    for hop in range(2, chips):
        gathered(1, second_right, second_left, hop)
        running = scattered(first_sums, running, hop - 1)
    first_back = send(first_others, swap)
    second_out, second_sums, second_sink, second_others = compute(1, second_right, second_left)
    if running is not None:
        running = after(running, second_sink)
    running = scattered(first_sums, running, chips - 1)

    blank = jnp.zeros_like(first_sink)
    sink_grad = jnp.concatenate([first_sink, second_sink])
    sink_grad = jnp.where(
        core == 0,
        jnp.concatenate([sink_grad, blank, blank]),
        jnp.concatenate([blank, blank, sink_grad]),
    )
    sink_grad = jnp.pad(sink_grad.reshape(1, -1), ((0, 7), (0, 128 - head_count)))
    steps = [("dp", 1 << at) for at in range((lax.axis_size("dp") - 1).bit_length())]
    steps += [("ctx", 1 << at) for at in range((2 * chips - 1).bit_length())]

    def exchange(value, step):
        name, bit = step
        size = lax.axis_size(name)
        return value + lax.ppermute(value, name, [(at, at ^ bit) for at in range(size)])

    tail = None
    per_hop = -(-len(steps) // (chips - 1))
    for hop in range(1, chips):
        tail = scattered(second_sums, tail, hop)
        if hop == 1:
            first_total = finished(first_sums, running)
        for step in steps[:per_hop]:
            sink_grad = exchange(sink_grad, step)
        steps = steps[per_hop:]
        if hop < chips - 1:
            tail = after(tail, sink_grad)
    second_back = send(second_others, swap)
    second_total = finished(second_sums, tail)
    sink_grad = sink_grad[0, :head_count]

    def whole(mine, other):
        return jnp.where(
            core == 0, jnp.concatenate(mine + other, axis=1), jnp.concatenate(other + mine, axis=1)
        )

    wide = width * ratio
    attn_out, query_grad = [
        whole(
            [part[at][:local_rows] for part in (first_out, second_out)],
            [part[:, at * wide : (at + 1) * wide] for part in (first_back, second_back)],
        )
        for at in range(2)
    ]
    key_grad, value_grad = [
        whole(
            *[
                [
                    part[side][:, at : at + HD]
                    for part in (first_total, second_total)
                    for at in range(first, 2 * width, 2 * HD)
                ]
                for side in range(2)
            ]
        )
        for first in (0, HD)
    ]
    return (attn_out, query_grad, key_grad, value_grad, sink_grad)


def solution(mesh):
    rows = P(("dp", "ctx"), None)
    return jax.shard_map(
        per_device,
        mesh=mesh,
        in_specs=(rows, rows, rows, rows, P(), P(), P(), P()),
        out_specs=(rows, rows, rows, rows, P()),
        check_vma=False,
    )
```

time: 166 us -> 151 us (0.910)
  blocking collectives: 41.5 us -> 0 us
  starting transfers between devices: 52.2 us -> 71.8 us
  waiting for transfers between devices: 22.5 us -> 33.7 us
  Pallas kernels: 25.5 us -> 15.9 us
  local copies, waits for them, and re-layouts: 11.6 us -> 16 us
    psum x1 -> x0, blocking collectives: 41.5 us -> none  [per_device(): sink_grad = lax.psum(sink_own, ('dp', 'ctx'))]
    ppermute x29 -> x30, starting transfers between devices: 52.2 us -> 64.3 us  [send(): return lax.ppermute(value, 'ctx', pairs)]
    pallas_call x2, Pallas kernels: 22.5 us -> 12.9 us  [attend(): pl.pallas_call(functools.partial(attention_kernel, shape), in_specs=[smem...]
    ppermute x0 -> x5, starting transfers between devices: none -> 7.5 us  [exchange(): lax.ppermute(value, name, [(at, at ^ bit) for at in range(size)])]
    ppermute x0 -> x5, waiting for transfers between devices: none -> 6.21 us  [exchange(): lax.ppermute(value, name, [(at, at ^ bit) for at in range(size)])]
    ppermute x29 -> x30, waiting for transfers between devices: 22.5 us -> 27.5 us  [send(): return lax.ppermute(value, 'ctx', pairs)]
    slice x6 -> x9, local copies, waits for them, and re-layouts: 0.33 us -> 3.59 us  [the longest x2 1.89 us: per_device(): part[:, at * wide:(at + 1) * wide]]
    unnamed x67 -> x79, local copies, waits for them, and re-layouts: 9.62 us -> 9.19 us
  transfers between devices with their start and end apart: 29 -> 35, of which waited for: 8 -> 11; matrix products, arithmetic and copies ran while one was open for 4% -> 10% of each run, Pallas kernels for 15% -> 11%
where the time goes in v2:
time: 151 us; the launch traced here: 150 us
  starting transfers between devices  71.8 us (48%)
  waiting for transfers between devices  33.7 us (22%)
  local copies, waits for them, and re-layouts  16 us (11%)
  Pallas kernels  15.9 us (11%)
  other arithmetic  11.5 us (8%)
    ppermute x30, starting transfers between devices, send(): return lax.ppermute(value, 'ctx', pairs)  64.3 us
    ppermute x30, waiting for transfers between devices, send(): return lax.ppermute(value, 'ctx', pairs)  27.5 us
    pallas_call x2, Pallas kernels, attend(): pl.pallas_call(functools.partial(attention_kernel, shape), in_specs=[smem...  12.9 us
    unnamed x79, local copies, waits for them, and re-layouts  9.19 us
    ppermute x5, starting transfers between devices, exchange(): lax.ppermute(value, name, [(at, at ^ bit) for at in range(size)])  7.5 us
    ppermute x5, waiting for transfers between devices, exchange(): lax.ppermute(value, name, [(at, at ^ bit) for at in range(size)])  6.21 us
    convert_element_type x6, other arithmetic, add(): (left.astype(jnp.float32) + right.astype(jnp.float32)).astype(jnp.bfloat16)  4.42 us
    select_n x4, other arithmetic, whole(): jnp.where(core == 0, jnp.concatenate(mine + other, axis=1), jnp.concatena...  3.91 us
  transfers between devices with their start and end apart: 35, of which 11 were waited for; matrix products, arithmetic and copies ran while one was open for 10% of the time, Pallas kernels for 11%

profile of v2, /device:TPU:0, one launch (start us, length us, event | category | flops | bytes accessed | tf_op | source)
XLA Modules:
  0.0 150.4 jit_solution(17505569370169512773)
XLA Ops:
  0.7 1.2 constant_dynamic-slice_fusion.6
  2.4 1.1 constant_dynamic-slice_fusion.8
  3.5 1.1 pad_maximum_fusion
  4.8 4.9 %collective-permute-start.2 = (bf16[256,512]{1,0:T(8,128)(2,1)S(1)}, bf16[256,512]{1,0:T(8,128)(2,1)S(1)}, u32[]{:S(2)}, u32[]{:S(2)}) collective-permute-start(bf16[256,512]{1,0:T(8,128)(2,1)S(1)} %pad_maximum_fusion.4.refs_0_), channel_id=1, source_target_pairs={{0,2},{1,3},{2,4},{3,5},{4,6},{5,7},{8,10},{9,11},{10,12},{11,13},... | collective-permute-start | bytes 786440 | tf_op jit(solution)/shard_map/ppermute | solution.py:259
  9.7 1.3 collective-permute-start.5
  11.0 4.7 %collective-permute-done.2.refs_1_ = bf16[256,512]{1,0:T(8,128)(2,1)S(1)} collective-permute-done((bf16[256,512]{1,0:T(8,128)(2,1)S(1)}, bf16[256,512]{1,0:T(8,128)(2,1)S(1)}, u32[]{:S(2)}, u32[]{:S(2)}) %collective-permute-start.2) | collective-permute-done | bytes 262176 | tf_op jit(solution)/shard_map/ppermute | solution.py:259
  16.3 3.5 %collective-permute-done.5.refs_4_ = bf16[256,512]{1,0:T(8,128)(2,1)S(1)} collective-permute-done((bf16[256,512]{1,0:T(8,128)(2,1)S(1)}, bf16[256,512]{1,0:T(8,128)(2,1)S(1)}, u32[]{:S(2)}, u32[]{:S(2)}) %collective-permute-start.5) | collective-permute-done | bytes 262176 | tf_op jit(solution)/shard_map/ppermute | solution.py:259
  19.8 1.3 collective-permute-start.6
  21.1 1.4 collective-permute-start.4
  23.2 6.2 %collective-permute-done.6.refs_5_ = bf16[256,512]{1,0:T(8,128)(2,1)} collective-permute-done((bf16[256,512]{1,0:T(8,128)(2,1)S(1)}, bf16[256,512]{1,0:T(8,128)(2,1)}, u32[]{:S(2)}, u32[]{:S(2)}) %collective-permute-start.6) | collective-permute-done | bytes 262176 | tf_op jit(solution)/shard_map/ppermute | solution.py:259
  29.3 1.3 collective-permute-start.7
  31.2 3.0 %shard_map.119.table_ref = s32[4,17]{1,0:T(4,128)} custom-call(s32[7]{0:T(128)} %pad_add_fusion.1.place_ref, s32[16]{0:T(128)} %map_ref.1, s32[4,4]{1,0:T(4,128)} %lengths_ref.1, s32[4]{0:T(128)} %assign_ref.1), custom_call_target="tpu_custom_call" | custom-call | tf_op jit(solution)/shard_map/pallas_call | solution.py:350
  34.3 5.3 %collective-permute-start.8 = (bf16[256,512]{1,0:T(8,128)(2,1)S(1)}, bf16[256,512]{1,0:T(8,128)(2,1)S(1)}, u32[]{:S(2)}, u32[]{:S(2)}) collective-permute-start(bf16[256,512]{1,0:T(8,128)(2,1)S(1)} %pad_maximum_fusion.5.refs_0_), channel_id=1, source_target_pairs={{0,2},{1,3},{2,4},{3,5},{4,6},{5,7},{8,10},{9,11},{10,12},{11,13},... | collective-permute-start | bytes 786440 | tf_op jit(solution)/shard_map/ppermute | solution.py:259
  39.6 1.3 collective-permute-start.9
  42.2 0.9 copy-done.21
  43.2 0.9 copy-done.23
  44.1 0.9 copy-done.25
  45.1 6.5 %shard_map.120 = (bf16[256,1024]{1,0:T(8,128)(2,1)S(1)}, bf16[256,1024]{1,0:T(8,128)(2,1)S(1)}, bf16[256,512]{1,0:T(8,128)(2,1)S(1)}, bf16[256,512]{1,0:T(8,128)...) custom-call(s32[7]{0:T(128)S(1)} %copy-done.16, ...), custom_call_target="tpu_custom_call" | custom-call | flops 1610612736 | bytes 4194304 | tf_op jit(solution)/shard_map/pallas_call | solution.py:235
  54.7 1.3 collective-permute-start.12
  56.0 8.7 %collective-permute-start.16 = (bf16[256,512]{1,0:T(8,128)(2,1)S(1)}, bf16[256,512]{1,0:T(8,128)(2,1)}, u32[]{:S(2)}, u32[]{:S(2)}) collective-permute-start(bf16[256,512]{1,0:T(8,128)(2,1)S(1)} %get-tuple-element.38), channel_id=1, source_target_pairs={{0,2},{1,3},{8,10},{9,11},{16,18},{17,19},{24,26},{25,27}} | collective-permute-start | bytes 786440 | tf_op jit(solution)/shard_map/ppermute | solution.py:259
  64.8 1.4 collective-permute-start.18
  67.1 2.0 %collective-permute-done.12.refs_5_ = bf16[256,512]{1,0:T(8,128)(2,1)} collective-permute-done((bf16[256,512]{1,0:T(8,128)(2,1)}, bf16[256,512]{1,0:T(8,128)(2,1)}, u32[]{:S(2)}, u32[]{:S(2)}) %collective-permute-start.12) | collective-permute-done | bytes 262176 | tf_op jit(solution)/shard_map/ppermute | solution.py:259
  69.1 1.3 collective-permute-start.13
  70.4 2.0 %fusion.1 = (bf16[256,512]{1,0:T(8,128)(2,1)}, bf16[256,512]{1,0:T(8,128)(2,1)}) fusion(bf16[256,512]{1,0:T(8,128)(2,1)S(1)} %get-tuple-element.37, bf16[256,512]{1,0:T(8,128)(2,1)} %collective-permute-done.18, bf16[256,512]{1,0:T(8,128)(2,1)} %collective-permute-done.16), kind=kLoop, calls=%fused_computation.8 | loop fusion | flops 917504 | bytes 1310720 | tf_op jit(solution)/shard_map/convert_element_type | solution.py:290
  72.4 5.3 %collective-permute-start.17 = (bf16[256,512]{1,0:T(8,128)(2,1)}, bf16[256,512]{1,0:T(8,128)(2,1)}, u32[]{:S(2)}, u32[]{:S(2)}) collective-permute-start(bf16[256,512]{1,0:T(8,128)(2,1)} %get-tuple-element.80), channel_id=1, source_target_pairs={{0,2},{1,3},{2,4},{3,5},{8,10},{9,11},{10,12},{11,13},{16,18},{17,... | collective-permute-start | bytes 786440 | tf_op jit(solution)/shard_map/ppermute | solution.py:259
  77.7 1.4 collective-permute-start.19
  79.1 1.9 %fusion.6 = (bf16[128,1024]{1,0:T(8,128)(2,1)}, bf16[128,1024]{1,0:T(8,128)(2,1)}) fusion(bf16[128,2048]{1,0:T(8,128)(2,1)} %collective-permute-done.14), kind=kLoop, calls=%fused_computation.72 | loop fusion | bytes 1048576 | tf_op jit(solution)/shard_map/slice | solution.py:443
  81.0 0.9 copy-done.19
  81.9 0.9 copy-done.27
  82.9 6.4 %shard_map.121 = (bf16[256,1024]{1,0:T(8,128)(2,1)S(1)}, bf16[256,1024]{1,0:T(8,128)(2,1)S(1)}, bf16[256,512]{1,0:T(8,128)(2,1)S(1)}, bf16[256,512]{1,0:T(8,128)...) custom-call(s32[7]{0:T(128)S(1)} %copy-done.17, ...), custom_call_target="tpu_custom_call" | custom-call | flops 1610612736 | bytes 4194304 | tf_op jit(solution)/shard_map/pallas_call | solution.py:235
  92.5 1.1 add_convert_fusion.5
  93.6 4.3 %collective-permute-start.20 = (bf16[256,512]{1,0:T(8,128)(2,1)S(1)}, bf16[256,512]{1,0:T(8,128)(2,1)S(1)}, u32[]{:S(2)}, u32[]{:S(2)}) collective-permute-start(bf16[256,512]{1,0:T(8,128)(2,1)S(1)} %add_convert_fusion.5), channel_id=1, source_target_pairs={{0,2},{1,3},{2,4},{3,5},{4,6},{5,7},{8,10},{9,11},{10,12},{11,13},... | collective-permute-start | bytes 786440 | tf_op jit(solution)/shard_map/ppermute | solution.py:259
  98.0 2.7 %collective-permute-start.25 = (f32[8,128]{1,0:T(8,128)S(1)}, f32[8,128]{1,0:T(8,128)S(1)}, u32[]{:S(2)}, u32[]{:S(2)}) collective-permute-start(f32[8,128]{1,0:T(8,128)S(1)} %pad_add_fusion), channel_id=1, source_target_pairs={{0,16},{8,24},{16,0},{24,8},{1,17},{9,25},{17,1},{25,9},{2,18},{10... | collective-permute-start | bytes 12296 | tf_op jit(solution)/shard_map/ppermute | solution.py:417
  100.6 1.1 add_convert_fusion.4
  101.7 1.3 collective-permute-start.21
  103.0 5.2 %collective-permute-start.22 = (bf16[256,512]{1,0:T(8,128)(2,1)S(1)}, bf16[256,512]{1,0:T(8,128)(2,1)S(1)}, u32[]{:S(2)}, u32[]{:S(2)}) collective-permute-start(bf16[256,512]{1,0:T(8,128)(2,1)S(1)} %get-tuple-element.44), channel_id=1, source_target_pairs={{0,2},{1,3},{8,10},{9,11},{16,18},{17,19},{24,26},{25,27}} | collective-permute-start | bytes 786440 | tf_op jit(solution)/shard_map/ppermute | solution.py:259
  109.1 1.1 collective-permute-done.28
  110.2 3.6 %collective-permute-done.29 = f32[8,128]{1,0:T(8,128)S(1)} collective-permute-done((f32[8,128]{1,0:T(8,128)S(1)}, f32[8,128]{1,0:T(8,128)S(1)}, u32[]{:S(2)}, u32[]{:S(2)}) %collective-permute-start.29) | collective-permute-done | bytes 4128 | tf_op jit(solution)/shard_map/ppermute | solution.py:417
  113.8 4.0 %collective-permute-start.34 = (f32[8,128]{1,0:T(8,128)S(1)}, f32[8,128]{1,0:T(8,128)S(1)}, u32[]{:S(2)}, u32[]{:S(2)}) collective-permute-start(f32[8,128]{1,0:T(8,128)S(1)} %add.107), channel_id=1, source_target_pairs={{0,4},{1,5},{2,6},{3,7},{4,0},{5,1},{6,2},{7,3},{8,12},{9,13},{10,... | collective-permute-start | bytes 12296 | tf_op jit(solution)/shard_map/ppermute | solution.py:417
  117.9 1.5 %collective-permute-done.34 = f32[8,128]{1,0:T(8,128)S(1)} collective-permute-done((f32[8,128]{1,0:T(8,128)S(1)}, f32[8,128]{1,0:T(8,128)S(1)}, u32[]{:S(2)}, u32[]{:S(2)}) %collective-permute-start.34) | collective-permute-done | bytes 4128 | tf_op jit(solution)/shard_map/ppermute | solution.py:417
  120.8 1.7 %collective-permute-start.26 = (bf16[256,512]{1,0:T(8,128)(2,1)S(1)}, bf16[256,512]{1,0:T(8,128)(2,1)S(1)}, u32[]{:S(2)}, u32[]{:S(2)}) collective-permute-start(bf16[256,512]{1,0:T(8,128)(2,1)S(1)} %get-tuple-element.78), channel_id=1, source_target_pairs={{0,2},{1,3},{2,4},{3,5},{8,10},{9,11},{10,12},{11,13},{16,18},{17,... | collective-permute-start | bytes 786440 | tf_op jit(solution)/shard_map/ppermute | solution.py:259
  123.2 5.0 %collective-permute-done.26 = bf16[256,512]{1,0:T(8,128)(2,1)S(1)} collective-permute-done((bf16[256,512]{1,0:T(8,128)(2,1)S(1)}, bf16[256,512]{1,0:T(8,128)(2,1)S(1)}, u32[]{:S(2)}, u32[]{:S(2)}) %collective-permute-start.26) | collective-permute-done | bytes 262176 | tf_op jit(solution)/shard_map/ppermute | solution.py:259
  128.3 9.9 %collective-permute-start.30 = (bf16[256,512]{1,0:T(8,128)(2,1)S(1)}, bf16[256,512]{1,0:T(8,128)(2,1)S(1)}, u32[]{:S(2)}, u32[]{:S(2)}) collective-permute-start(bf16[256,512]{1,0:T(8,128)(2,1)S(1)} %add_convert_fusion.2), channel_id=1, source_target_pairs={{0,2},{1,3},{2,4},{3,5},{4,6},{5,7},{8,10},{9,11},{10,12},{11,13},... | collective-permute-start | bytes 786440 | tf_op jit(solution)/shard_map/ppermute | solution.py:259
  138.3 1.3 collective-permute-start.31
  139.7 1.2 maximum_select_fusion.1
  140.9 1.9 %collective-permute-done.30 = bf16[256,512]{1,0:T(8,128)(2,1)S(1)} collective-permute-done((bf16[256,512]{1,0:T(8,128)(2,1)S(1)}, bf16[256,512]{1,0:T(8,128)(2,1)S(1)}, u32[]{:S(2)}, u32[]{:S(2)}) %collective-permute-start.30) | collective-permute-done | bytes 262176 | tf_op jit(solution)/shard_map/ppermute | solution.py:259
  142.8 4.2 %collective-permute-done.31 = bf16[256,512]{1,0:T(8,128)(2,1)S(1)} collective-permute-done((bf16[256,512]{1,0:T(8,128)(2,1)S(1)}, bf16[256,512]{1,0:T(8,128)(2,1)S(1)}, u32[]{:S(2)}, u32[]{:S(2)}) %collective-permute-start.31) | collective-permute-done | bytes 262176 | tf_op jit(solution)/shard_map/ppermute | solution.py:259
  147.2 1.2 maximum_select_fusion
  (155 shorter events, 16.5 us)
Async XLA Ops:
  1.9 2.9 %collective-permute-start.1 = (bf16[128,1024]{1,0:T(8,128)(2,1)S(1)}, bf16[128,1024]{1,0:T(8,128)(2,1)S(1)}, u32[]{:S(2)}, u32[]{:S(2)}) collective-permute-start(bf16[128,1024]{1,0:T(8,128)(2,1)S(1)} %pad_maximum_fusion.3), channel_id=1, source_target_pairs={{0,1},{1,0},{2,3},{3,2},{4,5},{5,4},{6,7},{7,6},{8,9},{9,8},{10,11... | collective-permute-start | bytes 786440 | tf_op jit(solution)/shard_map/ppermute | solution.py:259
  4.6 36.3 %copy-start.1 = (bf16[128,4096]{1,0:T(8,128)(2,1)S(1)}, bf16[128,4096]{1,0:T(8,128)(2,1)}, u32[]{:S(2)}) copy-start(bf16[128,4096]{1,0:T(8,128)(2,1)} %g_hbm.3) | copy-start | bytes 3145732
  4.6 36.3 %copy-start.28 = (f32[32]{0:T(128)S(1)}, f32[32]{0:T(128)}, u32[]{:S(2)}) copy-start(f32[32]{0:T(128)} %sink_ref.3) | copy-start | bytes 388
  4.6 36.3 %collective-permute-start = (bf16[128,4096]{1,0:T(8,128)(2,1)}, bf16[128,4096]{1,0:T(8,128)(2,1)}, u32[]{:S(2)}, u32[]{:S(2)}) collective-permute-start(bf16[128,4096]{1,0:T(8,128)(2,1)} %pad_maximum_fusion), channel_id=1, source_target_pairs={{0,1},{1,0},{2,3},{3,2},{4,5},{5,4},{6,7},{7,6},{8,9},{9,8},{10,11... | collective-permute-start | bytes 3145736 | tf_op jit(solution)/shard_map/ppermute | solution.py:259
  4.8 10.8 %collective-permute-start.2 = (bf16[256,512]{1,0:T(8,128)(2,1)S(1)}, bf16[256,512]{1,0:T(8,128)(2,1)S(1)}, u32[]{:S(2)}, u32[]{:S(2)}) collective-permute-start(bf16[256,512]{1,0:T(8,128)(2,1)S(1)} %pad_maximum_fusion.4.refs_0_), channel_id=1, source_target_pairs={{0,2},{1,3},{2,4},{3,5},{4,6},{5,7},{8,10},{9,11},{10,12},{11,13},... | collective-permute-start | bytes 786440 | tf_op jit(solution)/shard_map/ppermute | solution.py:259
  9.7 10.1 %collective-permute-start.5 = (bf16[256,512]{1,0:T(8,128)(2,1)S(1)}, bf16[256,512]{1,0:T(8,128)(2,1)S(1)}, u32[]{:S(2)}, u32[]{:S(2)}) collective-permute-start(bf16[256,512]{1,0:T(8,128)(2,1)S(1)} %pad_maximum_fusion.4.refs_0_), channel_id=1, source_target_pairs={{2,0},{3,1},{4,2},{5,3},{6,4},{7,5},{10,8},{11,9},{12,10},{13,11},... | collective-permute-start | bytes 786440 | tf_op jit(solution)/shard_map/ppermute | solution.py:259
  15.7 25.2 %copy-start.20 = (bf16[256,512]{1,0:T(8,128)(2,1)}, bf16[256,512]{1,0:T(8,128)(2,1)S(1)}, u32[]{:S(2)}) copy-start(bf16[256,512]{1,0:T(8,128)(2,1)S(1)} %collective-permute-done.2.refs_1_) | copy-start | bytes 786436
  15.7 5.4 %collective-permute-start.3 = (bf16[256,512]{1,0:T(8,128)(2,1)S(1)}, bf16[256,512]{1,0:T(8,128)(2,1)S(1)}, u32[]{:S(2)}, u32[]{:S(2)}) collective-permute-start(bf16[256,512]{1,0:T(8,128)(2,1)S(1)} %collective-permute-done.2.refs_1_), channel_id=1, source_target_pairs={{2,4},{3,5},{4,6},{5,7},{10,12},{11,13},{12,14},{13,15},{18,20},{1... | collective-permute-start | bytes 786440 | tf_op jit(solution)/shard_map/ppermute | solution.py:259
  19.8 21.1 %copy-start.22 = (bf16[256,512]{1,0:T(8,128)(2,1)}, bf16[256,512]{1,0:T(8,128)(2,1)S(1)}, u32[]{:S(2)}) copy-start(bf16[256,512]{1,0:T(8,128)(2,1)S(1)} %collective-permute-done.5.refs_4_) | copy-start | bytes 786436
  19.8 9.5 %collective-permute-start.6 = (bf16[256,512]{1,0:T(8,128)(2,1)S(1)}, bf16[256,512]{1,0:T(8,128)(2,1)}, u32[]{:S(2)}, u32[]{:S(2)}) collective-permute-start(bf16[256,512]{1,0:T(8,128)(2,1)S(1)} %collective-permute-done.5.refs_4_), channel_id=1, source_target_pairs={{2,0},{3,1},{4,2},{5,3},{10,8},{11,9},{12,10},{13,11},{18,16},{19,... | collective-permute-start | bytes 786440 | tf_op jit(solution)/shard_map/ppermute | solution.py:259
  21.1 19.8 %collective-permute-start.4 = (bf16[256,512]{1,0:T(8,128)(2,1)S(1)}, bf16[256,512]{1,0:T(8,128)(2,1)}, u32[]{:S(2)}, u32[]{:S(2)}) collective-permute-start(bf16[256,512]{1,0:T(8,128)(2,1)S(1)} %collective-permute-done.3.refs_2_), channel_id=1, source_target_pairs={{4,6},{5,7},{12,14},{13,15},{20,22},{21,23},{28,30},{29,31}} | collective-permute-start | bytes 786440 | tf_op jit(solution)/shard_map/ppermute | solution.py:259
  29.3 11.6 %collective-permute-start.7 = (bf16[256,512]{1,0:T(8,128)(2,1)}, bf16[256,512]{1,0:T(8,128)(2,1)}, u32[]{:S(2)}, u32[]{:S(2)}) collective-permute-start(bf16[256,512]{1,0:T(8,128)(2,1)} %collective-permute-done.6.refs_5_), channel_id=1, source_target_pairs={{2,0},{3,1},{10,8},{11,9},{18,16},{19,17},{26,24},{27,25}} | collective-permute-start | bytes 786440 | tf_op jit(solution)/shard_map/ppermute | solution.py:259
  34.3 17.3 %copy-start.8 = (bf16[256,512]{1,0:T(8,128)(2,1)}, bf16[256,512]{1,0:T(8,128)(2,1)S(1)}, u32[]{:S(2)}) copy-start(bf16[256,512]{1,0:T(8,128)(2,1)S(1)} %pad_maximum_fusion.5.refs_0_) | copy-start | bytes 786436
  34.3 19.7 %collective-permute-start.8 = (bf16[256,512]{1,0:T(8,128)(2,1)S(1)}, bf16[256,512]{1,0:T(8,128)(2,1)S(1)}, u32[]{:S(2)}, u32[]{:S(2)}) collective-permute-start(bf16[256,512]{1,0:T(8,128)(2,1)S(1)} %pad_maximum_fusion.5.refs_0_), channel_id=1, source_target_pairs={{0,2},{1,3},{2,4},{3,5},{4,6},{5,7},{8,10},{9,11},{10,12},{11,13},... | collective-permute-start | bytes 786440 | tf_op jit(solution)/shard_map/ppermute | solution.py:259
  39.6 14.5 %collective-permute-start.9 = (bf16[256,512]{1,0:T(8,128)(2,1)S(1)}, bf16[256,512]{1,0:T(8,128)(2,1)}, u32[]{:S(2)}, u32[]{:S(2)}) collective-permute-start(bf16[256,512]{1,0:T(8,128)(2,1)S(1)} %pad_maximum_fusion.5.refs_0_), channel_id=1, source_target_pairs={{2,0},{3,1},{4,2},{5,3},{6,4},{7,5},{10,8},{11,9},{12,10},{13,11},... | collective-permute-start | bytes 786440 | tf_op jit(solution)/shard_map/ppermute | solution.py:259
  51.6 13.2 %copy-start.7 = (bf16[256,512]{1,0:T(8,128)(2,1)}, bf16[256,512]{1,0:T(8,128)(2,1)S(1)}, u32[]{:S(2)}) copy-start(bf16[256,512]{1,0:T(8,128)(2,1)S(1)} %get-tuple-element.36) | copy-start | bytes 786436
  54.0 25.1 %collective-permute-start.14 = (bf16[128,2048]{1,0:T(8,128)(2,1)}, bf16[128,2048]{1,0:T(8,128)(2,1)}, u32[]{:S(2)}, u32[]{:S(2)}) collective-permute-start(bf16[128,2048]{1,0:T(8,128)(2,1)} %pad_maximum_fusion.1), channel_id=1, source_target_pairs={{0,1},{1,0},{2,3},{3,2},{4,5},{5,4},{6,7},{7,6},{8,9},{9,8},{10,11... | collective-permute-start | bytes 1572872 | tf_op jit(solution)/shard_map/ppermute | solution.py:259
  54.0 26.9 %copy-start.18 = (bf16[256,512]{1,0:T(8,128)(2,1)}, bf16[256,512]{1,0:T(8,128)(2,1)S(1)}, u32[]{:S(2)}) copy-start(bf16[256,512]{1,0:T(8,128)(2,1)S(1)} %collective-permute-done.8.refs_1_) | copy-start | bytes 786436
  54.0 12.4 %collective-permute-start.10 = (bf16[256,512]{1,0:T(8,128)(2,1)S(1)}, bf16[256,512]{1,0:T(8,128)(2,1)S(1)}, u32[]{:S(2)}, u32[]{:S(2)}) collective-permute-start(bf16[256,512]{1,0:T(8,128)(2,1)S(1)} %collective-permute-done.8.refs_1_), channel_id=1, source_target_pairs={{2,4},{3,5},{4,6},{5,7},{10,12},{11,13},{12,14},{13,15},{18,20},{1... | collective-permute-start | bytes 786440 | tf_op jit(solution)/shard_map/ppermute | solution.py:259
  54.7 14.4 %collective-permute-start.12 = (bf16[256,512]{1,0:T(8,128)(2,1)}, bf16[256,512]{1,0:T(8,128)(2,1)}, u32[]{:S(2)}, u32[]{:S(2)}) collective-permute-start(bf16[256,512]{1,0:T(8,128)(2,1)} %collective-permute-done.9.refs_4_), channel_id=1, source_target_pairs={{2,0},{3,1},{4,2},{5,3},{10,8},{11,9},{12,10},{13,11},{18,16},{19,... | collective-permute-start | bytes 786440 | tf_op jit(solution)/shard_map/ppermute | solution.py:259
  56.0 14.4 %collective-permute-start.16 = (bf16[256,512]{1,0:T(8,128)(2,1)S(1)}, bf16[256,512]{1,0:T(8,128)(2,1)}, u32[]{:S(2)}, u32[]{:S(2)}) collective-permute-start(bf16[256,512]{1,0:T(8,128)(2,1)S(1)} %get-tuple-element.38), channel_id=1, source_target_pairs={{0,2},{1,3},{8,10},{9,11},{16,18},{17,19},{24,26},{25,27}} | collective-permute-start | bytes 786440 | tf_op jit(solution)/shard_map/ppermute | solution.py:259
  64.8 5.6 %collective-permute-start.18 = (bf16[256,512]{1,0:T(8,128)(2,1)S(1)}, bf16[256,512]{1,0:T(8,128)(2,1)}, u32[]{:S(2)}, u32[]{:S(2)}) collective-permute-start(bf16[256,512]{1,0:T(8,128)(2,1)S(1)} %get-tuple-element.36), channel_id=1, source_target_pairs={{6,4},{7,5},{14,12},{15,13},{22,20},{23,21},{30,28},{31,29}} | collective-permute-start | bytes 786440 | tf_op jit(solution)/shard_map/ppermute | solution.py:259
  66.4 14.5 %copy-start.26 = (bf16[256,512]{1,0:T(8,128)(2,1)}, bf16[256,512]{1,0:T(8,128)(2,1)S(1)}, u32[]{:S(2)}) copy-start(bf16[256,512]{1,0:T(8,128)(2,1)S(1)} %collective-permute-done.10.refs_2_) | copy-start | bytes 786436
  66.4 14.5 %collective-permute-start.11 = (bf16[256,512]{1,0:T(8,128)(2,1)S(1)}, bf16[256,512]{1,0:T(8,128)(2,1)S(1)}, u32[]{:S(2)}, u32[]{:S(2)}) collective-permute-start(bf16[256,512]{1,0:T(8,128)(2,1)S(1)} %collective-permute-done.10.refs_2_), channel_id=1, source_target_pairs={{4,6},{5,7},{12,14},{13,15},{20,22},{21,23},{28,30},{29,31}} | collective-permute-start | bytes 786440 | tf_op jit(solution)/shard_map/ppermute | solution.py:259
  69.1 11.8 %collective-permute-start.13 = (bf16[256,512]{1,0:T(8,128)(2,1)}, bf16[256,512]{1,0:T(8,128)(2,1)S(1)}, u32[]{:S(2)}, u32[]{:S(2)}) collective-permute-start(bf16[256,512]{1,0:T(8,128)(2,1)} %collective-permute-done.12.refs_5_), channel_id=1, source_target_pairs={{2,0},{3,1},{10,8},{11,9},{18,16},{19,17},{26,24},{27,25}} | collective-permute-start | bytes 786440 | tf_op jit(solution)/shard_map/ppermute | solution.py:259
  70.4 10.5 %copy-start.9 = (bf16[256,512]{1,0:T(8,128)(2,1)S(1)}, bf16[256,512]{1,0:T(8,128)(2,1)}, u32[]{:S(2)}) copy-start(bf16[256,512]{1,0:T(8,128)(2,1)} %copy-done.8) | copy-start | bytes 786436
  70.4 10.5 %copy-start.15 = (s32[4,17]{1,0:T(4,128)S(1)}, s32[4,17]{1,0:T(4,128)}, u32[]{:S(2)}) copy-start(s32[4,17]{1,0:T(4,128)} %shard_map.119.table_ref) | copy-start | bytes 820
  72.4 20.1 %collective-permute-start.17 = (bf16[256,512]{1,0:T(8,128)(2,1)}, bf16[256,512]{1,0:T(8,128)(2,1)}, u32[]{:S(2)}, u32[]{:S(2)}) collective-permute-start(bf16[256,512]{1,0:T(8,128)(2,1)} %get-tuple-element.80), channel_id=1, source_target_pairs={{0,2},{1,3},{2,4},{3,5},{8,10},{9,11},{10,12},{11,13},{16,18},{17,... | collective-permute-start | bytes 786440 | tf_op jit(solution)/shard_map/ppermute | solution.py:259
  77.7 14.8 %collective-permute-start.19 = (bf16[256,512]{1,0:T(8,128)(2,1)}, bf16[256,512]{1,0:T(8,128)(2,1)}, u32[]{:S(2)}, u32[]{:S(2)}) collective-permute-start(bf16[256,512]{1,0:T(8,128)(2,1)} %get-tuple-element.79), channel_id=1, source_target_pairs={{4,2},{5,3},{6,4},{7,5},{12,10},{13,11},{14,12},{15,13},{20,18},{2... | collective-permute-start | bytes 786440 | tf_op jit(solution)/shard_map/ppermute | solution.py:259
  91.4 16.8 %copy-start.3 = (bf16[256,512]{1,0:T(8,128)(2,1)S(1)}, bf16[256,512]{1,0:T(8,128)(2,1)}, u32[]{:S(2)}) copy-start(bf16[256,512]{1,0:T(8,128)(2,1)} %copy-done.2) | copy-start | bytes 786436
  91.8 6.2 %collective-permute-start.24 = (f32[8,128]{1,0:T(8,128)S(1)}, f32[8,128]{1,0:T(8,128)S(1)}, u32[]{:S(2)}, u32[]{:S(2)}) collective-permute-start(f32[8,128]{1,0:T(8,128)S(1)} %pad.4), channel_id=1, source_target_pairs={{0,8},{8,0},{16,24},{24,16},{1,9},{9,1},{17,25},{25,17},{2,10},{10... | collective-permute-start | bytes 12296 | tf_op jit(solution)/shard_map/ppermute | solution.py:417
  93.6 26.4 %collective-permute-start.20 = (bf16[256,512]{1,0:T(8,128)(2,1)S(1)}, bf16[256,512]{1,0:T(8,128)(2,1)S(1)}, u32[]{:S(2)}, u32[]{:S(2)}) collective-permute-start(bf16[256,512]{1,0:T(8,128)(2,1)S(1)} %add_convert_fusion.5), channel_id=1, source_target_pairs={{0,2},{1,3},{2,4},{3,5},{4,6},{5,7},{8,10},{9,11},{10,12},{11,13},... | collective-permute-start | bytes 786440 | tf_op jit(solution)/shard_map/ppermute | solution.py:259
  98.0 11.0 %collective-permute-start.25 = (f32[8,128]{1,0:T(8,128)S(1)}, f32[8,128]{1,0:T(8,128)S(1)}, u32[]{:S(2)}, u32[]{:S(2)}) collective-permute-start(f32[8,128]{1,0:T(8,128)S(1)} %pad_add_fusion), channel_id=1, source_target_pairs={{0,16},{8,24},{16,0},{24,8},{1,17},{9,25},{17,1},{25,9},{2,18},{10... | collective-permute-start | bytes 12296 | tf_op jit(solution)/shard_map/ppermute | solution.py:417
  101.7 18.2 %collective-permute-start.21 = (bf16[256,512]{1,0:T(8,128)(2,1)S(1)}, bf16[256,512]{1,0:T(8,128)(2,1)S(1)}, u32[]{:S(2)}, u32[]{:S(2)}) collective-permute-start(bf16[256,512]{1,0:T(8,128)(2,1)S(1)} %add_convert_fusion.4), channel_id=1, source_target_pairs={{2,0},{3,1},{4,2},{5,3},{6,4},{7,5},{10,8},{11,9},{12,10},{13,11},... | collective-permute-start | bytes 786440 | tf_op jit(solution)/shard_map/ppermute | solution.py:259
  103.0 17.6 %collective-permute-start.22 = (bf16[256,512]{1,0:T(8,128)(2,1)S(1)}, bf16[256,512]{1,0:T(8,128)(2,1)S(1)}, u32[]{:S(2)}, u32[]{:S(2)}) collective-permute-start(bf16[256,512]{1,0:T(8,128)(2,1)S(1)} %get-tuple-element.44), channel_id=1, source_target_pairs={{0,2},{1,3},{8,10},{9,11},{16,18},{17,19},{24,26},{25,27}} | collective-permute-start | bytes 786440 | tf_op jit(solution)/shard_map/ppermute | solution.py:259
  108.2 12.4 %collective-permute-start.23 = (bf16[256,512]{1,0:T(8,128)(2,1)S(1)}, bf16[256,512]{1,0:T(8,128)(2,1)S(1)}, u32[]{:S(2)}, u32[]{:S(2)}) collective-permute-start(bf16[256,512]{1,0:T(8,128)(2,1)S(1)} %copy-done.3), channel_id=1, source_target_pairs={{6,4},{7,5},{14,12},{15,13},{22,20},{23,21},{30,28},{31,29}} | collective-permute-start | bytes 786440 | tf_op jit(solution)/shard_map/ppermute | solution.py:259
  109.0 1.2 collective-permute-start.28
  110.2 3.6 %collective-permute-start.29 = (f32[8,128]{1,0:T(8,128)S(1)}, f32[8,128]{1,0:T(8,128)S(1)}, u32[]{:S(2)}, u32[]{:S(2)}) collective-permute-start(f32[8,128]{1,0:T(8,128)S(1)} %add.106), channel_id=1, source_target_pairs={{0,2},{1,3},{2,0},{3,1},{4,6},{5,7},{6,4},{7,5},{8,10},{9,11},{10,... | collective-permute-start | bytes 12296 | tf_op jit(solution)/shard_map/ppermute | solution.py:417
  113.8 5.6 %collective-permute-start.34 = (f32[8,128]{1,0:T(8,128)S(1)}, f32[8,128]{1,0:T(8,128)S(1)}, u32[]{:S(2)}, u32[]{:S(2)}) collective-permute-start(f32[8,128]{1,0:T(8,128)S(1)} %add.107), channel_id=1, source_target_pairs={{0,4},{1,5},{2,6},{3,7},{4,0},{5,1},{6,2},{7,3},{8,12},{9,13},{10,... | collective-permute-start | bytes 12296 | tf_op jit(solution)/shard_map/ppermute | solution.py:417
  119.4 20.2 %collective-permute-start.15 = (bf16[128,2048]{1,0:T(8,128)(2,1)S(1)}, bf16[128,2048]{1,0:T(8,128)(2,1)S(1)}, u32[]{:S(2)}, u32[]{:S(2)}) collective-permute-start(bf16[128,2048]{1,0:T(8,128)(2,1)S(1)} %pad_maximum_fusion.2), channel_id=1, source_target_pairs={{0,1},{1,0},{2,3},{3,2},{4,5},{5,4},{6,7},{7,6},{8,9},{9,8},{10,11... | collective-permute-start | bytes 1572872 | tf_op jit(solution)/shard_map/ppermute | solution.py:259
  120.1 3.1 %collective-permute-start.32 = (bf16[128,512]{1,0:T(8,128)(2,1)S(1)}, bf16[128,512]{1,0:T(8,128)(2,1)S(1)}, u32[]{:S(2)}, u32[]{:S(2)}) collective-permute-start(bf16[128,512]{1,0:T(8,128)(2,1)S(1)} %slice.152), channel_id=1, source_target_pairs={{0,1},{1,0},{2,3},{3,2},{4,5},{5,4},{6,7},{7,6},{8,9},{9,8},{10,11... | collective-permute-start | bytes 393224 | tf_op jit(solution)/shard_map/ppermute | solution.py:259
  120.8 7.4 %collective-permute-start.26 = (bf16[256,512]{1,0:T(8,128)(2,1)S(1)}, bf16[256,512]{1,0:T(8,128)(2,1)S(1)}, u32[]{:S(2)}, u32[]{:S(2)}) collective-permute-start(bf16[256,512]{1,0:T(8,128)(2,1)S(1)} %get-tuple-element.78), channel_id=1, source_target_pairs={{0,2},{1,3},{2,4},{3,5},{8,10},{9,11},{10,12},{11,13},{16,18},{17,... | collective-permute-start | bytes 786440 | tf_op jit(solution)/shard_map/ppermute | solution.py:259
  122.5 5.7 %collective-permute-start.27 = (bf16[256,512]{1,0:T(8,128)(2,1)S(1)}, bf16[256,512]{1,0:T(8,128)(2,1)S(1)}, u32[]{:S(2)}, u32[]{:S(2)}) collective-permute-start(bf16[256,512]{1,0:T(8,128)(2,1)S(1)} %get-tuple-element.77), channel_id=1, source_target_pairs={{4,2},{5,3},{6,4},{7,5},{12,10},{13,11},{14,12},{15,13},{20,18},{2... | collective-permute-start | bytes 786440 | tf_op jit(solution)/shard_map/ppermute | solution.py:259
  128.3 11.4 %copy-start.30 = (bf16[128,1024]{1,0:T(8,128)(2,1)S(1)}, bf16[128,1024]{1,0:T(8,128)(2,1)}, u32[]{:S(2)}) copy-start(bf16[128,1024]{1,0:T(8,128)(2,1)} %get-tuple-element.51) | copy-start | bytes 786436
  128.3 11.4 %copy-start.32 = (bf16[128,1024]{1,0:T(8,128)(2,1)S(1)}, bf16[128,1024]{1,0:T(8,128)(2,1)}, u32[]{:S(2)}) copy-start(bf16[128,1024]{1,0:T(8,128)(2,1)} %get-tuple-element.55) | copy-start | bytes 786436
  128.3 14.5 %collective-permute-start.30 = (bf16[256,512]{1,0:T(8,128)(2,1)S(1)}, bf16[256,512]{1,0:T(8,128)(2,1)S(1)}, u32[]{:S(2)}, u32[]{:S(2)}) collective-permute-start(bf16[256,512]{1,0:T(8,128)(2,1)S(1)} %add_convert_fusion.2), channel_id=1, source_target_pairs={{0,2},{1,3},{2,4},{3,5},{4,6},{5,7},{8,10},{9,11},{10,12},{11,13},... | collective-permute-start | bytes 786440 | tf_op jit(solution)/shard_map/ppermute | solution.py:259
  138.3 8.7 %collective-permute-start.31 = (bf16[256,512]{1,0:T(8,128)(2,1)S(1)}, bf16[256,512]{1,0:T(8,128)(2,1)S(1)}, u32[]{:S(2)}, u32[]{:S(2)}) collective-permute-start(bf16[256,512]{1,0:T(8,128)(2,1)S(1)} %add_convert_fusion.1), channel_id=1, source_target_pairs={{2,0},{3,1},{4,2},{5,3},{6,4},{7,5},{10,8},{11,9},{12,10},{13,11},... | collective-permute-start | bytes 786440 | tf_op jit(solution)/shard_map/ppermute | solution.py:259
  147.1 1.4 collective-permute-start.33
  (20 other events, 59.8 us)

commit v3 on v2

--- a/solution.py
+++ b/solution.py
@@ -16,11 +16,11 @@
 MASKED = -1e30
 
 
-def plan_kernel(stretch_len, place_ref, map_ref, lengths_ref, assign_ref, table_ref):
-    chip, core, group = place_ref[0], place_ref[1], place_ref[2]
+def fill_table(
+    chip, core, group, chips, stretch_len, map_ref, lengths_ref, assign_ref, table_ref
+):
     stretches = map_ref.shape[0]
     sequences, documents = lengths_ref.shape
-    chips = place_ref.shape[0] - 3
     per_chip = stretches // chips
     per_core = per_chip // 2
     limit = (table_ref.shape[1] - 1) // 2
@@ -79,14 +79,17 @@
         table_ref[row, 0] = lax.fori_loop(0, stretches, visit, jnp.int32(1))
 
 
-def attention_kernel(shape, place_ref, table_ref, sink_ref, q_hbm, g_hbm, partner_hbm, *refs):
+def attention_kernel(
+    shape, map_ref, lengths_ref, assign_ref, sink_ref, q_hbm, g_hbm, partner_hbm, *refs
+):
     heads, ratio, stretch_len, per_chip, chips, limit, stream = shape
     count_in = 2 * chips - 1
     sources, outs = refs[:count_in], refs[count_in : count_in + 2]
     partials = refs[count_in + 2 : count_in + 2 + chips]
     sink_out = refs[count_in + 2 + chips]
-    kv, q_buf, g_buf, sums, sems = refs[count_in + 3 + chips :]
-    chip, core = place_ref[0], place_ref[1]
+    kv, q_buf, g_buf, sums, table_ref, sems = refs[count_in + 3 + chips :]
+    index = lax.axis_index("ctx")
+    chip, core = index // 2, index % 2
     rows = per_chip * stretch_len
     local_rows = rows // 2
     wide = heads * ratio * HD
@@ -107,6 +110,17 @@
     loads = [pltpu.make_async_copy(*pair, sems.at[at]) for at, pair in enumerate(loads)]
     for load in loads:
         load.start()
+    fill_table(
+        chip,
+        core,
+        lax.axis_index("dp"),
+        chips,
+        stretch_len,
+        map_ref,
+        lengths_ref,
+        assign_ref,
+        table_ref,
+    )
     sums[...] = jnp.zeros_like(sums)
     sink_out[...] = jnp.zeros_like(sink_out)
     block = ratio * stretch_len
@@ -191,8 +205,8 @@
             for spot, at in enumerate(order):
                 part = slice(spot * stretch_len, (spot + 1) * stretch_len)
                 target = pl.ds(sum_rows[at], stretch_len)
-                sums[target, 2 * head * HD : (2 * head + 1) * HD] += dk[part]
-                sums[target, (2 * head + 1) * HD : (2 * head + 2) * HD] += dv[part]
+                sums[target, head * HD : (head + 1) * HD] += dk[part]
+                sums[target, (heads + head) * HD : (heads + head + 1) * HD] += dv[part]
             sink_out[head] -= sink_term * inverse * row_dot
 
     widths = []
@@ -216,43 +230,42 @@
 
     lax.fori_loop(0, per_chip, one_row, 0)
     for at, partial in enumerate(partials):
-        for head in range(heads):
-            left = slice(2 * head * HD, (2 * head + 1) * HD)
-            partial[:, left] = (sums[at * rows : (at + 1) * rows, left] * SCALE).astype(partial.dtype)
-            right = slice((2 * head + 1) * HD, (2 * head + 2) * HD)
-            partial[:, right] = sums[at * rows : (at + 1) * rows, right].astype(partial.dtype)
-
-
-def attend(stream, place, table, sinks, queries, out_grad, partner, sources, chips, limit, ratio):
+        part = slice(at * rows, (at + 1) * rows)
+        partial[:, : heads * HD] = (sums[part, : heads * HD] * SCALE).astype(partial.dtype)
+        partial[:, heads * HD :] = sums[part, heads * HD :].astype(partial.dtype)
+
+
+def attend(stream, layout, sinks, queries, out_grad, partner, sources, chips, limit, ratio):
     heads = sources[0].shape[1] // (2 * HD)
     rows = sources[0].shape[0]
-    per_chip = table.shape[0]
+    per_chip = layout[0].shape[0] // chips
     stretch_len = rows // per_chip
     wide = heads * ratio * HD
     shape = (heads, ratio, stretch_len, per_chip, chips, limit, stream)
-    smem, hbm = pl.BlockSpec(memory_space=pltpu.SMEM), pl.BlockSpec(memory_space=pl.ANY)
+    smem, hbm = pl.BlockSpec(memory_space=pltpu.SMEM), pl.BlockSpec(memory_space=pltpu.HBM)
     vmem = pl.BlockSpec(memory_space=pltpu.VMEM)
     return pl.pallas_call(
         functools.partial(attention_kernel, shape),
-        in_specs=[smem] * 3 + [hbm] * (3 + len(sources)),
+        in_specs=[smem] * 4 + [hbm] * (3 + len(sources)),
         out_specs=[vmem] * (3 + chips),
         scratch_shapes=[
             pltpu.VMEM((len(sources) * rows, heads * 2 * HD), jnp.bfloat16),
             pltpu.VMEM((rows, wide), jnp.bfloat16),
             pltpu.VMEM((rows, wide), jnp.bfloat16),
             pltpu.VMEM((chips * rows, heads * 2 * HD), jnp.float32),
+            pltpu.SMEM((per_chip, 1 + 2 * limit), jnp.int32),
             pltpu.SemaphoreType.DMA((4 + len(sources),)),
         ],
         out_shape=[jax.ShapeDtypeStruct((rows, wide), jnp.bfloat16)] * 2
         + [jax.ShapeDtypeStruct((rows, heads * 2 * HD), jnp.bfloat16)] * chips
         + [jax.ShapeDtypeStruct((heads, 1, ratio * stretch_len), jnp.float32)],
-        compiler_params=pltpu.CompilerParams(vmem_limit_bytes=16 << 20),
+        compiler_params=pltpu.CompilerParams(vmem_limit_bytes=60 << 20),
         cost_estimate=pl.CostEstimate(
             flops=6 * 2 * heads * rows * ratio * limit * stretch_len * HD,
             transcendentals=heads * rows * ratio * limit * stretch_len,
             bytes_accessed=4 << 20,
         ),
-    )(place, table, sinks, queries, out_grad, partner, *sources)
+    )(*layout, sinks, queries, out_grad, partner, *sources)
 
 
 def send(value, pairs):
@@ -280,10 +293,6 @@
         send(rightward, along(chips, 1, range(0, hop))),
         send(leftward, along(chips, -1, range(chips - hop, chips))),
     )
-
-
-def after(values, *earlier):
-    return lax.optimization_barrier((tuple(values), earlier))[0]
 
 
 def add(left, right):
@@ -343,20 +352,11 @@
         ),
         swap,
     )
-    place = jnp.concatenate(
-        [jnp.stack([chip, core, group]).astype(jnp.int32), jnp.zeros((chips,), jnp.int32)]
-    )
-    smem = pl.BlockSpec(memory_space=pltpu.SMEM)
-    table = pl.pallas_call(
-        functools.partial(plan_kernel, stretch_len),
-        in_specs=[smem] * 4,
-        out_specs=smem,
-        out_shape=jax.ShapeDtypeStruct((per_chip, 1 + 2 * limit), jnp.int32),
-    )(place, stretch_map, doc_lengths, assignment)
+    layout = (stretch_map, doc_lengths, assignment)
 
     def compute(stream, right, left):
         results = attend(
-            stream, place, table, sink_logits, queries, out_grad, partner,
+            stream, layout, sink_logits, queries, out_grad, partner,
             [own[stream]] + right + left, chips, limit, ratio,
         )
         heads = results[-1].shape[0]
@@ -383,22 +383,12 @@
 
     first_right, first_left, second_right, second_left = [], [], [], []
     for hop in range(1, chips):
-        if hop == chips - 1:
-            if first_right:
-                (own[1],) = after([own[1]], first_right[-1], first_left[-1])
-            gathered(1, second_right, second_left, 1)
         gathered(0, first_right, first_left, hop)
+        gathered(1, second_right, second_left, hop)
     first_out, first_sums, first_sink, first_others = compute(0, first_right, first_left)
-    second_right[0], second_left[0] = after([second_right[0], second_left[0]], first_sink)
-    running = None
-    for hop in range(2, chips):
-        gathered(1, second_right, second_left, hop)
-        running = scattered(first_sums, running, hop - 1)
-    first_back = send(first_others, swap)
+    first_run = scattered(first_sums, None, 1)
     second_out, second_sums, second_sink, second_others = compute(1, second_right, second_left)
-    if running is not None:
-        running = after(running, second_sink)
-    running = scattered(first_sums, running, chips - 1)
+    second_run = scattered(second_sums, None, 1)
 
     blank = jnp.zeros_like(first_sink)
     sink_grad = jnp.concatenate([first_sink, second_sink])
@@ -416,20 +406,23 @@
         size = lax.axis_size(name)
         return value + lax.ppermute(value, name, [(at, at ^ bit) for at in range(size)])
 
-    tail = None
     per_hop = -(-len(steps) // (chips - 1))
     for hop in range(1, chips):
-        tail = scattered(second_sums, tail, hop)
-        if hop == 1:
-            first_total = finished(first_sums, running)
+        if hop > 1:
+            first_run = scattered(first_sums, first_run, hop)
+            second_run = scattered(second_sums, second_run, hop)
         for step in steps[:per_hop]:
             sink_grad = exchange(sink_grad, step)
         steps = steps[per_hop:]
         if hop < chips - 1:
-            tail = after(tail, sink_grad)
+            sink_grad, first_run, second_run = lax.optimization_barrier(
+                (sink_grad, first_run, second_run)
+            )
+    sink_grad = sink_grad[0, :head_count]
+    first_total = finished(first_sums, first_run)
+    first_back = send(first_others, swap)
     second_back = send(second_others, swap)
-    second_total = finished(second_sums, tail)
-    sink_grad = sink_grad[0, :head_count]
+    second_total = finished(second_sums, second_run)
 
     def whole(mine, other):
         return jnp.where(
@@ -447,15 +440,11 @@
     key_grad, value_grad = [
         whole(
             *[
-                [
-                    part[side][:, at : at + HD]
-                    for part in (first_total, second_total)
-                    for at in range(first, 2 * width, 2 * HD)
-                ]
+                [part[side][:, first : first + width] for part in (first_total, second_total)]
                 for side in range(2)
             ]
         )
-        for first in (0, HD)
+        for first in (0, width)
     ]
     return (attn_out, query_grad, key_grad, value_grad, sink_grad)
 

time: 151 us -> 122 us (0.81)
  starting transfers between devices: 71.8 us -> 57.5 us
  local copies, waits for them, and re-layouts: 16 us -> 4.62 us
  other arithmetic: 11.5 us -> 6.62 us
    ppermute x30, starting transfers between devices: 64.3 us -> 48.6 us  [send(): return lax.ppermute(value, 'ctx', pairs)]
    unnamed x79 -> x44, local copies, waits for them, and re-layouts: 9.19 us -> 1.16 us
    convert_element_type x6, other arithmetic: 4.42 us -> 0.5 us  [add(): (left.astype(jnp.float32) + right.astype(jnp.float32)).astype(jnp.bfloat16)]
    pallas_call x2, Pallas kernels: 12.9 us -> 16.4 us  [attend(): pl.pallas_call(functools.partial(attention_kernel, shape), in_specs=[smem...]
    pallas_call x1 -> x0, Pallas kernels: 3.01 us -> none  [per_device(): pl.pallas_call(functools.partial(plan_kernel, stretch_len), in_specs=[sme...]
    slice x2, local copies, waits for them, and re-layouts: 1.89 us -> 0.07 us  [per_device(): part[:, at * wide:(at + 1) * wide]]
    slice x4, local copies, waits for them, and re-layouts: 1.66 us -> 0.14 us  [per_device(): part[at][:local_rows]]
  transfers between devices with their start and end apart: 35 -> 35, of which waited for: 11 -> 12; matrix products, arithmetic and copies ran while one was open for 10% -> 5% of each run, Pallas kernels for 11% -> 7%
where the time goes in v3:
time: 122 us; the launch traced here: 120 us
  starting transfers between devices  57.5 us (47%)
  waiting for transfers between devices  33.7 us (28%)
  Pallas kernels  16.4 us (13%)
  other arithmetic  6.62 us (5%)
  local copies, waits for them, and re-layouts  4.62 us (4%)
  between operations  1.44 us (1%)
    ppermute x30, starting transfers between devices, send(): return lax.ppermute(value, 'ctx', pairs)  48.6 us
    ppermute x30, waiting for transfers between devices, send(): return lax.ppermute(value, 'ctx', pairs)  27.6 us
    pallas_call x2, Pallas kernels, attend(): pl.pallas_call(functools.partial(attention_kernel, shape), in_specs=[smem...  16.4 us
    ppermute x5, starting transfers between devices, exchange(): lax.ppermute(value, name, [(at, at ^ bit) for at in range(size)])  8.94 us
    ppermute x5, waiting for transfers between devices, exchange(): lax.ppermute(value, name, [(at, at ^ bit) for at in range(size)])  6.11 us
    select_n x4, other arithmetic, whole(): jnp.where(core == 0, jnp.concatenate(mine + other, axis=1), jnp.concatena...  4 us
  transfers between devices with their start and end apart: 35, of which 12 were waited for; matrix products, arithmetic and copies ran while one was open for 5% of the time, Pallas kernels for 7%

profile of v3, /device:TPU:0, one launch (start us, length us, event | category | flops | bytes accessed | tf_op | source)
XLA Modules:
  0.0 120.3 jit_solution(5324592186643218032)
XLA Ops:
  0.7 1.2 constant_dynamic-slice_fusion.6
  2.4 1.1 constant_dynamic-slice_fusion.8
  3.9 4.9 %collective-permute-start.2 = (bf16[256,512]{1,0:T(8,128)(2,1)S(1)}, bf16[256,512]{1,0:T(8,128)(2,1)S(1)}, u32[]{:S(2)}, u32[]{:S(2)}) collective-permute-start(bf16[256,512]{1,0:T(8,128)(2,1)S(1)} %pad_maximum_fusion.4.refs_0_), channel_id=1, source_target_pairs={{0,2},{1,3},{2,4},{3,5},{4,6},{5,7},{8,10},{9,11},{10,12},{11,13},... | collective-permute-start | bytes 786440 | tf_op jit(solution)/shard_map/ppermute | solution.py:272
  8.8 1.3 %collective-permute-start.5 = (bf16[256,512]{1,0:T(8,128)(2,1)S(1)}, bf16[256,512]{1,0:T(8,128)(2,1)S(1)}, u32[]{:S(2)}, u32[]{:S(2)}) collective-permute-start(bf16[256,512]{1,0:T(8,128)(2,1)S(1)} %pad_maximum_fusion.4.refs_0_), channel_id=1, source_target_pairs={{2,0},{3,1},{4,2},{5,3},{6,4},{7,5},{10,8},{11,9},{12,10},{13,11},... | collective-permute-start | bytes 786440 | tf_op jit(solution)/shard_map/ppermute | solution.py:272
  10.1 4.6 %collective-permute-start.8 = (bf16[256,512]{1,0:T(8,128)(2,1)S(1)}, bf16[256,512]{1,0:T(8,128)(2,1)S(1)}, u32[]{:S(2)}, u32[]{:S(2)}) collective-permute-start(bf16[256,512]{1,0:T(8,128)(2,1)S(1)} %pad_maximum_fusion.5.refs_0_), channel_id=1, source_target_pairs={{0,2},{1,3},{2,4},{3,5},{4,6},{5,7},{8,10},{9,11},{10,12},{11,13},... | collective-permute-start | bytes 786440 | tf_op jit(solution)/shard_map/ppermute | solution.py:272
  14.7 1.3 %collective-permute-start.11 = (bf16[256,512]{1,0:T(8,128)(2,1)S(1)}, bf16[256,512]{1,0:T(8,128)(2,1)S(1)}, u32[]{:S(2)}, u32[]{:S(2)}) collective-permute-start(bf16[256,512]{1,0:T(8,128)(2,1)S(1)} %pad_maximum_fusion.5.refs_0_), channel_id=1, source_target_pairs={{2,0},{3,1},{4,2},{5,3},{6,4},{7,5},{10,8},{11,9},{12,10},{13,11},... | collective-permute-start | bytes 786440 | tf_op jit(solution)/shard_map/ppermute | solution.py:272
  16.0 0.7 collective-permute-start.3
  16.7 2.3 %collective-permute-done.5.refs_4_ = bf16[256,512]{1,0:T(8,128)(2,1)S(1)} collective-permute-done((bf16[256,512]{1,0:T(8,128)(2,1)S(1)}, bf16[256,512]{1,0:T(8,128)(2,1)S(1)}, u32[]{:S(2)}, u32[]{:S(2)}) %collective-permute-start.5) | collective-permute-done | bytes 262176 | tf_op jit(solution)/shard_map/ppermute | solution.py:272
  18.9 1.3 %collective-permute-start.6 = (bf16[256,512]{1,0:T(8,128)(2,1)S(1)}, bf16[256,512]{1,0:T(8,128)(2,1)}, u32[]{:S(2)}, u32[]{:S(2)}) collective-permute-start(bf16[256,512]{1,0:T(8,128)(2,1)S(1)} %collective-permute-done.5.refs_4_), channel_id=1, source_target_pairs={{2,0},{3,1},{4,2},{5,3},{10,8},{11,9},{12,10},{13,11},{18,16},{19,... | collective-permute-start | bytes 786440 | tf_op jit(solution)/shard_map/ppermute | solution.py:272
  20.2 0.7 collective-permute-start.9
  20.9 4.1 %collective-permute-done.11.refs_4_ = bf16[256,512]{1,0:T(8,128)(2,1)S(1)} collective-permute-done((bf16[256,512]{1,0:T(8,128)(2,1)S(1)}, bf16[256,512]{1,0:T(8,128)(2,1)S(1)}, u32[]{:S(2)}, u32[]{:S(2)}) %collective-permute-start.11) | collective-permute-done | bytes 262176 | tf_op jit(solution)/shard_map/ppermute | solution.py:272
  25.0 1.3 %collective-permute-start.12 = (bf16[256,512]{1,0:T(8,128)(2,1)S(1)}, bf16[256,512]{1,0:T(8,128)(2,1)S(1)}, u32[]{:S(2)}, u32[]{:S(2)}) collective-permute-start(bf16[256,512]{1,0:T(8,128)(2,1)S(1)} %collective-permute-done.11.refs_4_), channel_id=1, source_target_pairs={{2,0},{3,1},{4,2},{5,3},{10,8},{11,9},{12,10},{13,11},{18,16},{19,... | collective-permute-start | bytes 786440 | tf_op jit(solution)/shard_map/ppermute | solution.py:272
  26.3 1.4 %collective-permute-start.4 = (bf16[256,512]{1,0:T(8,128)(2,1)S(1)}, bf16[256,512]{1,0:T(8,128)(2,1)}, u32[]{:S(2)}, u32[]{:S(2)}) collective-permute-start(bf16[256,512]{1,0:T(8,128)(2,1)S(1)} %collective-permute-done.3.refs_2_), channel_id=1, source_target_pairs={{4,6},{5,7},{12,14},{13,15},{20,22},{21,23},{28,30},{29,31}} | collective-permute-start | bytes 786440 | tf_op jit(solution)/shard_map/ppermute | solution.py:272
  27.7 2.6 %collective-permute-done.6.refs_5_ = bf16[256,512]{1,0:T(8,128)(2,1)} collective-permute-done((bf16[256,512]{1,0:T(8,128)(2,1)S(1)}, bf16[256,512]{1,0:T(8,128)(2,1)}, u32[]{:S(2)}, u32[]{:S(2)}) %collective-permute-start.6) | collective-permute-done | bytes 262176 | tf_op jit(solution)/shard_map/ppermute | solution.py:272
  30.3 1.3 %collective-permute-start.7 = (bf16[256,512]{1,0:T(8,128)(2,1)}, bf16[256,512]{1,0:T(8,128)(2,1)}, u32[]{:S(2)}, u32[]{:S(2)}) collective-permute-start(bf16[256,512]{1,0:T(8,128)(2,1)} %collective-permute-done.6.refs_5_), channel_id=1, source_target_pairs={{2,0},{3,1},{10,8},{11,9},{18,16},{19,17},{26,24},{27,25}} | collective-permute-start | bytes 786440 | tf_op jit(solution)/shard_map/ppermute | solution.py:272
  31.6 1.4 %collective-permute-start.10 = (bf16[256,512]{1,0:T(8,128)(2,1)S(1)}, bf16[256,512]{1,0:T(8,128)(2,1)}, u32[]{:S(2)}, u32[]{:S(2)}) collective-permute-start(bf16[256,512]{1,0:T(8,128)(2,1)S(1)} %collective-permute-done.9.refs_2_), channel_id=1, source_target_pairs={{4,6},{5,7},{12,14},{13,15},{20,22},{21,23},{28,30},{29,31}} | collective-permute-start | bytes 786440 | tf_op jit(solution)/shard_map/ppermute | solution.py:272
  33.0 4.6 %collective-permute-done.12.refs_5_ = bf16[256,512]{1,0:T(8,128)(2,1)S(1)} collective-permute-done((bf16[256,512]{1,0:T(8,128)(2,1)S(1)}, bf16[256,512]{1,0:T(8,128)(2,1)S(1)}, u32[]{:S(2)}, u32[]{:S(2)}) %collective-permute-start.12) | collective-permute-done | bytes 262176 | tf_op jit(solution)/shard_map/ppermute | solution.py:272
  37.5 1.3 %collective-permute-start.13 = (bf16[256,512]{1,0:T(8,128)(2,1)S(1)}, bf16[256,512]{1,0:T(8,128)(2,1)}, u32[]{:S(2)}, u32[]{:S(2)}) collective-permute-start(bf16[256,512]{1,0:T(8,128)(2,1)S(1)} %collective-permute-done.12.refs_5_), channel_id=1, source_target_pairs={{2,0},{3,1},{10,8},{11,9},{18,16},{19,17},{26,24},{27,25}} | collective-permute-start | bytes 786440 | tf_op jit(solution)/shard_map/ppermute | solution.py:272
  38.8 4.4 %collective-permute-done.7.refs_6_ = bf16[256,512]{1,0:T(8,128)(2,1)} collective-permute-done((bf16[256,512]{1,0:T(8,128)(2,1)}, bf16[256,512]{1,0:T(8,128)(2,1)}, u32[]{:S(2)}, u32[]{:S(2)}) %collective-permute-start.7) | collective-permute-done | bytes 262176 | tf_op jit(solution)/shard_map/ppermute | solution.py:272
  43.3 8.1 %shard_map.119 = (bf16[256,1024]{1,0:T(8,128)(2,1)}, bf16[256,1024]{1,0:T(8,128)(2,1)}, bf16[256,512]{1,0:T(8,128)(2,1)}, bf16[256,512]{1,0:T(8,128)(2,1)}, bf16...) custom-call(s32[16]{0:T(128)} %map_ref.3, s32[4,4]{1,0:T(4,128)} %lengths_ref.3, ...), custom_call_target="tpu_custom_call" | custom-call | flops 1610612736 | bytes 4194304 | tf_op jit(solution)/shard_map/pallas_call | solution.py:247
  51.5 0.7 reduce
  52.5 8.2 %shard_map.120 = (bf16[256,1024]{1,0:T(8,128)(2,1)}, bf16[256,1024]{1,0:T(8,128)(2,1)}, bf16[256,512]{1,0:T(8,128)(2,1)}, bf16[256,512]{1,0:T(8,128)(2,1)}, bf16...) custom-call(s32[16]{0:T(128)} %map_ref.3, s32[4,4]{1,0:T(4,128)} %lengths_ref.3, ...), custom_call_target="tpu_custom_call" | custom-call | flops 1610612736 | bytes 4194304 | tf_op jit(solution)/shard_map/pallas_call | solution.py:247
  60.7 0.7 reduce.1
  61.8 4.0 %collective-permute-start.18 = (bf16[256,512]{1,0:T(8,128)(2,1)S(1)}, bf16[256,512]{1,0:T(8,128)(2,1)S(1)}, u32[]{:S(2)}, u32[]{:S(2)}) collective-permute-start(bf16[256,512]{1,0:T(8,128)(2,1)S(1)} %copy-done.5), channel_id=1, source_target_pairs={{0,2},{1,3},{8,10},{9,11},{16,18},{17,19},{24,26},{25,27}} | collective-permute-start | bytes 786440 | tf_op jit(solution)/shard_map/ppermute | solution.py:272
  65.9 0.7 collective-permute-start.19
  66.6 1.3 %collective-permute-start.20 = (bf16[256,512]{1,0:T(8,128)(2,1)}, bf16[256,512]{1,0:T(8,128)(2,1)S(1)}, u32[]{:S(2)}, u32[]{:S(2)}) collective-permute-start(bf16[256,512]{1,0:T(8,128)(2,1)} %get-tuple-element.38), channel_id=1, source_target_pairs={{0,2},{1,3},{8,10},{9,11},{16,18},{17,19},{24,26},{25,27}} | collective-permute-start | bytes 786440 | tf_op jit(solution)/shard_map/ppermute | solution.py:272
  67.9 0.9 collective-permute-start.21
  68.9 0.9 copy-done.3
  70.1 1.1 collective-permute-start.17
  71.2 2.6 %collective-permute-done.17 = f32[8,128]{1,0:T(8,128)S(1)} collective-permute-done((f32[8,128]{1,0:T(8,128)S(1)}, f32[8,128]{1,0:T(8,128)S(1)}, u32[]{:S(2)}, u32[]{:S(2)}) %collective-permute-start.17) | collective-permute-done | bytes 4128 | tf_op jit(solution)/shard_map/ppermute | solution.py:407
  74.6 3.1 %collective-permute-start.26 = (bf16[256,512]{1,0:T(8,128)(2,1)S(1)}, bf16[256,512]{1,0:T(8,128)(2,1)S(1)}, u32[]{:S(2)}, u32[]{:S(2)}) collective-permute-start(bf16[256,512]{1,0:T(8,128)(2,1)S(1)} %get-tuple-element.70), channel_id=1, source_target_pairs={{0,2},{1,3},{2,4},{3,5},{8,10},{9,11},{10,12},{11,13},{16,18},{17,... | collective-permute-start | bytes 786440 | tf_op jit(solution)/shard_map/ppermute | solution.py:272
  77.7 0.7 collective-permute-start.27
  78.4 1.9 %collective-permute-start.23 = (f32[8,128]{1,0:T(8,128)S(1)}, f32[8,128]{1,0:T(8,128)S(1)}, u32[]{:S(2)}, u32[]{:S(2)}) collective-permute-start(f32[8,128]{1,0:T(8,128)S(1)} %add.97), channel_id=1, source_target_pairs={{0,2},{1,3},{2,0},{3,1},{4,6},{5,7},{6,4},{7,5},{8,10},{9,11},{10,... | collective-permute-start | bytes 12296 | tf_op jit(solution)/shard_map/ppermute | solution.py:407
  80.4 3.5 %collective-permute-done.23 = f32[8,128]{1,0:T(8,128)S(1)} collective-permute-done((f32[8,128]{1,0:T(8,128)S(1)}, f32[8,128]{1,0:T(8,128)S(1)}, u32[]{:S(2)}, u32[]{:S(2)}) %collective-permute-start.23) | collective-permute-done | bytes 4128 | tf_op jit(solution)/shard_map/ppermute | solution.py:407
  83.9 4.4 %collective-permute-start.24 = (bf16[256,512]{1,0:T(8,128)(2,1)S(1)}, bf16[256,512]{1,0:T(8,128)(2,1)S(1)}, u32[]{:S(2)}, u32[]{:S(2)}) collective-permute-start(bf16[256,512]{1,0:T(8,128)(2,1)S(1)} %get-tuple-element.72), channel_id=1, source_target_pairs={{0,2},{1,3},{2,4},{3,5},{8,10},{9,11},{10,12},{11,13},{16,18},{17,... | collective-permute-start | bytes 786440 | tf_op jit(solution)/shard_map/ppermute | solution.py:272
  89.1 1.2 %maximum_select_fusion.1 = bf16[128,4096]{1,0:T(8,128)(2,1)} fusion(bf16[128,1024]{1,0:T(8,128)(2,1)S(1)} %get-tuple-element.59, bf16[128,1024]{1,0:T(8,128)(2,1)S(1)} %get-tuple-element.57, bf16[128,1024]{1,0:T(8,128)(2,1)S(1)} %get-tuple-element.55, bf16[128,1024]{1,0:T(8,128)(2,1)S(1)} %get-tuple-element.53, pred[]{:T(512)S(6)} %eq.4), kind=kLoop, calls=%fused_computation.2 | loop fusion | flops 8912896 | bytes 2097153 | tf_op jit(solution)/shard_map/jit(_where)/select_n | solution.py:428
  90.4 1.2 %maximum_select_fusion = bf16[128,4096]{1,0:T(8,128)(2,1)} fusion(bf16[128,1024]{1,0:T(8,128)(2,1)S(1)} %get-tuple-element.60, bf16[128,1024]{1,0:T(8,128)(2,1)S(1)} %get-tuple-element.58, bf16[128,1024]{1,0:T(8,128)(2,1)S(1)} %get-tuple-element.63, bf16[128,1024]{1,0:T(8,128)(2,1)S(1)} %get-tuple-element.61, pred[]{:T(512)S(6)} %eq.4), kind=kLoop, calls=%fused_computation.1 | loop fusion | flops 8912896 | bytes 2097153 | tf_op jit(solution)/shard_map/jit(_where)/select_n | solution.py:428
  91.6 2.2 %collective-permute-done.24 = bf16[256,512]{1,0:T(8,128)(2,1)S(1)} collective-permute-done((bf16[256,512]{1,0:T(8,128)(2,1)S(1)}, bf16[256,512]{1,0:T(8,128)(2,1)S(1)}, u32[]{:S(2)}, u32[]{:S(2)}) %collective-permute-start.24) | collective-permute-done | bytes 262176 | tf_op jit(solution)/shard_map/ppermute | solution.py:272
  93.8 5.8 %collective-permute-start.34 = (f32[8,128]{1,0:T(8,128)S(1)}, f32[8,128]{1,0:T(8,128)S(1)}, u32[]{:S(2)}, u32[]{:S(2)}) collective-permute-start(f32[8,128]{1,0:T(8,128)S(1)} %add.98), channel_id=1, source_target_pairs={{0,4},{1,5},{2,6},{3,7},{4,0},{5,1},{6,2},{7,3},{8,12},{9,13},{10,... | collective-permute-start | bytes 12296 | tf_op jit(solution)/shard_map/ppermute | solution.py:407
  99.6 3.0 %collective-permute-start.28 = (bf16[256,512]{1,0:T(8,128)(2,1)S(1)}, bf16[256,512]{1,0:T(8,128)(2,1)S(1)}, u32[]{:S(2)}, u32[]{:S(2)}) collective-permute-start(bf16[256,512]{1,0:T(8,128)(2,1)S(1)} %add_convert_fusion.5), channel_id=1, source_target_pairs={{0,2},{1,3},{2,4},{3,5},{4,6},{5,7},{8,10},{9,11},{10,12},{11,13},... | collective-permute-start | bytes 786440 | tf_op jit(solution)/shard_map/ppermute | solution.py:272
  102.7 1.3 %collective-permute-start.29 = (bf16[256,512]{1,0:T(8,128)(2,1)S(1)}, bf16[256,512]{1,0:T(8,128)(2,1)S(1)}, u32[]{:S(2)}, u32[]{:S(2)}) collective-permute-start(bf16[256,512]{1,0:T(8,128)(2,1)S(1)} %add_convert_fusion.4), channel_id=1, source_target_pairs={{2,0},{3,1},{4,2},{5,3},{6,4},{7,5},{10,8},{11,9},{12,10},{13,11},... | collective-permute-start | bytes 786440 | tf_op jit(solution)/shard_map/ppermute | solution.py:272
  104.1 4.7 %collective-permute-start.30 = (bf16[256,512]{1,0:T(8,128)(2,1)S(1)}, bf16[256,512]{1,0:T(8,128)(2,1)S(1)}, u32[]{:S(2)}, u32[]{:S(2)}) collective-permute-start(bf16[256,512]{1,0:T(8,128)(2,1)S(1)} %add_convert_fusion.2), channel_id=1, source_target_pairs={{0,2},{1,3},{2,4},{3,5},{4,6},{5,7},{8,10},{9,11},{10,12},{11,13},... | collective-permute-start | bytes 786440 | tf_op jit(solution)/shard_map/ppermute | solution.py:272
  108.9 1.3 %collective-permute-start.31 = (bf16[256,512]{1,0:T(8,128)(2,1)S(1)}, bf16[256,512]{1,0:T(8,128)(2,1)S(1)}, u32[]{:S(2)}, u32[]{:S(2)}) collective-permute-start(bf16[256,512]{1,0:T(8,128)(2,1)S(1)} %add_convert_fusion.1), channel_id=1, source_target_pairs={{2,0},{3,1},{4,2},{5,3},{6,4},{7,5},{10,8},{11,9},{12,10},{13,11},... | collective-permute-start | bytes 786440 | tf_op jit(solution)/shard_map/ppermute | solution.py:272
  111.3 1.4 %collective-permute-done.30 = bf16[256,512]{1,0:T(8,128)(2,1)S(1)} collective-permute-done((bf16[256,512]{1,0:T(8,128)(2,1)S(1)}, bf16[256,512]{1,0:T(8,128)(2,1)S(1)}, u32[]{:S(2)}, u32[]{:S(2)}) %collective-permute-start.30) | collective-permute-done | bytes 262176 | tf_op jit(solution)/shard_map/ppermute | solution.py:272
  112.7 4.5 %collective-permute-done.31 = bf16[256,512]{1,0:T(8,128)(2,1)S(1)} collective-permute-done((bf16[256,512]{1,0:T(8,128)(2,1)S(1)}, bf16[256,512]{1,0:T(8,128)(2,1)S(1)}, u32[]{:S(2)}, u32[]{:S(2)}) %collective-permute-start.31) | collective-permute-done | bytes 262176 | tf_op jit(solution)/shard_map/ppermute | solution.py:272
  117.4 1.3 %collective-permute-done.33 = bf16[128,512]{1,0:T(8,128)(2,1)S(1)} collective-permute-done((bf16[128,512]{1,0:T(8,128)(2,1)S(1)}, bf16[128,512]{1,0:T(8,128)(2,1)S(1)}, u32[]{:S(2)}, u32[]{:S(2)}) %collective-permute-start.33) | collective-permute-done | bytes 131104 | tf_op jit(solution)/shard_map/ppermute | solution.py:272
  118.7 0.8 maximum_select_fusion.3
  119.5 0.8 maximum_select_fusion.2
  (118 shorter events, 5.2 us)
Async XLA Ops:
  1.9 1.9 %collective-permute-start.1 = (bf16[128,1024]{1,0:T(8,128)(2,1)S(1)}, bf16[128,1024]{1,0:T(8,128)(2,1)S(1)}, u32[]{:S(2)}, u32[]{:S(2)}) collective-permute-start(bf16[128,1024]{1,0:T(8,128)(2,1)S(1)} %pad_maximum_fusion.3), channel_id=1, source_target_pairs={{0,1},{1,0},{2,3},{3,2},{4,5},{5,4},{6,7},{7,6},{8,9},{9,8},{10,11... | collective-permute-start | bytes 786440 | tf_op jit(solution)/shard_map/ppermute | solution.py:272
  3.6 39.6 %collective-permute-start = (bf16[128,4096]{1,0:T(8,128)(2,1)S(1)}, bf16[128,4096]{1,0:T(8,128)(2,1)}, u32[]{:S(2)}, u32[]{:S(2)}) collective-permute-start(bf16[128,4096]{1,0:T(8,128)(2,1)S(1)} %pad_maximum_fusion), channel_id=1, source_target_pairs={{0,1},{1,0},{2,3},{3,2},{4,5},{5,4},{6,7},{7,6},{8,9},{9,8},{10,11... | collective-permute-start | bytes 3145736 | tf_op jit(solution)/shard_map/ppermute | solution.py:272
  3.9 39.4 %copy-start.12 = (bf16[256,512]{1,0:T(8,128)(2,1)}, bf16[256,512]{1,0:T(8,128)(2,1)S(1)}, u32[]{:S(2)}) copy-start(bf16[256,512]{1,0:T(8,128)(2,1)S(1)} %pad_maximum_fusion.4.refs_0_) | copy-start | bytes 786436
  3.9 12.1 %collective-permute-start.2 = (bf16[256,512]{1,0:T(8,128)(2,1)S(1)}, bf16[256,512]{1,0:T(8,128)(2,1)S(1)}, u32[]{:S(2)}, u32[]{:S(2)}) collective-permute-start(bf16[256,512]{1,0:T(8,128)(2,1)S(1)} %pad_maximum_fusion.4.refs_0_), channel_id=1, source_target_pairs={{0,2},{1,3},{2,4},{3,5},{4,6},{5,7},{8,10},{9,11},{10,12},{11,13},... | collective-permute-start | bytes 786440 | tf_op jit(solution)/shard_map/ppermute | solution.py:272
  8.8 10.2 %collective-permute-start.5 = (bf16[256,512]{1,0:T(8,128)(2,1)S(1)}, bf16[256,512]{1,0:T(8,128)(2,1)S(1)}, u32[]{:S(2)}, u32[]{:S(2)}) collective-permute-start(bf16[256,512]{1,0:T(8,128)(2,1)S(1)} %pad_maximum_fusion.4.refs_0_), channel_id=1, source_target_pairs={{2,0},{3,1},{4,2},{5,3},{6,4},{7,5},{10,8},{11,9},{12,10},{13,11},... | collective-permute-start | bytes 786440 | tf_op jit(solution)/shard_map/ppermute | solution.py:272
  10.1 41.4 %copy-start.11 = (bf16[256,512]{1,0:T(8,128)(2,1)}, bf16[256,512]{1,0:T(8,128)(2,1)S(1)}, u32[]{:S(2)}) copy-start(bf16[256,512]{1,0:T(8,128)(2,1)S(1)} %pad_maximum_fusion.5.refs_0_) | copy-start | bytes 786436
  10.1 10.1 %collective-permute-start.8 = (bf16[256,512]{1,0:T(8,128)(2,1)S(1)}, bf16[256,512]{1,0:T(8,128)(2,1)S(1)}, u32[]{:S(2)}, u32[]{:S(2)}) collective-permute-start(bf16[256,512]{1,0:T(8,128)(2,1)S(1)} %pad_maximum_fusion.5.refs_0_), channel_id=1, source_target_pairs={{0,2},{1,3},{2,4},{3,5},{4,6},{5,7},{8,10},{9,11},{10,12},{11,13},... | collective-permute-start | bytes 786440 | tf_op jit(solution)/shard_map/ppermute | solution.py:272
  14.7 10.3 %collective-permute-start.11 = (bf16[256,512]{1,0:T(8,128)(2,1)S(1)}, bf16[256,512]{1,0:T(8,128)(2,1)S(1)}, u32[]{:S(2)}, u32[]{:S(2)}) collective-permute-start(bf16[256,512]{1,0:T(8,128)(2,1)S(1)} %pad_maximum_fusion.5.refs_0_), channel_id=1, source_target_pairs={{2,0},{3,1},{4,2},{5,3},{6,4},{7,5},{10,8},{11,9},{12,10},{13,11},... | collective-permute-start | bytes 786440 | tf_op jit(solution)/shard_map/ppermute | solution.py:272
  16.0 27.3 %copy-start.17 = (bf16[256,512]{1,0:T(8,128)(2,1)}, bf16[256,512]{1,0:T(8,128)(2,1)S(1)}, u32[]{:S(2)}) copy-start(bf16[256,512]{1,0:T(8,128)(2,1)S(1)} %collective-permute-done.2.refs_1_) | copy-start | bytes 786436
  16.0 10.3 %collective-permute-start.3 = (bf16[256,512]{1,0:T(8,128)(2,1)S(1)}, bf16[256,512]{1,0:T(8,128)(2,1)S(1)}, u32[]{:S(2)}, u32[]{:S(2)}) collective-permute-start(bf16[256,512]{1,0:T(8,128)(2,1)S(1)} %collective-permute-done.2.refs_1_), channel_id=1, source_target_pairs={{2,4},{3,5},{4,6},{5,7},{10,12},{11,13},{12,14},{13,15},{18,20},{1... | collective-permute-start | bytes 786440 | tf_op jit(solution)/shard_map/ppermute | solution.py:272
  18.9 24.3 %copy-start.18 = (bf16[256,512]{1,0:T(8,128)(2,1)}, bf16[256,512]{1,0:T(8,128)(2,1)S(1)}, u32[]{:S(2)}) copy-start(bf16[256,512]{1,0:T(8,128)(2,1)S(1)} %collective-permute-done.5.refs_4_) | copy-start | bytes 786436
  18.9 11.4 %collective-permute-start.6 = (bf16[256,512]{1,0:T(8,128)(2,1)S(1)}, bf16[256,512]{1,0:T(8,128)(2,1)}, u32[]{:S(2)}, u32[]{:S(2)}) collective-permute-start(bf16[256,512]{1,0:T(8,128)(2,1)S(1)} %collective-permute-done.5.refs_4_), channel_id=1, source_target_pairs={{2,0},{3,1},{4,2},{5,3},{10,8},{11,9},{12,10},{13,11},{18,16},{19,... | collective-permute-start | bytes 786440 | tf_op jit(solution)/shard_map/ppermute | solution.py:272
  20.2 31.2 %copy-start.15 = (bf16[256,512]{1,0:T(8,128)(2,1)}, bf16[256,512]{1,0:T(8,128)(2,1)S(1)}, u32[]{:S(2)}) copy-start(bf16[256,512]{1,0:T(8,128)(2,1)S(1)} %collective-permute-done.8.refs_1_) | copy-start | bytes 786436
  20.2 11.3 %collective-permute-start.9 = (bf16[256,512]{1,0:T(8,128)(2,1)S(1)}, bf16[256,512]{1,0:T(8,128)(2,1)S(1)}, u32[]{:S(2)}, u32[]{:S(2)}) collective-permute-start(bf16[256,512]{1,0:T(8,128)(2,1)S(1)} %collective-permute-done.8.refs_1_), channel_id=1, source_target_pairs={{2,4},{3,5},{4,6},{5,7},{10,12},{11,13},{12,14},{13,15},{18,20},{1... | collective-permute-start | bytes 786440 | tf_op jit(solution)/shard_map/ppermute | solution.py:272
  25.0 26.5 %copy-start.16 = (bf16[256,512]{1,0:T(8,128)(2,1)}, bf16[256,512]{1,0:T(8,128)(2,1)S(1)}, u32[]{:S(2)}) copy-start(bf16[256,512]{1,0:T(8,128)(2,1)S(1)} %collective-permute-done.11.refs_4_) | copy-start | bytes 786436
  25.0 12.5 %collective-permute-start.12 = (bf16[256,512]{1,0:T(8,128)(2,1)S(1)}, bf16[256,512]{1,0:T(8,128)(2,1)S(1)}, u32[]{:S(2)}, u32[]{:S(2)}) collective-permute-start(bf16[256,512]{1,0:T(8,128)(2,1)S(1)} %collective-permute-done.11.refs_4_), channel_id=1, source_target_pairs={{2,0},{3,1},{4,2},{5,3},{10,8},{11,9},{12,10},{13,11},{18,16},{19,... | collective-permute-start | bytes 786440 | tf_op jit(solution)/shard_map/ppermute | solution.py:272
  26.3 17.0 %copy-start.21 = (bf16[256,512]{1,0:T(8,128)(2,1)}, bf16[256,512]{1,0:T(8,128)(2,1)S(1)}, u32[]{:S(2)}) copy-start(bf16[256,512]{1,0:T(8,128)(2,1)S(1)} %collective-permute-done.3.refs_2_) | copy-start | bytes 786436
  26.3 12.5 %collective-permute-start.4 = (bf16[256,512]{1,0:T(8,128)(2,1)S(1)}, bf16[256,512]{1,0:T(8,128)(2,1)}, u32[]{:S(2)}, u32[]{:S(2)}) collective-permute-start(bf16[256,512]{1,0:T(8,128)(2,1)S(1)} %collective-permute-done.3.refs_2_), channel_id=1, source_target_pairs={{4,6},{5,7},{12,14},{13,15},{20,22},{21,23},{28,30},{29,31}} | collective-permute-start | bytes 786440 | tf_op jit(solution)/shard_map/ppermute | solution.py:272
  30.3 13.0 %collective-permute-start.7 = (bf16[256,512]{1,0:T(8,128)(2,1)}, bf16[256,512]{1,0:T(8,128)(2,1)}, u32[]{:S(2)}, u32[]{:S(2)}) collective-permute-start(bf16[256,512]{1,0:T(8,128)(2,1)} %collective-permute-done.6.refs_5_), channel_id=1, source_target_pairs={{2,0},{3,1},{10,8},{11,9},{18,16},{19,17},{26,24},{27,25}} | collective-permute-start | bytes 786440 | tf_op jit(solution)/shard_map/ppermute | solution.py:272
  31.6 19.9 %copy-start.19 = (bf16[256,512]{1,0:T(8,128)(2,1)}, bf16[256,512]{1,0:T(8,128)(2,1)S(1)}, u32[]{:S(2)}) copy-start(bf16[256,512]{1,0:T(8,128)(2,1)S(1)} %collective-permute-done.9.refs_2_) | copy-start | bytes 786436
  31.6 20.8 %collective-permute-start.10 = (bf16[256,512]{1,0:T(8,128)(2,1)S(1)}, bf16[256,512]{1,0:T(8,128)(2,1)}, u32[]{:S(2)}, u32[]{:S(2)}) collective-permute-start(bf16[256,512]{1,0:T(8,128)(2,1)S(1)} %collective-permute-done.9.refs_2_), channel_id=1, source_target_pairs={{4,6},{5,7},{12,14},{13,15},{20,22},{21,23},{28,30},{29,31}} | collective-permute-start | bytes 786440 | tf_op jit(solution)/shard_map/ppermute | solution.py:272
  37.5 14.0 %copy-start.20 = (bf16[256,512]{1,0:T(8,128)(2,1)}, bf16[256,512]{1,0:T(8,128)(2,1)S(1)}, u32[]{:S(2)}) copy-start(bf16[256,512]{1,0:T(8,128)(2,1)S(1)} %collective-permute-done.12.refs_5_) | copy-start | bytes 786436
  37.5 14.9 %collective-permute-start.13 = (bf16[256,512]{1,0:T(8,128)(2,1)S(1)}, bf16[256,512]{1,0:T(8,128)(2,1)}, u32[]{:S(2)}, u32[]{:S(2)}) collective-permute-start(bf16[256,512]{1,0:T(8,128)(2,1)S(1)} %collective-permute-done.12.refs_5_), channel_id=1, source_target_pairs={{2,0},{3,1},{10,8},{11,9},{18,16},{19,17},{26,24},{27,25}} | collective-permute-start | bytes 786440 | tf_op jit(solution)/shard_map/ppermute | solution.py:272
  52.4 13.4 %copy-start.6 = (bf16[256,512]{1,0:T(8,128)(2,1)S(1)}, bf16[256,512]{1,0:T(8,128)(2,1)}, u32[]{:S(2)}) copy-start(bf16[256,512]{1,0:T(8,128)(2,1)} %get-tuple-element.34) | copy-start | bytes 786436
  52.4 16.3 %copy-start.1 = (bf16[256,1024]{1,0:T(8,128)(2,1)S(1)}, bf16[256,1024]{1,0:T(8,128)(2,1)}, u32[]{:S(2)}) copy-start(bf16[256,1024]{1,0:T(8,128)(2,1)} %get-tuple-element.31) | copy-start | bytes 1572868
  61.8 8.3 %collective-permute-start.16 = (f32[8,128]{1,0:T(8,128)S(1)}, f32[8,128]{1,0:T(8,128)S(1)}, u32[]{:S(2)}, u32[]{:S(2)}) collective-permute-start(f32[8,128]{1,0:T(8,128)S(1)} %pad.4), channel_id=1, source_target_pairs={{0,8},{8,0},{16,24},{24,16},{1,9},{9,1},{17,25},{25,17},{2,10},{10... | collective-permute-start | bytes 12296 | tf_op jit(solution)/shard_map/ppermute | solution.py:407
  61.8 11.9 %collective-permute-start.18 = (bf16[256,512]{1,0:T(8,128)(2,1)S(1)}, bf16[256,512]{1,0:T(8,128)(2,1)S(1)}, u32[]{:S(2)}, u32[]{:S(2)}) collective-permute-start(bf16[256,512]{1,0:T(8,128)(2,1)S(1)} %copy-done.5), channel_id=1, source_target_pairs={{0,2},{1,3},{8,10},{9,11},{16,18},{17,19},{24,26},{25,27}} | collective-permute-start | bytes 786440 | tf_op jit(solution)/shard_map/ppermute | solution.py:272
  65.9 8.5 %collective-permute-start.19 = (bf16[256,512]{1,0:T(8,128)(2,1)S(1)}, bf16[256,512]{1,0:T(8,128)(2,1)S(1)}, u32[]{:S(2)}, u32[]{:S(2)}) collective-permute-start(bf16[256,512]{1,0:T(8,128)(2,1)S(1)} %copy-done.6), channel_id=1, source_target_pairs={{6,4},{7,5},{14,12},{15,13},{22,20},{23,21},{30,28},{31,29}} | collective-permute-start | bytes 786440 | tf_op jit(solution)/shard_map/ppermute | solution.py:272
  66.6 7.8 %collective-permute-start.20 = (bf16[256,512]{1,0:T(8,128)(2,1)}, bf16[256,512]{1,0:T(8,128)(2,1)S(1)}, u32[]{:S(2)}, u32[]{:S(2)}) collective-permute-start(bf16[256,512]{1,0:T(8,128)(2,1)} %get-tuple-element.38), channel_id=1, source_target_pairs={{0,2},{1,3},{8,10},{9,11},{16,18},{17,19},{24,26},{25,27}} | collective-permute-start | bytes 786440 | tf_op jit(solution)/shard_map/ppermute | solution.py:272
  67.9 6.5 %collective-permute-start.21 = (bf16[256,512]{1,0:T(8,128)(2,1)}, bf16[256,512]{1,0:T(8,128)(2,1)S(1)}, u32[]{:S(2)}, u32[]{:S(2)}) collective-permute-start(bf16[256,512]{1,0:T(8,128)(2,1)} %get-tuple-element.39), channel_id=1, source_target_pairs={{6,4},{7,5},{14,12},{15,13},{22,20},{23,21},{30,28},{31,29}} | collective-permute-start | bytes 786440 | tf_op jit(solution)/shard_map/ppermute | solution.py:272
  70.1 3.7 %collective-permute-start.17 = (f32[8,128]{1,0:T(8,128)S(1)}, f32[8,128]{1,0:T(8,128)S(1)}, u32[]{:S(2)}, u32[]{:S(2)}) collective-permute-start(f32[8,128]{1,0:T(8,128)S(1)} %pad_add_fusion), channel_id=1, source_target_pairs={{0,16},{8,24},{16,0},{24,8},{1,17},{9,25},{17,1},{25,9},{2,18},{10... | collective-permute-start | bytes 12296 | tf_op jit(solution)/shard_map/ppermute | solution.py:407
  73.7 14.6 %collective-permute-start.14 = (bf16[128,2048]{1,0:T(8,128)(2,1)S(1)}, bf16[128,2048]{1,0:T(8,128)(2,1)S(1)}, u32[]{:S(2)}, u32[]{:S(2)}) collective-permute-start(bf16[128,2048]{1,0:T(8,128)(2,1)S(1)} %pad_maximum_fusion.1), channel_id=1, source_target_pairs={{0,1},{1,0},{2,3},{3,2},{4,5},{5,4},{6,7},{7,6},{8,9},{9,8},{10,11... | collective-permute-start | bytes 1572872 | tf_op jit(solution)/shard_map/ppermute | solution.py:272
  73.8 15.3 %collective-permute-start.15 = (bf16[128,2048]{1,0:T(8,128)(2,1)S(1)}, bf16[128,2048]{1,0:T(8,128)(2,1)S(1)}, u32[]{:S(2)}, u32[]{:S(2)}) collective-permute-start(bf16[128,2048]{1,0:T(8,128)(2,1)S(1)} %pad_maximum_fusion.2), channel_id=1, source_target_pairs={{0,1},{1,0},{2,3},{3,2},{4,5},{5,4},{6,7},{7,6},{8,9},{9,8},{10,11... | collective-permute-start | bytes 1572872 | tf_op jit(solution)/shard_map/ppermute | solution.py:272
  74.3 4.0 %collective-permute-start.22 = (f32[8,128]{1,0:T(8,128)S(1)}, f32[8,128]{1,0:T(8,128)S(1)}, u32[]{:S(2)}, u32[]{:S(2)}) collective-permute-start(f32[8,128]{1,0:T(8,128)S(1)} %fusion.15), channel_id=1, source_target_pairs={{0,1},{1,0},{2,3},{3,2},{4,5},{5,4},{6,7},{7,6},{8,9},{9,8},{10,11... | collective-permute-start | bytes 12296 | tf_op jit(solution)/shard_map/ppermute | solution.py:407
  74.6 17.0 %collective-permute-start.26 = (bf16[256,512]{1,0:T(8,128)(2,1)S(1)}, bf16[256,512]{1,0:T(8,128)(2,1)S(1)}, u32[]{:S(2)}, u32[]{:S(2)}) collective-permute-start(bf16[256,512]{1,0:T(8,128)(2,1)S(1)} %get-tuple-element.70), channel_id=1, source_target_pairs={{0,2},{1,3},{2,4},{3,5},{8,10},{9,11},{10,12},{11,13},{16,18},{17,... | collective-permute-start | bytes 786440 | tf_op jit(solution)/shard_map/ppermute | solution.py:272
  77.7 13.9 %collective-permute-start.27 = (bf16[256,512]{1,0:T(8,128)(2,1)S(1)}, bf16[256,512]{1,0:T(8,128)(2,1)S(1)}, u32[]{:S(2)}, u32[]{:S(2)}) collective-permute-start(bf16[256,512]{1,0:T(8,128)(2,1)S(1)} %get-tuple-element.69), channel_id=1, source_target_pairs={{4,2},{5,3},{6,4},{7,5},{12,10},{13,11},{14,12},{15,13},{20,18},{2... | collective-permute-start | bytes 786440 | tf_op jit(solution)/shard_map/ppermute | solution.py:272
  78.4 5.6 %collective-permute-start.23 = (f32[8,128]{1,0:T(8,128)S(1)}, f32[8,128]{1,0:T(8,128)S(1)}, u32[]{:S(2)}, u32[]{:S(2)}) collective-permute-start(f32[8,128]{1,0:T(8,128)S(1)} %add.97), channel_id=1, source_target_pairs={{0,2},{1,3},{2,0},{3,1},{4,6},{5,7},{6,4},{7,5},{8,10},{9,11},{10,... | collective-permute-start | bytes 12296 | tf_op jit(solution)/shard_map/ppermute | solution.py:407
  83.9 9.8 %collective-permute-start.24 = (bf16[256,512]{1,0:T(8,128)(2,1)S(1)}, bf16[256,512]{1,0:T(8,128)(2,1)S(1)}, u32[]{:S(2)}, u32[]{:S(2)}) collective-permute-start(bf16[256,512]{1,0:T(8,128)(2,1)S(1)} %get-tuple-element.72), channel_id=1, source_target_pairs={{0,2},{1,3},{2,4},{3,5},{8,10},{9,11},{10,12},{11,13},{16,18},{17,... | collective-permute-start | bytes 786440 | tf_op jit(solution)/shard_map/ppermute | solution.py:272
  88.4 5.4 %collective-permute-start.25 = (bf16[256,512]{1,0:T(8,128)(2,1)S(1)}, bf16[256,512]{1,0:T(8,128)(2,1)S(1)}, u32[]{:S(2)}, u32[]{:S(2)}) collective-permute-start(bf16[256,512]{1,0:T(8,128)(2,1)S(1)} %get-tuple-element.71), channel_id=1, source_target_pairs={{4,2},{5,3},{6,4},{7,5},{12,10},{13,11},{14,12},{15,13},{20,18},{2... | collective-permute-start | bytes 786440 | tf_op jit(solution)/shard_map/ppermute | solution.py:272
  91.6 17.2 %copy-start.7 = (bf16[256,512]{1,0:T(8,128)(2,1)S(1)}, bf16[256,512]{1,0:T(8,128)(2,1)}, u32[]{:S(2)}) copy-start(bf16[256,512]{1,0:T(8,128)(2,1)} %get-tuple-element.38) | copy-start | bytes 786436
  93.8 16.4 %collective-permute-start.34 = (f32[8,128]{1,0:T(8,128)S(1)}, f32[8,128]{1,0:T(8,128)S(1)}, u32[]{:S(2)}, u32[]{:S(2)}) collective-permute-start(f32[8,128]{1,0:T(8,128)S(1)} %add.98), channel_id=1, source_target_pairs={{0,4},{1,5},{2,6},{3,7},{4,0},{5,1},{6,2},{7,3},{8,12},{9,13},{10,... | collective-permute-start | bytes 12296 | tf_op jit(solution)/shard_map/ppermute | solution.py:407
  99.6 11.1 %collective-permute-start.28 = (bf16[256,512]{1,0:T(8,128)(2,1)S(1)}, bf16[256,512]{1,0:T(8,128)(2,1)S(1)}, u32[]{:S(2)}, u32[]{:S(2)}) collective-permute-start(bf16[256,512]{1,0:T(8,128)(2,1)S(1)} %add_convert_fusion.5), channel_id=1, source_target_pairs={{0,2},{1,3},{2,4},{3,5},{4,6},{5,7},{8,10},{9,11},{10,12},{11,13},... | collective-permute-start | bytes 786440 | tf_op jit(solution)/shard_map/ppermute | solution.py:272
  102.7 8.3 %collective-permute-start.29 = (bf16[256,512]{1,0:T(8,128)(2,1)S(1)}, bf16[256,512]{1,0:T(8,128)(2,1)S(1)}, u32[]{:S(2)}, u32[]{:S(2)}) collective-permute-start(bf16[256,512]{1,0:T(8,128)(2,1)S(1)} %add_convert_fusion.4), channel_id=1, source_target_pairs={{2,0},{3,1},{4,2},{5,3},{6,4},{7,5},{10,8},{11,9},{12,10},{13,11},... | collective-permute-start | bytes 786440 | tf_op jit(solution)/shard_map/ppermute | solution.py:272
  104.1 13.1 %copy-start.14 = (bf16[256,512]{1,0:T(8,128)(2,1)S(1)}, bf16[256,512]{1,0:T(8,128)(2,1)}, u32[]{:S(2)}) copy-start(bf16[256,512]{1,0:T(8,128)(2,1)} %get-tuple-element.49) | copy-start | bytes 786436
  104.1 8.6 %collective-permute-start.30 = (bf16[256,512]{1,0:T(8,128)(2,1)S(1)}, bf16[256,512]{1,0:T(8,128)(2,1)S(1)}, u32[]{:S(2)}, u32[]{:S(2)}) collective-permute-start(bf16[256,512]{1,0:T(8,128)(2,1)S(1)} %add_convert_fusion.2), channel_id=1, source_target_pairs={{0,2},{1,3},{2,4},{3,5},{4,6},{5,7},{8,10},{9,11},{10,12},{11,13},... | collective-permute-start | bytes 786440 | tf_op jit(solution)/shard_map/ppermute | solution.py:272
  108.9 8.3 %collective-permute-start.31 = (bf16[256,512]{1,0:T(8,128)(2,1)S(1)}, bf16[256,512]{1,0:T(8,128)(2,1)S(1)}, u32[]{:S(2)}, u32[]{:S(2)}) collective-permute-start(bf16[256,512]{1,0:T(8,128)(2,1)S(1)} %add_convert_fusion.1), channel_id=1, source_target_pairs={{2,0},{3,1},{4,2},{5,3},{6,4},{7,5},{10,8},{11,9},{12,10},{13,11},... | collective-permute-start | bytes 786440 | tf_op jit(solution)/shard_map/ppermute | solution.py:272
  111.2 6.2 %collective-permute-start.32 = (bf16[128,512]{1,0:T(8,128)(2,1)S(1)}, bf16[128,512]{1,0:T(8,128)(2,1)S(1)}, u32[]{:S(2)}, u32[]{:S(2)}) collective-permute-start(bf16[128,512]{1,0:T(8,128)(2,1)S(1)} %slice.114), channel_id=1, source_target_pairs={{0,1},{1,0},{2,3},{3,2},{4,5},{5,4},{6,7},{7,6},{8,9},{9,8},{10,11... | collective-permute-start | bytes 393224 | tf_op jit(solution)/shard_map/ppermute | solution.py:272
  117.3 1.4 %collective-permute-start.33 = (bf16[128,512]{1,0:T(8,128)(2,1)S(1)}, bf16[128,512]{1,0:T(8,128)(2,1)S(1)}, u32[]{:S(2)}, u32[]{:S(2)}) collective-permute-start(bf16[128,512]{1,0:T(8,128)(2,1)S(1)} %slice.116), channel_id=1, source_target_pairs={{0,1},{1,0},{2,3},{3,2},{4,5},{5,4},{6,7},{7,6},{8,9},{9,8},{10,11... | collective-permute-start | bytes 393224 | tf_op jit(solution)/shard_map/ppermute | solution.py:272
  (9 other events, 59.0 us)

commit v4 on v3

--- a/solution.py
+++ b/solution.py
@@ -52,7 +52,8 @@
             inner = inner - key_core * per_core
             inner = inner + jnp.where(key_core == core, 0, per_core)
             ahead = key_chip - chip
-            table = jnp.where(ahead > 0, chips - 1 + ahead, -ahead)
+            table = jnp.where(ahead > 0, chips - 2 + ahead, -ahead)
+            table = jnp.where(abs(ahead) == chips - 1, 2 * chips - 3, table)
             partial = jnp.where(ahead < 0, ahead + chips, ahead)
             return (
                 (table * per_chip + inner) * stretch_len,
@@ -80,20 +81,30 @@
 
 
 def attention_kernel(
-    shape, map_ref, lengths_ref, assign_ref, sink_ref, q_hbm, g_hbm, partner_hbm, *refs
+    shape, map_hbm, lengths_hbm, assign_hbm, sink_hbm, q_hbm, g_hbm, partner_hbm, *refs
 ):
     heads, ratio, stretch_len, per_chip, chips, limit, stream = shape
-    count_in = 2 * chips - 1
-    sources, outs = refs[:count_in], refs[count_in : count_in + 2]
-    partials = refs[count_in + 2 : count_in + 2 + chips]
-    sink_out = refs[count_in + 2 + chips]
-    kv, q_buf, g_buf, sums, table_ref, sems = refs[count_in + 3 + chips :]
+    count_in = 2 * chips - 2
+    sources, refs = refs[:count_in], refs[count_in:]
+    earlier, refs = refs[:stream], refs[stream:]
+    o_hbm, dq_hbm, back_hbm, far_hbm = refs[:4]
+    partials, refs = refs[4 : 4 + chips], refs[4 + chips :]
+    sink_out, kv, q_buf, g_buf, sums, out_buf, part_buf, table_ref, *small, sems = refs
+    tiny = (map_hbm, lengths_hbm, assign_hbm, sink_hbm)
+    map_ref, lengths_ref, assign_ref, sink_ref = small
     index = lax.axis_index("ctx")
     chip, core = index // 2, index % 2
     rows = per_chip * stretch_len
     local_rows = rows // 2
     wide = heads * ratio * HD
     here = pl.ds(pl.multiple_of((core * STREAMS + stream) * wide, HD), wide)
+    last = 4 + count_in
+    tables = [
+        pltpu.make_async_copy(source, target, sems.at[last + at])
+        for at, (source, target) in enumerate(zip(tiny, small))
+    ]
+    for load in tables:
+        load.start()
     loads = [
         (q_hbm.at[:, here], q_buf.at[pl.ds(0, local_rows)]),
         (g_hbm.at[:, here], g_buf.at[pl.ds(0, local_rows)]),
@@ -110,6 +121,8 @@
     loads = [pltpu.make_async_copy(*pair, sems.at[at]) for at, pair in enumerate(loads)]
     for load in loads:
         load.start()
+    for load in tables:
+        load.wait()
     fill_table(
         chip,
         core,
@@ -164,6 +177,7 @@
         seen = jnp.where(place < stretch_len, empty, place - stretch_len) <= token
         across = (((1,), (1,)), ((), ()))
         down = (((0,), (0,)), ((), ()))
+        lists = [[] for _ in range(6)]
         for head in range(heads):
             query, grad = take(q_buf, first, head), take(g_buf, first, head)
             keys = jnp.concatenate(
@@ -182,6 +196,11 @@
             )
             scores = lax.dot_general(keys, query, across, preferred_element_type=jnp.float32)
             grad_weights = lax.dot_general(values, grad, across, preferred_element_type=jnp.float32)
+            for part, value in zip(lists, (query, grad, keys, values, scores, grad_weights)):
+                part.append(value)
+        mixed = []
+        for head in range(heads):
+            scores, grad_weights = lists[4][head], lists[5][head]
             edge = jnp.where(seen, scores[(slots - 2) * stretch_len :], MASKED)
             if slots > 2:
                 scores = jnp.concatenate([scores[: (slots - 2) * stretch_len], edge], axis=0)
@@ -193,21 +212,24 @@
             sink_term = jnp.exp2(sinks[head] - row_max)
             inverse = 1.0 / (sink_term + jnp.sum(terms, axis=0, keepdims=True))
             weights = terms * inverse
-            weights_b = weights.astype(jnp.bfloat16)
             row_dot = jnp.sum(weights * grad_weights, axis=0, keepdims=True)
             grad_scores = (weights * (grad_weights - row_dot)).astype(jnp.bfloat16)
+            mixed.append((weights.astype(jnp.bfloat16), grad_scores))
+            sink_out[head] -= sink_term * inverse * row_dot
+        for head in range(heads):
+            query, grad, keys, values = (part[head] for part in lists[:4])
+            weights_b, grad_scores = mixed[head]
             dv = jnp.dot(weights_b, grad, preferred_element_type=jnp.float32)
             dk = jnp.dot(grad_scores, query, preferred_element_type=jnp.float32)
             attended = lax.dot_general(weights_b, values, down, preferred_element_type=jnp.float32)
             dq = lax.dot_general(grad_scores, keys, down, preferred_element_type=jnp.float32) * SCALE
-            put(outs[0], first, head, attended)
-            put(outs[1], first, head, dq)
+            put(out_buf, first, head, attended)
+            put(out_buf, first, heads + head, dq)
             for spot, at in enumerate(order):
                 part = slice(spot * stretch_len, (spot + 1) * stretch_len)
                 target = pl.ds(sum_rows[at], stretch_len)
                 sums[target, head * HD : (head + 1) * HD] += dk[part]
                 sums[target, (heads + head) * HD : (heads + head + 1) * HD] += dv[part]
-            sink_out[head] -= sink_term * inverse * row_dot
 
     widths = []
     width = 2
@@ -229,43 +251,80 @@
         return carry
 
     lax.fori_loop(0, per_chip, one_row, 0)
-    for at, partial in enumerate(partials):
+    mine, theirs = pl.ds(0, local_rows), pl.ds(local_rows, local_rows)
+    stores = [
+        (out_buf.at[mine, pl.ds(0, wide)], o_hbm),
+        (out_buf.at[mine, pl.ds(wide, wide)], dq_hbm),
+        (out_buf.at[theirs], back_hbm),
+    ]
+    stores = [pltpu.make_async_copy(*pair, sems.at[at]) for at, pair in enumerate(stores)]
+    for store in stores:
+        store.start()
+    if stream:
+        vectors = [jnp.concatenate([ref[at] for at in range(heads)], axis=1) for ref in earlier]
+        vectors.append(jnp.concatenate([sink_out[at] for at in range(heads)], axis=1))
+        slots = part_buf.shape[1] - rows
+        slot = lax.broadcasted_iota(jnp.int32, (slots, heads * ratio * stretch_len), 0)
+        filled = jnp.zeros(slot.shape, jnp.float32)
+        for at, vector in enumerate(vectors):
+            for piece in range(3):
+                top = vector.astype(jnp.bfloat16).astype(jnp.float32)
+                filled = jnp.where(slot == (3 * at + piece) * chips + chip, top, filled)
+                vector = vector - top
+        filled = filled.astype(jnp.bfloat16)
+    far = jnp.where(chip == 0, chips - 1, 1)
+    for at in range(chips):
         part = slice(at * rows, (at + 1) * rows)
-        partial[:, : heads * HD] = (sums[part, : heads * HD] * SCALE).astype(partial.dtype)
-        partial[:, heads * HD :] = sums[part, heads * HD :].astype(partial.dtype)
-
-
-def attend(stream, layout, sinks, queries, out_grad, partner, sources, chips, limit, ratio):
+        part_buf[at, :rows, : heads * HD] = (sums[part, : heads * HD] * SCALE).astype(jnp.bfloat16)
+        part_buf[at, :rows, heads * HD :] = sums[part, heads * HD :].astype(jnp.bfloat16)
+        if stream:
+            part_buf[at, rows:] = filled
+        stores.append(pltpu.make_async_copy(part_buf.at[at], partials[at], sems.at[3 + at]))
+        stores[-1].start()
+    stores.append(pltpu.make_async_copy(part_buf.at[far], far_hbm, sems.at[3 + chips]))
+    stores[-1].start()
+    for store in stores:
+        store.wait()
+
+
+def attend(
+    stream, layout, sinks, queries, out_grad, partner, sources, earlier, chips, limit, ratio
+):
     heads = sources[0].shape[1] // (2 * HD)
     rows = sources[0].shape[0]
     per_chip = layout[0].shape[0] // chips
     stretch_len = rows // per_chip
     wide = heads * ratio * HD
     shape = (heads, ratio, stretch_len, per_chip, chips, limit, stream)
-    smem, hbm = pl.BlockSpec(memory_space=pltpu.SMEM), pl.BlockSpec(memory_space=pltpu.HBM)
-    vmem = pl.BlockSpec(memory_space=pltpu.VMEM)
+    hbm, vmem = pl.BlockSpec(memory_space=pltpu.HBM), pl.BlockSpec(memory_space=pltpu.VMEM)
+    sent_rows = rows + (-(-3 * STREAMS * chips // 16) * 16 if stream else 0)
+    own = jax.ShapeDtypeStruct((rows // 2, wide), jnp.bfloat16)
+    sent = jax.ShapeDtypeStruct((sent_rows, heads * 2 * HD), jnp.bfloat16)
     return pl.pallas_call(
         functools.partial(attention_kernel, shape),
-        in_specs=[smem] * 4 + [hbm] * (3 + len(sources)),
-        out_specs=[vmem] * (3 + chips),
+        in_specs=[hbm] * (7 + len(sources)) + [vmem] * len(earlier),
+        out_specs=[hbm] * (4 + chips) + [vmem],
         scratch_shapes=[
             pltpu.VMEM((len(sources) * rows, heads * 2 * HD), jnp.bfloat16),
             pltpu.VMEM((rows, wide), jnp.bfloat16),
             pltpu.VMEM((rows, wide), jnp.bfloat16),
             pltpu.VMEM((chips * rows, heads * 2 * HD), jnp.float32),
+            pltpu.VMEM((rows, 2 * wide), jnp.bfloat16),
+            pltpu.VMEM((chips, sent_rows, heads * 2 * HD), jnp.bfloat16),
             pltpu.SMEM((per_chip, 1 + 2 * limit), jnp.int32),
-            pltpu.SemaphoreType.DMA((4 + len(sources),)),
+            *[pltpu.SMEM(part.shape, part.dtype) for part in (*layout, sinks)],
+            pltpu.SemaphoreType.DMA((8 + len(sources),)),
         ],
-        out_shape=[jax.ShapeDtypeStruct((rows, wide), jnp.bfloat16)] * 2
-        + [jax.ShapeDtypeStruct((rows, heads * 2 * HD), jnp.bfloat16)] * chips
+        out_shape=[own, own, jax.ShapeDtypeStruct((rows // 2, 2 * wide), jnp.bfloat16)]
+        + [sent] * (1 + chips)
         + [jax.ShapeDtypeStruct((heads, 1, ratio * stretch_len), jnp.float32)],
         compiler_params=pltpu.CompilerParams(vmem_limit_bytes=60 << 20),
         cost_estimate=pl.CostEstimate(
             flops=6 * 2 * heads * rows * ratio * limit * stretch_len * HD,
             transcendentals=heads * rows * ratio * limit * stretch_len,
-            bytes_accessed=4 << 20,
+            bytes_accessed=8 << 20,
         ),
-    )(*layout, sinks, queries, out_grad, partner, *sources)
+    )(*layout, sinks, queries, out_grad, partner, *sources, *earlier)
 
 
 def send(value, pairs):
@@ -354,75 +413,67 @@
     )
     layout = (stretch_map, doc_lengths, assignment)
 
-    def compute(stream, right, left):
+    def gathered(stream, hops):
+        right, left = hops[-1] if hops else (own[stream], own[stream])
+        hop = len(hops) + 1
+        if hop < chips - 1:
+            return hops + [gather_hop(right, left, hop, chips)]
+        ends = along(chips, 1, [chips - 2]) + along(chips, -1, [1])
+        return hops + [(send(jnp.where(chip >= chips // 2, right, left), ends),)]
+
+    def compute(stream, hops, earlier):
+        right, left = [hop[0] for hop in hops[:-1]], [hop[1] for hop in hops[:-1]]
         results = attend(
             stream, layout, sink_logits, queries, out_grad, partner,
-            [own[stream]] + right + left, chips, limit, ratio,
-        )
-        heads = results[-1].shape[0]
-        sinks = jnp.sum(results[-1].reshape(heads, ratio, -1), axis=2).reshape(-1)
-        others = jnp.concatenate([part[local_rows:] for part in results[:2]], axis=1)
-        return results[:2], results[2:-1], sinks, others
-
-    def gathered(stream, right, left, hop):
-        rightward, leftward = (right[-1], left[-1]) if right else (own[stream], own[stream])
-        rightward, leftward = gather_hop(rightward, leftward, hop, chips)
-        right.append(rightward)
-        left.append(leftward)
-
-    def scattered(partials, running, hop):
-        if running is None:
-            return scatter_hop(partials[chips - 1], partials[1], hop, chips)
+            [own[stream]] + right + left + list(hops[-1]), earlier, chips, limit, ratio,
+        )
+        return results[:3], results[3], results[4:-1], results[-1]
+
+    def scattered(far, partials, running, hop):
+        if hop == 1:
+            ends = along(chips, 1, [0]) + along(chips, -1, [chips - 1])
+            return (send(far, ends),) * 2
         return scatter_hop(
             add(partials[chips - hop], running[0]), add(partials[hop], running[1]), hop, chips
         )
 
     def finished(partials, running):
         total = add3(partials[0], *running)
-        return total[:local_rows], send(total[local_rows:], swap)
-
-    first_right, first_left, second_right, second_left = [], [], [], []
-    for hop in range(1, chips):
-        gathered(0, first_right, first_left, hop)
-        gathered(1, second_right, second_left, hop)
-    first_out, first_sums, first_sink, first_others = compute(0, first_right, first_left)
-    first_run = scattered(first_sums, None, 1)
-    second_out, second_sums, second_sink, second_others = compute(1, second_right, second_left)
-    second_run = scattered(second_sums, None, 1)
-
-    blank = jnp.zeros_like(first_sink)
-    sink_grad = jnp.concatenate([first_sink, second_sink])
-    sink_grad = jnp.where(
-        core == 0,
-        jnp.concatenate([sink_grad, blank, blank]),
-        jnp.concatenate([blank, blank, sink_grad]),
-    )
-    sink_grad = jnp.pad(sink_grad.reshape(1, -1), ((0, 7), (0, 128 - head_count)))
-    steps = [("dp", 1 << at) for at in range((lax.axis_size("dp") - 1).bit_length())]
-    steps += [("ctx", 1 << at) for at in range((2 * chips - 1).bit_length())]
-
-    def exchange(value, step):
-        name, bit = step
-        size = lax.axis_size(name)
-        return value + lax.ppermute(value, name, [(at, at ^ bit) for at in range(size)])
-
-    per_hop = -(-len(steps) // (chips - 1))
-    for hop in range(1, chips):
-        if hop > 1:
-            first_run = scattered(first_sums, first_run, hop)
-            second_run = scattered(second_sums, second_run, hop)
-        for step in steps[:per_hop]:
-            sink_grad = exchange(sink_grad, step)
-        steps = steps[per_hop:]
-        if hop < chips - 1:
-            sink_grad, first_run, second_run = lax.optimization_barrier(
-                (sink_grad, first_run, second_run)
-            )
-    sink_grad = sink_grad[0, :head_count]
+        return total, send(total[local_rows:], swap)
+
+    first_hops, second_hops = [], []
+    for _ in range(1, chips):
+        first_hops = gathered(0, first_hops)
+        second_hops = gathered(1, second_hops)
+    first_out, first_far, first_sums, first_sink = compute(0, first_hops, [])
+    first_run = scattered(first_far, None, None, 1)
+    second_out, second_far, second_sums, _ = compute(1, second_hops, [first_sink])
+    second_run = scattered(second_far, None, None, 1)
+    for hop in range(2, chips):
+        second_run = scattered(None, second_sums, second_run, hop)
+        first_run = scattered(None, first_sums, first_run, hop)
+    second_total = finished(second_sums, second_run)
     first_total = finished(first_sums, first_run)
-    first_back = send(first_others, swap)
-    second_back = send(second_others, swap)
-    second_total = finished(second_sums, second_run)
+    first_back, second_back = send(first_out[2], swap), send(second_out[2], swap)
+
+    def sink_sums(slots):
+        slots = slots.astype(jnp.float32)[: 3 * STREAMS * chips]
+        slots = jnp.sum(slots.reshape(STREAMS, 3 * chips, -1), axis=1)
+        return jnp.sum(slots.reshape(head_count // 2, -1), axis=1)
+
+    mine, theirs = sink_sums(second_total[0][2 * local_rows :]), sink_sums(
+        second_total[1][local_rows:]
+    )
+    sink_grad = jnp.where(core == 0, jnp.concatenate([mine, theirs]), jnp.concatenate([theirs, mine]))
+    size = lax.axis_size("dp")
+    slot = lax.broadcasted_iota(jnp.int32, (max(size, 8), 128), 0)
+    sink_grad = jnp.pad(sink_grad.reshape(1, -1), ((0, 0), (0, 128 - head_count)))
+    sink_grad = jnp.where(slot == lax.axis_index("dp"), sink_grad, 0.0)
+    others = [
+        lax.ppermute(sink_grad, "dp", [(at, at ^ bit) for at in range(size)])
+        for bit in range(1, size)
+    ]
+    sink_grad = jnp.sum(functools.reduce(jnp.add, others, sink_grad), axis=0)[:head_count]
 
     def whole(mine, other):
         return jnp.where(
@@ -432,7 +483,7 @@
     wide = width * ratio
     attn_out, query_grad = [
         whole(
-            [part[at][:local_rows] for part in (first_out, second_out)],
+            [part[at] for part in (first_out, second_out)],
             [part[:, at * wide : (at + 1) * wide] for part in (first_back, second_back)],
         )
         for at in range(2)
@@ -440,11 +491,11 @@
     key_grad, value_grad = [
         whole(
             *[
-                [part[side][:, first : first + width] for part in (first_total, second_total)]
+                [part[side][:local_rows, at : at + width] for part in (first_total, second_total)]
                 for side in range(2)
             ]
         )
-        for first in (0, width)
+        for at in (0, width)
     ]
     return (attn_out, query_grad, key_grad, value_grad, sink_grad)
 

time: 122 us -> 107 us (0.88); the launches traced: 120 us -> 107 us
  waiting for transfers between devices: 33.7 us -> 26.5 us
  starting transfers between devices: 57.5 us -> 53.2 us
  local copies, waits for them, and re-layouts: 4.62 us -> 2.75 us
    ppermute x5 -> x3, starting transfers between devices: 8.94 us -> 3.48 us  [per_device(): lax.ppermute(sink_grad, 'dp', [(at, at ^ bit) for at in range(size)])]
    ppermute x5 -> x3, waiting for transfers between devices: 6.11 us -> 1.49 us  [per_device(): lax.ppermute(sink_grad, 'dp', [(at, at ^ bit) for at in range(size)])]
    ppermute x30 -> x26, waiting for transfers between devices: 27.6 us -> 25 us  [send(): return lax.ppermute(value, 'ctx', pairs)]
    pallas_call x2 -> x0, other arithmetic: 1.42 us -> none  [attend(): pl.pallas_call(functools.partial(attention_kernel, shape), in_specs=[smem...]
    ppermute x30 -> x26, starting transfers between devices: 48.6 us -> 49.7 us  [send(): return lax.ppermute(value, 'ctx', pairs)]
  transfers between devices with their start and end apart: 35 -> 29, of which waited for: 12 -> 10; matrix products, arithmetic and copies ran while one was open for 5% -> 7% of each run, Pallas kernels for 7% -> 15%
where the time goes in v4:
time: 107 us
  starting transfers between devices  53.2 us (50%)
  waiting for transfers between devices  26.5 us (25%)
  Pallas kernels  16.2 us (15%)
  other arithmetic  6.86 us (6%)
  local copies, waits for them, and re-layouts  2.75 us (3%)
  between operations  1.43 us (1%)
    ppermute x26, starting transfers between devices, send(): return lax.ppermute(value, 'ctx', pairs)  49.7 us
    ppermute x26, waiting for transfers between devices, send(): return lax.ppermute(value, 'ctx', pairs)  25 us
    pallas_call x2, Pallas kernels, attend(): pl.pallas_call(functools.partial(attention_kernel, shape), in_specs=[hbm]...  16.2 us
    select_n x4, other arithmetic, whole(): jnp.where(core == 0, jnp.concatenate(mine + other, axis=1), jnp.concatena...  4 us
    ppermute x3, starting transfers between devices, per_device(): lax.ppermute(sink_grad, 'dp', [(at, at ^ bit) for at in range(size)])  3.48 us
    dynamic_slice x2, local copies, waits for them, and re-layouts, columns(): return lax.dynamic_slice_in_dim(table, first, count, 1)  2.31 us
  transfers between devices with their start and end apart: 29, of which 10 were waited for; matrix products, arithmetic and copies ran while one was open for 7% of the time, Pallas kernels for 15%

profile of v4, /device:TPU:0, one launch (start us, length us, event | category | flops | bytes accessed | tf_op | source)
XLA Modules:
  0.0 106.9 jit_solution(11772236375214573166)
XLA Ops:
  0.7 1.2 %constant_dynamic-slice_fusion.6 = (bf16[128,256]{1,0:T(8,128)(2,1)S(1)}, bf16[128,256]{1,0:T(8,128)(2,1)S(1)}, bf16[128,256]{1,0:T(8,128)(2,1)S(1)}, bf16[128,2...) fusion(bf16[128,1024]{1,0:T(8,128)(2,1)} %param.10, ...), kind=kLoop, calls=%fused_computation.27 | loop fusion | bytes 1048592 | tf_op jit(solution)/shard_map/dynamic_slice | solution.py:367
  1.9 0.5 collective-permute-start.1
  2.4 1.1 %constant_dynamic-slice_fusion.8 = (bf16[128,2048]{1,0:T(8,128)(2,1)S(1)}, bf16[128,2048]{1,0:T(8,128)(2,1)S(1)}) fusion(bf16[128,4096]{1,0:T(8,128)(2,1)} %g_hbm.3, s32[]{:T(128)S(6)} %select_n.88, bf16[128,4096]{1,0:T(8,128)(2,1)S(1)} %copy-done.3), kind=kLoop, calls=%fused_computation.29 | loop fusion | bytes 2097156 | tf_op jit(solution)/shard_map/dynamic_slice | solution.py:367
  3.6 1.3 %collective-permute-start.4 = (bf16[256,512]{1,0:T(8,128)(2,1)S(1)}, bf16[256,512]{1,0:T(8,128)(2,1)S(1)}, u32[]{:S(2)}, u32[]{:S(2)}) collective-permute-start(bf16[256,512]{1,0:T(8,128)(2,1)S(1)} %pad_maximum_fusion.2.refs_0_), channel_id=1, source_target_pairs={{2,0},{3,1},{4,2},{5,3},{6,4},{7,5},{10,8},{11,9},{12,10},{13,11},... | collective-permute-start | bytes 786440 | tf_op jit(solution)/shard_map/ppermute | solution.py:331
  4.9 5.5 %collective-permute-start.2 = (bf16[256,512]{1,0:T(8,128)(2,1)S(1)}, bf16[256,512]{1,0:T(8,128)(2,1)S(1)}, u32[]{:S(2)}, u32[]{:S(2)}) collective-permute-start(bf16[256,512]{1,0:T(8,128)(2,1)S(1)} %pad_maximum_fusion.2.refs_0_), channel_id=1, source_target_pairs={{0,2},{1,3},{2,4},{3,5},{4,6},{5,7},{8,10},{9,11},{10,12},{11,13},... | collective-permute-start | bytes 786440 | tf_op jit(solution)/shard_map/ppermute | solution.py:331
  10.7 1.3 %collective-permute-start.9 = (bf16[256,512]{1,0:T(8,128)(2,1)S(1)}, bf16[256,512]{1,0:T(8,128)(2,1)S(1)}, u32[]{:S(2)}, u32[]{:S(2)}) collective-permute-start(bf16[256,512]{1,0:T(8,128)(2,1)S(1)} %pad_maximum_fusion.3.refs_0_), channel_id=1, source_target_pairs={{2,0},{3,1},{4,2},{5,3},{6,4},{7,5},{10,8},{11,9},{12,10},{13,11},... | collective-permute-start | bytes 786440 | tf_op jit(solution)/shard_map/ppermute | solution.py:331
  12.0 4.6 %collective-permute-start.7 = (bf16[256,512]{1,0:T(8,128)(2,1)S(1)}, bf16[256,512]{1,0:T(8,128)(2,1)S(1)}, u32[]{:S(2)}, u32[]{:S(2)}) collective-permute-start(bf16[256,512]{1,0:T(8,128)(2,1)S(1)} %pad_maximum_fusion.3.refs_0_), channel_id=1, source_target_pairs={{0,2},{1,3},{2,4},{3,5},{4,6},{5,7},{8,10},{9,11},{10,12},{11,13},... | collective-permute-start | bytes 786440 | tf_op jit(solution)/shard_map/ppermute | solution.py:331
  16.5 1.3 %collective-permute-start.5 = (bf16[256,512]{1,0:T(8,128)(2,1)S(1)}, bf16[256,512]{1,0:T(8,128)(2,1)S(1)}, u32[]{:S(2)}, u32[]{:S(2)}) collective-permute-start(bf16[256,512]{1,0:T(8,128)(2,1)S(1)} %collective-permute-done.4.refs_3_), channel_id=1, source_target_pairs={{2,0},{3,1},{4,2},{5,3},{10,8},{11,9},{12,10},{13,11},{18,16},{19,... | collective-permute-start | bytes 786440 | tf_op jit(solution)/shard_map/ppermute | solution.py:331
  17.9 0.7 collective-permute-start.3
  18.5 3.2 %collective-permute-done.9.refs_3_ = bf16[256,512]{1,0:T(8,128)(2,1)S(1)} collective-permute-done((bf16[256,512]{1,0:T(8,128)(2,1)S(1)}, bf16[256,512]{1,0:T(8,128)(2,1)S(1)}, u32[]{:S(2)}, u32[]{:S(2)}) %collective-permute-start.9) | collective-permute-done | bytes 262176 | tf_op jit(solution)/shard_map/ppermute | solution.py:331
  21.7 1.3 %collective-permute-start.10 = (bf16[256,512]{1,0:T(8,128)(2,1)S(1)}, bf16[256,512]{1,0:T(8,128)(2,1)S(1)}, u32[]{:S(2)}, u32[]{:S(2)}) collective-permute-start(bf16[256,512]{1,0:T(8,128)(2,1)S(1)} %collective-permute-done.9.refs_3_), channel_id=1, source_target_pairs={{2,0},{3,1},{4,2},{5,3},{10,8},{11,9},{12,10},{13,11},{18,16},{19,... | collective-permute-start | bytes 786440 | tf_op jit(solution)/shard_map/ppermute | solution.py:331
  23.0 0.7 collective-permute-start.8
  23.7 3.9 %collective-permute-done.5.refs_4_ = bf16[256,512]{1,0:T(8,128)(2,1)S(1)} collective-permute-done((bf16[256,512]{1,0:T(8,128)(2,1)S(1)}, bf16[256,512]{1,0:T(8,128)(2,1)S(1)}, u32[]{:S(2)}, u32[]{:S(2)}) %collective-permute-start.5) | collective-permute-done | bytes 262176 | tf_op jit(solution)/shard_map/ppermute | solution.py:331
  27.7 1.3 %collective-permute-start.6 = (bf16[256,512]{1,0:T(8,128)(2,1)S(1)}, bf16[256,512]{1,0:T(8,128)(2,1)}, u32[]{:S(2)}, u32[]{:S(2)}) collective-permute-start(bf16[256,512]{1,0:T(8,128)(2,1)S(1)} %broadcast_select_fusion.1), channel_id=1, source_target_pairs={{4,6},{5,7},{2,0},{3,1},{12,14},{13,15},{10,8},{11,9},{20,22},{21,... | collective-permute-start | bytes 786440 | tf_op jit(solution)/shard_map/ppermute | solution.py:331
  29.0 4.6 %collective-permute-done.10.refs_4_ = bf16[256,512]{1,0:T(8,128)(2,1)S(1)} collective-permute-done((bf16[256,512]{1,0:T(8,128)(2,1)S(1)}, bf16[256,512]{1,0:T(8,128)(2,1)S(1)}, u32[]{:S(2)}, u32[]{:S(2)}) %collective-permute-start.10) | collective-permute-done | bytes 262176 | tf_op jit(solution)/shard_map/ppermute | solution.py:331
  33.6 1.3 %collective-permute-start.11 = (bf16[256,512]{1,0:T(8,128)(2,1)S(1)}, bf16[256,512]{1,0:T(8,128)(2,1)}, u32[]{:S(2)}, u32[]{:S(2)}) collective-permute-start(bf16[256,512]{1,0:T(8,128)(2,1)S(1)} %broadcast_select_fusion), channel_id=1, source_target_pairs={{4,6},{5,7},{2,0},{3,1},{12,14},{13,15},{10,8},{11,9},{20,22},{21,... | collective-permute-start | bytes 786440 | tf_op jit(solution)/shard_map/ppermute | solution.py:331
  34.9 4.4 %collective-permute-done.6.refs_5_ = bf16[256,512]{1,0:T(8,128)(2,1)} collective-permute-done((bf16[256,512]{1,0:T(8,128)(2,1)S(1)}, bf16[256,512]{1,0:T(8,128)(2,1)}, u32[]{:S(2)}, u32[]{:S(2)}) %collective-permute-start.6) | collective-permute-done | bytes 262176 | tf_op jit(solution)/shard_map/ppermute | solution.py:331
  39.3 7.7 %shard_map.119 = (bf16[128,1024]{1,0:T(8,128)(2,1)}, bf16[128,1024]{1,0:T(8,128)(2,1)}, bf16[128,2048]{1,0:T(8,128)(2,1)}, bf16[256,512]{1,0:T(8,128)(2,1)}, bf1...) custom-call(s32[16]{0:T(128)} %map_hbm.3, ...), custom_call_target="tpu_custom_call" | custom-call | flops 1610612736 | bytes 8388608 | tf_op jit(solution)/shard_map/pallas_call | solution.py:303
  47.1 1.8 %collective-permute-start.14 = (bf16[256,512]{1,0:T(8,128)(2,1)}, bf16[256,512]{1,0:T(8,128)(2,1)S(1)}, u32[]{:S(2)}, u32[]{:S(2)}) collective-permute-start(bf16[256,512]{1,0:T(8,128)(2,1)} %get-tuple-element.32), channel_id=1, source_target_pairs={{0,2},{1,3},{6,4},{7,5},{8,10},{9,11},{14,12},{15,13},{16,18},{17,... | collective-permute-start | bytes 786440 | tf_op jit(solution)/shard_map/ppermute | solution.py:331
  49.0 8.5 %shard_map.120 = (bf16[128,1024]{1,0:T(8,128)(2,1)}, bf16[128,1024]{1,0:T(8,128)(2,1)}, bf16[128,2048]{1,0:T(8,128)(2,1)}, bf16[288,512]{1,0:T(8,128)(2,1)}, bf1...) custom-call(s32[16]{0:T(128)} %map_hbm.3, ...), custom_call_target="tpu_custom_call" | custom-call | flops 1610612736 | bytes 8388608 | tf_op jit(solution)/shard_map/pallas_call | solution.py:303
  57.5 1.8 %collective-permute-start.19 = (bf16[288,512]{1,0:T(8,128)(2,1)}, bf16[288,512]{1,0:T(8,128)(2,1)S(1)}, u32[]{:S(2)}, u32[]{:S(2)}) collective-permute-start(bf16[288,512]{1,0:T(8,128)(2,1)} %get-tuple-element.37), channel_id=1, source_target_pairs={{0,2},{1,3},{6,4},{7,5},{8,10},{9,11},{14,12},{15,13},{16,18},{17,... | collective-permute-start | bytes 884744 | tf_op jit(solution)/shard_map/ppermute | solution.py:331
  59.4 0.5 collective-permute-start.12
  59.9 0.7 collective-permute-start.17
  60.6 1.9 %collective-permute-start.15 = (bf16[256,512]{1,0:T(8,128)(2,1)S(1)}, bf16[256,512]{1,0:T(8,128)(2,1)S(1)}, u32[]{:S(2)}, u32[]{:S(2)}) collective-permute-start(bf16[256,512]{1,0:T(8,128)(2,1)S(1)} %add_convert_fusion.7), channel_id=1, source_target_pairs={{0,2},{1,3},{2,4},{3,5},{8,10},{9,11},{10,12},{11,13},{16,18},{17,... | collective-permute-start | bytes 786440 | tf_op jit(solution)/shard_map/ppermute | solution.py:331
  62.5 3.6 %collective-permute-done.19 = bf16[288,512]{1,0:T(8,128)(2,1)S(1)} collective-permute-done((bf16[288,512]{1,0:T(8,128)(2,1)}, bf16[288,512]{1,0:T(8,128)(2,1)S(1)}, u32[]{:S(2)}, u32[]{:S(2)}) %collective-permute-start.19) | collective-permute-done | bytes 294944 | tf_op jit(solution)/shard_map/ppermute | solution.py:331
  66.1 1.0 add_convert_fusion.3
  67.2 0.8 collective-permute-start.22
  68.0 5.5 %collective-permute-start.20 = (bf16[288,512]{1,0:T(8,128)(2,1)S(1)}, bf16[288,512]{1,0:T(8,128)(2,1)S(1)}, u32[]{:S(2)}, u32[]{:S(2)}) collective-permute-start(bf16[288,512]{1,0:T(8,128)(2,1)S(1)} %add_convert_fusion.3), channel_id=1, source_target_pairs={{0,2},{1,3},{2,4},{3,5},{8,10},{9,11},{10,12},{11,13},{16,18},{17,... | collective-permute-start | bytes 884744 | tf_op jit(solution)/shard_map/ppermute | solution.py:331
  73.6 1.2 %maximum_select_fusion.1 = bf16[128,4096]{1,0:T(8,128)(2,1)} fusion(bf16[128,1024]{1,0:T(8,128)(2,1)S(1)} %get-tuple-element.41, bf16[128,1024]{1,0:T(8,128)(2,1)S(1)} %get-tuple-element.39, bf16[128,1024]{1,0:T(8,128)(2,1)S(1)} %copy-done.9, bf16[128,1024]{1,0:T(8,128)(2,1)S(1)} %copy-done.7, pred[]{:T(512)S(6)} %eq.16), kind=kLoop, calls=%fused_computation.2 | loop fusion | flops 8912896 | bytes 2097153 | tf_op jit(solution)/shard_map/jit(_where)/select_n | solution.py:479
  74.8 1.2 %maximum_select_fusion = bf16[128,4096]{1,0:T(8,128)(2,1)} fusion(bf16[128,1024]{1,0:T(8,128)(2,1)S(1)} %get-tuple-element.42, bf16[128,1024]{1,0:T(8,128)(2,1)S(1)} %get-tuple-element.40, bf16[128,1024]{1,0:T(8,128)(2,1)S(1)} %copy-done.8, bf16[128,1024]{1,0:T(8,128)(2,1)S(1)} %copy-done.6, pred[]{:T(512)S(6)} %eq.16), kind=kLoop, calls=%fused_computation.1 | loop fusion | flops 8912896 | bytes 2097153 | tf_op jit(solution)/shard_map/jit(_where)/select_n | solution.py:479
  76.1 1.4 %collective-permute-start.18 = (bf16[256,512]{1,0:T(8,128)(2,1)S(1)}, bf16[256,512]{1,0:T(8,128)(2,1)S(1)}, u32[]{:S(2)}, u32[]{:S(2)}) collective-permute-start(bf16[256,512]{1,0:T(8,128)(2,1)S(1)} %add_convert_fusion.5), channel_id=1, source_target_pairs={{2,0},{3,1},{4,2},{5,3},{6,4},{7,5},{10,8},{11,9},{12,10},{13,11},... | collective-permute-start | bytes 786440 | tf_op jit(solution)/shard_map/ppermute | solution.py:331
  77.7 9.5 %collective-permute-start.16 = (bf16[256,512]{1,0:T(8,128)(2,1)S(1)}, bf16[256,512]{1,0:T(8,128)(2,1)S(1)}, u32[]{:S(2)}, u32[]{:S(2)}) collective-permute-start(bf16[256,512]{1,0:T(8,128)(2,1)S(1)} %add_convert_fusion.6), channel_id=1, source_target_pairs={{0,2},{1,3},{2,4},{3,5},{4,6},{5,7},{8,10},{9,11},{10,12},{11,13},... | collective-permute-start | bytes 786440 | tf_op jit(solution)/shard_map/ppermute | solution.py:331
  87.3 1.3 %collective-permute-start.23 = (bf16[288,512]{1,0:T(8,128)(2,1)S(1)}, bf16[288,512]{1,0:T(8,128)(2,1)S(1)}, u32[]{:S(2)}, u32[]{:S(2)}) collective-permute-start(bf16[288,512]{1,0:T(8,128)(2,1)S(1)} %add_convert_fusion.1), channel_id=1, source_target_pairs={{2,0},{3,1},{4,2},{5,3},{6,4},{7,5},{10,8},{11,9},{12,10},{13,11},... | collective-permute-start | bytes 884744 | tf_op jit(solution)/shard_map/ppermute | solution.py:331
  88.7 4.6 %collective-permute-start.21 = (bf16[288,512]{1,0:T(8,128)(2,1)S(1)}, bf16[288,512]{1,0:T(8,128)(2,1)S(1)}, u32[]{:S(2)}, u32[]{:S(2)}) collective-permute-start(bf16[288,512]{1,0:T(8,128)(2,1)S(1)} %add_convert_fusion.2), channel_id=1, source_target_pairs={{0,2},{1,3},{2,4},{3,5},{4,6},{5,7},{8,10},{9,11},{10,12},{11,13},... | collective-permute-start | bytes 884744 | tf_op jit(solution)/shard_map/ppermute | solution.py:331
  93.3 0.6 collective-permute-done.16
  93.8 0.1 add_convert_fusion.4
  94.1 1.8 %collective-permute-done.23 = bf16[288,512]{1,0:T(8,128)(2,1)S(1)} collective-permute-done((bf16[288,512]{1,0:T(8,128)(2,1)S(1)}, bf16[288,512]{1,0:T(8,128)(2,1)S(1)}, u32[]{:S(2)}, u32[]{:S(2)}) %collective-permute-start.23) | collective-permute-done | bytes 294944 | tf_op jit(solution)/shard_map/ppermute | solution.py:331
  95.9 1.6 %collective-permute-done.21 = bf16[288,512]{1,0:T(8,128)(2,1)S(1)} collective-permute-done((bf16[288,512]{1,0:T(8,128)(2,1)S(1)}, bf16[288,512]{1,0:T(8,128)(2,1)S(1)}, u32[]{:S(2)}, u32[]{:S(2)}) %collective-permute-start.21) | collective-permute-done | bytes 294944 | tf_op jit(solution)/shard_map/ppermute | solution.py:331
  97.5 0.1 add_convert_fusion
  97.8 0.1 reduce_sum.46
  98.0 1.3 %collective-permute-done.25 = bf16[160,512]{1,0:T(8,128)(2,1)S(1)} collective-permute-done((bf16[160,512]{1,0:T(8,128)(2,1)S(1)}, bf16[160,512]{1,0:T(8,128)(2,1)S(1)}, u32[]{:S(2)}, u32[]{:S(2)}) %collective-permute-start.25) | collective-permute-done | bytes 163872 | tf_op jit(solution)/shard_map/ppermute | solution.py:331
  99.4 0.1 reduce_sum.48
  99.7 3.0 %collective-permute-start.28 = (f32[8,128]{1,0:T(8,128)S(1)}, f32[8,128]{1,0:T(8,128)S(1)}, u32[]{:S(2)}, u32[]{:S(2)}) collective-permute-start(f32[8,128]{1,0:T(8,128)S(1)} %broadcast_select_fusion.2), channel_id=1, source_target_pairs={{0,24},{8,16},{16,8},{24,0},{1,25},{9,17},{17,9},{25,1},{2,26},{10... | collective-permute-start | bytes 12296 | tf_op jit(solution)/shard_map/ppermute | solution.py:473
  102.7 0.5 collective-permute-start.26
  103.2 0.8 maximum_select_fusion.3
  104.0 0.8 maximum_select_fusion.2
  104.8 1.5 %collective-permute-done.26 = f32[8,128]{1,0:T(8,128)S(1)} collective-permute-done((f32[8,128]{1,0:T(8,128)S(1)}, f32[8,128]{1,0:T(8,128)S(1)}, u32[]{:S(2)}, u32[]{:S(2)}) %collective-permute-start.26) | collective-permute-done | bytes 4128 | tf_op jit(solution)/shard_map/ppermute | solution.py:473
  106.3 0.6 add_reduce_fusion
  (102 shorter events, 1.6 us)
Async XLA Ops:
  1.9 1.7 %collective-permute-start.1 = (bf16[128,1024]{1,0:T(8,128)(2,1)S(1)}, bf16[128,1024]{1,0:T(8,128)(2,1)S(1)}, u32[]{:S(2)}, u32[]{:S(2)}) collective-permute-start(bf16[128,1024]{1,0:T(8,128)(2,1)S(1)} %pad_maximum_fusion.1), channel_id=1, source_target_pairs={{0,1},{1,0},{2,3},{3,2},{4,5},{5,4},{6,7},{7,6},{8,9},{9,8},{10,11... | collective-permute-start | bytes 786440 | tf_op jit(solution)/shard_map/ppermute | solution.py:331
  3.6 6.9 %copy-start.12 = (bf16[256,512]{1,0:T(8,128)(2,1)}, bf16[256,512]{1,0:T(8,128)(2,1)S(1)}, u32[]{:S(2)}) copy-start(bf16[256,512]{1,0:T(8,128)(2,1)S(1)} %pad_maximum_fusion.2.refs_0_) | copy-start | bytes 786436
  3.6 12.9 %collective-permute-start.4 = (bf16[256,512]{1,0:T(8,128)(2,1)S(1)}, bf16[256,512]{1,0:T(8,128)(2,1)S(1)}, u32[]{:S(2)}, u32[]{:S(2)}) collective-permute-start(bf16[256,512]{1,0:T(8,128)(2,1)S(1)} %pad_maximum_fusion.2.refs_0_), channel_id=1, source_target_pairs={{2,0},{3,1},{4,2},{5,3},{6,4},{7,5},{10,8},{11,9},{12,10},{13,11},... | collective-permute-start | bytes 786440 | tf_op jit(solution)/shard_map/ppermute | solution.py:331
  4.9 12.9 %collective-permute-start.2 = (bf16[256,512]{1,0:T(8,128)(2,1)S(1)}, bf16[256,512]{1,0:T(8,128)(2,1)S(1)}, u32[]{:S(2)}, u32[]{:S(2)}) collective-permute-start(bf16[256,512]{1,0:T(8,128)(2,1)S(1)} %pad_maximum_fusion.2.refs_0_), channel_id=1, source_target_pairs={{0,2},{1,3},{2,4},{3,5},{4,6},{5,7},{8,10},{9,11},{10,12},{11,13},... | collective-permute-start | bytes 786440 | tf_op jit(solution)/shard_map/ppermute | solution.py:331
  10.5 28.8 %collective-permute-start = (bf16[128,4096]{1,0:T(8,128)(2,1)S(1)}, bf16[128,4096]{1,0:T(8,128)(2,1)}, u32[]{:S(2)}, u32[]{:S(2)}) collective-permute-start(bf16[128,4096]{1,0:T(8,128)(2,1)S(1)} %pad_maximum_fusion), channel_id=1, source_target_pairs={{0,1},{1,0},{2,3},{3,2},{4,5},{5,4},{6,7},{7,6},{8,9},{9,8},{10,11... | collective-permute-start | bytes 3145736 | tf_op jit(solution)/shard_map/ppermute | solution.py:331
  10.6 36.4 %copy-start.11 = (bf16[256,512]{1,0:T(8,128)(2,1)}, bf16[256,512]{1,0:T(8,128)(2,1)S(1)}, u32[]{:S(2)}) copy-start(bf16[256,512]{1,0:T(8,128)(2,1)S(1)} %pad_maximum_fusion.3.refs_0_) | copy-start | bytes 786436
  10.7 11.1 %collective-permute-start.9 = (bf16[256,512]{1,0:T(8,128)(2,1)S(1)}, bf16[256,512]{1,0:T(8,128)(2,1)S(1)}, u32[]{:S(2)}, u32[]{:S(2)}) collective-permute-start(bf16[256,512]{1,0:T(8,128)(2,1)S(1)} %pad_maximum_fusion.3.refs_0_), channel_id=1, source_target_pairs={{2,0},{3,1},{4,2},{5,3},{6,4},{7,5},{10,8},{11,9},{12,10},{13,11},... | collective-permute-start | bytes 786440 | tf_op jit(solution)/shard_map/ppermute | solution.py:331
  12.0 11.1 %collective-permute-start.7 = (bf16[256,512]{1,0:T(8,128)(2,1)S(1)}, bf16[256,512]{1,0:T(8,128)(2,1)S(1)}, u32[]{:S(2)}, u32[]{:S(2)}) collective-permute-start(bf16[256,512]{1,0:T(8,128)(2,1)S(1)} %pad_maximum_fusion.3.refs_0_), channel_id=1, source_target_pairs={{0,2},{1,3},{2,4},{3,5},{4,6},{5,7},{8,10},{9,11},{10,12},{11,13},... | collective-permute-start | bytes 786440 | tf_op jit(solution)/shard_map/ppermute | solution.py:331
  16.5 22.8 %copy-start.20 = (bf16[256,512]{1,0:T(8,128)(2,1)}, bf16[256,512]{1,0:T(8,128)(2,1)S(1)}, u32[]{:S(2)}) copy-start(bf16[256,512]{1,0:T(8,128)(2,1)S(1)} %collective-permute-done.4.refs_3_) | copy-start | bytes 786436
  16.5 11.1 %collective-permute-start.5 = (bf16[256,512]{1,0:T(8,128)(2,1)S(1)}, bf16[256,512]{1,0:T(8,128)(2,1)S(1)}, u32[]{:S(2)}, u32[]{:S(2)}) collective-permute-start(bf16[256,512]{1,0:T(8,128)(2,1)S(1)} %collective-permute-done.4.refs_3_), channel_id=1, source_target_pairs={{2,0},{3,1},{4,2},{5,3},{10,8},{11,9},{12,10},{13,11},{18,16},{19,... | collective-permute-start | bytes 786440 | tf_op jit(solution)/shard_map/ppermute | solution.py:331
  17.9 9.8 %copy-start.22 = (bf16[256,512]{1,0:T(8,128)(2,1)}, bf16[256,512]{1,0:T(8,128)(2,1)S(1)}, u32[]{:S(2)}) copy-start(bf16[256,512]{1,0:T(8,128)(2,1)S(1)} %collective-permute-done.2.refs_1_) | copy-start | bytes 786436
  17.9 9.8 %collective-permute-start.3 = (bf16[256,512]{1,0:T(8,128)(2,1)S(1)}, bf16[256,512]{1,0:T(8,128)(2,1)S(1)}, u32[]{:S(2)}, u32[]{:S(2)}) collective-permute-start(bf16[256,512]{1,0:T(8,128)(2,1)S(1)} %collective-permute-done.2.refs_1_), channel_id=1, source_target_pairs={{2,4},{3,5},{4,6},{5,7},{10,12},{11,13},{12,14},{13,15},{18,20},{1... | collective-permute-start | bytes 786440 | tf_op jit(solution)/shard_map/ppermute | solution.py:331
  21.7 25.3 %copy-start.19 = (bf16[256,512]{1,0:T(8,128)(2,1)}, bf16[256,512]{1,0:T(8,128)(2,1)S(1)}, u32[]{:S(2)}) copy-start(bf16[256,512]{1,0:T(8,128)(2,1)S(1)} %collective-permute-done.9.refs_3_) | copy-start | bytes 786436
  21.7 11.8 %collective-permute-start.10 = (bf16[256,512]{1,0:T(8,128)(2,1)S(1)}, bf16[256,512]{1,0:T(8,128)(2,1)S(1)}, u32[]{:S(2)}, u32[]{:S(2)}) collective-permute-start(bf16[256,512]{1,0:T(8,128)(2,1)S(1)} %collective-permute-done.9.refs_3_), channel_id=1, source_target_pairs={{2,0},{3,1},{4,2},{5,3},{10,8},{11,9},{12,10},{13,11},{18,16},{19,... | collective-permute-start | bytes 786440 | tf_op jit(solution)/shard_map/ppermute | solution.py:331
  23.0 10.5 %copy-start.21 = (bf16[256,512]{1,0:T(8,128)(2,1)}, bf16[256,512]{1,0:T(8,128)(2,1)S(1)}, u32[]{:S(2)}) copy-start(bf16[256,512]{1,0:T(8,128)(2,1)S(1)} %collective-permute-done.7.refs_1_) | copy-start | bytes 786436
  23.0 10.5 %collective-permute-start.8 = (bf16[256,512]{1,0:T(8,128)(2,1)S(1)}, bf16[256,512]{1,0:T(8,128)(2,1)S(1)}, u32[]{:S(2)}, u32[]{:S(2)}) collective-permute-start(bf16[256,512]{1,0:T(8,128)(2,1)S(1)} %collective-permute-done.7.refs_1_), channel_id=1, source_target_pairs={{2,4},{3,5},{4,6},{5,7},{10,12},{11,13},{12,14},{13,15},{18,20},{1... | collective-permute-start | bytes 786440 | tf_op jit(solution)/shard_map/ppermute | solution.py:331
  27.6 11.7 %copy-start.16 = (bf16[256,512]{1,0:T(8,128)(2,1)}, bf16[256,512]{1,0:T(8,128)(2,1)S(1)}, u32[]{:S(2)}) copy-start(bf16[256,512]{1,0:T(8,128)(2,1)S(1)} %collective-permute-done.5.refs_4_) | copy-start | bytes 786436
  27.6 11.7 %copy-start.17 = (bf16[256,512]{1,0:T(8,128)(2,1)}, bf16[256,512]{1,0:T(8,128)(2,1)S(1)}, u32[]{:S(2)}) copy-start(bf16[256,512]{1,0:T(8,128)(2,1)S(1)} %collective-permute-done.3.refs_2_) | copy-start | bytes 786436
  27.7 11.6 %collective-permute-start.6 = (bf16[256,512]{1,0:T(8,128)(2,1)S(1)}, bf16[256,512]{1,0:T(8,128)(2,1)}, u32[]{:S(2)}, u32[]{:S(2)}) collective-permute-start(bf16[256,512]{1,0:T(8,128)(2,1)S(1)} %broadcast_select_fusion.1), channel_id=1, source_target_pairs={{4,6},{5,7},{2,0},{3,1},{12,14},{13,15},{10,8},{11,9},{20,22},{21,... | collective-permute-start | bytes 786440 | tf_op jit(solution)/shard_map/ppermute | solution.py:331
  33.6 13.5 %copy-start.14 = (bf16[256,512]{1,0:T(8,128)(2,1)}, bf16[256,512]{1,0:T(8,128)(2,1)S(1)}, u32[]{:S(2)}) copy-start(bf16[256,512]{1,0:T(8,128)(2,1)S(1)} %collective-permute-done.10.refs_4_) | copy-start | bytes 786436
  33.6 13.5 %copy-start.15 = (bf16[256,512]{1,0:T(8,128)(2,1)}, bf16[256,512]{1,0:T(8,128)(2,1)S(1)}, u32[]{:S(2)}) copy-start(bf16[256,512]{1,0:T(8,128)(2,1)S(1)} %collective-permute-done.8.refs_2_) | copy-start | bytes 786436
  33.6 15.3 %collective-permute-start.11 = (bf16[256,512]{1,0:T(8,128)(2,1)S(1)}, bf16[256,512]{1,0:T(8,128)(2,1)}, u32[]{:S(2)}, u32[]{:S(2)}) collective-permute-start(bf16[256,512]{1,0:T(8,128)(2,1)S(1)} %broadcast_select_fusion), channel_id=1, source_target_pairs={{4,6},{5,7},{2,0},{3,1},{12,14},{13,15},{10,8},{11,9},{20,22},{21,... | collective-permute-start | bytes 786440 | tf_op jit(solution)/shard_map/ppermute | solution.py:331
  47.1 12.8 %collective-permute-start.14 = (bf16[256,512]{1,0:T(8,128)(2,1)}, bf16[256,512]{1,0:T(8,128)(2,1)S(1)}, u32[]{:S(2)}, u32[]{:S(2)}) collective-permute-start(bf16[256,512]{1,0:T(8,128)(2,1)} %get-tuple-element.32), channel_id=1, source_target_pairs={{0,2},{1,3},{6,4},{7,5},{8,10},{9,11},{14,12},{15,13},{16,18},{17,... | collective-permute-start | bytes 786440 | tf_op jit(solution)/shard_map/ppermute | solution.py:331
  48.9 10.4 %copy-start.18 = (bf16[128,2048]{1,0:T(8,128)(2,1)S(1)}, bf16[128,2048]{1,0:T(8,128)(2,1)}, u32[]{:S(2)}) copy-start(bf16[128,2048]{1,0:T(8,128)(2,1)} %get-tuple-element.25) | copy-start | bytes 1572868
  48.9 10.9 %copy-start.10 = (bf16[256,512]{1,0:T(8,128)(2,1)S(1)}, bf16[256,512]{1,0:T(8,128)(2,1)}, u32[]{:S(2)}) copy-start(bf16[256,512]{1,0:T(8,128)(2,1)} %get-tuple-element.31) | copy-start | bytes 786436
  57.5 8.6 %collective-permute-start.19 = (bf16[288,512]{1,0:T(8,128)(2,1)}, bf16[288,512]{1,0:T(8,128)(2,1)S(1)}, u32[]{:S(2)}, u32[]{:S(2)}) collective-permute-start(bf16[288,512]{1,0:T(8,128)(2,1)} %get-tuple-element.37), channel_id=1, source_target_pairs={{0,2},{1,3},{6,4},{7,5},{8,10},{9,11},{14,12},{15,13},{16,18},{17,... | collective-permute-start | bytes 884744 | tf_op jit(solution)/shard_map/ppermute | solution.py:331
  59.2 8.7 %collective-permute-start.13 = (bf16[128,2048]{1,0:T(8,128)(2,1)}, bf16[128,2048]{1,0:T(8,128)(2,1)S(1)}, u32[]{:S(2)}, u32[]{:S(2)}) collective-permute-start(bf16[128,2048]{1,0:T(8,128)(2,1)} %get-tuple-element.26), channel_id=1, source_target_pairs={{0,1},{1,0},{2,3},{3,2},{4,5},{5,4},{6,7},{7,6},{8,9},{9,8},{10,11... | collective-permute-start | bytes 1572872 | tf_op jit(solution)/shard_map/ppermute | solution.py:331
  59.4 14.1 %collective-permute-start.12 = (bf16[128,2048]{1,0:T(8,128)(2,1)S(1)}, bf16[128,2048]{1,0:T(8,128)(2,1)S(1)}, u32[]{:S(2)}, u32[]{:S(2)}) collective-permute-start(bf16[128,2048]{1,0:T(8,128)(2,1)S(1)} %copy-done.18), channel_id=1, source_target_pairs={{0,1},{1,0},{2,3},{3,2},{4,5},{5,4},{6,7},{7,6},{8,9},{9,8},{10,11... | collective-permute-start | bytes 1572872 | tf_op jit(solution)/shard_map/ppermute | solution.py:331
  59.9 16.1 %collective-permute-start.17 = (bf16[256,512]{1,0:T(8,128)(2,1)S(1)}, bf16[256,512]{1,0:T(8,128)(2,1)S(1)}, u32[]{:S(2)}, u32[]{:S(2)}) collective-permute-start(bf16[256,512]{1,0:T(8,128)(2,1)S(1)} %add_convert_fusion.7), channel_id=1, source_target_pairs={{4,2},{5,3},{6,4},{7,5},{12,10},{13,11},{14,12},{15,13},{20,18},{2... | collective-permute-start | bytes 786440 | tf_op jit(solution)/shard_map/ppermute | solution.py:331
  60.6 17.0 %collective-permute-start.15 = (bf16[256,512]{1,0:T(8,128)(2,1)S(1)}, bf16[256,512]{1,0:T(8,128)(2,1)S(1)}, u32[]{:S(2)}, u32[]{:S(2)}) collective-permute-start(bf16[256,512]{1,0:T(8,128)(2,1)S(1)} %add_convert_fusion.7), channel_id=1, source_target_pairs={{0,2},{1,3},{2,4},{3,5},{8,10},{9,11},{10,12},{11,13},{16,18},{17,... | collective-permute-start | bytes 786440 | tf_op jit(solution)/shard_map/ppermute | solution.py:331
  67.1 6.4 %copy-start.7 = (bf16[128,1024]{1,0:T(8,128)(2,1)S(1)}, bf16[128,1024]{1,0:T(8,128)(2,1)}, u32[]{:S(2)}) copy-start(bf16[128,1024]{1,0:T(8,128)(2,1)} %get-tuple-element.27) | copy-start | bytes 786436
  67.1 6.4 %copy-start.9 = (bf16[128,1024]{1,0:T(8,128)(2,1)S(1)}, bf16[128,1024]{1,0:T(8,128)(2,1)}, u32[]{:S(2)}) copy-start(bf16[128,1024]{1,0:T(8,128)(2,1)} %get-tuple-element.28) | copy-start | bytes 786436
  67.2 20.0 %collective-permute-start.22 = (bf16[288,512]{1,0:T(8,128)(2,1)S(1)}, bf16[288,512]{1,0:T(8,128)(2,1)S(1)}, u32[]{:S(2)}, u32[]{:S(2)}) collective-permute-start(bf16[288,512]{1,0:T(8,128)(2,1)S(1)} %add_convert_fusion.3), channel_id=1, source_target_pairs={{4,2},{5,3},{6,4},{7,5},{12,10},{13,11},{14,12},{15,13},{20,18},{2... | collective-permute-start | bytes 884744 | tf_op jit(solution)/shard_map/ppermute | solution.py:331
  68.0 20.6 %collective-permute-start.20 = (bf16[288,512]{1,0:T(8,128)(2,1)S(1)}, bf16[288,512]{1,0:T(8,128)(2,1)S(1)}, u32[]{:S(2)}, u32[]{:S(2)}) collective-permute-start(bf16[288,512]{1,0:T(8,128)(2,1)S(1)} %add_convert_fusion.3), channel_id=1, source_target_pairs={{0,2},{1,3},{2,4},{3,5},{8,10},{9,11},{10,12},{11,13},{16,18},{17,... | collective-permute-start | bytes 884744 | tf_op jit(solution)/shard_map/ppermute | solution.py:331
  74.8 2.8 %copy-start.4 = (bf16[256,512]{1,0:T(8,128)(2,1)S(1)}, bf16[256,512]{1,0:T(8,128)(2,1)}, u32[]{:S(2)}) copy-start(bf16[256,512]{1,0:T(8,128)(2,1)} %get-tuple-element.30) | copy-start | bytes 786436
  76.0 11.2 %copy-start.1 = (bf16[288,512]{1,0:T(8,128)(2,1)S(1)}, bf16[288,512]{1,0:T(8,128)(2,1)}, u32[]{:S(2)}) copy-start(bf16[288,512]{1,0:T(8,128)(2,1)} %get-tuple-element.38) | copy-start | bytes 884740
  76.0 12.6 %copy-start = (bf16[288,512]{1,0:T(8,128)(2,1)S(1)}, bf16[288,512]{1,0:T(8,128)(2,1)}, u32[]{:S(2)}) copy-start(bf16[288,512]{1,0:T(8,128)(2,1)} %get-tuple-element.35) | copy-start | bytes 884740
  76.1 17.2 %collective-permute-start.18 = (bf16[256,512]{1,0:T(8,128)(2,1)S(1)}, bf16[256,512]{1,0:T(8,128)(2,1)S(1)}, u32[]{:S(2)}, u32[]{:S(2)}) collective-permute-start(bf16[256,512]{1,0:T(8,128)(2,1)S(1)} %add_convert_fusion.5), channel_id=1, source_target_pairs={{2,0},{3,1},{4,2},{5,3},{6,4},{7,5},{10,8},{11,9},{12,10},{13,11},... | collective-permute-start | bytes 786440 | tf_op jit(solution)/shard_map/ppermute | solution.py:331
  77.6 16.2 %copy-start.13 = (bf16[256,512]{1,0:T(8,128)(2,1)S(1)}, bf16[256,512]{1,0:T(8,128)(2,1)}, u32[]{:S(2)}) copy-start(bf16[256,512]{1,0:T(8,128)(2,1)} %get-tuple-element.29) | copy-start | bytes 786436
  77.7 16.2 %collective-permute-start.16 = (bf16[256,512]{1,0:T(8,128)(2,1)S(1)}, bf16[256,512]{1,0:T(8,128)(2,1)S(1)}, u32[]{:S(2)}, u32[]{:S(2)}) collective-permute-start(bf16[256,512]{1,0:T(8,128)(2,1)S(1)} %add_convert_fusion.6), channel_id=1, source_target_pairs={{0,2},{1,3},{2,4},{3,5},{4,6},{5,7},{8,10},{9,11},{10,12},{11,13},... | collective-permute-start | bytes 786440 | tf_op jit(solution)/shard_map/ppermute | solution.py:331
  87.3 8.6 %collective-permute-start.23 = (bf16[288,512]{1,0:T(8,128)(2,1)S(1)}, bf16[288,512]{1,0:T(8,128)(2,1)S(1)}, u32[]{:S(2)}, u32[]{:S(2)}) collective-permute-start(bf16[288,512]{1,0:T(8,128)(2,1)S(1)} %add_convert_fusion.1), channel_id=1, source_target_pairs={{2,0},{3,1},{4,2},{5,3},{6,4},{7,5},{10,8},{11,9},{12,10},{13,11},... | collective-permute-start | bytes 884744 | tf_op jit(solution)/shard_map/ppermute | solution.py:331
  88.6 8.9 %copy-start.2 = (bf16[288,512]{1,0:T(8,128)(2,1)S(1)}, bf16[288,512]{1,0:T(8,128)(2,1)}, u32[]{:S(2)}) copy-start(bf16[288,512]{1,0:T(8,128)(2,1)} %get-tuple-element.34) | copy-start | bytes 884740
  88.7 8.8 %collective-permute-start.21 = (bf16[288,512]{1,0:T(8,128)(2,1)S(1)}, bf16[288,512]{1,0:T(8,128)(2,1)S(1)}, u32[]{:S(2)}, u32[]{:S(2)}) collective-permute-start(bf16[288,512]{1,0:T(8,128)(2,1)S(1)} %add_convert_fusion.2), channel_id=1, source_target_pairs={{0,2},{1,3},{2,4},{3,5},{4,6},{5,7},{8,10},{9,11},{10,12},{11,13},... | collective-permute-start | bytes 884744 | tf_op jit(solution)/shard_map/ppermute | solution.py:331
  94.0 4.0 %collective-permute-start.24 = (bf16[128,512]{1,0:T(8,128)(2,1)S(1)}, bf16[128,512]{1,0:T(8,128)(2,1)S(1)}, u32[]{:S(2)}, u32[]{:S(2)}) collective-permute-start(bf16[128,512]{1,0:T(8,128)(2,1)S(1)} %slice.90), channel_id=1, source_target_pairs={{0,1},{1,0},{2,3},{3,2},{4,5},{5,4},{6,7},{7,6},{8,9},{9,8},{10,11... | collective-permute-start | bytes 393224 | tf_op jit(solution)/shard_map/ppermute | solution.py:331
  97.9 1.5 %collective-permute-start.25 = (bf16[160,512]{1,0:T(8,128)(2,1)S(1)}, bf16[160,512]{1,0:T(8,128)(2,1)S(1)}, u32[]{:S(2)}, u32[]{:S(2)}) collective-permute-start(bf16[160,512]{1,0:T(8,128)(2,1)S(1)} %slice.92), channel_id=1, source_target_pairs={{0,1},{1,0},{2,3},{3,2},{4,5},{5,4},{6,7},{7,6},{8,9},{9,8},{10,11... | collective-permute-start | bytes 491528 | tf_op jit(solution)/shard_map/ppermute | solution.py:331
  99.7 5.1 %collective-permute-start.27 = (f32[8,128]{1,0:T(8,128)S(1)}, f32[8,128]{1,0:T(8,128)S(1)}, u32[]{:S(2)}, u32[]{:S(2)}) collective-permute-start(f32[8,128]{1,0:T(8,128)S(1)} %broadcast_select_fusion.2), channel_id=1, source_target_pairs={{0,16},{8,24},{16,0},{24,8},{1,17},{9,25},{17,1},{25,9},{2,18},{10... | collective-permute-start | bytes 12296 | tf_op jit(solution)/shard_map/ppermute | solution.py:473
  99.7 5.1 %collective-permute-start.28 = (f32[8,128]{1,0:T(8,128)S(1)}, f32[8,128]{1,0:T(8,128)S(1)}, u32[]{:S(2)}, u32[]{:S(2)}) collective-permute-start(f32[8,128]{1,0:T(8,128)S(1)} %broadcast_select_fusion.2), channel_id=1, source_target_pairs={{0,24},{8,16},{16,8},{24,0},{1,25},{9,17},{17,9},{25,1},{2,26},{10... | collective-permute-start | bytes 12296 | tf_op jit(solution)/shard_map/ppermute | solution.py:473
  102.7 3.6 %collective-permute-start.26 = (f32[8,128]{1,0:T(8,128)S(1)}, f32[8,128]{1,0:T(8,128)S(1)}, u32[]{:S(2)}, u32[]{:S(2)}) collective-permute-start(f32[8,128]{1,0:T(8,128)S(1)} %broadcast_select_fusion.2), channel_id=1, source_target_pairs={{0,8},{8,0},{16,24},{24,16},{1,9},{9,1},{17,25},{25,17},{2,10},{10... | collective-permute-start | bytes 12296 | tf_op jit(solution)/shard_map/ppermute | solution.py:473
  (4 other events, 5.5 us)

commit v5 on v4

--- a/solution.py
+++ b/solution.py
@@ -39,59 +39,50 @@
             first = jnp.where(stretch >= end, end, first)
         return first
 
+    def rows_of(key_slot):
+        key_chip, inner = key_slot // per_chip, key_slot % per_chip
+        inner = inner % per_core + jnp.where(inner // per_core == core, 0, per_core)
+        ahead = key_chip - chip
+        table = jnp.where(ahead > 0, chips - 2 + ahead, -ahead)
+        table = jnp.where(abs(ahead) == chips - 1, 2 * chips - 3, table)
+        partial = jnp.where(ahead < 0, ahead + chips, ahead)
+        return (table * per_chip + inner) * stretch_len, (partial * per_chip + inner) * stretch_len
+
+    own, firsts, counts, own_rows = [], [], [], []
     for row in range(per_chip):
-        core_of_row = core if row < per_core else 1 - core
-        slot = chip * per_chip + core_of_row * per_core + row % per_core
-        mine = map_ref[slot]
-        first = first_of_document(mine)
-
-        def rows_of(key_slot):
-            key_chip = key_slot // per_chip
-            inner = key_slot - key_chip * per_chip
-            key_core = inner // per_core
-            inner = inner - key_core * per_core
-            inner = inner + jnp.where(key_core == core, 0, per_core)
-            ahead = key_chip - chip
-            table = jnp.where(ahead > 0, chips - 2 + ahead, -ahead)
-            table = jnp.where(abs(ahead) == chips - 1, 2 * chips - 3, table)
-            partial = jnp.where(ahead < 0, ahead + chips, ahead)
-            return (
-                (table * per_chip + inner) * stretch_len,
-                (partial * per_chip + inner) * stretch_len,
-            )
-
-        key_row, sum_row = rows_of(slot)
-        for at in range(limit):
-            table_ref[row, 1 + 2 * at] = key_row
-            table_ref[row, 2 + 2 * at] = sum_row
-
-        def visit(key_slot, count):
-            other = map_ref[key_slot]
-            seen = (other >= first) & (other < mine)
-
-            @pl.when(seen)
-            def _():
-                key_row, sum_row = rows_of(key_slot)
-                table_ref[row, 1 + 2 * count] = key_row
-                table_ref[row, 2 + 2 * count] = sum_row
-
-            return count + seen.astype(jnp.int32)
-
-        table_ref[row, 0] = lax.fori_loop(0, stretches, visit, jnp.int32(1))
-
-
-def attention_kernel(
-    shape, map_hbm, lengths_hbm, assign_hbm, sink_hbm, q_hbm, g_hbm, partner_hbm, *refs
-):
+        own.append(map_ref[chip * per_chip + (core if row < per_core else 1 - core) * per_core + row % per_core])
+        firsts.append(first_of_document(own[row]))
+        own_rows.append((row * stretch_len, row * stretch_len))
+        table_ref[row, 1], table_ref[row, 2] = own_rows[row]
+        counts.append(jnp.int32(1))
+    for key_slot in range(stretches):
+        other = map_ref[key_slot]
+        key_row, sum_row = rows_of(key_slot)
+        for row in range(per_chip):
+            table_ref[row, 1 + 2 * counts[row]] = key_row
+            table_ref[row, 2 + 2 * counts[row]] = sum_row
+            seen = (other >= firsts[row]) & (other < own[row])
+            counts[row] = counts[row] + seen.astype(jnp.int32)
+    for row in range(per_chip):
+        table_ref[row, 1 + 2 * counts[row]], table_ref[row, 2 + 2 * counts[row]] = own_rows[row]
+        table_ref[row, 0] = counts[row]
+
+
+def attention_kernel(shape, sink_hbm, q_hbm, g_hbm, partner_hbm, *refs):
     heads, ratio, stretch_len, per_chip, chips, limit, stream = shape
     count_in = 2 * chips - 2
     sources, refs = refs[:count_in], refs[count_in:]
+    layout, refs = (refs[:1], refs[1:]) if stream else (refs[:3], refs[3:])
     earlier, refs = refs[:stream], refs[stream:]
     o_hbm, dq_hbm, back_hbm, far_hbm = refs[:4]
     partials, refs = refs[4 : 4 + chips], refs[4 + chips :]
-    sink_out, kv, q_buf, g_buf, sums, out_buf, part_buf, table_ref, *small, sems = refs
-    tiny = (map_hbm, lengths_hbm, assign_hbm, sink_hbm)
-    map_ref, lengths_ref, assign_ref, sink_ref = small
+    if stream:
+        sink_out, *refs = refs
+    else:
+        sink_out, table_ref, *refs = refs
+    kv, q_buf, g_buf, sums, out_buf, part_buf, *small, sink_ref, sems = refs
+    if stream:
+        (table_ref,) = small
     index = lax.axis_index("ctx")
     chip, core = index // 2, index % 2
     rows = per_chip * stretch_len
@@ -101,7 +92,7 @@
     last = 4 + count_in
     tables = [
         pltpu.make_async_copy(source, target, sems.at[last + at])
-        for at, (source, target) in enumerate(zip(tiny, small))
+        for at, (source, target) in enumerate(zip((*layout, sink_hbm), (*small, sink_ref)))
     ]
     for load in tables:
         load.start()
@@ -117,23 +108,23 @@
             g_buf.at[pl.ds(local_rows, local_rows)],
         ),
     ]
+    held = [chip >= 0] * 5
+    held += [chip >= hop for hop in range(1, chips - 1)]
+    held += [chip < chips - hop for hop in range(1, chips - 1)]
+    held.append((chip == 0) | (chip == chips - 1))
     loads += [(source, kv.at[pl.ds(at * rows, rows)]) for at, source in enumerate(sources)]
     loads = [pltpu.make_async_copy(*pair, sems.at[at]) for at, pair in enumerate(loads)]
-    for load in loads:
-        load.start()
+    for at, load in enumerate(loads):
+        if at < 5:
+            load.start()
+        else:
+            pl.when(held[at])(load.start)
     for load in tables:
         load.wait()
-    fill_table(
-        chip,
-        core,
-        lax.axis_index("dp"),
-        chips,
-        stretch_len,
-        map_ref,
-        lengths_ref,
-        assign_ref,
-        table_ref,
-    )
+    if not stream:
+        fill_table(
+            chip, core, lax.axis_index("dp"), chips, stretch_len, *small, table_ref
+        )
     sums[...] = jnp.zeros_like(sums)
     sink_out[...] = jnp.zeros_like(sink_out)
     block = ratio * stretch_len
@@ -147,8 +138,11 @@
         for at in range(ratio):
             sink = jnp.where(owner == at, sink_ref[first_head + at] * LOG2E, sink)
         sinks.append(sink)
-    for load in loads:
-        load.wait()
+    for at, load in enumerate(loads):
+        if at < 5:
+            load.wait()
+        else:
+            pl.when(held[at])(load.wait)
 
     def take(ref, first, head):
         first_lane = head * ratio * HD
@@ -292,18 +286,19 @@
 ):
     heads = sources[0].shape[1] // (2 * HD)
     rows = sources[0].shape[0]
-    per_chip = layout[0].shape[0] // chips
+    per_chip = layout[0].shape[0] // (1 if stream else chips)
     stretch_len = rows // per_chip
     wide = heads * ratio * HD
     shape = (heads, ratio, stretch_len, per_chip, chips, limit, stream)
-    hbm, vmem = pl.BlockSpec(memory_space=pltpu.HBM), pl.BlockSpec(memory_space=pltpu.VMEM)
+    smem, hbm = pl.BlockSpec(memory_space=pltpu.SMEM), pl.BlockSpec(memory_space=pltpu.HBM)
+    vmem = pl.BlockSpec(memory_space=pltpu.VMEM)
     sent_rows = rows + (-(-3 * STREAMS * chips // 16) * 16 if stream else 0)
     own = jax.ShapeDtypeStruct((rows // 2, wide), jnp.bfloat16)
     sent = jax.ShapeDtypeStruct((sent_rows, heads * 2 * HD), jnp.bfloat16)
     return pl.pallas_call(
         functools.partial(attention_kernel, shape),
-        in_specs=[hbm] * (7 + len(sources)) + [vmem] * len(earlier),
-        out_specs=[hbm] * (4 + chips) + [vmem],
+        in_specs=[hbm] * (4 + len(sources) + len(layout)) + [vmem] * len(earlier),
+        out_specs=[hbm] * (4 + chips) + [vmem] + ([] if stream else [smem]),
         scratch_shapes=[
             pltpu.VMEM((len(sources) * rows, heads * 2 * HD), jnp.bfloat16),
             pltpu.VMEM((rows, wide), jnp.bfloat16),
@@ -311,20 +306,21 @@
             pltpu.VMEM((chips * rows, heads * 2 * HD), jnp.float32),
             pltpu.VMEM((rows, 2 * wide), jnp.bfloat16),
             pltpu.VMEM((chips, sent_rows, heads * 2 * HD), jnp.bfloat16),
-            pltpu.SMEM((per_chip, 1 + 2 * limit), jnp.int32),
-            *[pltpu.SMEM(part.shape, part.dtype) for part in (*layout, sinks)],
+            *[pltpu.SMEM(part.shape, part.dtype) for part in layout],
+            pltpu.SMEM(sinks.shape, sinks.dtype),
             pltpu.SemaphoreType.DMA((8 + len(sources),)),
         ],
         out_shape=[own, own, jax.ShapeDtypeStruct((rows // 2, 2 * wide), jnp.bfloat16)]
         + [sent] * (1 + chips)
-        + [jax.ShapeDtypeStruct((heads, 1, ratio * stretch_len), jnp.float32)],
+        + [jax.ShapeDtypeStruct((heads, 1, ratio * stretch_len), jnp.float32)]
+        + ([] if stream else [jax.ShapeDtypeStruct((per_chip, 3 + 2 * limit), jnp.int32)]),
         compiler_params=pltpu.CompilerParams(vmem_limit_bytes=60 << 20),
         cost_estimate=pl.CostEstimate(
             flops=6 * 2 * heads * rows * ratio * limit * stretch_len * HD,
             transcendentals=heads * rows * ratio * limit * stretch_len,
             bytes_accessed=8 << 20,
         ),
-    )(*layout, sinks, queries, out_grad, partner, *sources, *earlier)
+    )(sinks, queries, out_grad, partner, *sources, *layout, *earlier)
 
 
 def send(value, pairs):
@@ -411,8 +407,6 @@
         ),
         swap,
     )
-    layout = (stretch_map, doc_lengths, assignment)
-
     def gathered(stream, hops):
         right, left = hops[-1] if hops else (own[stream], own[stream])
         hop = len(hops) + 1
@@ -421,40 +415,61 @@
         ends = along(chips, 1, [chips - 2]) + along(chips, -1, [1])
         return hops + [(send(jnp.where(chip >= chips // 2, right, left), ends),)]
 
-    def compute(stream, hops, earlier):
+    def compute(stream, layout, hops, earlier):
         right, left = [hop[0] for hop in hops[:-1]], [hop[1] for hop in hops[:-1]]
         results = attend(
             stream, layout, sink_logits, queries, out_grad, partner,
             [own[stream]] + right + left + list(hops[-1]), earlier, chips, limit, ratio,
         )
-        return results[:3], results[3], results[4:-1], results[-1]
+        return results[:3], results[3], results[4 : 4 + chips], results[4 + chips :]
+
+    def added(partials, running, hop):
+        return add(partials[chips - hop], running[0]), add(partials[hop], running[1])
 
     def scattered(far, partials, running, hop):
         if hop == 1:
             ends = along(chips, 1, [0]) + along(chips, -1, [chips - 1])
             return (send(far, ends),) * 2
-        return scatter_hop(
-            add(partials[chips - hop], running[0]), add(partials[hop], running[1]), hop, chips
-        )
+        return scatter_hop(*added(partials, running, hop), hop, chips)
 
     def finished(partials, running):
         total = add3(partials[0], *running)
         return total, send(total[local_rows:], swap)
 
     first_hops, second_hops = [], []
-    for _ in range(1, chips):
+    for hop in range(1, chips):
         first_hops = gathered(0, first_hops)
         second_hops = gathered(1, second_hops)
-    first_out, first_far, first_sums, first_sink = compute(0, first_hops, [])
+        if hop == chips - 2:
+            partner, first_hops[-1] = lax.optimization_barrier((partner, first_hops[-1]))
+    layout = (stretch_map, doc_lengths, assignment)
+    first_out, first_far, first_sums, (first_sink, table) = compute(0, layout, first_hops, [])
     first_run = scattered(first_far, None, None, 1)
-    second_out, second_far, second_sums, _ = compute(1, second_hops, [first_sink])
+    second_out, second_far, second_sums, _ = compute(1, (table,), second_hops, [first_sink])
     second_run = scattered(second_far, None, None, 1)
+    both = send(jnp.concatenate([first_out[2], second_out[2]], axis=1), swap)
+    first_back, second_back = both[:, : both.shape[1] // 2], both[:, both.shape[1] // 2 :]
     for hop in range(2, chips):
         second_run = scattered(None, second_sums, second_run, hop)
         first_run = scattered(None, first_sums, first_run, hop)
+    def whole(mine, other):
+        return jnp.where(
+            core == 0, jnp.concatenate(mine + other, axis=1), jnp.concatenate(other + mine, axis=1)
+        )
+
+    wide = width * ratio
+    attn_out, query_grad = [
+        whole(
+            [part[at] for part in (first_out, second_out)],
+            [part[:, at * wide : (at + 1) * wide] for part in (first_back, second_back)],
+        )
+        for at in range(2)
+    ]
+    (attn_out, query_grad), first_run, second_run = lax.optimization_barrier(
+        ((attn_out, query_grad), first_run, second_run)
+    )
     second_total = finished(second_sums, second_run)
     first_total = finished(first_sums, first_run)
-    first_back, second_back = send(first_out[2], swap), send(second_out[2], swap)
 
     def sink_sums(slots):
         slots = slots.astype(jnp.float32)[: 3 * STREAMS * chips]
@@ -475,19 +490,6 @@
     ]
     sink_grad = jnp.sum(functools.reduce(jnp.add, others, sink_grad), axis=0)[:head_count]
 
-    def whole(mine, other):
-        return jnp.where(
-            core == 0, jnp.concatenate(mine + other, axis=1), jnp.concatenate(other + mine, axis=1)
-        )
-
-    wide = width * ratio
-    attn_out, query_grad = [
-        whole(
-            [part[at] for part in (first_out, second_out)],
-            [part[:, at * wide : (at + 1) * wide] for part in (first_back, second_back)],
-        )
-        for at in range(2)
-    ]
     key_grad, value_grad = [
         whole(
             *[

time: 107 us -> 103 us (0.963)
  the two profiles are of different devices: /device:TPU:0 before, /device:TPU:24 now
where the time goes in v5:
time: 103 us; the launch traced here: 101 us
  starting transfers between devices  44.1 us (43%)
  waiting for transfers between devices  31.2 us (30%)
  Pallas kernels  12.8 us (12%)
  other arithmetic  7.08 us (7%)
  local copies, waits for them, and re-layouts  4.3 us (4%)
  between operations  1.41 us (1%)
    ppermute x25, starting transfers between devices, send(): return lax.ppermute(value, 'ctx', pairs)  40.6 us
    ppermute x25, waiting for transfers between devices, send(): return lax.ppermute(value, 'ctx', pairs)  29.8 us
    pallas_call x2, Pallas kernels, attend(): pl.pallas_call(functools.partial(attention_kernel, shape), in_specs=[hbm]...  12.8 us
    select_n x4, other arithmetic, whole(): jnp.where(core == 0, jnp.concatenate(mine + other, axis=1), jnp.concatena...  4 us
    ppermute x3, starting transfers between devices, per_device(): lax.ppermute(sink_grad, 'dp', [(at, at ^ bit) for at in range(size)])  3.49 us
    dynamic_slice x2, local copies, waits for them, and re-layouts, columns(): return lax.dynamic_slice_in_dim(table, first, count, 1)  2.31 us
  transfers between devices with their start and end apart: 28, of which 14 were waited for; matrix products, arithmetic and copies ran while one was open for 7% of the time, Pallas kernels for 13%

profile of v5, /device:TPU:24, one launch (start us, length us, event | category | flops | bytes accessed | tf_op | source)
XLA Modules:
  0.0 101.0 jit_solution(571771683257993703)
XLA Ops:
  0.7 1.2 %constant_dynamic-slice_fusion = (bf16[128,256]{1,0:T(8,128)(2,1)S(1)}, bf16[128,256]{1,0:T(8,128)(2,1)S(1)}, bf16[128,256]{1,0:T(8,128)(2,1)S(1)}, bf16[128,256...) fusion(bf16[128,1024]{1,0:T(8,128)(2,1)} %param.10, ...), kind=kLoop, calls=%fused_computation.22 | loop fusion | bytes 1048592 | tf_op jit(solution)/shard_map/dynamic_slice | solution.py:363
  2.1 1.1 %constant_dynamic-slice_fusion.8 = (bf16[128,2048]{1,0:T(8,128)(2,1)S(1)}, bf16[128,2048]{1,0:T(8,128)(2,1)S(1)}) fusion(bf16[128,4096]{1,0:T(8,128)(2,1)} %g_hbm.3, s32[]{:T(128)S(6)} %select_n.88, bf16[128,4096]{1,0:T(8,128)(2,1)S(1)} %copy-done.5), kind=kLoop, calls=%fused_computation.30 | loop fusion | bytes 2097156 | tf_op jit(solution)/shard_map/dynamic_slice | solution.py:363
  3.3 0.4 collective-permute-start
  3.8 2.4 %collective-permute-start.4 = (bf16[256,512]{1,0:T(8,128)(2,1)S(1)}, bf16[256,512]{1,0:T(8,128)(2,1)S(1)}, u32[]{:S(2)}, u32[]{:S(2)}) collective-permute-start(bf16[256,512]{1,0:T(8,128)(2,1)S(1)} %pad_maximum_fusion.3.refs_0_), channel_id=1, source_target_pairs={{2,0},{3,1},{4,2},{5,3},{6,4},{7,5},{10,8},{11,9},{12,10},{13,11},... | collective-permute-start | bytes 786440 | tf_op jit(solution)/shard_map/ppermute | solution.py:327
  6.2 1.3 %collective-permute-start.2 = (bf16[256,512]{1,0:T(8,128)(2,1)S(1)}, bf16[256,512]{1,0:T(8,128)(2,1)}, u32[]{:S(2)}, u32[]{:S(2)}) collective-permute-start(bf16[256,512]{1,0:T(8,128)(2,1)S(1)} %pad_maximum_fusion.3.refs_0_), channel_id=1, source_target_pairs={{0,2},{1,3},{2,4},{3,5},{4,6},{5,7},{8,10},{9,11},{10,12},{11,13},... | collective-permute-start | bytes 786440 | tf_op jit(solution)/shard_map/ppermute | solution.py:327
  7.5 4.6 %collective-permute-start.9 = (bf16[256,512]{1,0:T(8,128)(2,1)S(1)}, bf16[256,512]{1,0:T(8,128)(2,1)S(1)}, u32[]{:S(2)}, u32[]{:S(2)}) collective-permute-start(bf16[256,512]{1,0:T(8,128)(2,1)S(1)} %pad_maximum_fusion.4.refs_0_), channel_id=1, source_target_pairs={{2,0},{3,1},{4,2},{5,3},{6,4},{7,5},{10,8},{11,9},{12,10},{13,11},... | collective-permute-start | bytes 786440 | tf_op jit(solution)/shard_map/ppermute | solution.py:327
  12.1 1.3 %collective-permute-start.7 = (bf16[256,512]{1,0:T(8,128)(2,1)S(1)}, bf16[256,512]{1,0:T(8,128)(2,1)S(1)}, u32[]{:S(2)}, u32[]{:S(2)}) collective-permute-start(bf16[256,512]{1,0:T(8,128)(2,1)S(1)} %pad_maximum_fusion.4.refs_0_), channel_id=1, source_target_pairs={{0,2},{1,3},{2,4},{3,5},{4,6},{5,7},{8,10},{9,11},{10,12},{11,13},... | collective-permute-start | bytes 786440 | tf_op jit(solution)/shard_map/ppermute | solution.py:327
  13.4 0.7 collective-permute-start.5
  14.1 2.4 %collective-permute-done.2.refs_1_ = bf16[256,512]{1,0:T(8,128)(2,1)} collective-permute-done((bf16[256,512]{1,0:T(8,128)(2,1)S(1)}, bf16[256,512]{1,0:T(8,128)(2,1)}, u32[]{:S(2)}, u32[]{:S(2)}) %collective-permute-start.2) | collective-permute-done | bytes 262176 | tf_op jit(solution)/shard_map/ppermute | solution.py:327
  16.5 1.3 %collective-permute-start.3 = (bf16[256,512]{1,0:T(8,128)(2,1)}, bf16[256,512]{1,0:T(8,128)(2,1)S(1)}, u32[]{:S(2)}, u32[]{:S(2)}) collective-permute-start(bf16[256,512]{1,0:T(8,128)(2,1)} %collective-permute-done.2.refs_1_), channel_id=1, source_target_pairs={{2,4},{3,5},{4,6},{5,7},{10,12},{11,13},{12,14},{13,15},{18,20},{1... | collective-permute-start | bytes 786440 | tf_op jit(solution)/shard_map/ppermute | solution.py:327
  17.8 0.7 collective-permute-start.10
  18.5 4.8 %collective-permute-done.7.refs_1_ = bf16[256,512]{1,0:T(8,128)(2,1)S(1)} collective-permute-done((bf16[256,512]{1,0:T(8,128)(2,1)S(1)}, bf16[256,512]{1,0:T(8,128)(2,1)S(1)}, u32[]{:S(2)}, u32[]{:S(2)}) %collective-permute-start.7) | collective-permute-done | bytes 262176 | tf_op jit(solution)/shard_map/ppermute | solution.py:327
  23.2 1.3 %collective-permute-start.8 = (bf16[256,512]{1,0:T(8,128)(2,1)S(1)}, bf16[256,512]{1,0:T(8,128)(2,1)S(1)}, u32[]{:S(2)}, u32[]{:S(2)}) collective-permute-start(bf16[256,512]{1,0:T(8,128)(2,1)S(1)} %collective-permute-done.7.refs_1_), channel_id=1, source_target_pairs={{2,4},{3,5},{4,6},{5,7},{10,12},{11,13},{12,14},{13,15},{18,20},{1... | collective-permute-start | bytes 786440 | tf_op jit(solution)/shard_map/ppermute | solution.py:327
  24.6 4.3 %collective-permute-done.3.refs_2_ = bf16[256,512]{1,0:T(8,128)(2,1)S(1)} collective-permute-done((bf16[256,512]{1,0:T(8,128)(2,1)}, bf16[256,512]{1,0:T(8,128)(2,1)S(1)}, u32[]{:S(2)}, u32[]{:S(2)}) %collective-permute-start.3) | collective-permute-done | bytes 262176 | tf_op jit(solution)/shard_map/ppermute | solution.py:327
  28.9 1.3 %collective-permute-start.6 = (bf16[256,512]{1,0:T(8,128)(2,1)S(1)}, bf16[256,512]{1,0:T(8,128)(2,1)S(1)}, u32[]{:S(2)}, u32[]{:S(2)}) collective-permute-start(bf16[256,512]{1,0:T(8,128)(2,1)S(1)} %broadcast_select_fusion.1), channel_id=1, source_target_pairs={{4,6},{5,7},{2,0},{3,1},{12,14},{13,15},{10,8},{11,9},{20,22},{21,... | collective-permute-start | bytes 786440 | tf_op jit(solution)/shard_map/ppermute | solution.py:327
  30.2 4.2 %collective-permute-done.8.refs_2_ = bf16[256,512]{1,0:T(8,128)(2,1)S(1)} collective-permute-done((bf16[256,512]{1,0:T(8,128)(2,1)S(1)}, bf16[256,512]{1,0:T(8,128)(2,1)S(1)}, u32[]{:S(2)}, u32[]{:S(2)}) %collective-permute-start.8) | collective-permute-done | bytes 262176 | tf_op jit(solution)/shard_map/ppermute | solution.py:327
  34.5 1.3 %collective-permute-start.11 = (bf16[256,512]{1,0:T(8,128)(2,1)S(1)}, bf16[256,512]{1,0:T(8,128)(2,1)S(1)}, u32[]{:S(2)}, u32[]{:S(2)}) collective-permute-start(bf16[256,512]{1,0:T(8,128)(2,1)S(1)} %broadcast_select_fusion), channel_id=1, source_target_pairs={{4,6},{5,7},{2,0},{3,1},{12,14},{13,15},{10,8},{11,9},{20,22},{21,... | collective-permute-start | bytes 786440 | tf_op jit(solution)/shard_map/ppermute | solution.py:327
  35.8 4.3 %collective-permute-done.6.refs_5_ = bf16[256,512]{1,0:T(8,128)(2,1)S(1)} collective-permute-done((bf16[256,512]{1,0:T(8,128)(2,1)S(1)}, bf16[256,512]{1,0:T(8,128)(2,1)S(1)}, u32[]{:S(2)}, u32[]{:S(2)}) %collective-permute-start.6) | collective-permute-done | bytes 262176 | tf_op jit(solution)/shard_map/ppermute | solution.py:327
  40.1 0.7 copy-done.24
  40.8 6.0 %shard_map.119 = (bf16[128,1024]{1,0:T(8,128)(2,1)}, bf16[128,1024]{1,0:T(8,128)(2,1)}, bf16[128,2048]{1,0:T(8,128)(2,1)}, bf16[256,512]{1,0:T(8,128)(2,1)}, bf1...) custom-call(f32[32]{0:T(128)} %sink_hbm.3, ...), custom_call_target="tpu_custom_call" | custom-call | flops 1610612736 | bytes 8388608 | tf_op jit(solution)/shard_map/pallas_call | solution.py:298
  46.9 2.4 %collective-permute-start.13 = (bf16[256,512]{1,0:T(8,128)(2,1)}, bf16[256,512]{1,0:T(8,128)(2,1)S(1)}, u32[]{:S(2)}, u32[]{:S(2)}) collective-permute-start(bf16[256,512]{1,0:T(8,128)(2,1)} %get-tuple-element.45), channel_id=1, source_target_pairs={{0,2},{1,3},{6,4},{7,5},{8,10},{9,11},{14,12},{15,13},{16,18},{17,... | collective-permute-start | bytes 786440 | tf_op jit(solution)/shard_map/ppermute | solution.py:327
  49.4 0.7 copy-done.23
  50.1 6.8 %shard_map.120 = (bf16[128,1024]{1,0:T(8,128)(2,1)}, bf16[128,1024]{1,0:T(8,128)(2,1)}, bf16[128,2048]{1,0:T(8,128)(2,1)}, bf16[288,512]{1,0:T(8,128)(2,1)}, bf1...) custom-call(f32[32]{0:T(128)} %sink_hbm.3, ...), custom_call_target="tpu_custom_call" | custom-call | flops 1610612736 | bytes 8388608 | tf_op jit(solution)/shard_map/pallas_call | solution.py:298
  56.9 2.4 %collective-permute-start.18 = (bf16[288,512]{1,0:T(8,128)(2,1)}, bf16[288,512]{1,0:T(8,128)(2,1)S(1)}, u32[]{:S(2)}, u32[]{:S(2)}) collective-permute-start(bf16[288,512]{1,0:T(8,128)(2,1)} %get-tuple-element.49), channel_id=1, source_target_pairs={{0,2},{1,3},{6,4},{7,5},{8,10},{9,11},{14,12},{15,13},{16,18},{17,... | collective-permute-start | bytes 884744 | tf_op jit(solution)/shard_map/ppermute | solution.py:327
  59.4 1.3 %collective-permute-start.16 = (bf16[256,512]{1,0:T(8,128)(2,1)S(1)}, bf16[256,512]{1,0:T(8,128)(2,1)S(1)}, u32[]{:S(2)}, u32[]{:S(2)}) collective-permute-start(bf16[256,512]{1,0:T(8,128)(2,1)S(1)} %add_convert_fusion.7), channel_id=1, source_target_pairs={{4,2},{5,3},{6,4},{7,5},{12,10},{13,11},{14,12},{15,13},{20,18},{2... | collective-permute-start | bytes 786440 | tf_op jit(solution)/shard_map/ppermute | solution.py:327
  60.8 1.2 %pad_maximum_fusion.1 = bf16[128,4096]{1,0:T(8,128)(2,1)S(1)} fusion(bf16[128,2048]{1,0:T(8,128)(2,1)} %get-tuple-element.40, bf16[128,2048]{1,0:T(8,128)(2,1)S(1)} %copy-done), kind=kLoop, calls=%fused_computation.1 | loop fusion | flops 2097152 | bytes 2097152 | tf_op jit(solution)/shard_map/concatenate | solution.py:450
  62.1 0.7 collective-permute-start.14
  62.7 3.3 %collective-permute-done.18 = bf16[288,512]{1,0:T(8,128)(2,1)S(1)} collective-permute-done((bf16[288,512]{1,0:T(8,128)(2,1)}, bf16[288,512]{1,0:T(8,128)(2,1)S(1)}, u32[]{:S(2)}, u32[]{:S(2)}) %collective-permute-start.18) | collective-permute-done | bytes 294944 | tf_op jit(solution)/shard_map/ppermute | solution.py:327
  66.1 4.3 %collective-permute-start.21 = (bf16[288,512]{1,0:T(8,128)(2,1)S(1)}, bf16[288,512]{1,0:T(8,128)(2,1)S(1)}, u32[]{:S(2)}, u32[]{:S(2)}) collective-permute-start(bf16[288,512]{1,0:T(8,128)(2,1)S(1)} %add_convert_fusion.3), channel_id=1, source_target_pairs={{4,2},{5,3},{6,4},{7,5},{12,10},{13,11},{14,12},{15,13},{20,18},{2... | collective-permute-start | bytes 884744 | tf_op jit(solution)/shard_map/ppermute | solution.py:327
  70.4 0.7 collective-permute-start.19
  71.5 4.5 %collective-permute-start.17 = (bf16[256,512]{1,0:T(8,128)(2,1)S(1)}, bf16[256,512]{1,0:T(8,128)(2,1)S(1)}, u32[]{:S(2)}, u32[]{:S(2)}) collective-permute-start(bf16[256,512]{1,0:T(8,128)(2,1)S(1)} %add_convert_fusion.5), channel_id=1, source_target_pairs={{2,0},{3,1},{4,2},{5,3},{6,4},{7,5},{10,8},{11,9},{12,10},{13,11},... | collective-permute-start | bytes 786440 | tf_op jit(solution)/shard_map/ppermute | solution.py:327
  76.1 1.3 %collective-permute-start.15 = (bf16[256,512]{1,0:T(8,128)(2,1)S(1)}, bf16[256,512]{1,0:T(8,128)(2,1)S(1)}, u32[]{:S(2)}, u32[]{:S(2)}) collective-permute-start(bf16[256,512]{1,0:T(8,128)(2,1)S(1)} %add_convert_fusion.6), channel_id=1, source_target_pairs={{0,2},{1,3},{2,4},{3,5},{4,6},{5,7},{8,10},{9,11},{10,12},{11,13},... | collective-permute-start | bytes 786440 | tf_op jit(solution)/shard_map/ppermute | solution.py:327
  77.9 4.4 %collective-permute-start.22 = (bf16[288,512]{1,0:T(8,128)(2,1)S(1)}, bf16[288,512]{1,0:T(8,128)(2,1)S(1)}, u32[]{:S(2)}, u32[]{:S(2)}) collective-permute-start(bf16[288,512]{1,0:T(8,128)(2,1)S(1)} %add_convert_fusion.1), channel_id=1, source_target_pairs={{2,0},{3,1},{4,2},{5,3},{6,4},{7,5},{10,8},{11,9},{12,10},{13,11},... | collective-permute-start | bytes 884744 | tf_op jit(solution)/shard_map/ppermute | solution.py:327
  82.5 1.4 %collective-permute-start.20 = (bf16[288,512]{1,0:T(8,128)(2,1)S(1)}, bf16[288,512]{1,0:T(8,128)(2,1)S(1)}, u32[]{:S(2)}, u32[]{:S(2)}) collective-permute-start(bf16[288,512]{1,0:T(8,128)(2,1)S(1)} %add_convert_fusion.2), channel_id=1, source_target_pairs={{0,2},{1,3},{2,4},{3,5},{4,6},{5,7},{8,10},{9,11},{10,12},{11,13},... | collective-permute-start | bytes 884744 | tf_op jit(solution)/shard_map/ppermute | solution.py:327
  84.0 1.2 %maximum_select_fusion.1 = bf16[128,4096]{1,0:T(8,128)(2,1)} fusion(bf16[128,1024]{1,0:T(8,128)(2,1)S(1)} %get-tuple-element.60, bf16[128,1024]{1,0:T(8,128)(2,1)S(1)} %get-tuple-element.59, bf16[128,1024]{1,0:T(8,128)(2,1)S(1)} %copy-done.9, bf16[128,1024]{1,0:T(8,128)(2,1)S(1)} %copy-done.7, pred[]{:T(512)S(6)} %eq.16), kind=kLoop, calls=%fused_computation.3 | loop fusion | flops 8912896 | bytes 2097153 | tf_op jit(solution)/shard_map/jit(_where)/select_n | solution.py:456
  85.3 1.2 %maximum_select_fusion = bf16[128,4096]{1,0:T(8,128)(2,1)} fusion(bf16[128,1024]{1,0:T(8,128)(2,1)S(1)} %get-tuple-element.61, bf16[128,1024]{1,0:T(8,128)(2,1)S(1)} %get-tuple-element.62, bf16[128,1024]{1,0:T(8,128)(2,1)S(1)} %copy-done.8, bf16[128,1024]{1,0:T(8,128)(2,1)S(1)} %copy-done.6, pred[]{:T(512)S(6)} %eq.16), kind=kLoop, calls=%fused_computation.2 | loop fusion | flops 8912896 | bytes 2097153 | tf_op jit(solution)/shard_map/jit(_where)/select_n | solution.py:456
  86.5 0.5 collective-permute-done.15
  87.0 4.2 %collective-permute-done.20 = bf16[288,512]{1,0:T(8,128)(2,1)S(1)} collective-permute-done((bf16[288,512]{1,0:T(8,128)(2,1)S(1)}, bf16[288,512]{1,0:T(8,128)(2,1)S(1)}, u32[]{:S(2)}, u32[]{:S(2)}) %collective-permute-start.20) | collective-permute-done | bytes 294944 | tf_op jit(solution)/shard_map/ppermute | solution.py:327
  91.8 0.5 collective-permute-start.24
  92.3 0.8 collective-permute-done.23
  93.8 1.5 %collective-permute-start.26 = (f32[8,128]{1,0:T(8,128)S(1)}, f32[8,128]{1,0:T(8,128)S(1)}, u32[]{:S(2)}, u32[]{:S(2)}) collective-permute-start(f32[8,128]{1,0:T(8,128)S(1)} %broadcast_select_fusion.2), channel_id=1, source_target_pairs={{0,16},{8,24},{16,0},{24,8},{1,17},{9,25},{17,1},{25,9},{2,18},{10... | collective-permute-start | bytes 12296 | tf_op jit(solution)/shard_map/ppermute | solution.py:488
  95.3 1.4 %collective-permute-start.27 = (f32[8,128]{1,0:T(8,128)S(1)}, f32[8,128]{1,0:T(8,128)S(1)}, u32[]{:S(2)}, u32[]{:S(2)}) collective-permute-start(f32[8,128]{1,0:T(8,128)S(1)} %broadcast_select_fusion.2), channel_id=1, source_target_pairs={{0,24},{8,16},{16,8},{24,0},{1,25},{9,17},{17,9},{25,1},{2,26},{10... | collective-permute-start | bytes 12296 | tf_op jit(solution)/shard_map/ppermute | solution.py:488
  96.8 0.5 collective-permute-start.25
  97.3 0.8 maximum_select_fusion.3
  98.1 0.8 maximum_select_fusion.2
  98.9 0.9 collective-permute-done.27
  99.8 0.5 collective-permute-done.25
  100.4 0.6 add_reduce_fusion
  (104 shorter events, 3.1 us)
Async XLA Ops:
  1.9 1.9 %collective-permute-start.1 = (bf16[128,1024]{1,0:T(8,128)(2,1)S(1)}, bf16[128,1024]{1,0:T(8,128)(2,1)S(1)}, u32[]{:S(2)}, u32[]{:S(2)}) collective-permute-start(bf16[128,1024]{1,0:T(8,128)(2,1)S(1)} %pad_maximum_fusion.2), channel_id=1, source_target_pairs={{0,1},{1,0},{2,3},{3,2},{4,5},{5,4},{6,7},{7,6},{8,9},{9,8},{10,11... | collective-permute-start | bytes 786440 | tf_op jit(solution)/shard_map/ppermute | solution.py:327
  3.3 25.5 %collective-permute-start = (bf16[128,4096]{1,0:T(8,128)(2,1)S(1)}, bf16[128,4096]{1,0:T(8,128)(2,1)}, u32[]{:S(2)}, u32[]{:S(2)}) collective-permute-start(bf16[128,4096]{1,0:T(8,128)(2,1)S(1)} %pad_maximum_fusion), channel_id=1, source_target_pairs={{0,1},{1,0},{2,3},{3,2},{4,5},{5,4},{6,7},{7,6},{8,9},{9,8},{10,11... | collective-permute-start | bytes 3145736 | tf_op jit(solution)/shard_map/ppermute | solution.py:327
  3.8 30.7 %copy-start.14 = (bf16[256,512]{1,0:T(8,128)(2,1)}, bf16[256,512]{1,0:T(8,128)(2,1)S(1)}, u32[]{:S(2)}) copy-start(bf16[256,512]{1,0:T(8,128)(2,1)S(1)} %pad_maximum_fusion.3.refs_0_) | copy-start | bytes 786436
  3.8 9.6 %collective-permute-start.4 = (bf16[256,512]{1,0:T(8,128)(2,1)S(1)}, bf16[256,512]{1,0:T(8,128)(2,1)S(1)}, u32[]{:S(2)}, u32[]{:S(2)}) collective-permute-start(bf16[256,512]{1,0:T(8,128)(2,1)S(1)} %pad_maximum_fusion.3.refs_0_), channel_id=1, source_target_pairs={{2,0},{3,1},{4,2},{5,3},{6,4},{7,5},{10,8},{11,9},{12,10},{13,11},... | collective-permute-start | bytes 786440 | tf_op jit(solution)/shard_map/ppermute | solution.py:327
  6.2 10.3 %collective-permute-start.2 = (bf16[256,512]{1,0:T(8,128)(2,1)S(1)}, bf16[256,512]{1,0:T(8,128)(2,1)}, u32[]{:S(2)}, u32[]{:S(2)}) collective-permute-start(bf16[256,512]{1,0:T(8,128)(2,1)S(1)} %pad_maximum_fusion.3.refs_0_), channel_id=1, source_target_pairs={{0,2},{1,3},{2,4},{3,5},{4,6},{5,7},{8,10},{9,11},{10,12},{11,13},... | collective-permute-start | bytes 786440 | tf_op jit(solution)/shard_map/ppermute | solution.py:327
  7.5 39.4 %copy-start.13 = (bf16[256,512]{1,0:T(8,128)(2,1)}, bf16[256,512]{1,0:T(8,128)(2,1)S(1)}, u32[]{:S(2)}) copy-start(bf16[256,512]{1,0:T(8,128)(2,1)S(1)} %pad_maximum_fusion.4.refs_0_) | copy-start | bytes 786436
  7.5 10.2 %collective-permute-start.9 = (bf16[256,512]{1,0:T(8,128)(2,1)S(1)}, bf16[256,512]{1,0:T(8,128)(2,1)S(1)}, u32[]{:S(2)}, u32[]{:S(2)}) collective-permute-start(bf16[256,512]{1,0:T(8,128)(2,1)S(1)} %pad_maximum_fusion.4.refs_0_), channel_id=1, source_target_pairs={{2,0},{3,1},{4,2},{5,3},{6,4},{7,5},{10,8},{11,9},{12,10},{13,11},... | collective-permute-start | bytes 786440 | tf_op jit(solution)/shard_map/ppermute | solution.py:327
  12.1 11.1 %collective-permute-start.7 = (bf16[256,512]{1,0:T(8,128)(2,1)S(1)}, bf16[256,512]{1,0:T(8,128)(2,1)S(1)}, u32[]{:S(2)}, u32[]{:S(2)}) collective-permute-start(bf16[256,512]{1,0:T(8,128)(2,1)S(1)} %pad_maximum_fusion.4.refs_0_), channel_id=1, source_target_pairs={{0,2},{1,3},{2,4},{3,5},{4,6},{5,7},{8,10},{9,11},{10,12},{11,13},... | collective-permute-start | bytes 786440 | tf_op jit(solution)/shard_map/ppermute | solution.py:327
  13.4 26.7 %copy-start.22 = (bf16[256,512]{1,0:T(8,128)(2,1)}, bf16[256,512]{1,0:T(8,128)(2,1)S(1)}, u32[]{:S(2)}) copy-start(bf16[256,512]{1,0:T(8,128)(2,1)S(1)} %collective-permute-done.4.refs_3_) | copy-start | bytes 786436
  13.4 11.1 %collective-permute-start.5 = (bf16[256,512]{1,0:T(8,128)(2,1)S(1)}, bf16[256,512]{1,0:T(8,128)(2,1)S(1)}, u32[]{:S(2)}, u32[]{:S(2)}) collective-permute-start(bf16[256,512]{1,0:T(8,128)(2,1)S(1)} %collective-permute-done.4.refs_3_), channel_id=1, source_target_pairs={{2,0},{3,1},{4,2},{5,3},{10,8},{11,9},{12,10},{13,11},{18,16},{19,... | collective-permute-start | bytes 786440 | tf_op jit(solution)/shard_map/ppermute | solution.py:327
  16.5 12.4 %collective-permute-start.3 = (bf16[256,512]{1,0:T(8,128)(2,1)}, bf16[256,512]{1,0:T(8,128)(2,1)S(1)}, u32[]{:S(2)}, u32[]{:S(2)}) collective-permute-start(bf16[256,512]{1,0:T(8,128)(2,1)} %collective-permute-done.2.refs_1_), channel_id=1, source_target_pairs={{2,4},{3,5},{4,6},{5,7},{10,12},{11,13},{12,14},{13,15},{18,20},{1... | collective-permute-start | bytes 786440 | tf_op jit(solution)/shard_map/ppermute | solution.py:327
  17.8 29.1 %copy-start.20 = (bf16[256,512]{1,0:T(8,128)(2,1)}, bf16[256,512]{1,0:T(8,128)(2,1)S(1)}, u32[]{:S(2)}) copy-start(bf16[256,512]{1,0:T(8,128)(2,1)S(1)} %collective-permute-done.9.refs_3_) | copy-start | bytes 786436
  17.8 12.4 %collective-permute-start.10 = (bf16[256,512]{1,0:T(8,128)(2,1)S(1)}, bf16[256,512]{1,0:T(8,128)(2,1)S(1)}, u32[]{:S(2)}, u32[]{:S(2)}) collective-permute-start(bf16[256,512]{1,0:T(8,128)(2,1)S(1)} %collective-permute-done.9.refs_3_), channel_id=1, source_target_pairs={{2,0},{3,1},{4,2},{5,3},{10,8},{11,9},{12,10},{13,11},{18,16},{19,... | collective-permute-start | bytes 786440 | tf_op jit(solution)/shard_map/ppermute | solution.py:327
  23.2 23.7 %copy-start.21 = (bf16[256,512]{1,0:T(8,128)(2,1)}, bf16[256,512]{1,0:T(8,128)(2,1)S(1)}, u32[]{:S(2)}) copy-start(bf16[256,512]{1,0:T(8,128)(2,1)S(1)} %collective-permute-done.7.refs_1_) | copy-start | bytes 786436
  23.2 11.2 %collective-permute-start.8 = (bf16[256,512]{1,0:T(8,128)(2,1)S(1)}, bf16[256,512]{1,0:T(8,128)(2,1)S(1)}, u32[]{:S(2)}, u32[]{:S(2)}) collective-permute-start(bf16[256,512]{1,0:T(8,128)(2,1)S(1)} %collective-permute-done.7.refs_1_), channel_id=1, source_target_pairs={{2,4},{3,5},{4,6},{5,7},{10,12},{11,13},{12,14},{13,15},{18,20},{1... | collective-permute-start | bytes 786440 | tf_op jit(solution)/shard_map/ppermute | solution.py:327
  24.5 15.6 %copy-start.16 = (bf16[256,512]{1,0:T(8,128)(2,1)}, bf16[256,512]{1,0:T(8,128)(2,1)S(1)}, u32[]{:S(2)}) copy-start(bf16[256,512]{1,0:T(8,128)(2,1)S(1)} %collective-permute-done.5.refs_4_) | copy-start | bytes 786436
  28.9 11.2 %copy-start.17 = (bf16[256,512]{1,0:T(8,128)(2,1)}, bf16[256,512]{1,0:T(8,128)(2,1)S(1)}, u32[]{:S(2)}) copy-start(bf16[256,512]{1,0:T(8,128)(2,1)S(1)} %collective-permute-done.3.refs_2_) | copy-start | bytes 786436
  28.9 11.2 %collective-permute-start.6 = (bf16[256,512]{1,0:T(8,128)(2,1)S(1)}, bf16[256,512]{1,0:T(8,128)(2,1)S(1)}, u32[]{:S(2)}, u32[]{:S(2)}) collective-permute-start(bf16[256,512]{1,0:T(8,128)(2,1)S(1)} %broadcast_select_fusion.1), channel_id=1, source_target_pairs={{4,6},{5,7},{2,0},{3,1},{12,14},{13,15},{10,8},{11,9},{20,22},{21,... | collective-permute-start | bytes 786440 | tf_op jit(solution)/shard_map/ppermute | solution.py:327
  30.2 16.7 %copy-start.18 = (bf16[256,512]{1,0:T(8,128)(2,1)}, bf16[256,512]{1,0:T(8,128)(2,1)S(1)}, u32[]{:S(2)}) copy-start(bf16[256,512]{1,0:T(8,128)(2,1)S(1)} %collective-permute-done.10.refs_4_) | copy-start | bytes 786436
  34.5 12.4 %copy-start.19 = (bf16[256,512]{1,0:T(8,128)(2,1)}, bf16[256,512]{1,0:T(8,128)(2,1)S(1)}, u32[]{:S(2)}) copy-start(bf16[256,512]{1,0:T(8,128)(2,1)S(1)} %collective-permute-done.8.refs_2_) | copy-start | bytes 786436
  34.5 14.9 %collective-permute-start.11 = (bf16[256,512]{1,0:T(8,128)(2,1)S(1)}, bf16[256,512]{1,0:T(8,128)(2,1)S(1)}, u32[]{:S(2)}, u32[]{:S(2)}) collective-permute-start(bf16[256,512]{1,0:T(8,128)(2,1)S(1)} %broadcast_select_fusion), channel_id=1, source_target_pairs={{4,6},{5,7},{2,0},{3,1},{12,14},{13,15},{10,8},{11,9},{20,22},{21,... | collective-permute-start | bytes 786440 | tf_op jit(solution)/shard_map/ppermute | solution.py:327
  46.9 12.4 %collective-permute-start.13 = (bf16[256,512]{1,0:T(8,128)(2,1)}, bf16[256,512]{1,0:T(8,128)(2,1)S(1)}, u32[]{:S(2)}, u32[]{:S(2)}) collective-permute-start(bf16[256,512]{1,0:T(8,128)(2,1)} %get-tuple-element.45), channel_id=1, source_target_pairs={{0,2},{1,3},{6,4},{7,5},{8,10},{9,11},{14,12},{15,13},{16,18},{17,... | collective-permute-start | bytes 786440 | tf_op jit(solution)/shard_map/ppermute | solution.py:327
  50.1 9.2 %copy-start.12 = (bf16[256,512]{1,0:T(8,128)(2,1)S(1)}, bf16[256,512]{1,0:T(8,128)(2,1)}, u32[]{:S(2)}) copy-start(bf16[256,512]{1,0:T(8,128)(2,1)} %get-tuple-element.44) | copy-start | bytes 786436
  56.9 3.8 %copy-start = (bf16[128,2048]{1,0:T(8,128)(2,1)S(1)}, bf16[128,2048]{1,0:T(8,128)(2,1)}, u32[]{:S(2)}) copy-start(bf16[128,2048]{1,0:T(8,128)(2,1)} %get-tuple-element.39) | copy-start | bytes 1572868
  56.9 9.1 %collective-permute-start.18 = (bf16[288,512]{1,0:T(8,128)(2,1)}, bf16[288,512]{1,0:T(8,128)(2,1)S(1)}, u32[]{:S(2)}, u32[]{:S(2)}) collective-permute-start(bf16[288,512]{1,0:T(8,128)(2,1)} %get-tuple-element.49), channel_id=1, source_target_pairs={{0,2},{1,3},{6,4},{7,5},{8,10},{9,11},{14,12},{15,13},{16,18},{17,... | collective-permute-start | bytes 884744 | tf_op jit(solution)/shard_map/ppermute | solution.py:327
  59.4 12.0 %collective-permute-start.16 = (bf16[256,512]{1,0:T(8,128)(2,1)S(1)}, bf16[256,512]{1,0:T(8,128)(2,1)S(1)}, u32[]{:S(2)}, u32[]{:S(2)}) collective-permute-start(bf16[256,512]{1,0:T(8,128)(2,1)S(1)} %add_convert_fusion.7), channel_id=1, source_target_pairs={{4,2},{5,3},{6,4},{7,5},{12,10},{13,11},{14,12},{15,13},{20,18},{2... | collective-permute-start | bytes 786440 | tf_op jit(solution)/shard_map/ppermute | solution.py:327
  60.7 5.3 %copy-start.3 = (bf16[288,512]{1,0:T(8,128)(2,1)S(1)}, bf16[288,512]{1,0:T(8,128)(2,1)}, u32[]{:S(2)}) copy-start(bf16[288,512]{1,0:T(8,128)(2,1)} %get-tuple-element.48) | copy-start | bytes 884740
  60.8 10.7 %copy-start.11 = (bf16[256,512]{1,0:T(8,128)(2,1)S(1)}, bf16[256,512]{1,0:T(8,128)(2,1)}, u32[]{:S(2)}) copy-start(bf16[256,512]{1,0:T(8,128)(2,1)} %get-tuple-element.46) | copy-start | bytes 786436
  62.0 14.1 %copy-start.10 = (bf16[256,512]{1,0:T(8,128)(2,1)S(1)}, bf16[256,512]{1,0:T(8,128)(2,1)}, u32[]{:S(2)}) copy-start(bf16[256,512]{1,0:T(8,128)(2,1)} %get-tuple-element.43) | copy-start | bytes 786436
  62.0 21.9 %collective-permute-start.12 = (bf16[128,4096]{1,0:T(8,128)(2,1)S(1)}, bf16[128,4096]{1,0:T(8,128)(2,1)S(1)}, u32[]{:S(2)}, u32[]{:S(2)}) collective-permute-start(bf16[128,4096]{1,0:T(8,128)(2,1)S(1)} %pad_maximum_fusion.1), channel_id=1, source_target_pairs={{0,1},{1,0},{2,3},{3,2},{4,5},{5,4},{6,7},{7,6},{8,9},{9,8},{10,11... | collective-permute-start | bytes 3145736 | tf_op jit(solution)/shard_map/ppermute | solution.py:327
  62.1 14.0 %collective-permute-start.14 = (bf16[256,512]{1,0:T(8,128)(2,1)S(1)}, bf16[256,512]{1,0:T(8,128)(2,1)S(1)}, u32[]{:S(2)}, u32[]{:S(2)}) collective-permute-start(bf16[256,512]{1,0:T(8,128)(2,1)S(1)} %add_convert_fusion.7), channel_id=1, source_target_pairs={{0,2},{1,3},{2,4},{3,5},{8,10},{9,11},{10,12},{11,13},{16,18},{17,... | collective-permute-start | bytes 786440 | tf_op jit(solution)/shard_map/ppermute | solution.py:327
  66.0 11.8 %copy-start.2 = (bf16[288,512]{1,0:T(8,128)(2,1)S(1)}, bf16[288,512]{1,0:T(8,128)(2,1)}, u32[]{:S(2)}) copy-start(bf16[288,512]{1,0:T(8,128)(2,1)} %get-tuple-element.50) | copy-start | bytes 884740
  66.1 11.7 %collective-permute-start.21 = (bf16[288,512]{1,0:T(8,128)(2,1)S(1)}, bf16[288,512]{1,0:T(8,128)(2,1)S(1)}, u32[]{:S(2)}, u32[]{:S(2)}) collective-permute-start(bf16[288,512]{1,0:T(8,128)(2,1)S(1)} %add_convert_fusion.3), channel_id=1, source_target_pairs={{4,2},{5,3},{6,4},{7,5},{12,10},{13,11},{14,12},{15,13},{20,18},{2... | collective-permute-start | bytes 884744 | tf_op jit(solution)/shard_map/ppermute | solution.py:327
  70.4 11.9 %collective-permute-start.19 = (bf16[288,512]{1,0:T(8,128)(2,1)S(1)}, bf16[288,512]{1,0:T(8,128)(2,1)S(1)}, u32[]{:S(2)}, u32[]{:S(2)}) collective-permute-start(bf16[288,512]{1,0:T(8,128)(2,1)S(1)} %add_convert_fusion.3), channel_id=1, source_target_pairs={{0,2},{1,3},{2,4},{3,5},{8,10},{9,11},{10,12},{11,13},{16,18},{17,... | collective-permute-start | bytes 884744 | tf_op jit(solution)/shard_map/ppermute | solution.py:327
  71.4 10.9 %copy-start.1 = (bf16[288,512]{1,0:T(8,128)(2,1)S(1)}, bf16[288,512]{1,0:T(8,128)(2,1)}, u32[]{:S(2)}) copy-start(bf16[288,512]{1,0:T(8,128)(2,1)} %get-tuple-element.47) | copy-start | bytes 884740
  71.5 15.0 %collective-permute-start.17 = (bf16[256,512]{1,0:T(8,128)(2,1)S(1)}, bf16[256,512]{1,0:T(8,128)(2,1)S(1)}, u32[]{:S(2)}, u32[]{:S(2)}) collective-permute-start(bf16[256,512]{1,0:T(8,128)(2,1)S(1)} %add_convert_fusion.5), channel_id=1, source_target_pairs={{2,0},{3,1},{4,2},{5,3},{6,4},{7,5},{10,8},{11,9},{12,10},{13,11},... | collective-permute-start | bytes 786440 | tf_op jit(solution)/shard_map/ppermute | solution.py:327
  76.1 10.8 %collective-permute-start.15 = (bf16[256,512]{1,0:T(8,128)(2,1)S(1)}, bf16[256,512]{1,0:T(8,128)(2,1)S(1)}, u32[]{:S(2)}, u32[]{:S(2)}) collective-permute-start(bf16[256,512]{1,0:T(8,128)(2,1)S(1)} %add_convert_fusion.6), channel_id=1, source_target_pairs={{0,2},{1,3},{2,4},{3,5},{4,6},{5,7},{8,10},{9,11},{10,12},{11,13},... | collective-permute-start | bytes 786440 | tf_op jit(solution)/shard_map/ppermute | solution.py:327
  77.9 9.1 %collective-permute-start.22 = (bf16[288,512]{1,0:T(8,128)(2,1)S(1)}, bf16[288,512]{1,0:T(8,128)(2,1)S(1)}, u32[]{:S(2)}, u32[]{:S(2)}) collective-permute-start(bf16[288,512]{1,0:T(8,128)(2,1)S(1)} %add_convert_fusion.1), channel_id=1, source_target_pairs={{2,0},{3,1},{4,2},{5,3},{6,4},{7,5},{10,8},{11,9},{12,10},{13,11},... | collective-permute-start | bytes 884744 | tf_op jit(solution)/shard_map/ppermute | solution.py:327
  82.4 1.6 %copy-start.7 = (bf16[128,1024]{1,0:T(8,128)(2,1)S(1)}, bf16[128,1024]{1,0:T(8,128)(2,1)}, u32[]{:S(2)}) copy-start(bf16[128,1024]{1,0:T(8,128)(2,1)} %get-tuple-element.41) | copy-start | bytes 786436
  82.5 1.6 %copy-start.9 = (bf16[128,1024]{1,0:T(8,128)(2,1)S(1)}, bf16[128,1024]{1,0:T(8,128)(2,1)}, u32[]{:S(2)}) copy-start(bf16[128,1024]{1,0:T(8,128)(2,1)} %get-tuple-element.42) | copy-start | bytes 786436
  82.5 8.7 %collective-permute-start.20 = (bf16[288,512]{1,0:T(8,128)(2,1)S(1)}, bf16[288,512]{1,0:T(8,128)(2,1)S(1)}, u32[]{:S(2)}, u32[]{:S(2)}) collective-permute-start(bf16[288,512]{1,0:T(8,128)(2,1)S(1)} %add_convert_fusion.2), channel_id=1, source_target_pairs={{0,2},{1,3},{2,4},{3,5},{4,6},{5,7},{8,10},{9,11},{10,12},{11,13},... | collective-permute-start | bytes 884744 | tf_op jit(solution)/shard_map/ppermute | solution.py:327
  85.3 6.0 %copy-start.15 = (bf16[256,512]{1,0:T(8,128)(2,1)S(1)}, bf16[256,512]{1,0:T(8,128)(2,1)}, u32[]{:S(2)}) copy-start(bf16[256,512]{1,0:T(8,128)(2,1)} %get-tuple-element.53) | copy-start | bytes 786436
  86.5 4.9 %copy-start.4 = (bf16[288,512]{1,0:T(8,128)(2,1)S(1)}, bf16[288,512]{1,0:T(8,128)(2,1)}, u32[]{:S(2)}) copy-start(bf16[288,512]{1,0:T(8,128)(2,1)} %get-tuple-element.56) | copy-start | bytes 884740
  91.8 1.4 %collective-permute-start.23 = (bf16[128,512]{1,0:T(8,128)(2,1)S(1)}, bf16[128,512]{1,0:T(8,128)(2,1)S(1)}, u32[]{:S(2)}, u32[]{:S(2)}) collective-permute-start(bf16[128,512]{1,0:T(8,128)(2,1)S(1)} %slice.96), channel_id=1, source_target_pairs={{0,1},{1,0},{2,3},{3,2},{4,5},{5,4},{6,7},{7,6},{8,9},{9,8},{10,11... | collective-permute-start | bytes 393224 | tf_op jit(solution)/shard_map/ppermute | solution.py:327
  91.8 1.6 %collective-permute-start.24 = (bf16[160,512]{1,0:T(8,128)(2,1)S(1)}, bf16[160,512]{1,0:T(8,128)(2,1)S(1)}, u32[]{:S(2)}, u32[]{:S(2)}) collective-permute-start(bf16[160,512]{1,0:T(8,128)(2,1)S(1)} %slice.98), channel_id=1, source_target_pairs={{0,1},{1,0},{2,3},{3,2},{4,5},{5,4},{6,7},{7,6},{8,9},{9,8},{10,11... | collective-permute-start | bytes 491528 | tf_op jit(solution)/shard_map/ppermute | solution.py:327
  93.8 5.1 %collective-permute-start.26 = (f32[8,128]{1,0:T(8,128)S(1)}, f32[8,128]{1,0:T(8,128)S(1)}, u32[]{:S(2)}, u32[]{:S(2)}) collective-permute-start(f32[8,128]{1,0:T(8,128)S(1)} %broadcast_select_fusion.2), channel_id=1, source_target_pairs={{0,16},{8,24},{16,0},{24,8},{1,17},{9,25},{17,1},{25,9},{2,18},{10... | collective-permute-start | bytes 12296 | tf_op jit(solution)/shard_map/ppermute | solution.py:488
  95.3 4.5 %collective-permute-start.27 = (f32[8,128]{1,0:T(8,128)S(1)}, f32[8,128]{1,0:T(8,128)S(1)}, u32[]{:S(2)}, u32[]{:S(2)}) collective-permute-start(f32[8,128]{1,0:T(8,128)S(1)} %broadcast_select_fusion.2), channel_id=1, source_target_pairs={{0,24},{8,16},{16,8},{24,0},{1,25},{9,17},{17,9},{25,1},{2,26},{10... | collective-permute-start | bytes 12296 | tf_op jit(solution)/shard_map/ppermute | solution.py:488
  96.8 3.6 %collective-permute-start.25 = (f32[8,128]{1,0:T(8,128)S(1)}, f32[8,128]{1,0:T(8,128)S(1)}, u32[]{:S(2)}, u32[]{:S(2)}) collective-permute-start(f32[8,128]{1,0:T(8,128)S(1)} %broadcast_select_fusion.2), channel_id=1, source_target_pairs={{0,8},{8,0},{16,24},{24,16},{1,9},{9,1},{17,25},{25,17},{2,10},{10... | collective-permute-start | bytes 12296 | tf_op jit(solution)/shard_map/ppermute | solution.py:488
  (5 other events, 5.4 us)

commit v6 on v5

--- a/solution.py
+++ b/solution.py
@@ -316,9 +316,9 @@
         + ([] if stream else [jax.ShapeDtypeStruct((per_chip, 3 + 2 * limit), jnp.int32)]),
         compiler_params=pltpu.CompilerParams(vmem_limit_bytes=60 << 20),
         cost_estimate=pl.CostEstimate(
-            flops=6 * 2 * heads * rows * ratio * limit * stretch_len * HD,
-            transcendentals=heads * rows * ratio * limit * stretch_len,
-            bytes_accessed=8 << 20,
+            flops=0 if stream else 6 * 2 * heads * rows * ratio * limit * stretch_len * HD,
+            transcendentals=0,
+            bytes_accessed=1024 if stream else 8 << 20,
         ),
     )(sinks, queries, out_grad, partner, *sources, *layout, *earlier)
 

time: 103 us -> 103 us (level)
  the two profiles are of different devices: /device:TPU:24 before, /device:TPU:0 now
where the time goes in v6:
time: 103 us; the launch traced here: 102 us
  starting transfers between devices  53.1 us (52%)
  waiting for transfers between devices  20.3 us (20%)
  Pallas kernels  14.4 us (14%)
  other arithmetic  8.23 us (8%)
  local copies, waits for them, and re-layouts  4.15 us (4%)
  between operations  1.36 us (1%)
    ppermute x25, starting transfers between devices, send(): return lax.ppermute(value, 'ctx', pairs)  49.6 us
    ppermute x25, waiting for transfers between devices, send(): return lax.ppermute(value, 'ctx', pairs)  19.2 us
    pallas_call x2, Pallas kernels, attend(): pl.pallas_call(functools.partial(attention_kernel, shape), in_specs=[hbm]...  14.4 us
    select_n x4, other arithmetic, whole(): jnp.where(core == 0, jnp.concatenate(mine + other, axis=1), jnp.concatena...  4 us
    ppermute x3, starting transfers between devices, per_device(): lax.ppermute(sink_grad, 'dp', [(at, at ^ bit) for at in range(size)])  3.49 us
    dynamic_slice x2, local copies, waits for them, and re-layouts, columns(): return lax.dynamic_slice_in_dim(table, first, count, 1)  2.31 us
  transfers between devices with their start and end apart: 28, of which 10 were waited for; matrix products, arithmetic and copies ran while one was open for 8% of the time, Pallas kernels for 14%

profile of v6, /device:TPU:0, one launch (start us, length us, event | category | flops | bytes accessed | tf_op | source)
XLA Modules:
  0.0 101.6 jit_solution(8671758075029073833)
XLA Ops:
  0.7 1.2 %constant_dynamic-slice_fusion = (bf16[128,256]{1,0:T(8,128)(2,1)S(1)}, bf16[128,256]{1,0:T(8,128)(2,1)S(1)}, bf16[128,256]{1,0:T(8,128)(2,1)S(1)}, bf16[128,256...) fusion(bf16[128,1024]{1,0:T(8,128)(2,1)} %param.10, ...), kind=kLoop, calls=%fused_computation.22 | loop fusion | bytes 1048592 | tf_op jit(solution)/shard_map/dynamic_slice | solution.py:363
  1.9 0.5 collective-permute-start.1
  2.4 1.1 %constant_dynamic-slice_fusion.8 = (bf16[128,2048]{1,0:T(8,128)(2,1)S(1)}, bf16[128,2048]{1,0:T(8,128)(2,1)S(1)}) fusion(bf16[128,4096]{1,0:T(8,128)(2,1)} %g_hbm.3, s32[]{:T(128)S(6)} %select_n.88, bf16[128,4096]{1,0:T(8,128)(2,1)S(1)} %copy-done), kind=kLoop, calls=%fused_computation.30 | loop fusion | bytes 2097156 | tf_op jit(solution)/shard_map/dynamic_slice | solution.py:363
  3.6 0.2 collective-permute-start
  3.9 1.3 %collective-permute-start.4 = (bf16[256,512]{1,0:T(8,128)(2,1)S(1)}, bf16[256,512]{1,0:T(8,128)(2,1)}, u32[]{:S(2)}, u32[]{:S(2)}) collective-permute-start(bf16[256,512]{1,0:T(8,128)(2,1)S(1)} %pad_maximum_fusion.3.refs_0_), channel_id=1, source_target_pairs={{2,0},{3,1},{4,2},{5,3},{6,4},{7,5},{10,8},{11,9},{12,10},{13,11},... | collective-permute-start | bytes 786440 | tf_op jit(solution)/shard_map/ppermute | solution.py:327
  5.2 6.2 %collective-permute-start.2 = (bf16[256,512]{1,0:T(8,128)(2,1)S(1)}, bf16[256,512]{1,0:T(8,128)(2,1)}, u32[]{:S(2)}, u32[]{:S(2)}) collective-permute-start(bf16[256,512]{1,0:T(8,128)(2,1)S(1)} %pad_maximum_fusion.3.refs_0_), channel_id=1, source_target_pairs={{0,2},{1,3},{2,4},{3,5},{4,6},{5,7},{8,10},{9,11},{10,12},{11,13},... | collective-permute-start | bytes 786440 | tf_op jit(solution)/shard_map/ppermute | solution.py:327
  11.4 1.3 %collective-permute-start.9 = (bf16[256,512]{1,0:T(8,128)(2,1)S(1)}, bf16[256,512]{1,0:T(8,128)(2,1)S(1)}, u32[]{:S(2)}, u32[]{:S(2)}) collective-permute-start(bf16[256,512]{1,0:T(8,128)(2,1)S(1)} %pad_maximum_fusion.4.refs_0_), channel_id=1, source_target_pairs={{2,0},{3,1},{4,2},{5,3},{6,4},{7,5},{10,8},{11,9},{12,10},{13,11},... | collective-permute-start | bytes 786440 | tf_op jit(solution)/shard_map/ppermute | solution.py:327
  12.7 4.6 %collective-permute-start.7 = (bf16[256,512]{1,0:T(8,128)(2,1)S(1)}, bf16[256,512]{1,0:T(8,128)(2,1)S(1)}, u32[]{:S(2)}, u32[]{:S(2)}) collective-permute-start(bf16[256,512]{1,0:T(8,128)(2,1)S(1)} %pad_maximum_fusion.4.refs_0_), channel_id=1, source_target_pairs={{0,2},{1,3},{2,4},{3,5},{4,6},{5,7},{8,10},{9,11},{10,12},{11,13},... | collective-permute-start | bytes 786440 | tf_op jit(solution)/shard_map/ppermute | solution.py:327
  17.3 1.3 %collective-permute-start.5 = (bf16[256,512]{1,0:T(8,128)(2,1)}, bf16[256,512]{1,0:T(8,128)(2,1)}, u32[]{:S(2)}, u32[]{:S(2)}) collective-permute-start(bf16[256,512]{1,0:T(8,128)(2,1)} %collective-permute-done.4.refs_3_), channel_id=1, source_target_pairs={{2,0},{3,1},{4,2},{5,3},{10,8},{11,9},{12,10},{13,11},{18,16},{19,... | collective-permute-start | bytes 786440 | tf_op jit(solution)/shard_map/ppermute | solution.py:327
  18.6 1.4 %collective-permute-start.3 = (bf16[256,512]{1,0:T(8,128)(2,1)}, bf16[256,512]{1,0:T(8,128)(2,1)}, u32[]{:S(2)}, u32[]{:S(2)}) collective-permute-start(bf16[256,512]{1,0:T(8,128)(2,1)} %collective-permute-done.2.refs_1_), channel_id=1, source_target_pairs={{2,4},{3,5},{4,6},{5,7},{10,12},{11,13},{12,14},{13,15},{18,20},{1... | collective-permute-start | bytes 786440 | tf_op jit(solution)/shard_map/ppermute | solution.py:327
  20.0 1.4 %collective-permute-done.9.refs_3_ = bf16[256,512]{1,0:T(8,128)(2,1)S(1)} collective-permute-done((bf16[256,512]{1,0:T(8,128)(2,1)S(1)}, bf16[256,512]{1,0:T(8,128)(2,1)S(1)}, u32[]{:S(2)}, u32[]{:S(2)}) %collective-permute-start.9) | collective-permute-done | bytes 262176 | tf_op jit(solution)/shard_map/ppermute | solution.py:327
  21.4 1.3 %collective-permute-start.10 = (bf16[256,512]{1,0:T(8,128)(2,1)S(1)}, bf16[256,512]{1,0:T(8,128)(2,1)S(1)}, u32[]{:S(2)}, u32[]{:S(2)}) collective-permute-start(bf16[256,512]{1,0:T(8,128)(2,1)S(1)} %collective-permute-done.9.refs_3_), channel_id=1, source_target_pairs={{2,0},{3,1},{4,2},{5,3},{10,8},{11,9},{12,10},{13,11},{18,16},{19,... | collective-permute-start | bytes 786440 | tf_op jit(solution)/shard_map/ppermute | solution.py:327
  22.7 0.7 collective-permute-start.8
  23.4 3.7 %collective-permute-done.5.refs_4_ = bf16[256,512]{1,0:T(8,128)(2,1)} collective-permute-done((bf16[256,512]{1,0:T(8,128)(2,1)}, bf16[256,512]{1,0:T(8,128)(2,1)}, u32[]{:S(2)}, u32[]{:S(2)}) %collective-permute-start.5) | collective-permute-done | bytes 262176 | tf_op jit(solution)/shard_map/ppermute | solution.py:327
  27.1 1.2 %broadcast_select_fusion.1 = bf16[256,512]{1,0:T(8,128)(2,1)S(1)} fusion(bf16[256,512]{1,0:T(8,128)(2,1)} %collective-permute-done.3.refs_2_, bf16[256,512]{1,0:T(8,128)(2,1)} %collective-permute-done.5.refs_4_, pred[]{:T(512)S(6)} %ge.4), kind=kLoop, calls=%fused_computation.18 | loop fusion | flops 131072 | bytes 786433 | tf_op jit(solution)/shard_map/jit(_where)/select_n | solution.py:416
  28.3 1.3 %collective-permute-start.6 = (bf16[256,512]{1,0:T(8,128)(2,1)S(1)}, bf16[256,512]{1,0:T(8,128)(2,1)S(1)}, u32[]{:S(2)}, u32[]{:S(2)}) collective-permute-start(bf16[256,512]{1,0:T(8,128)(2,1)S(1)} %broadcast_select_fusion.1), channel_id=1, source_target_pairs={{4,6},{5,7},{2,0},{3,1},{12,14},{13,15},{10,8},{11,9},{20,22},{21,... | collective-permute-start | bytes 786440 | tf_op jit(solution)/shard_map/ppermute | solution.py:327
  29.6 3.6 %collective-permute-done.10.refs_4_ = bf16[256,512]{1,0:T(8,128)(2,1)S(1)} collective-permute-done((bf16[256,512]{1,0:T(8,128)(2,1)S(1)}, bf16[256,512]{1,0:T(8,128)(2,1)S(1)}, u32[]{:S(2)}, u32[]{:S(2)}) %collective-permute-start.10) | collective-permute-done | bytes 262176 | tf_op jit(solution)/shard_map/ppermute | solution.py:327
  33.3 1.3 %collective-permute-start.11 = (bf16[256,512]{1,0:T(8,128)(2,1)S(1)}, bf16[256,512]{1,0:T(8,128)(2,1)S(1)}, u32[]{:S(2)}, u32[]{:S(2)}) collective-permute-start(bf16[256,512]{1,0:T(8,128)(2,1)S(1)} %broadcast_select_fusion), channel_id=1, source_target_pairs={{4,6},{5,7},{2,0},{3,1},{12,14},{13,15},{10,8},{11,9},{20,22},{21,... | collective-permute-start | bytes 786440 | tf_op jit(solution)/shard_map/ppermute | solution.py:327
  34.6 7.2 %collective-permute-done.6.refs_5_ = bf16[256,512]{1,0:T(8,128)(2,1)S(1)} collective-permute-done((bf16[256,512]{1,0:T(8,128)(2,1)S(1)}, bf16[256,512]{1,0:T(8,128)(2,1)S(1)}, u32[]{:S(2)}, u32[]{:S(2)}) %collective-permute-start.6) | collective-permute-done | bytes 262176 | tf_op jit(solution)/shard_map/ppermute | solution.py:327
  41.8 0.7 copy-done.22
  42.5 6.8 %shard_map.119 = (bf16[128,1024]{1,0:T(8,128)(2,1)}, bf16[128,1024]{1,0:T(8,128)(2,1)}, bf16[128,2048]{1,0:T(8,128)(2,1)}, bf16[256,512]{1,0:T(8,128)(2,1)}, bf1...) custom-call(f32[32]{0:T(128)} %sink_hbm.3, ...), custom_call_target="tpu_custom_call" | custom-call | flops 1610612736 | bytes 8388608 | tf_op jit(solution)/shard_map/pallas_call | solution.py:298
  49.4 1.6 %collective-permute-start.13 = (bf16[256,512]{1,0:T(8,128)(2,1)}, bf16[256,512]{1,0:T(8,128)(2,1)S(1)}, u32[]{:S(2)}, u32[]{:S(2)}) collective-permute-start(bf16[256,512]{1,0:T(8,128)(2,1)} %get-tuple-element.45), channel_id=1, source_target_pairs={{0,2},{1,3},{6,4},{7,5},{8,10},{9,11},{14,12},{15,13},{16,18},{17,... | collective-permute-start | bytes 786440 | tf_op jit(solution)/shard_map/ppermute | solution.py:327
  51.0 0.7 copy-done.19
  51.7 7.6 %shard_map.120 = (bf16[128,1024]{1,0:T(8,128)(2,1)}, bf16[128,1024]{1,0:T(8,128)(2,1)}, bf16[128,2048]{1,0:T(8,128)(2,1)}, bf16[288,512]{1,0:T(8,128)(2,1)}, bf1...) custom-call(f32[32]{0:T(128)} %sink_hbm.3, ...), custom_call_target="tpu_custom_call" | custom-call | bytes 1024 | tf_op jit(solution)/shard_map/pallas_call | solution.py:298
  59.4 1.6 %collective-permute-start.18 = (bf16[288,512]{1,0:T(8,128)(2,1)}, bf16[288,512]{1,0:T(8,128)(2,1)S(1)}, u32[]{:S(2)}, u32[]{:S(2)}) collective-permute-start(bf16[288,512]{1,0:T(8,128)(2,1)} %get-tuple-element.49), channel_id=1, source_target_pairs={{0,2},{1,3},{6,4},{7,5},{8,10},{9,11},{14,12},{15,13},{16,18},{17,... | collective-permute-start | bytes 884744 | tf_op jit(solution)/shard_map/ppermute | solution.py:327
  61.0 0.7 collective-permute-start.16
  61.7 1.2 %pad_maximum_fusion.1 = bf16[128,4096]{1,0:T(8,128)(2,1)S(1)} fusion(bf16[128,2048]{1,0:T(8,128)(2,1)} %get-tuple-element.40, bf16[128,2048]{1,0:T(8,128)(2,1)S(1)} %copy-done.5), kind=kLoop, calls=%fused_computation.1 | loop fusion | flops 2097152 | bytes 2097152 | tf_op jit(solution)/shard_map/concatenate | solution.py:450
  63.0 1.9 %collective-permute-start.14 = (bf16[256,512]{1,0:T(8,128)(2,1)S(1)}, bf16[256,512]{1,0:T(8,128)(2,1)S(1)}, u32[]{:S(2)}, u32[]{:S(2)}) collective-permute-start(bf16[256,512]{1,0:T(8,128)(2,1)S(1)} %add_convert_fusion.7), channel_id=1, source_target_pairs={{0,2},{1,3},{2,4},{3,5},{8,10},{9,11},{10,12},{11,13},{16,18},{17,... | collective-permute-start | bytes 786440 | tf_op jit(solution)/shard_map/ppermute | solution.py:327
  64.9 0.5 collective-permute-done.18
  65.5 0.7 collective-permute-start.21
  66.2 7.4 %collective-permute-start.19 = (bf16[288,512]{1,0:T(8,128)(2,1)S(1)}, bf16[288,512]{1,0:T(8,128)(2,1)S(1)}, u32[]{:S(2)}, u32[]{:S(2)}) collective-permute-start(bf16[288,512]{1,0:T(8,128)(2,1)S(1)} %add_convert_fusion.3), channel_id=1, source_target_pairs={{0,2},{1,3},{2,4},{3,5},{8,10},{9,11},{10,12},{11,13},{16,18},{17,... | collective-permute-start | bytes 884744 | tf_op jit(solution)/shard_map/ppermute | solution.py:327
  73.8 1.3 %collective-permute-start.17 = (bf16[256,512]{1,0:T(8,128)(2,1)S(1)}, bf16[256,512]{1,0:T(8,128)(2,1)S(1)}, u32[]{:S(2)}, u32[]{:S(2)}) collective-permute-start(bf16[256,512]{1,0:T(8,128)(2,1)S(1)} %add_convert_fusion.5), channel_id=1, source_target_pairs={{2,0},{3,1},{4,2},{5,3},{6,4},{7,5},{10,8},{11,9},{12,10},{13,11},... | collective-permute-start | bytes 786440 | tf_op jit(solution)/shard_map/ppermute | solution.py:327
  75.2 6.5 %collective-permute-start.15 = (bf16[256,512]{1,0:T(8,128)(2,1)S(1)}, bf16[256,512]{1,0:T(8,128)(2,1)S(1)}, u32[]{:S(2)}, u32[]{:S(2)}) collective-permute-start(bf16[256,512]{1,0:T(8,128)(2,1)S(1)} %add_convert_fusion.6), channel_id=1, source_target_pairs={{0,2},{1,3},{2,4},{3,5},{4,6},{5,7},{8,10},{9,11},{10,12},{11,13},... | collective-permute-start | bytes 786440 | tf_op jit(solution)/shard_map/ppermute | solution.py:327
  81.8 1.3 %collective-permute-start.22 = (bf16[288,512]{1,0:T(8,128)(2,1)S(1)}, bf16[288,512]{1,0:T(8,128)(2,1)S(1)}, u32[]{:S(2)}, u32[]{:S(2)}) collective-permute-start(bf16[288,512]{1,0:T(8,128)(2,1)S(1)} %add_convert_fusion.1), channel_id=1, source_target_pairs={{2,0},{3,1},{4,2},{5,3},{6,4},{7,5},{10,8},{11,9},{12,10},{13,11},... | collective-permute-start | bytes 884744 | tf_op jit(solution)/shard_map/ppermute | solution.py:327
  83.2 4.7 %collective-permute-start.20 = (bf16[288,512]{1,0:T(8,128)(2,1)S(1)}, bf16[288,512]{1,0:T(8,128)(2,1)S(1)}, u32[]{:S(2)}, u32[]{:S(2)}) collective-permute-start(bf16[288,512]{1,0:T(8,128)(2,1)S(1)} %add_convert_fusion.2), channel_id=1, source_target_pairs={{0,2},{1,3},{2,4},{3,5},{4,6},{5,7},{8,10},{9,11},{10,12},{11,13},... | collective-permute-start | bytes 884744 | tf_op jit(solution)/shard_map/ppermute | solution.py:327
  88.1 1.2 %maximum_select_fusion.1 = bf16[128,4096]{1,0:T(8,128)(2,1)} fusion(bf16[128,1024]{1,0:T(8,128)(2,1)S(1)} %get-tuple-element.60, bf16[128,1024]{1,0:T(8,128)(2,1)S(1)} %get-tuple-element.59, bf16[128,1024]{1,0:T(8,128)(2,1)S(1)} %copy-done.15, bf16[128,1024]{1,0:T(8,128)(2,1)S(1)} %copy-done.11, pred[]{:T(512)S(6)} %eq.16), kind=kLoop, calls=%fused_computation.3 | loop fusion | flops 8912896 | bytes 2097153 | tf_op jit(solution)/shard_map/jit(_where)/select_n | solution.py:456
  89.3 1.2 %maximum_select_fusion = bf16[128,4096]{1,0:T(8,128)(2,1)} fusion(bf16[128,1024]{1,0:T(8,128)(2,1)S(1)} %get-tuple-element.61, bf16[128,1024]{1,0:T(8,128)(2,1)S(1)} %get-tuple-element.62, bf16[128,1024]{1,0:T(8,128)(2,1)S(1)} %copy-done.14, bf16[128,1024]{1,0:T(8,128)(2,1)S(1)} %copy-done.10, pred[]{:T(512)S(6)} %eq.16), kind=kLoop, calls=%fused_computation.2 | loop fusion | flops 8912896 | bytes 2097153 | tf_op jit(solution)/shard_map/jit(_where)/select_n | solution.py:456
  90.5 0.2 collective-permute-done.22
  90.8 1.5 %collective-permute-done.20 = bf16[288,512]{1,0:T(8,128)(2,1)S(1)} collective-permute-done((bf16[288,512]{1,0:T(8,128)(2,1)S(1)}, bf16[288,512]{1,0:T(8,128)(2,1)S(1)}, u32[]{:S(2)}, u32[]{:S(2)}) %collective-permute-start.20) | collective-permute-done | bytes 294944 | tf_op jit(solution)/shard_map/ppermute | solution.py:327
  92.8 0.5 collective-permute-start.24
  93.4 0.8 collective-permute-done.23
  94.2 0.2 collective-permute-done.24
  94.8 2.5 %collective-permute-start.27 = (f32[8,128]{1,0:T(8,128)S(1)}, f32[8,128]{1,0:T(8,128)S(1)}, u32[]{:S(2)}, u32[]{:S(2)}) collective-permute-start(f32[8,128]{1,0:T(8,128)S(1)} %broadcast_select_fusion.2), channel_id=1, source_target_pairs={{0,24},{8,16},{16,8},{24,0},{1,25},{9,17},{17,9},{25,1},{2,26},{10... | collective-permute-start | bytes 12296 | tf_op jit(solution)/shard_map/ppermute | solution.py:488
  97.4 0.9 collective-permute-start.25
  98.3 0.8 maximum_select_fusion.3
  99.1 0.8 maximum_select_fusion.2
  99.9 1.1 %collective-permute-done.25 = f32[8,128]{1,0:T(8,128)S(1)} collective-permute-done((f32[8,128]{1,0:T(8,128)S(1)}, f32[8,128]{1,0:T(8,128)S(1)}, u32[]{:S(2)}, u32[]{:S(2)}) %collective-permute-start.25) | collective-permute-done | bytes 4128 | tf_op jit(solution)/shard_map/ppermute | solution.py:488
  101.0 0.6 add_reduce_fusion
  (100 shorter events, 1.9 us)
Async XLA Ops:
  0.6 1.8 %copy-start = (bf16[128,4096]{1,0:T(8,128)(2,1)S(1)}, bf16[128,4096]{1,0:T(8,128)(2,1)}, u32[]{:S(2)}) copy-start(bf16[128,4096]{1,0:T(8,128)(2,1)} %q_hbm.3) | copy-start | bytes 3145732
  1.9 1.9 %collective-permute-start.1 = (bf16[128,1024]{1,0:T(8,128)(2,1)S(1)}, bf16[128,1024]{1,0:T(8,128)(2,1)S(1)}, u32[]{:S(2)}, u32[]{:S(2)}) collective-permute-start(bf16[128,1024]{1,0:T(8,128)(2,1)S(1)} %pad_maximum_fusion.2), channel_id=1, source_target_pairs={{0,1},{1,0},{2,3},{3,2},{4,5},{5,4},{6,7},{7,6},{8,9},{9,8},{10,11... | collective-permute-start | bytes 786440 | tf_op jit(solution)/shard_map/ppermute | solution.py:327
  3.6 23.5 %collective-permute-start = (bf16[128,4096]{1,0:T(8,128)(2,1)S(1)}, bf16[128,4096]{1,0:T(8,128)(2,1)S(1)}, u32[]{:S(2)}, u32[]{:S(2)}) collective-permute-start(bf16[128,4096]{1,0:T(8,128)(2,1)S(1)} %pad_maximum_fusion), channel_id=1, source_target_pairs={{0,1},{1,0},{2,3},{3,2},{4,5},{5,4},{6,7},{7,6},{8,9},{9,8},{10,11... | collective-permute-start | bytes 3145736 | tf_op jit(solution)/shard_map/ppermute | solution.py:327
  3.9 18.8 %copy-start.20 = (bf16[256,512]{1,0:T(8,128)(2,1)}, bf16[256,512]{1,0:T(8,128)(2,1)S(1)}, u32[]{:S(2)}) copy-start(bf16[256,512]{1,0:T(8,128)(2,1)S(1)} %pad_maximum_fusion.3.refs_0_) | copy-start | bytes 786436
  3.9 13.4 %collective-permute-start.4 = (bf16[256,512]{1,0:T(8,128)(2,1)S(1)}, bf16[256,512]{1,0:T(8,128)(2,1)}, u32[]{:S(2)}, u32[]{:S(2)}) collective-permute-start(bf16[256,512]{1,0:T(8,128)(2,1)S(1)} %pad_maximum_fusion.3.refs_0_), channel_id=1, source_target_pairs={{2,0},{3,1},{4,2},{5,3},{6,4},{7,5},{10,8},{11,9},{12,10},{13,11},... | collective-permute-start | bytes 786440 | tf_op jit(solution)/shard_map/ppermute | solution.py:327
  5.2 13.4 %collective-permute-start.2 = (bf16[256,512]{1,0:T(8,128)(2,1)S(1)}, bf16[256,512]{1,0:T(8,128)(2,1)}, u32[]{:S(2)}, u32[]{:S(2)}) collective-permute-start(bf16[256,512]{1,0:T(8,128)(2,1)S(1)} %pad_maximum_fusion.3.refs_0_), channel_id=1, source_target_pairs={{0,2},{1,3},{2,4},{3,5},{4,6},{5,7},{8,10},{9,11},{10,12},{11,13},... | collective-permute-start | bytes 786440 | tf_op jit(solution)/shard_map/ppermute | solution.py:327
  11.4 37.9 %copy-start.1 = (bf16[256,512]{1,0:T(8,128)(2,1)}, bf16[256,512]{1,0:T(8,128)(2,1)S(1)}, u32[]{:S(2)}) copy-start(bf16[256,512]{1,0:T(8,128)(2,1)S(1)} %pad_maximum_fusion.4.refs_0_) | copy-start | bytes 786436
  11.4 10.0 %collective-permute-start.9 = (bf16[256,512]{1,0:T(8,128)(2,1)S(1)}, bf16[256,512]{1,0:T(8,128)(2,1)S(1)}, u32[]{:S(2)}, u32[]{:S(2)}) collective-permute-start(bf16[256,512]{1,0:T(8,128)(2,1)S(1)} %pad_maximum_fusion.4.refs_0_), channel_id=1, source_target_pairs={{2,0},{3,1},{4,2},{5,3},{6,4},{7,5},{10,8},{11,9},{12,10},{13,11},... | collective-permute-start | bytes 786440 | tf_op jit(solution)/shard_map/ppermute | solution.py:327
  12.7 10.0 %collective-permute-start.7 = (bf16[256,512]{1,0:T(8,128)(2,1)S(1)}, bf16[256,512]{1,0:T(8,128)(2,1)S(1)}, u32[]{:S(2)}, u32[]{:S(2)}) collective-permute-start(bf16[256,512]{1,0:T(8,128)(2,1)S(1)} %pad_maximum_fusion.4.refs_0_), channel_id=1, source_target_pairs={{0,2},{1,3},{2,4},{3,5},{4,6},{5,7},{8,10},{9,11},{10,12},{11,13},... | collective-permute-start | bytes 786440 | tf_op jit(solution)/shard_map/ppermute | solution.py:327
  17.3 9.8 %collective-permute-start.5 = (bf16[256,512]{1,0:T(8,128)(2,1)}, bf16[256,512]{1,0:T(8,128)(2,1)}, u32[]{:S(2)}, u32[]{:S(2)}) collective-permute-start(bf16[256,512]{1,0:T(8,128)(2,1)} %collective-permute-done.4.refs_3_), channel_id=1, source_target_pairs={{2,0},{3,1},{4,2},{5,3},{10,8},{11,9},{12,10},{13,11},{18,16},{19,... | collective-permute-start | bytes 786440 | tf_op jit(solution)/shard_map/ppermute | solution.py:327
  18.6 8.5 %collective-permute-start.3 = (bf16[256,512]{1,0:T(8,128)(2,1)}, bf16[256,512]{1,0:T(8,128)(2,1)}, u32[]{:S(2)}, u32[]{:S(2)}) collective-permute-start(bf16[256,512]{1,0:T(8,128)(2,1)} %collective-permute-done.2.refs_1_), channel_id=1, source_target_pairs={{2,4},{3,5},{4,6},{5,7},{10,12},{11,13},{12,14},{13,15},{18,20},{1... | collective-permute-start | bytes 786440 | tf_op jit(solution)/shard_map/ppermute | solution.py:327
  21.4 27.9 %copy-start.12 = (bf16[256,512]{1,0:T(8,128)(2,1)}, bf16[256,512]{1,0:T(8,128)(2,1)S(1)}, u32[]{:S(2)}) copy-start(bf16[256,512]{1,0:T(8,128)(2,1)S(1)} %collective-permute-done.9.refs_3_) | copy-start | bytes 786436
  21.4 11.8 %collective-permute-start.10 = (bf16[256,512]{1,0:T(8,128)(2,1)S(1)}, bf16[256,512]{1,0:T(8,128)(2,1)S(1)}, u32[]{:S(2)}, u32[]{:S(2)}) collective-permute-start(bf16[256,512]{1,0:T(8,128)(2,1)S(1)} %collective-permute-done.9.refs_3_), channel_id=1, source_target_pairs={{2,0},{3,1},{4,2},{5,3},{10,8},{11,9},{12,10},{13,11},{18,16},{19,... | collective-permute-start | bytes 786440 | tf_op jit(solution)/shard_map/ppermute | solution.py:327
  22.7 26.6 %copy-start.13 = (bf16[256,512]{1,0:T(8,128)(2,1)}, bf16[256,512]{1,0:T(8,128)(2,1)S(1)}, u32[]{:S(2)}) copy-start(bf16[256,512]{1,0:T(8,128)(2,1)S(1)} %collective-permute-done.7.refs_1_) | copy-start | bytes 786436
  22.7 10.5 %collective-permute-start.8 = (bf16[256,512]{1,0:T(8,128)(2,1)S(1)}, bf16[256,512]{1,0:T(8,128)(2,1)S(1)}, u32[]{:S(2)}, u32[]{:S(2)}) collective-permute-start(bf16[256,512]{1,0:T(8,128)(2,1)S(1)} %collective-permute-done.7.refs_1_), channel_id=1, source_target_pairs={{2,4},{3,5},{4,6},{5,7},{10,12},{11,13},{12,14},{13,15},{18,20},{1... | collective-permute-start | bytes 786440 | tf_op jit(solution)/shard_map/ppermute | solution.py:327
  27.1 14.7 %copy-start.4 = (bf16[128,4096]{1,0:T(8,128)(2,1)}, bf16[128,4096]{1,0:T(8,128)(2,1)S(1)}, u32[]{:S(2)}) copy-start(bf16[128,4096]{1,0:T(8,128)(2,1)S(1)} %collective-permute-done.partner_hbm) | copy-start | bytes 3145732
  28.3 13.5 %collective-permute-start.6 = (bf16[256,512]{1,0:T(8,128)(2,1)S(1)}, bf16[256,512]{1,0:T(8,128)(2,1)S(1)}, u32[]{:S(2)}, u32[]{:S(2)}) collective-permute-start(bf16[256,512]{1,0:T(8,128)(2,1)S(1)} %broadcast_select_fusion.1), channel_id=1, source_target_pairs={{4,6},{5,7},{2,0},{3,1},{12,14},{13,15},{10,8},{11,9},{20,22},{21,... | collective-permute-start | bytes 786440 | tf_op jit(solution)/shard_map/ppermute | solution.py:327
  33.3 16.1 %copy-start.2 = (bf16[256,512]{1,0:T(8,128)(2,1)}, bf16[256,512]{1,0:T(8,128)(2,1)S(1)}, u32[]{:S(2)}) copy-start(bf16[256,512]{1,0:T(8,128)(2,1)S(1)} %collective-permute-done.10.refs_4_) | copy-start | bytes 786436
  33.3 16.1 %copy-start.3 = (bf16[256,512]{1,0:T(8,128)(2,1)}, bf16[256,512]{1,0:T(8,128)(2,1)S(1)}, u32[]{:S(2)}) copy-start(bf16[256,512]{1,0:T(8,128)(2,1)S(1)} %collective-permute-done.8.refs_2_) | copy-start | bytes 786436
  33.3 17.7 %collective-permute-start.11 = (bf16[256,512]{1,0:T(8,128)(2,1)S(1)}, bf16[256,512]{1,0:T(8,128)(2,1)S(1)}, u32[]{:S(2)}, u32[]{:S(2)}) collective-permute-start(bf16[256,512]{1,0:T(8,128)(2,1)S(1)} %broadcast_select_fusion), channel_id=1, source_target_pairs={{4,6},{5,7},{2,0},{3,1},{12,14},{13,15},{10,8},{11,9},{20,22},{21,... | collective-permute-start | bytes 786440 | tf_op jit(solution)/shard_map/ppermute | solution.py:327
  49.4 11.5 %collective-permute-start.13 = (bf16[256,512]{1,0:T(8,128)(2,1)}, bf16[256,512]{1,0:T(8,128)(2,1)S(1)}, u32[]{:S(2)}, u32[]{:S(2)}) collective-permute-start(bf16[256,512]{1,0:T(8,128)(2,1)} %get-tuple-element.45), channel_id=1, source_target_pairs={{0,2},{1,3},{6,4},{7,5},{8,10},{9,11},{14,12},{15,13},{16,18},{17,... | collective-permute-start | bytes 786440 | tf_op jit(solution)/shard_map/ppermute | solution.py:327
  51.7 9.2 %copy-start.18 = (bf16[256,512]{1,0:T(8,128)(2,1)S(1)}, bf16[256,512]{1,0:T(8,128)(2,1)}, u32[]{:S(2)}) copy-start(bf16[256,512]{1,0:T(8,128)(2,1)} %get-tuple-element.44) | copy-start | bytes 786436
  59.3 2.4 %copy-start.5 = (bf16[128,2048]{1,0:T(8,128)(2,1)S(1)}, bf16[128,2048]{1,0:T(8,128)(2,1)}, u32[]{:S(2)}) copy-start(bf16[128,2048]{1,0:T(8,128)(2,1)} %get-tuple-element.39) | copy-start | bytes 1572868
  59.4 6.1 %collective-permute-start.18 = (bf16[288,512]{1,0:T(8,128)(2,1)}, bf16[288,512]{1,0:T(8,128)(2,1)S(1)}, u32[]{:S(2)}, u32[]{:S(2)}) collective-permute-start(bf16[288,512]{1,0:T(8,128)(2,1)} %get-tuple-element.49), channel_id=1, source_target_pairs={{0,2},{1,3},{6,4},{7,5},{8,10},{9,11},{14,12},{15,13},{16,18},{17,... | collective-permute-start | bytes 884744 | tf_op jit(solution)/shard_map/ppermute | solution.py:327
  61.0 12.7 %collective-permute-start.16 = (bf16[256,512]{1,0:T(8,128)(2,1)S(1)}, bf16[256,512]{1,0:T(8,128)(2,1)S(1)}, u32[]{:S(2)}, u32[]{:S(2)}) collective-permute-start(bf16[256,512]{1,0:T(8,128)(2,1)S(1)} %add_convert_fusion.7), channel_id=1, source_target_pairs={{4,2},{5,3},{6,4},{7,5},{12,10},{13,11},{14,12},{15,13},{20,18},{2... | collective-permute-start | bytes 786440 | tf_op jit(solution)/shard_map/ppermute | solution.py:327
  61.7 3.7 %copy-start.8 = (bf16[288,512]{1,0:T(8,128)(2,1)S(1)}, bf16[288,512]{1,0:T(8,128)(2,1)}, u32[]{:S(2)}) copy-start(bf16[288,512]{1,0:T(8,128)(2,1)} %get-tuple-element.48) | copy-start | bytes 884740
  61.7 12.0 %copy-start.17 = (bf16[256,512]{1,0:T(8,128)(2,1)S(1)}, bf16[256,512]{1,0:T(8,128)(2,1)}, u32[]{:S(2)}) copy-start(bf16[256,512]{1,0:T(8,128)(2,1)} %get-tuple-element.46) | copy-start | bytes 786436
  62.9 12.2 %copy-start.16 = (bf16[256,512]{1,0:T(8,128)(2,1)S(1)}, bf16[256,512]{1,0:T(8,128)(2,1)}, u32[]{:S(2)}) copy-start(bf16[256,512]{1,0:T(8,128)(2,1)} %get-tuple-element.43) | copy-start | bytes 786436
  62.9 25.0 %collective-permute-start.12 = (bf16[128,4096]{1,0:T(8,128)(2,1)S(1)}, bf16[128,4096]{1,0:T(8,128)(2,1)S(1)}, u32[]{:S(2)}, u32[]{:S(2)}) collective-permute-start(bf16[128,4096]{1,0:T(8,128)(2,1)S(1)} %pad_maximum_fusion.1), channel_id=1, source_target_pairs={{0,1},{1,0},{2,3},{3,2},{4,5},{5,4},{6,7},{7,6},{8,9},{9,8},{10,11... | collective-permute-start | bytes 3145736 | tf_op jit(solution)/shard_map/ppermute | solution.py:327
  63.0 12.1 %collective-permute-start.14 = (bf16[256,512]{1,0:T(8,128)(2,1)S(1)}, bf16[256,512]{1,0:T(8,128)(2,1)S(1)}, u32[]{:S(2)}, u32[]{:S(2)}) collective-permute-start(bf16[256,512]{1,0:T(8,128)(2,1)S(1)} %add_convert_fusion.7), channel_id=1, source_target_pairs={{0,2},{1,3},{2,4},{3,5},{8,10},{9,11},{10,12},{11,13},{16,18},{17,... | collective-permute-start | bytes 786440 | tf_op jit(solution)/shard_map/ppermute | solution.py:327
  65.5 16.3 %copy-start.7 = (bf16[288,512]{1,0:T(8,128)(2,1)S(1)}, bf16[288,512]{1,0:T(8,128)(2,1)}, u32[]{:S(2)}) copy-start(bf16[288,512]{1,0:T(8,128)(2,1)} %get-tuple-element.50) | copy-start | bytes 884740
  65.5 16.2 %collective-permute-start.21 = (bf16[288,512]{1,0:T(8,128)(2,1)S(1)}, bf16[288,512]{1,0:T(8,128)(2,1)S(1)}, u32[]{:S(2)}, u32[]{:S(2)}) collective-permute-start(bf16[288,512]{1,0:T(8,128)(2,1)S(1)} %add_convert_fusion.3), channel_id=1, source_target_pairs={{4,2},{5,3},{6,4},{7,5},{12,10},{13,11},{14,12},{15,13},{20,18},{2... | collective-permute-start | bytes 884744 | tf_op jit(solution)/shard_map/ppermute | solution.py:327
  66.2 16.9 %collective-permute-start.19 = (bf16[288,512]{1,0:T(8,128)(2,1)S(1)}, bf16[288,512]{1,0:T(8,128)(2,1)S(1)}, u32[]{:S(2)}, u32[]{:S(2)}) collective-permute-start(bf16[288,512]{1,0:T(8,128)(2,1)S(1)} %add_convert_fusion.3), channel_id=1, source_target_pairs={{0,2},{1,3},{2,4},{3,5},{8,10},{9,11},{10,12},{11,13},{16,18},{17,... | collective-permute-start | bytes 884744 | tf_op jit(solution)/shard_map/ppermute | solution.py:327
  73.7 9.4 %copy-start.6 = (bf16[288,512]{1,0:T(8,128)(2,1)S(1)}, bf16[288,512]{1,0:T(8,128)(2,1)}, u32[]{:S(2)}) copy-start(bf16[288,512]{1,0:T(8,128)(2,1)} %get-tuple-element.47) | copy-start | bytes 884740
  73.8 16.7 %collective-permute-start.17 = (bf16[256,512]{1,0:T(8,128)(2,1)S(1)}, bf16[256,512]{1,0:T(8,128)(2,1)S(1)}, u32[]{:S(2)}, u32[]{:S(2)}) collective-permute-start(bf16[256,512]{1,0:T(8,128)(2,1)S(1)} %add_convert_fusion.5), channel_id=1, source_target_pairs={{2,0},{3,1},{4,2},{5,3},{6,4},{7,5},{10,8},{11,9},{12,10},{13,11},... | collective-permute-start | bytes 786440 | tf_op jit(solution)/shard_map/ppermute | solution.py:327
  75.2 15.3 %collective-permute-start.15 = (bf16[256,512]{1,0:T(8,128)(2,1)S(1)}, bf16[256,512]{1,0:T(8,128)(2,1)S(1)}, u32[]{:S(2)}, u32[]{:S(2)}) collective-permute-start(bf16[256,512]{1,0:T(8,128)(2,1)S(1)} %add_convert_fusion.6), channel_id=1, source_target_pairs={{0,2},{1,3},{2,4},{3,5},{4,6},{5,7},{8,10},{9,11},{10,12},{11,13},... | collective-permute-start | bytes 786440 | tf_op jit(solution)/shard_map/ppermute | solution.py:327
  81.8 8.9 %collective-permute-start.22 = (bf16[288,512]{1,0:T(8,128)(2,1)S(1)}, bf16[288,512]{1,0:T(8,128)(2,1)S(1)}, u32[]{:S(2)}, u32[]{:S(2)}) collective-permute-start(bf16[288,512]{1,0:T(8,128)(2,1)S(1)} %add_convert_fusion.1), channel_id=1, source_target_pairs={{2,0},{3,1},{4,2},{5,3},{6,4},{7,5},{10,8},{11,9},{12,10},{13,11},... | collective-permute-start | bytes 884744 | tf_op jit(solution)/shard_map/ppermute | solution.py:327
  83.2 4.8 %copy-start.11 = (bf16[128,1024]{1,0:T(8,128)(2,1)S(1)}, bf16[128,1024]{1,0:T(8,128)(2,1)}, u32[]{:S(2)}) copy-start(bf16[128,1024]{1,0:T(8,128)(2,1)} %get-tuple-element.41) | copy-start | bytes 786436
  83.2 4.8 %copy-start.15 = (bf16[128,1024]{1,0:T(8,128)(2,1)S(1)}, bf16[128,1024]{1,0:T(8,128)(2,1)}, u32[]{:S(2)}) copy-start(bf16[128,1024]{1,0:T(8,128)(2,1)} %get-tuple-element.42) | copy-start | bytes 786436
  83.2 9.0 %collective-permute-start.20 = (bf16[288,512]{1,0:T(8,128)(2,1)S(1)}, bf16[288,512]{1,0:T(8,128)(2,1)S(1)}, u32[]{:S(2)}, u32[]{:S(2)}) collective-permute-start(bf16[288,512]{1,0:T(8,128)(2,1)S(1)} %add_convert_fusion.2), channel_id=1, source_target_pairs={{0,2},{1,3},{2,4},{3,5},{4,6},{5,7},{8,10},{9,11},{10,12},{11,13},... | collective-permute-start | bytes 884744 | tf_op jit(solution)/shard_map/ppermute | solution.py:327
  88.1 1.2 %copy-start.10 = (bf16[128,1024]{1,0:T(8,128)(2,1)S(1)}, bf16[128,1024]{1,0:T(8,128)(2,1)}, u32[]{:S(2)}) copy-start(bf16[128,1024]{1,0:T(8,128)(2,1)} %get-tuple-element.35) | copy-start | bytes 786436
  89.3 2.9 %copy-start.21 = (bf16[256,512]{1,0:T(8,128)(2,1)S(1)}, bf16[256,512]{1,0:T(8,128)(2,1)}, u32[]{:S(2)}) copy-start(bf16[256,512]{1,0:T(8,128)(2,1)} %get-tuple-element.53) | copy-start | bytes 786436
  90.5 1.9 %copy-start.9 = (bf16[288,512]{1,0:T(8,128)(2,1)S(1)}, bf16[288,512]{1,0:T(8,128)(2,1)}, u32[]{:S(2)}) copy-start(bf16[288,512]{1,0:T(8,128)(2,1)} %get-tuple-element.56) | copy-start | bytes 884740
  92.8 1.4 %collective-permute-start.23 = (bf16[128,512]{1,0:T(8,128)(2,1)S(1)}, bf16[128,512]{1,0:T(8,128)(2,1)S(1)}, u32[]{:S(2)}, u32[]{:S(2)}) collective-permute-start(bf16[128,512]{1,0:T(8,128)(2,1)S(1)} %slice.96), channel_id=1, source_target_pairs={{0,1},{1,0},{2,3},{3,2},{4,5},{5,4},{6,7},{7,6},{8,9},{9,8},{10,11... | collective-permute-start | bytes 393224 | tf_op jit(solution)/shard_map/ppermute | solution.py:327
  92.8 1.6 %collective-permute-start.24 = (bf16[160,512]{1,0:T(8,128)(2,1)S(1)}, bf16[160,512]{1,0:T(8,128)(2,1)S(1)}, u32[]{:S(2)}, u32[]{:S(2)}) collective-permute-start(bf16[160,512]{1,0:T(8,128)(2,1)S(1)} %slice.98), channel_id=1, source_target_pairs={{0,1},{1,0},{2,3},{3,2},{4,5},{5,4},{6,7},{7,6},{8,9},{9,8},{10,11... | collective-permute-start | bytes 491528 | tf_op jit(solution)/shard_map/ppermute | solution.py:327
  94.8 5.1 %collective-permute-start.26 = (f32[8,128]{1,0:T(8,128)S(1)}, f32[8,128]{1,0:T(8,128)S(1)}, u32[]{:S(2)}, u32[]{:S(2)}) collective-permute-start(f32[8,128]{1,0:T(8,128)S(1)} %broadcast_select_fusion.2), channel_id=1, source_target_pairs={{0,16},{8,24},{16,0},{24,8},{1,17},{9,25},{17,1},{25,9},{2,18},{10... | collective-permute-start | bytes 12296 | tf_op jit(solution)/shard_map/ppermute | solution.py:488
  94.8 5.1 %collective-permute-start.27 = (f32[8,128]{1,0:T(8,128)S(1)}, f32[8,128]{1,0:T(8,128)S(1)}, u32[]{:S(2)}, u32[]{:S(2)}) collective-permute-start(f32[8,128]{1,0:T(8,128)S(1)} %broadcast_select_fusion.2), channel_id=1, source_target_pairs={{0,24},{8,16},{16,8},{24,0},{1,25},{9,17},{17,9},{25,1},{2,26},{10... | collective-permute-start | bytes 12296 | tf_op jit(solution)/shard_map/ppermute | solution.py:488
  97.4 3.6 %collective-permute-start.25 = (f32[8,128]{1,0:T(8,128)S(1)}, f32[8,128]{1,0:T(8,128)S(1)}, u32[]{:S(2)}, u32[]{:S(2)}) collective-permute-start(f32[8,128]{1,0:T(8,128)S(1)} %broadcast_select_fusion.2), channel_id=1, source_target_pairs={{0,8},{8,0},{16,24},{24,16},{1,9},{9,1},{17,25},{25,17},{2,10},{10... | collective-permute-start | bytes 12296 | tf_op jit(solution)/shard_map/ppermute | solution.py:488
  (3 other events, 2.6 us)

commit v7 on v6

--- a/solution.py
+++ b/solution.py
@@ -432,10 +432,6 @@
             return (send(far, ends),) * 2
         return scatter_hop(*added(partials, running, hop), hop, chips)
 
-    def finished(partials, running):
-        total = add3(partials[0], *running)
-        return total, send(total[local_rows:], swap)
-
     first_hops, second_hops = [], []
     for hop in range(1, chips):
         first_hops = gathered(0, first_hops)
@@ -468,8 +464,13 @@
     (attn_out, query_grad), first_run, second_run = lax.optimization_barrier(
         ((attn_out, query_grad), first_run, second_run)
     )
-    second_total = finished(second_sums, second_run)
-    first_total = finished(first_sums, first_run)
+    second_sum = add3(second_sums[0], *second_run)
+    first_sum = add3(first_sums[0], *first_run)
+    theirs = send(
+        jnp.concatenate([second_sum[local_rows:], first_sum[local_rows:]], axis=0), swap
+    )
+    count = second_sum.shape[0] - local_rows
+    second_total, first_total = (second_sum, theirs[:count]), (first_sum, theirs[count:])
 
     def sink_sums(slots):
         slots = slots.astype(jnp.float32)[: 3 * STREAMS * chips]

time: 103 us -> 103 us (level)
  starting transfers between devices: 53.1 us -> 49.7 us
  Pallas kernels: 14.4 us -> 15.8 us
  waiting for transfers between devices: 20.3 us -> 21.7 us
    ppermute x25 -> x24, starting transfers between devices: 49.6 us -> 46 us  [send(): return lax.ppermute(value, 'ctx', pairs)]
    pallas_call x2, Pallas kernels: 14.4 us -> 15.8 us  [attend(): pl.pallas_call(functools.partial(attention_kernel, shape), in_specs=[hbm]...]
    ppermute x25 -> x24, waiting for transfers between devices: 19.2 us -> 20.1 us  [send(): return lax.ppermute(value, 'ctx', pairs)]
  transfers between devices with their start and end apart: 28 -> 27, of which waited for: 10 -> 10; matrix products, arithmetic and copies ran while one was open for 8% -> 8% of each run, Pallas kernels for 14% -> 16%
where the time goes in v7:
time: 103 us; the launch traced here: 101 us
  starting transfers between devices  49.7 us (48%)
  waiting for transfers between devices  21.7 us (21%)
  Pallas kernels  15.8 us (15%)
  other arithmetic  8.26 us (8%)
  local copies, waits for them, and re-layouts  4.17 us (4%)
  between operations  1.36 us (1%)
    ppermute x24, starting transfers between devices, send(): return lax.ppermute(value, 'ctx', pairs)  46 us
    ppermute x24, waiting for transfers between devices, send(): return lax.ppermute(value, 'ctx', pairs)  20.1 us
    pallas_call x2, Pallas kernels, attend(): pl.pallas_call(functools.partial(attention_kernel, shape), in_specs=[hbm]...  15.8 us
    select_n x4, other arithmetic, whole(): jnp.where(core == 0, jnp.concatenate(mine + other, axis=1), jnp.concatena...  4 us
    ppermute x3, starting transfers between devices, per_device(): lax.ppermute(sink_grad, 'dp', [(at, at ^ bit) for at in range(size)])  3.64 us
    dynamic_slice x2, local copies, waits for them, and re-layouts, columns(): return lax.dynamic_slice_in_dim(table, first, count, 1)  2.31 us
  transfers between devices with their start and end apart: 27, of which 10 were waited for; matrix products, arithmetic and copies ran while one was open for 8% of the time, Pallas kernels for 16%

profile of v7, /device:TPU:0, one launch (start us, length us, event | category | flops | bytes accessed | tf_op | source)
XLA Modules:
  0.0 100.9 jit_solution(10556556859654741229)
XLA Ops:
  0.7 1.2 %constant_dynamic-slice_fusion = (bf16[128,256]{1,0:T(8,128)(2,1)S(1)}, bf16[128,256]{1,0:T(8,128)(2,1)S(1)}, bf16[128,256]{1,0:T(8,128)(2,1)S(1)}, bf16[128,256...) fusion(bf16[128,1024]{1,0:T(8,128)(2,1)} %param.10, ...), kind=kLoop, calls=%fused_computation.23 | loop fusion | bytes 1048592 | tf_op jit(solution)/shard_map/dynamic_slice | solution.py:363
  1.9 0.5 collective-permute-start.1
  2.4 1.1 %constant_dynamic-slice_fusion.8 = (bf16[128,2048]{1,0:T(8,128)(2,1)S(1)}, bf16[128,2048]{1,0:T(8,128)(2,1)S(1)}) fusion(bf16[128,4096]{1,0:T(8,128)(2,1)} %g_hbm.3, s32[]{:T(128)S(6)} %select_n.88, bf16[128,4096]{1,0:T(8,128)(2,1)S(1)} %copy-done), kind=kLoop, calls=%fused_computation.31 | loop fusion | bytes 2097156 | tf_op jit(solution)/shard_map/dynamic_slice | solution.py:363
  3.6 0.2 collective-permute-start
  3.9 1.3 %collective-permute-start.4 = (bf16[256,512]{1,0:T(8,128)(2,1)S(1)}, bf16[256,512]{1,0:T(8,128)(2,1)}, u32[]{:S(2)}, u32[]{:S(2)}) collective-permute-start(bf16[256,512]{1,0:T(8,128)(2,1)S(1)} %pad_maximum_fusion.4.refs_0_), channel_id=1, source_target_pairs={{2,0},{3,1},{4,2},{5,3},{6,4},{7,5},{10,8},{11,9},{12,10},{13,11},... | collective-permute-start | bytes 786440 | tf_op jit(solution)/shard_map/ppermute | solution.py:327
  5.2 6.2 %collective-permute-start.2 = (bf16[256,512]{1,0:T(8,128)(2,1)S(1)}, bf16[256,512]{1,0:T(8,128)(2,1)}, u32[]{:S(2)}, u32[]{:S(2)}) collective-permute-start(bf16[256,512]{1,0:T(8,128)(2,1)S(1)} %pad_maximum_fusion.4.refs_0_), channel_id=1, source_target_pairs={{0,2},{1,3},{2,4},{3,5},{4,6},{5,7},{8,10},{9,11},{10,12},{11,13},... | collective-permute-start | bytes 786440 | tf_op jit(solution)/shard_map/ppermute | solution.py:327
  11.4 1.3 %collective-permute-start.9 = (bf16[256,512]{1,0:T(8,128)(2,1)S(1)}, bf16[256,512]{1,0:T(8,128)(2,1)S(1)}, u32[]{:S(2)}, u32[]{:S(2)}) collective-permute-start(bf16[256,512]{1,0:T(8,128)(2,1)S(1)} %pad_maximum_fusion.5.refs_0_), channel_id=1, source_target_pairs={{2,0},{3,1},{4,2},{5,3},{6,4},{7,5},{10,8},{11,9},{12,10},{13,11},... | collective-permute-start | bytes 786440 | tf_op jit(solution)/shard_map/ppermute | solution.py:327
  12.7 4.6 %collective-permute-start.7 = (bf16[256,512]{1,0:T(8,128)(2,1)S(1)}, bf16[256,512]{1,0:T(8,128)(2,1)S(1)}, u32[]{:S(2)}, u32[]{:S(2)}) collective-permute-start(bf16[256,512]{1,0:T(8,128)(2,1)S(1)} %pad_maximum_fusion.5.refs_0_), channel_id=1, source_target_pairs={{0,2},{1,3},{2,4},{3,5},{4,6},{5,7},{8,10},{9,11},{10,12},{11,13},... | collective-permute-start | bytes 786440 | tf_op jit(solution)/shard_map/ppermute | solution.py:327
  17.3 1.3 %collective-permute-start.5 = (bf16[256,512]{1,0:T(8,128)(2,1)}, bf16[256,512]{1,0:T(8,128)(2,1)}, u32[]{:S(2)}, u32[]{:S(2)}) collective-permute-start(bf16[256,512]{1,0:T(8,128)(2,1)} %collective-permute-done.4.refs_3_), channel_id=1, source_target_pairs={{2,0},{3,1},{4,2},{5,3},{10,8},{11,9},{12,10},{13,11},{18,16},{19,... | collective-permute-start | bytes 786440 | tf_op jit(solution)/shard_map/ppermute | solution.py:327
  18.6 1.4 %collective-permute-start.3 = (bf16[256,512]{1,0:T(8,128)(2,1)}, bf16[256,512]{1,0:T(8,128)(2,1)}, u32[]{:S(2)}, u32[]{:S(2)}) collective-permute-start(bf16[256,512]{1,0:T(8,128)(2,1)} %collective-permute-done.2.refs_1_), channel_id=1, source_target_pairs={{2,4},{3,5},{4,6},{5,7},{10,12},{11,13},{12,14},{13,15},{18,20},{1... | collective-permute-start | bytes 786440 | tf_op jit(solution)/shard_map/ppermute | solution.py:327
  20.0 1.4 %collective-permute-done.9.refs_3_ = bf16[256,512]{1,0:T(8,128)(2,1)S(1)} collective-permute-done((bf16[256,512]{1,0:T(8,128)(2,1)S(1)}, bf16[256,512]{1,0:T(8,128)(2,1)S(1)}, u32[]{:S(2)}, u32[]{:S(2)}) %collective-permute-start.9) | collective-permute-done | bytes 262176 | tf_op jit(solution)/shard_map/ppermute | solution.py:327
  21.4 1.3 %collective-permute-start.10 = (bf16[256,512]{1,0:T(8,128)(2,1)S(1)}, bf16[256,512]{1,0:T(8,128)(2,1)S(1)}, u32[]{:S(2)}, u32[]{:S(2)}) collective-permute-start(bf16[256,512]{1,0:T(8,128)(2,1)S(1)} %collective-permute-done.9.refs_3_), channel_id=1, source_target_pairs={{2,0},{3,1},{4,2},{5,3},{10,8},{11,9},{12,10},{13,11},{18,16},{19,... | collective-permute-start | bytes 786440 | tf_op jit(solution)/shard_map/ppermute | solution.py:327
  22.7 0.7 collective-permute-start.8
  23.4 3.7 %collective-permute-done.5.refs_4_ = bf16[256,512]{1,0:T(8,128)(2,1)} collective-permute-done((bf16[256,512]{1,0:T(8,128)(2,1)}, bf16[256,512]{1,0:T(8,128)(2,1)}, u32[]{:S(2)}, u32[]{:S(2)}) %collective-permute-start.5) | collective-permute-done | bytes 262176 | tf_op jit(solution)/shard_map/ppermute | solution.py:327
  27.1 1.2 %broadcast_select_fusion.1 = bf16[256,512]{1,0:T(8,128)(2,1)S(1)} fusion(bf16[256,512]{1,0:T(8,128)(2,1)} %collective-permute-done.3.refs_2_, bf16[256,512]{1,0:T(8,128)(2,1)} %collective-permute-done.5.refs_4_, pred[]{:T(512)S(6)} %ge.4), kind=kLoop, calls=%fused_computation.19 | loop fusion | flops 131072 | bytes 786433 | tf_op jit(solution)/shard_map/jit(_where)/select_n | solution.py:416
  28.3 1.3 %collective-permute-start.6 = (bf16[256,512]{1,0:T(8,128)(2,1)S(1)}, bf16[256,512]{1,0:T(8,128)(2,1)S(1)}, u32[]{:S(2)}, u32[]{:S(2)}) collective-permute-start(bf16[256,512]{1,0:T(8,128)(2,1)S(1)} %broadcast_select_fusion.1), channel_id=1, source_target_pairs={{4,6},{5,7},{2,0},{3,1},{12,14},{13,15},{10,8},{11,9},{20,22},{21,... | collective-permute-start | bytes 786440 | tf_op jit(solution)/shard_map/ppermute | solution.py:327
  29.6 3.6 %collective-permute-done.10.refs_4_ = bf16[256,512]{1,0:T(8,128)(2,1)S(1)} collective-permute-done((bf16[256,512]{1,0:T(8,128)(2,1)S(1)}, bf16[256,512]{1,0:T(8,128)(2,1)S(1)}, u32[]{:S(2)}, u32[]{:S(2)}) %collective-permute-start.10) | collective-permute-done | bytes 262176 | tf_op jit(solution)/shard_map/ppermute | solution.py:327
  33.3 1.3 %collective-permute-start.11 = (bf16[256,512]{1,0:T(8,128)(2,1)S(1)}, bf16[256,512]{1,0:T(8,128)(2,1)S(1)}, u32[]{:S(2)}, u32[]{:S(2)}) collective-permute-start(bf16[256,512]{1,0:T(8,128)(2,1)S(1)} %broadcast_select_fusion), channel_id=1, source_target_pairs={{4,6},{5,7},{2,0},{3,1},{12,14},{13,15},{10,8},{11,9},{20,22},{21,... | collective-permute-start | bytes 786440 | tf_op jit(solution)/shard_map/ppermute | solution.py:327
  34.6 7.2 %collective-permute-done.6.refs_5_ = bf16[256,512]{1,0:T(8,128)(2,1)S(1)} collective-permute-done((bf16[256,512]{1,0:T(8,128)(2,1)S(1)}, bf16[256,512]{1,0:T(8,128)(2,1)S(1)}, u32[]{:S(2)}, u32[]{:S(2)}) %collective-permute-start.6) | collective-permute-done | bytes 262176 | tf_op jit(solution)/shard_map/ppermute | solution.py:327
  41.8 0.7 copy-done.22
  42.5 7.5 %shard_map.119 = (bf16[128,1024]{1,0:T(8,128)(2,1)}, bf16[128,1024]{1,0:T(8,128)(2,1)}, bf16[128,2048]{1,0:T(8,128)(2,1)}, bf16[256,512]{1,0:T(8,128)(2,1)}, bf1...) custom-call(f32[32]{0:T(128)} %sink_hbm.3, ...), custom_call_target="tpu_custom_call" | custom-call | flops 1610612736 | bytes 8388608 | tf_op jit(solution)/shard_map/pallas_call | solution.py:298
  50.1 1.3 %collective-permute-start.13 = (bf16[256,512]{1,0:T(8,128)(2,1)}, bf16[256,512]{1,0:T(8,128)(2,1)S(1)}, u32[]{:S(2)}, u32[]{:S(2)}) collective-permute-start(bf16[256,512]{1,0:T(8,128)(2,1)} %get-tuple-element.45), channel_id=1, source_target_pairs={{0,2},{1,3},{6,4},{7,5},{8,10},{9,11},{14,12},{15,13},{16,18},{17,... | collective-permute-start | bytes 786440 | tf_op jit(solution)/shard_map/ppermute | solution.py:327
  51.4 0.7 copy-done.19
  52.1 8.3 %shard_map.120 = (bf16[128,1024]{1,0:T(8,128)(2,1)}, bf16[128,1024]{1,0:T(8,128)(2,1)}, bf16[128,2048]{1,0:T(8,128)(2,1)}, bf16[288,512]{1,0:T(8,128)(2,1)}, bf1...) custom-call(f32[32]{0:T(128)} %sink_hbm.3, ...), custom_call_target="tpu_custom_call" | custom-call | bytes 1024 | tf_op jit(solution)/shard_map/pallas_call | solution.py:298
  60.4 1.4 %collective-permute-start.18 = (bf16[288,512]{1,0:T(8,128)(2,1)}, bf16[288,512]{1,0:T(8,128)(2,1)S(1)}, u32[]{:S(2)}, u32[]{:S(2)}) collective-permute-start(bf16[288,512]{1,0:T(8,128)(2,1)} %get-tuple-element.49), channel_id=1, source_target_pairs={{0,2},{1,3},{6,4},{7,5},{8,10},{9,11},{14,12},{15,13},{16,18},{17,... | collective-permute-start | bytes 884744 | tf_op jit(solution)/shard_map/ppermute | solution.py:327
  62.0 0.7 collective-permute-start.16
  62.7 1.2 %pad_maximum_fusion.1 = bf16[128,4096]{1,0:T(8,128)(2,1)S(1)} fusion(bf16[128,2048]{1,0:T(8,128)(2,1)} %get-tuple-element.40, bf16[128,2048]{1,0:T(8,128)(2,1)S(1)} %copy-done.5), kind=kLoop, calls=%fused_computation.1 | loop fusion | flops 2097152 | bytes 2097152 | tf_op jit(solution)/shard_map/concatenate | solution.py:446
  64.0 1.3 %collective-permute-start.14 = (bf16[256,512]{1,0:T(8,128)(2,1)S(1)}, bf16[256,512]{1,0:T(8,128)(2,1)S(1)}, u32[]{:S(2)}, u32[]{:S(2)}) collective-permute-start(bf16[256,512]{1,0:T(8,128)(2,1)S(1)} %add_convert_fusion.7), channel_id=1, source_target_pairs={{0,2},{1,3},{2,4},{3,5},{8,10},{9,11},{10,12},{11,13},{16,18},{17,... | collective-permute-start | bytes 786440 | tf_op jit(solution)/shard_map/ppermute | solution.py:327
  65.3 1.2 %collective-permute-done.18 = bf16[288,512]{1,0:T(8,128)(2,1)S(1)} collective-permute-done((bf16[288,512]{1,0:T(8,128)(2,1)}, bf16[288,512]{1,0:T(8,128)(2,1)S(1)}, u32[]{:S(2)}, u32[]{:S(2)}) %collective-permute-start.18) | collective-permute-done | bytes 294944 | tf_op jit(solution)/shard_map/ppermute | solution.py:327
  66.6 0.7 collective-permute-start.21
  67.3 5.4 %collective-permute-start.19 = (bf16[288,512]{1,0:T(8,128)(2,1)S(1)}, bf16[288,512]{1,0:T(8,128)(2,1)S(1)}, u32[]{:S(2)}, u32[]{:S(2)}) collective-permute-start(bf16[288,512]{1,0:T(8,128)(2,1)S(1)} %add_convert_fusion.3), channel_id=1, source_target_pairs={{0,2},{1,3},{2,4},{3,5},{8,10},{9,11},{10,12},{11,13},{16,18},{17,... | collective-permute-start | bytes 884744 | tf_op jit(solution)/shard_map/ppermute | solution.py:327
  72.7 1.3 %collective-permute-start.17 = (bf16[256,512]{1,0:T(8,128)(2,1)S(1)}, bf16[256,512]{1,0:T(8,128)(2,1)S(1)}, u32[]{:S(2)}, u32[]{:S(2)}) collective-permute-start(bf16[256,512]{1,0:T(8,128)(2,1)S(1)} %add_convert_fusion.5), channel_id=1, source_target_pairs={{2,0},{3,1},{4,2},{5,3},{6,4},{7,5},{10,8},{11,9},{12,10},{13,11},... | collective-permute-start | bytes 786440 | tf_op jit(solution)/shard_map/ppermute | solution.py:327
  74.1 6.6 %collective-permute-start.15 = (bf16[256,512]{1,0:T(8,128)(2,1)S(1)}, bf16[256,512]{1,0:T(8,128)(2,1)S(1)}, u32[]{:S(2)}, u32[]{:S(2)}) collective-permute-start(bf16[256,512]{1,0:T(8,128)(2,1)S(1)} %add_convert_fusion.6), channel_id=1, source_target_pairs={{0,2},{1,3},{2,4},{3,5},{4,6},{5,7},{8,10},{9,11},{10,12},{11,13},... | collective-permute-start | bytes 786440 | tf_op jit(solution)/shard_map/ppermute | solution.py:327
  80.8 1.3 %collective-permute-start.22 = (bf16[288,512]{1,0:T(8,128)(2,1)S(1)}, bf16[288,512]{1,0:T(8,128)(2,1)S(1)}, u32[]{:S(2)}, u32[]{:S(2)}) collective-permute-start(bf16[288,512]{1,0:T(8,128)(2,1)S(1)} %add_convert_fusion.1), channel_id=1, source_target_pairs={{2,0},{3,1},{4,2},{5,3},{6,4},{7,5},{10,8},{11,9},{12,10},{13,11},... | collective-permute-start | bytes 884744 | tf_op jit(solution)/shard_map/ppermute | solution.py:327
  82.2 4.7 %collective-permute-start.20 = (bf16[288,512]{1,0:T(8,128)(2,1)S(1)}, bf16[288,512]{1,0:T(8,128)(2,1)S(1)}, u32[]{:S(2)}, u32[]{:S(2)}) collective-permute-start(bf16[288,512]{1,0:T(8,128)(2,1)S(1)} %add_convert_fusion.2), channel_id=1, source_target_pairs={{0,2},{1,3},{2,4},{3,5},{4,6},{5,7},{8,10},{9,11},{10,12},{11,13},... | collective-permute-start | bytes 884744 | tf_op jit(solution)/shard_map/ppermute | solution.py:327
  87.1 1.2 %maximum_select_fusion.1 = bf16[128,4096]{1,0:T(8,128)(2,1)} fusion(bf16[128,1024]{1,0:T(8,128)(2,1)S(1)} %get-tuple-element.60, bf16[128,1024]{1,0:T(8,128)(2,1)S(1)} %get-tuple-element.59, bf16[128,1024]{1,0:T(8,128)(2,1)S(1)} %copy-done.15, bf16[128,1024]{1,0:T(8,128)(2,1)S(1)} %copy-done.11, pred[]{:T(512)S(6)} %eq.16), kind=kLoop, calls=%fused_computation.3 | loop fusion | flops 8912896 | bytes 2097153 | tf_op jit(solution)/shard_map/jit(_where)/select_n | solution.py:452
  88.3 1.2 %maximum_select_fusion = bf16[128,4096]{1,0:T(8,128)(2,1)} fusion(bf16[128,1024]{1,0:T(8,128)(2,1)S(1)} %get-tuple-element.61, bf16[128,1024]{1,0:T(8,128)(2,1)S(1)} %get-tuple-element.62, bf16[128,1024]{1,0:T(8,128)(2,1)S(1)} %copy-done.14, bf16[128,1024]{1,0:T(8,128)(2,1)S(1)} %copy-done.10, pred[]{:T(512)S(6)} %eq.16), kind=kLoop, calls=%fused_computation.2 | loop fusion | flops 8912896 | bytes 2097153 | tf_op jit(solution)/shard_map/jit(_where)/select_n | solution.py:452
  89.5 0.2 collective-permute-done.22
  89.7 1.5 %collective-permute-done.20 = bf16[288,512]{1,0:T(8,128)(2,1)S(1)} collective-permute-done((bf16[288,512]{1,0:T(8,128)(2,1)S(1)}, bf16[288,512]{1,0:T(8,128)(2,1)S(1)}, u32[]{:S(2)}, u32[]{:S(2)}) %collective-permute-start.20) | collective-permute-done | bytes 294944 | tf_op jit(solution)/shard_map/ppermute | solution.py:327
  91.9 1.3 %collective-permute-done.23 = bf16[288,512]{1,0:T(8,128)(2,1)S(1)} collective-permute-done((bf16[288,512]{1,0:T(8,128)(2,1)S(1)}, bf16[288,512]{1,0:T(8,128)(2,1)S(1)}, u32[]{:S(2)}, u32[]{:S(2)}) %collective-permute-start.23) | collective-permute-done | bytes 294944 | tf_op jit(solution)/shard_map/ppermute | solution.py:327
  93.6 2.0 %collective-permute-start.25 = (f32[8,128]{1,0:T(8,128)S(1)}, f32[8,128]{1,0:T(8,128)S(1)}, u32[]{:S(2)}, u32[]{:S(2)}) collective-permute-start(f32[8,128]{1,0:T(8,128)S(1)} %broadcast_select_fusion.2), channel_id=1, source_target_pairs={{0,16},{8,24},{16,0},{24,8},{1,17},{9,25},{17,1},{25,9},{2,18},{10... | collective-permute-start | bytes 12296 | tf_op jit(solution)/shard_map/ppermute | solution.py:489
  95.5 1.2 %collective-permute-start.26 = (f32[8,128]{1,0:T(8,128)S(1)}, f32[8,128]{1,0:T(8,128)S(1)}, u32[]{:S(2)}, u32[]{:S(2)}) collective-permute-start(f32[8,128]{1,0:T(8,128)S(1)} %broadcast_select_fusion.2), channel_id=1, source_target_pairs={{0,24},{8,16},{16,8},{24,0},{1,25},{9,17},{17,9},{25,1},{2,26},{10... | collective-permute-start | bytes 12296 | tf_op jit(solution)/shard_map/ppermute | solution.py:489
  96.7 0.5 collective-permute-start.24
  97.2 0.8 maximum_select_fusion.3
  98.0 0.8 maximum_select_fusion.2
  98.8 1.3 %collective-permute-done.26 = f32[8,128]{1,0:T(8,128)S(1)} collective-permute-done((f32[8,128]{1,0:T(8,128)S(1)}, f32[8,128]{1,0:T(8,128)S(1)}, u32[]{:S(2)}, u32[]{:S(2)}) %collective-permute-start.26) | collective-permute-done | bytes 4128 | tf_op jit(solution)/shard_map/ppermute | solution.py:489
  100.1 0.3 collective-permute-done.24
  100.3 0.6 add_reduce_fusion
  (98 shorter events, 1.9 us)
Async XLA Ops:
  0.6 1.8 %copy-start = (bf16[128,4096]{1,0:T(8,128)(2,1)S(1)}, bf16[128,4096]{1,0:T(8,128)(2,1)}, u32[]{:S(2)}) copy-start(bf16[128,4096]{1,0:T(8,128)(2,1)} %q_hbm.3) | copy-start | bytes 3145732
  1.9 1.9 %collective-permute-start.1 = (bf16[128,1024]{1,0:T(8,128)(2,1)S(1)}, bf16[128,1024]{1,0:T(8,128)(2,1)S(1)}, u32[]{:S(2)}, u32[]{:S(2)}) collective-permute-start(bf16[128,1024]{1,0:T(8,128)(2,1)S(1)} %pad_maximum_fusion.3), channel_id=1, source_target_pairs={{0,1},{1,0},{2,3},{3,2},{4,5},{5,4},{6,7},{7,6},{8,9},{9,8},{10,11... | collective-permute-start | bytes 786440 | tf_op jit(solution)/shard_map/ppermute | solution.py:327
  3.6 23.5 %collective-permute-start = (bf16[128,4096]{1,0:T(8,128)(2,1)S(1)}, bf16[128,4096]{1,0:T(8,128)(2,1)S(1)}, u32[]{:S(2)}, u32[]{:S(2)}) collective-permute-start(bf16[128,4096]{1,0:T(8,128)(2,1)S(1)} %pad_maximum_fusion), channel_id=1, source_target_pairs={{0,1},{1,0},{2,3},{3,2},{4,5},{5,4},{6,7},{7,6},{8,9},{9,8},{10,11... | collective-permute-start | bytes 3145736 | tf_op jit(solution)/shard_map/ppermute | solution.py:327
  3.9 18.8 %copy-start.20 = (bf16[256,512]{1,0:T(8,128)(2,1)}, bf16[256,512]{1,0:T(8,128)(2,1)S(1)}, u32[]{:S(2)}) copy-start(bf16[256,512]{1,0:T(8,128)(2,1)S(1)} %pad_maximum_fusion.4.refs_0_) | copy-start | bytes 786436
  3.9 13.4 %collective-permute-start.4 = (bf16[256,512]{1,0:T(8,128)(2,1)S(1)}, bf16[256,512]{1,0:T(8,128)(2,1)}, u32[]{:S(2)}, u32[]{:S(2)}) collective-permute-start(bf16[256,512]{1,0:T(8,128)(2,1)S(1)} %pad_maximum_fusion.4.refs_0_), channel_id=1, source_target_pairs={{2,0},{3,1},{4,2},{5,3},{6,4},{7,5},{10,8},{11,9},{12,10},{13,11},... | collective-permute-start | bytes 786440 | tf_op jit(solution)/shard_map/ppermute | solution.py:327
  5.2 13.4 %collective-permute-start.2 = (bf16[256,512]{1,0:T(8,128)(2,1)S(1)}, bf16[256,512]{1,0:T(8,128)(2,1)}, u32[]{:S(2)}, u32[]{:S(2)}) collective-permute-start(bf16[256,512]{1,0:T(8,128)(2,1)S(1)} %pad_maximum_fusion.4.refs_0_), channel_id=1, source_target_pairs={{0,2},{1,3},{2,4},{3,5},{4,6},{5,7},{8,10},{9,11},{10,12},{11,13},... | collective-permute-start | bytes 786440 | tf_op jit(solution)/shard_map/ppermute | solution.py:327
  11.4 38.6 %copy-start.1 = (bf16[256,512]{1,0:T(8,128)(2,1)}, bf16[256,512]{1,0:T(8,128)(2,1)S(1)}, u32[]{:S(2)}) copy-start(bf16[256,512]{1,0:T(8,128)(2,1)S(1)} %pad_maximum_fusion.5.refs_0_) | copy-start | bytes 786436
  11.4 10.0 %collective-permute-start.9 = (bf16[256,512]{1,0:T(8,128)(2,1)S(1)}, bf16[256,512]{1,0:T(8,128)(2,1)S(1)}, u32[]{:S(2)}, u32[]{:S(2)}) collective-permute-start(bf16[256,512]{1,0:T(8,128)(2,1)S(1)} %pad_maximum_fusion.5.refs_0_), channel_id=1, source_target_pairs={{2,0},{3,1},{4,2},{5,3},{6,4},{7,5},{10,8},{11,9},{12,10},{13,11},... | collective-permute-start | bytes 786440 | tf_op jit(solution)/shard_map/ppermute | solution.py:327
  12.7 10.0 %collective-permute-start.7 = (bf16[256,512]{1,0:T(8,128)(2,1)S(1)}, bf16[256,512]{1,0:T(8,128)(2,1)S(1)}, u32[]{:S(2)}, u32[]{:S(2)}) collective-permute-start(bf16[256,512]{1,0:T(8,128)(2,1)S(1)} %pad_maximum_fusion.5.refs_0_), channel_id=1, source_target_pairs={{0,2},{1,3},{2,4},{3,5},{4,6},{5,7},{8,10},{9,11},{10,12},{11,13},... | collective-permute-start | bytes 786440 | tf_op jit(solution)/shard_map/ppermute | solution.py:327
  17.3 9.8 %collective-permute-start.5 = (bf16[256,512]{1,0:T(8,128)(2,1)}, bf16[256,512]{1,0:T(8,128)(2,1)}, u32[]{:S(2)}, u32[]{:S(2)}) collective-permute-start(bf16[256,512]{1,0:T(8,128)(2,1)} %collective-permute-done.4.refs_3_), channel_id=1, source_target_pairs={{2,0},{3,1},{4,2},{5,3},{10,8},{11,9},{12,10},{13,11},{18,16},{19,... | collective-permute-start | bytes 786440 | tf_op jit(solution)/shard_map/ppermute | solution.py:327
  18.6 8.5 %collective-permute-start.3 = (bf16[256,512]{1,0:T(8,128)(2,1)}, bf16[256,512]{1,0:T(8,128)(2,1)}, u32[]{:S(2)}, u32[]{:S(2)}) collective-permute-start(bf16[256,512]{1,0:T(8,128)(2,1)} %collective-permute-done.2.refs_1_), channel_id=1, source_target_pairs={{2,4},{3,5},{4,6},{5,7},{10,12},{11,13},{12,14},{13,15},{18,20},{1... | collective-permute-start | bytes 786440 | tf_op jit(solution)/shard_map/ppermute | solution.py:327
  21.4 28.6 %copy-start.12 = (bf16[256,512]{1,0:T(8,128)(2,1)}, bf16[256,512]{1,0:T(8,128)(2,1)S(1)}, u32[]{:S(2)}) copy-start(bf16[256,512]{1,0:T(8,128)(2,1)S(1)} %collective-permute-done.9.refs_3_) | copy-start | bytes 786436
  21.4 11.8 %collective-permute-start.10 = (bf16[256,512]{1,0:T(8,128)(2,1)S(1)}, bf16[256,512]{1,0:T(8,128)(2,1)S(1)}, u32[]{:S(2)}, u32[]{:S(2)}) collective-permute-start(bf16[256,512]{1,0:T(8,128)(2,1)S(1)} %collective-permute-done.9.refs_3_), channel_id=1, source_target_pairs={{2,0},{3,1},{4,2},{5,3},{10,8},{11,9},{12,10},{13,11},{18,16},{19,... | collective-permute-start | bytes 786440 | tf_op jit(solution)/shard_map/ppermute | solution.py:327
  22.7 27.3 %copy-start.13 = (bf16[256,512]{1,0:T(8,128)(2,1)}, bf16[256,512]{1,0:T(8,128)(2,1)S(1)}, u32[]{:S(2)}) copy-start(bf16[256,512]{1,0:T(8,128)(2,1)S(1)} %collective-permute-done.7.refs_1_) | copy-start | bytes 786436
  22.7 10.5 %collective-permute-start.8 = (bf16[256,512]{1,0:T(8,128)(2,1)S(1)}, bf16[256,512]{1,0:T(8,128)(2,1)S(1)}, u32[]{:S(2)}, u32[]{:S(2)}) collective-permute-start(bf16[256,512]{1,0:T(8,128)(2,1)S(1)} %collective-permute-done.7.refs_1_), channel_id=1, source_target_pairs={{2,4},{3,5},{4,6},{5,7},{10,12},{11,13},{12,14},{13,15},{18,20},{1... | collective-permute-start | bytes 786440 | tf_op jit(solution)/shard_map/ppermute | solution.py:327
  27.1 14.7 %copy-start.4 = (bf16[128,4096]{1,0:T(8,128)(2,1)}, bf16[128,4096]{1,0:T(8,128)(2,1)S(1)}, u32[]{:S(2)}) copy-start(bf16[128,4096]{1,0:T(8,128)(2,1)S(1)} %collective-permute-done.partner_hbm) | copy-start | bytes 3145732
  28.3 13.5 %collective-permute-start.6 = (bf16[256,512]{1,0:T(8,128)(2,1)S(1)}, bf16[256,512]{1,0:T(8,128)(2,1)S(1)}, u32[]{:S(2)}, u32[]{:S(2)}) collective-permute-start(bf16[256,512]{1,0:T(8,128)(2,1)S(1)} %broadcast_select_fusion.1), channel_id=1, source_target_pairs={{4,6},{5,7},{2,0},{3,1},{12,14},{13,15},{10,8},{11,9},{20,22},{21,... | collective-permute-start | bytes 786440 | tf_op jit(solution)/shard_map/ppermute | solution.py:327
  33.2 16.8 %copy-start.2 = (bf16[256,512]{1,0:T(8,128)(2,1)}, bf16[256,512]{1,0:T(8,128)(2,1)S(1)}, u32[]{:S(2)}) copy-start(bf16[256,512]{1,0:T(8,128)(2,1)S(1)} %collective-permute-done.10.refs_4_) | copy-start | bytes 786436
  33.2 16.8 %copy-start.3 = (bf16[256,512]{1,0:T(8,128)(2,1)}, bf16[256,512]{1,0:T(8,128)(2,1)S(1)}, u32[]{:S(2)}) copy-start(bf16[256,512]{1,0:T(8,128)(2,1)S(1)} %collective-permute-done.8.refs_2_) | copy-start | bytes 786436
  33.3 18.1 %collective-permute-start.11 = (bf16[256,512]{1,0:T(8,128)(2,1)S(1)}, bf16[256,512]{1,0:T(8,128)(2,1)S(1)}, u32[]{:S(2)}, u32[]{:S(2)}) collective-permute-start(bf16[256,512]{1,0:T(8,128)(2,1)S(1)} %broadcast_select_fusion), channel_id=1, source_target_pairs={{4,6},{5,7},{2,0},{3,1},{12,14},{13,15},{10,8},{11,9},{20,22},{21,... | collective-permute-start | bytes 786440 | tf_op jit(solution)/shard_map/ppermute | solution.py:327
  50.1 11.8 %collective-permute-start.13 = (bf16[256,512]{1,0:T(8,128)(2,1)}, bf16[256,512]{1,0:T(8,128)(2,1)S(1)}, u32[]{:S(2)}, u32[]{:S(2)}) collective-permute-start(bf16[256,512]{1,0:T(8,128)(2,1)} %get-tuple-element.45), channel_id=1, source_target_pairs={{0,2},{1,3},{6,4},{7,5},{8,10},{9,11},{14,12},{15,13},{16,18},{17,... | collective-permute-start | bytes 786440 | tf_op jit(solution)/shard_map/ppermute | solution.py:327
  52.1 9.8 %copy-start.18 = (bf16[256,512]{1,0:T(8,128)(2,1)S(1)}, bf16[256,512]{1,0:T(8,128)(2,1)}, u32[]{:S(2)}) copy-start(bf16[256,512]{1,0:T(8,128)(2,1)} %get-tuple-element.44) | copy-start | bytes 786436
  60.4 2.2 %copy-start.5 = (bf16[128,2048]{1,0:T(8,128)(2,1)S(1)}, bf16[128,2048]{1,0:T(8,128)(2,1)}, u32[]{:S(2)}) copy-start(bf16[128,2048]{1,0:T(8,128)(2,1)} %get-tuple-element.39) | copy-start | bytes 1572868
  60.4 6.1 %collective-permute-start.18 = (bf16[288,512]{1,0:T(8,128)(2,1)}, bf16[288,512]{1,0:T(8,128)(2,1)S(1)}, u32[]{:S(2)}, u32[]{:S(2)}) collective-permute-start(bf16[288,512]{1,0:T(8,128)(2,1)} %get-tuple-element.49), channel_id=1, source_target_pairs={{0,2},{1,3},{6,4},{7,5},{8,10},{9,11},{14,12},{15,13},{16,18},{17,... | collective-permute-start | bytes 884744 | tf_op jit(solution)/shard_map/ppermute | solution.py:327
  62.0 10.7 %collective-permute-start.16 = (bf16[256,512]{1,0:T(8,128)(2,1)S(1)}, bf16[256,512]{1,0:T(8,128)(2,1)S(1)}, u32[]{:S(2)}, u32[]{:S(2)}) collective-permute-start(bf16[256,512]{1,0:T(8,128)(2,1)S(1)} %add_convert_fusion.7), channel_id=1, source_target_pairs={{4,2},{5,3},{6,4},{7,5},{12,10},{13,11},{14,12},{15,13},{20,18},{2... | collective-permute-start | bytes 786440 | tf_op jit(solution)/shard_map/ppermute | solution.py:327
  62.7 3.8 %copy-start.8 = (bf16[288,512]{1,0:T(8,128)(2,1)S(1)}, bf16[288,512]{1,0:T(8,128)(2,1)}, u32[]{:S(2)}) copy-start(bf16[288,512]{1,0:T(8,128)(2,1)} %get-tuple-element.48) | copy-start | bytes 884740
  62.7 10.0 %copy-start.17 = (bf16[256,512]{1,0:T(8,128)(2,1)S(1)}, bf16[256,512]{1,0:T(8,128)(2,1)}, u32[]{:S(2)}) copy-start(bf16[256,512]{1,0:T(8,128)(2,1)} %get-tuple-element.46) | copy-start | bytes 786436
  63.9 10.2 %copy-start.16 = (bf16[256,512]{1,0:T(8,128)(2,1)S(1)}, bf16[256,512]{1,0:T(8,128)(2,1)}, u32[]{:S(2)}) copy-start(bf16[256,512]{1,0:T(8,128)(2,1)} %get-tuple-element.43) | copy-start | bytes 786436
  63.9 23.1 %collective-permute-start.12 = (bf16[128,4096]{1,0:T(8,128)(2,1)S(1)}, bf16[128,4096]{1,0:T(8,128)(2,1)S(1)}, u32[]{:S(2)}, u32[]{:S(2)}) collective-permute-start(bf16[128,4096]{1,0:T(8,128)(2,1)S(1)} %pad_maximum_fusion.1), channel_id=1, source_target_pairs={{0,1},{1,0},{2,3},{3,2},{4,5},{5,4},{6,7},{7,6},{8,9},{9,8},{10,11... | collective-permute-start | bytes 3145736 | tf_op jit(solution)/shard_map/ppermute | solution.py:327
  64.0 10.1 %collective-permute-start.14 = (bf16[256,512]{1,0:T(8,128)(2,1)S(1)}, bf16[256,512]{1,0:T(8,128)(2,1)S(1)}, u32[]{:S(2)}, u32[]{:S(2)}) collective-permute-start(bf16[256,512]{1,0:T(8,128)(2,1)S(1)} %add_convert_fusion.7), channel_id=1, source_target_pairs={{0,2},{1,3},{2,4},{3,5},{8,10},{9,11},{10,12},{11,13},{16,18},{17,... | collective-permute-start | bytes 786440 | tf_op jit(solution)/shard_map/ppermute | solution.py:327
  66.5 14.2 %copy-start.7 = (bf16[288,512]{1,0:T(8,128)(2,1)S(1)}, bf16[288,512]{1,0:T(8,128)(2,1)}, u32[]{:S(2)}) copy-start(bf16[288,512]{1,0:T(8,128)(2,1)} %get-tuple-element.50) | copy-start | bytes 884740
  66.6 14.1 %collective-permute-start.21 = (bf16[288,512]{1,0:T(8,128)(2,1)S(1)}, bf16[288,512]{1,0:T(8,128)(2,1)S(1)}, u32[]{:S(2)}, u32[]{:S(2)}) collective-permute-start(bf16[288,512]{1,0:T(8,128)(2,1)S(1)} %add_convert_fusion.3), channel_id=1, source_target_pairs={{4,2},{5,3},{6,4},{7,5},{12,10},{13,11},{14,12},{15,13},{20,18},{2... | collective-permute-start | bytes 884744 | tf_op jit(solution)/shard_map/ppermute | solution.py:327
  67.3 14.8 %collective-permute-start.19 = (bf16[288,512]{1,0:T(8,128)(2,1)S(1)}, bf16[288,512]{1,0:T(8,128)(2,1)S(1)}, u32[]{:S(2)}, u32[]{:S(2)}) collective-permute-start(bf16[288,512]{1,0:T(8,128)(2,1)S(1)} %add_convert_fusion.3), channel_id=1, source_target_pairs={{0,2},{1,3},{2,4},{3,5},{8,10},{9,11},{10,12},{11,13},{16,18},{17,... | collective-permute-start | bytes 884744 | tf_op jit(solution)/shard_map/ppermute | solution.py:327
  72.7 9.5 %copy-start.6 = (bf16[288,512]{1,0:T(8,128)(2,1)S(1)}, bf16[288,512]{1,0:T(8,128)(2,1)}, u32[]{:S(2)}) copy-start(bf16[288,512]{1,0:T(8,128)(2,1)} %get-tuple-element.47) | copy-start | bytes 884740
  72.7 16.8 %collective-permute-start.17 = (bf16[256,512]{1,0:T(8,128)(2,1)S(1)}, bf16[256,512]{1,0:T(8,128)(2,1)S(1)}, u32[]{:S(2)}, u32[]{:S(2)}) collective-permute-start(bf16[256,512]{1,0:T(8,128)(2,1)S(1)} %add_convert_fusion.5), channel_id=1, source_target_pairs={{2,0},{3,1},{4,2},{5,3},{6,4},{7,5},{10,8},{11,9},{12,10},{13,11},... | collective-permute-start | bytes 786440 | tf_op jit(solution)/shard_map/ppermute | solution.py:327
  74.1 15.4 %collective-permute-start.15 = (bf16[256,512]{1,0:T(8,128)(2,1)S(1)}, bf16[256,512]{1,0:T(8,128)(2,1)S(1)}, u32[]{:S(2)}, u32[]{:S(2)}) collective-permute-start(bf16[256,512]{1,0:T(8,128)(2,1)S(1)} %add_convert_fusion.6), channel_id=1, source_target_pairs={{0,2},{1,3},{2,4},{3,5},{4,6},{5,7},{8,10},{9,11},{10,12},{11,13},... | collective-permute-start | bytes 786440 | tf_op jit(solution)/shard_map/ppermute | solution.py:327
  80.8 8.9 %collective-permute-start.22 = (bf16[288,512]{1,0:T(8,128)(2,1)S(1)}, bf16[288,512]{1,0:T(8,128)(2,1)S(1)}, u32[]{:S(2)}, u32[]{:S(2)}) collective-permute-start(bf16[288,512]{1,0:T(8,128)(2,1)S(1)} %add_convert_fusion.1), channel_id=1, source_target_pairs={{2,0},{3,1},{4,2},{5,3},{6,4},{7,5},{10,8},{11,9},{12,10},{13,11},... | collective-permute-start | bytes 884744 | tf_op jit(solution)/shard_map/ppermute | solution.py:327
  82.2 4.8 %copy-start.11 = (bf16[128,1024]{1,0:T(8,128)(2,1)S(1)}, bf16[128,1024]{1,0:T(8,128)(2,1)}, u32[]{:S(2)}) copy-start(bf16[128,1024]{1,0:T(8,128)(2,1)} %get-tuple-element.41) | copy-start | bytes 786436
  82.2 4.8 %copy-start.15 = (bf16[128,1024]{1,0:T(8,128)(2,1)S(1)}, bf16[128,1024]{1,0:T(8,128)(2,1)}, u32[]{:S(2)}) copy-start(bf16[128,1024]{1,0:T(8,128)(2,1)} %get-tuple-element.42) | copy-start | bytes 786436
  82.2 9.0 %collective-permute-start.20 = (bf16[288,512]{1,0:T(8,128)(2,1)S(1)}, bf16[288,512]{1,0:T(8,128)(2,1)S(1)}, u32[]{:S(2)}, u32[]{:S(2)}) collective-permute-start(bf16[288,512]{1,0:T(8,128)(2,1)S(1)} %add_convert_fusion.2), channel_id=1, source_target_pairs={{0,2},{1,3},{2,4},{3,5},{4,6},{5,7},{8,10},{9,11},{10,12},{11,13},... | collective-permute-start | bytes 884744 | tf_op jit(solution)/shard_map/ppermute | solution.py:327
  87.1 1.2 %copy-start.10 = (bf16[128,1024]{1,0:T(8,128)(2,1)S(1)}, bf16[128,1024]{1,0:T(8,128)(2,1)}, u32[]{:S(2)}) copy-start(bf16[128,1024]{1,0:T(8,128)(2,1)} %get-tuple-element.35) | copy-start | bytes 786436
  87.1 1.2 %copy-start.14 = (bf16[128,1024]{1,0:T(8,128)(2,1)S(1)}, bf16[128,1024]{1,0:T(8,128)(2,1)}, u32[]{:S(2)}) copy-start(bf16[128,1024]{1,0:T(8,128)(2,1)} %get-tuple-element.38) | copy-start | bytes 786436
  88.3 2.9 %copy-start.21 = (bf16[256,512]{1,0:T(8,128)(2,1)S(1)}, bf16[256,512]{1,0:T(8,128)(2,1)}, u32[]{:S(2)}) copy-start(bf16[256,512]{1,0:T(8,128)(2,1)} %get-tuple-element.53) | copy-start | bytes 786436
  89.5 1.8 %copy-start.9 = (bf16[288,512]{1,0:T(8,128)(2,1)S(1)}, bf16[288,512]{1,0:T(8,128)(2,1)}, u32[]{:S(2)}) copy-start(bf16[288,512]{1,0:T(8,128)(2,1)} %get-tuple-element.56) | copy-start | bytes 884740
  91.5 1.6 %collective-permute-start.23 = (bf16[288,512]{1,0:T(8,128)(2,1)S(1)}, bf16[288,512]{1,0:T(8,128)(2,1)S(1)}, u32[]{:S(2)}, u32[]{:S(2)}) collective-permute-start(bf16[288,512]{1,0:T(8,128)(2,1)S(1)} %pad_maximum_fusion.2), channel_id=1, source_target_pairs={{0,1},{1,0},{2,3},{3,2},{4,5},{5,4},{6,7},{7,6},{8,9},{9,8},{10,11... | collective-permute-start | bytes 884744 | tf_op jit(solution)/shard_map/ppermute | solution.py:327
  93.6 5.2 %collective-permute-start.25 = (f32[8,128]{1,0:T(8,128)S(1)}, f32[8,128]{1,0:T(8,128)S(1)}, u32[]{:S(2)}, u32[]{:S(2)}) collective-permute-start(f32[8,128]{1,0:T(8,128)S(1)} %broadcast_select_fusion.2), channel_id=1, source_target_pairs={{0,16},{8,24},{16,0},{24,8},{1,17},{9,25},{17,1},{25,9},{2,18},{10... | collective-permute-start | bytes 12296 | tf_op jit(solution)/shard_map/ppermute | solution.py:489
  95.5 4.5 %collective-permute-start.26 = (f32[8,128]{1,0:T(8,128)S(1)}, f32[8,128]{1,0:T(8,128)S(1)}, u32[]{:S(2)}, u32[]{:S(2)}) collective-permute-start(f32[8,128]{1,0:T(8,128)S(1)} %broadcast_select_fusion.2), channel_id=1, source_target_pairs={{0,24},{8,16},{16,8},{24,0},{1,25},{9,17},{17,9},{25,1},{2,26},{10... | collective-permute-start | bytes 12296 | tf_op jit(solution)/shard_map/ppermute | solution.py:489
  96.7 3.6 %collective-permute-start.24 = (f32[8,128]{1,0:T(8,128)S(1)}, f32[8,128]{1,0:T(8,128)S(1)}, u32[]{:S(2)}, u32[]{:S(2)}) collective-permute-start(f32[8,128]{1,0:T(8,128)S(1)} %broadcast_select_fusion.2), channel_id=1, source_target_pairs={{0,8},{8,0},{16,24},{24,16},{1,9},{9,1},{17,25},{25,17},{2,10},{10... | collective-permute-start | bytes 12296 | tf_op jit(solution)/shard_map/ppermute | solution.py:489
  (2 other events, 1.4 us)
